TPU v7x, 256 devices: a whole 4x4x8 slice. The times are simulated.
256 devices in a mesh: dp: 16 (over z, core), mp: 16 (over y, x).
Axes of the slice: x: 4, y: 4, z: 8, core: 2. Of those that a mesh axis runs over, the one named last changes fastest.
Arguments:
- hidden_states: bfloat16 [256, 640, 1280], P(('dp', 'mp')), may hold values from -6 to 6
- ln_attn_gain: float32 [1280], replicated, may hold values from 0.1 to 1.9
- w_qkv: bfloat16 [1280, 16, 192], P(None, 'mp'), may hold values from -0.15625 to 0.15625
- output_weight: bfloat16 [64, 16, 1280], P(None, 'mp'), may hold values from -0.75 to 0.75
- ln_final_gain: float32 [1280], replicated, may hold values from 0.1 to 1.9
- dense_weight: bfloat16 [1280, 1280], replicated, may hold values from -0.15625 to 0.15625
- decoder_weight: bfloat16 [1280, 33], replicated, may hold values from -0.5390625 to 0.5390625
- decoder_bias: float32 [33], replicated, may hold values from -4 to 4
- seq_tokens: int32 [24, 640], replicated, may hold values from 4 to 23
- seq_lengths: int32 [24], replicated, may hold values from 128 to 640
- copy_sequence: int32 [256], replicated, may hold values from 0 to 23
- mask_code: int32 [256, 64], replicated, may hold values from 0 to 1048575
- copy_owner: int32 [256], replicated, may hold values from 0 to 255, each once
Outputs:
- pll: float32 [256, 64], P('dp', 'mp')
Inputs may be any that keep to these rules, and one draw needn't show every extreme that they name: `seq_tokens`: amino-acid token ids. `copy_owner`: every row of pll is named by exactly one copy.
All inputs are finite; a program needn't handle non-finite values.
Results may differ from a plain program's by a relative error of at most 0.0038.
Values may be sent and summed in bfloat16 or wider, within the bound.
No kernel may reach another device: no remote copies, remote signals or barrier semaphores. Data moves between devices by JAX's collectives and lax.ppermute only.
A program may use at most 128 MiB of HBM per device.

v0:
```python
import jax
import jax.numpy as jnp
from jax import lax
from jax.sharding import PartitionSpec as P

epsilon = 1e-05


def layer_norm(inputs):
    average = jnp.mean(inputs, axis=-1, keepdims=True)
    centred = inputs - average
    variance = jnp.mean(centred * centred, axis=-1, keepdims=True)
    return centred * lax.rsqrt(variance + epsilon)


def rotary_tables(seq_span, head_size):
    half_width = head_size // 2
    frequency = 1.0 / 10000.0 ** (jnp.arange(half_width, dtype=jnp.float32) * (2.0 / head_size))
    angles = jnp.arange(seq_span, dtype=jnp.float32)[:, None] * frequency[None, :]
    angles = jnp.concatenate([angles, angles], axis=-1)
    return (jnp.cos(angles), jnp.sin(angles))


def rotate(inputs, cosine, sine):
    half_width = inputs.shape[-1] // 2
    turned = jnp.concatenate([-inputs[..., half_width:], inputs[..., :half_width]], axis=-1)
    return inputs * cosine + turned * sine


def score_rows(residual, ln_final_gain, dense_weight, decoder_weight, decoder_bias, targets):
    feature = residual.shape[-1]
    normed_final = (layer_norm(residual) * ln_final_gain).astype(jnp.bfloat16).reshape(-1, feature)
    dense_out = jnp.dot(normed_final, dense_weight, preferred_element_type=jnp.float32)
    headed = layer_norm(jax.nn.gelu(dense_out, approximate=False)).astype(jnp.bfloat16)
    logits = jnp.dot(headed, decoder_weight, preferred_element_type=jnp.float32) + decoder_bias
    log_probs = logits - jax.nn.logsumexp(logits, axis=-1, keepdims=True)
    vocab_ids = jnp.arange(logits.shape[-1], dtype=jnp.int32)
    flat_targets = targets.reshape(-1)
    picked = jnp.sum(
        jnp.where(flat_targets[:, None] == vocab_ids[None, :], log_probs, 0.0), axis=-1
    )
    return picked.reshape(targets.shape)


def copy_meta(first, amount, tables):
    seq_tokens, seq_lengths, copy_sequence, mask_code = tables
    sequence = lax.dynamic_slice_in_dim(copy_sequence, first, amount, 0)
    codes = lax.dynamic_slice_in_dim(mask_code, first, amount, 0)
    seq_ids = jnp.arange(seq_lengths.shape[0], dtype=jnp.int32)
    lengths = jnp.sum(
        jnp.where(sequence[:, None] == seq_ids[None, :], seq_lengths[None, :], 0), axis=1
    )
    positions = codes % lengths[:, None]
    return (sequence, lengths, positions)


def attend_projected(projected, out_part, lengths, positions, cosine, sine):
    copies, seq_span, head_count, three, head_size = projected.shape
    key_matrix = rotate(
        projected[:, :, :, 1], cosine[None, :, None, :], sine[None, :, None, :]
    ).astype(jnp.bfloat16)
    value_matrix = projected[:, :, :, 2].astype(jnp.bfloat16)
    query_matrix = projected[jnp.arange(copies)[:, None], positions, :, 0] * head_size ** (-0.5)
    query_matrix = rotate(
        query_matrix, cosine[positions][:, :, None, :], sine[positions][:, :, None, :]
    ).astype(jnp.bfloat16)
    attention_logits = jnp.einsum(
        "cmhd,clhd->chml", query_matrix, key_matrix, preferred_element_type=jnp.float32
    )
    alive = jnp.arange(seq_span, dtype=jnp.int32)[None, :] < lengths[:, None]
    attention_logits = jnp.where(alive[:, None, None, :], attention_logits, -1e30)
    largest = jnp.max(attention_logits, axis=-1, keepdims=True)
    weights = jnp.exp(attention_logits - largest)
    attention_probs = (weights / jnp.sum(weights, axis=-1, keepdims=True)).astype(jnp.bfloat16)
    context_vectors = jnp.einsum(
        "chml,clhd->cmhd", attention_probs, value_matrix, preferred_element_type=jnp.float32
    ).astype(jnp.bfloat16)
    return jnp.einsum(
        "cmhd,dhe->cme", context_vectors, out_part, preferred_element_type=jnp.float32
    )


def on_device(
    hidden_states,
    ln_attn_gain,
    w_qkv,
    output_weight,
    ln_final_gain,
    dense_weight,
    decoder_weight,
    decoder_bias,
    seq_tokens,
    seq_lengths,
    copy_sequence,
    mask_code,
    copy_owner,
):
    lane_copies, seq_span, feature = hidden_states.shape
    model_size = lax.axis_size("mp")
    model_index = lax.axis_index("mp")
    group_copies = lane_copies * model_size
    head_size = output_weight.shape[0]
    mask_count = mask_code.shape[1]
    own_masks = mask_count // model_size
    cosine, sine = rotary_tables(seq_span, head_size)
    tables = (seq_tokens, seq_lengths, copy_sequence, mask_code)
    group_first = lax.axis_index("dp") * group_copies
    sequence, lengths, positions = copy_meta(group_first, group_copies, tables)
    targets = jnp.take_along_axis(seq_tokens[sequence], positions, axis=1)
    own_targets = lax.dynamic_slice_in_dim(targets, model_index * own_masks, own_masks, 1)
    lane_start = model_index * lane_copies
    lane_positions = lax.dynamic_slice_in_dim(positions, lane_start, lane_copies, 0)
    normed = (layer_norm(hidden_states.astype(jnp.float32)) * ln_attn_gain).astype(jnp.bfloat16)
    own_rows = hidden_states[jnp.arange(lane_copies)[:, None], lane_positions].astype(jnp.float32)
    lane_lengths = lax.dynamic_slice_in_dim(lengths, lane_start, lane_copies, 0)
    qkv_part = lax.all_gather(w_qkv, "mp", axis=1, tiled=True)
    out_part = lax.all_gather(output_weight, "mp", axis=1, tiled=True)
    count = qkv_part.shape[1]
    made = jnp.dot(
        normed.reshape(-1, feature),
        qkv_part.reshape(feature, -1),
        preferred_element_type=jnp.float32,
    )
    made = made.reshape(lane_copies, seq_span, count, 3, head_size)
    attention_mixed = attend_projected(made, out_part, lane_lengths, lane_positions, cosine, sine)
    lane_rows = own_rows + attention_mixed
    residual = lax.all_to_all(lane_rows, "mp", split_axis=1, concat_axis=0, tiled=True)
    attention_logits = score_rows(
        residual, ln_final_gain, dense_weight, decoder_weight, decoder_bias, own_targets
    )
    everything = lax.all_gather(attention_logits, "dp", axis=0, tiled=True)
    wanted = group_first + jnp.arange(group_copies, dtype=jnp.int32)
    copy_ids = jnp.arange(copy_owner.shape[0], dtype=jnp.int32)
    source = jnp.sum(
        jnp.where(copy_owner[None, :] == wanted[:, None], copy_ids[None, :], 0), axis=1
    )
    return everything[source]


def solution(mesh):
    placed = (
        P(("dp", "mp"), None, None),
        P(),
        P(None, "mp", None),
        P(None, "mp", None),
        P(),
        P(),
        P(),
        P(),
        P(),
        P(),
        P(),
        P(),
        P(),
    )
    return jax.shard_map(
        on_device, mesh=mesh, in_specs=placed, out_specs=P("dp", "mp"), check_vma=False
    )
```

profile of v0, /device:TPU:1, one launch (start us, length us, event | category | flops | bytes accessed | tf_op | source)
XLA Modules:
  0.0 194.8 jit_solution(9055554466586441534)
XLA Ops:
  6.5 0.0 copy-start
  6.5 0.0 all-gather.4.cloned.1.call-start
  6.5 0.7 all-gather.4.cloned.1.call-update
  7.3 0.0 all-gather.6.cloned.1.call-start
  7.3 0.7 all-gather.6.cloned.1.call-update
  8.0 0.8 compare_select_fusion.3
  8.8 0.8 select_reduce_fusion.3
  9.6 0.8 constant_dynamic-slice_fusion.1
  10.5 0.1 copy.52
  10.5 0.2 compare_select_fusion
  10.8 0.7 dynamic_slice.19
  11.5 0.1 iota_multiply_fusion
  11.6 2.1 %fusion.52 = (f32[640,64]{1,0:T(8,128)}, f32[640,64]{1,0:T(8,128)}) fusion(f32[640,32]{1,0:T(8,128)S(1)} %iota_multiply_fusion), kind=kLoop, calls=%fused_computation.81 | loop fusion | flops 40960 | bytes 409600 | tf_op jit(solution)/shard_map/cos | solution.py:21
  13.7 1.2 iota_compare_fusion.2
  15.0 0.1 reshape.339
  15.0 1.4 gather_fusion
  16.5 8.6 %gather_fusion.6 = s32[1024]{0:T(1024)S(1)} fusion(s32[16,640]{1,0:T(8,128)S(1)} %gather_fusion, s32[1024]{0:T(1024)S(1)} %reshape.339), kind=kCustom, calls=%fused_computation.6 | custom fusion | bytes 16384 | tf_op jit(solution)/shard_map/jit(take_along_axis)/gather | solution.py:109
  25.1 0.0 copy-start.7
  25.1 0.1 reshape.342
  25.2 0.1 dynamic-slice_select_fusion
  25.2 1.1 copy.41
  26.4 1.6 gather_fusion.3
  28.0 1.6 gather_fusion.4
  29.5 1.8 copy.42
  31.3 0.6 eq.57
  31.9 2.6 %gather_fusion.1 = bf16[64,1280]{1,0:T(8,128)(2,1)} fusion(bf16[1,640,1280]{2,1,0:T(8,128)(2,1)} %param.13, s32[64]{0:T(128)S(1)} %or_bitcast_fusion.1), kind=kCustom, calls=%fused_computation.1 | custom fusion | bytes 328192 | tf_op jit(solution)/shard_map/gather | solution.py:114
  34.5 0.0 copy-done.7
  34.5 0.7 select_reduce_fusion.2
  35.2 1.8 convert_reduce_fusion
  36.9 0.0 copy-done.1
  37.0 0.6 fusion.3
  37.5 49.6 %all-gather.4.cloned.1.call-done = bf16[1280,16,192]{0,2,1:T(8,128)(2,1)} async-done(((bf16[1280,1,192]{0,2,1:T(8,128)(2,1)}), bf16[1280,16,192]{0,2,1:T(8,128)(2,1)}) %all-gather.4.cloned.1.call-update) | async-done | bytes 7864336 | tf_op jit(solution)/shard_map/all_gather | solution.py:116
  87.2 11.3 %convolution_bitcast_fusion = f32[1,640,16,3,64]{1,4,3,2,0:T(8,128)} fusion(bf16[16,3,64,1280]{3,2,1,0:T(8,128)(2,1)} %bitcast.96, bf16[1,640,1280]{2,1,0:T(8,128)(2,1)} %param.13, f32[1280]{0:T(1024)} %param.14, f32[640]{0:T(1024)S(1)} %add_rsqrt_fusion, f32[640]{0:T(1024)S(1)} %broadcast_multiply_fusion.1), kind=kOutput, calls=%fused_computation.15 | convolution fusion | flops 5037260800 | bytes 17377280 | tf_op jit(solution)/shard_map/dot_general | solution.py:119
  98.5 15.1 %copy.40 = f32[1,640,16,3,64]{4,2,3,1,0:T(8,128)} copy(f32[1,640,16,3,64]{1,4,3,2,0:T(8,128)} %convolution_bitcast_fusion) | data formatting | bytes 15728640 | tf_op jit(solution)/shard_map/dot_general | solution.py:119
  113.6 7.0 %gather_fusion.2 = f32[64,16,64]{2,1,0:T(8,128)} fusion(f32[1,640,16,3,64]{4,2,3,1,0:T(8,128)} %copy.40, s32[64]{0:T(128)S(1)} %or_bitcast_fusion), kind=kCustom, calls=%fused_computation.2 | custom fusion | bytes 525056 | tf_op jit(solution)/shard_map/gather | solution.py:63
  120.6 1.1 multiply_bitcast_fusion
  121.7 0.2 fusion.36
  121.9 0.0 copy-done.2
  122.0 0.2 fusion.38
  122.2 1.9 slice_bitcast_fusion
  124.1 0.0 copy-start.3
  124.1 0.2 fusion.23
  124.3 0.7 copy-done.3
  125.0 2.6 %fusion.18 = f32[16,64,640]{2,1,0:T(8,128)S(1)} fusion(f32[640,16,32]{0,2,1:T(8,128)S(1)} %get-tuple-element.10, f32[640,16,32]{0,2,1:T(8,128)S(1)} %get-tuple-element.9, f32[1,640,16,3,64]{1,4,3,2,0:T(8,128)} %convolution_bitcast_fusion, f32[640,64]{0,1:T(8,128)S(1)} %copy-done.3, f32[640,64]{0,1:T(8,128)S(1)} %copy.41, bf16[64,16,64]{2,1,0:T(8,128)(2,1)S(1)} %fusion.38), kind=kOutput, calls=%fused_computation.33 | convolution fusion | flops 87162880 | bytes 8323072 | tf_op jit(solution)/shard_map/cmhd,clhd->chml/dot_general | solution.py:67
  127.7 2.1 %fusion.66 = (f32[16,64]{1,0:T(8,128)S(1)}, f32[16,64,640]{2,1,0:T(8,128)}) fusion(f32[16,64,640]{2,1,0:T(8,128)S(1)} %fusion.18, pred[640]{0:T(1024)(128)(4,1)S(1)} %copy-done.8), kind=kOutput, calls=%fused_computation.128 | output fusion | flops 2622079 | bytes 5247616 | tf_op jit(solution)/shard_map/sub | solution.py:73
  129.8 10.6 %all-gather.6.cloned.1.call-done = bf16[64,16,1280]{2,0,1:T(8,128)(2,1)} async-done(((bf16[64,1,1280]{2,0,1:T(8,128)(2,1)}), bf16[64,16,1280]{2,0,1:T(8,128)(2,1)}) %all-gather.6.cloned.1.call-update) | async-done | bytes 2621456 | tf_op jit(solution)/shard_map/all_gather | solution.py:117
  140.3 5.1 %fusion.9 = f32[1,64,1280]{2,1,0:T(8,128)} fusion(bf16[64,16,1280]{2,0,1:T(8,128)(2,1)} %all-gather.6.cloned.1.call-done, f32[16,64,640]{2,1,0:T(8,128)} %get-tuple-element.16, f32[16,64]{1,0:T(8,128)S(1)} %get-tuple-element.15, f32[1,640,16,3,64]{1,4,3,2,0:T(8,128)} %convolution_bitcast_fusion, bf16[64,1280]{1,0:T(8,128)(2,1)S(1)} %copy-done.4), kind=kOutput, calls=%fused_computation.26 | convolution fusion | flops 253198336 | bytes 7049216 | tf_op jit(solution)/shard_map/cmhd,dhe->cme/dot_general | solution.py:78
  145.5 2.0 %copy.45 = f32[1,64,1280]{2,0,1:T(1,128)} copy(f32[1,64,1280]{2,1,0:T(8,128)} %fusion.9) | data formatting | bytes 655360 | tf_op jit(solution)/shard_map/add | solution.py:126
  147.5 4.4 %all-to-all-start = ((f32[1,64,1280]{2,0,1:T(1,128)}), f32[1,64,1280]{2,0,1:T(1,128)}, u32[]{:S(2)}, u32[]{:S(2)}) async-start(f32[1,64,1280]{2,0,1:T(1,128)} %copy.45), calls=%async_computation | async-start | bytes 655360 | tf_op jit(solution)/shard_map/all_to_all | solution.py:127
  151.9 7.8 %all-to-all-done = f32[1,64,1280]{2,0,1:T(1,128)} async-done(((f32[1,64,1280]{2,0,1:T(1,128)}), f32[1,64,1280]{2,0,1:T(1,128)}, u32[]{:S(2)}, u32[]{:S(2)}) %all-to-all-start) | async-done | bytes 327712 | tf_op jit(solution)/shard_map/all_to_all | solution.py:127
  159.7 1.5 reduce_sum.105
  161.3 2.0 %multiply_reduce_fusion.1 = f32[64]{0:T(128)S(1)} fusion(f32[1,64,1280]{2,0,1:T(1,128)} %all-to-all-done, f32[64]{0:T(128)S(1)} %broadcast_multiply_fusion.3), kind=kLoop, calls=%fused_computation.76 | loop fusion | flops 245696 | bytes 328192 | tf_op jit(solution)/shard_map/reduce_sum | solution.py:12
  163.3 0.0 copy-start.5
  163.3 0.0 copy-start.9
  163.3 2.3 %fusion.67 = (f32[64]{0:T(128)S(1)}, f32[64,1280]{1,0:T(8,128)S(1)}) fusion(bf16[1280,1280]{1,0:T(8,128)(2,1)S(1)} %copy-done, f32[1,64,1280]{2,0,1:T(1,128)} %all-to-all-done, f32[1280]{0:T(1024)S(1)} %copy-done.11, f32[64]{0:T(128)S(1)} %add_rsqrt_fusion.2, f32[64]{0:T(128)S(1)} %broadcast_multiply_fusion.3), kind=kOutput, calls=%fused_computation.129 | convolution fusion | flops 215367616 | bytes 3938048 | tf_op jit(solution)/shard_map/dot_general | solution.py:33
  165.6 0.2 multiply_reduce_fusion
  165.9 0.3 fusion.68
  166.2 0.0 copy-done.6
  166.2 0.1 reshape.362
  166.3 0.1 copy.46
  166.4 20.2 %all-gather = f32[16,16,4]{1,2,0:T(4,128)S(1)} all-gather(f32[1,16,4]{1,2,0:T(4,128)S(1)} %copy.46), channel_id=1, replica_groups=mesh['dp'=16,'mp'=16] {'dp'}, dimensions={0}, use_global_device_ids=true | all-gather | bytes 4352 | tf_op jit(solution)/shard_map/all_gather | solution.py:131
  186.6 0.2 copy.47
  186.8 0.6 gather_fusion.5
  187.3 0.7 copy.48
  (41 shorter events, 0.3 us)
Async XLA Ops:
  6.5 156.7 %copy-start = (bf16[1280,1280]{1,0:T(8,128)(2,1)S(1)}, bf16[1280,1280]{1,0:T(8,128)(2,1)}, u32[]{:S(2)}) copy-start(bf16[1280,1280]{1,0:T(8,128)(2,1)} %param.18) | copy-start | bytes 9830404
  6.5 80.7 %all-gather.4.cloned.1.call-start = ((), (), s32[]{:S(2)}) async-start(), calls=%async_computation.1 | async-start | bytes 8355840 | tf_op jit(solution)/shard_map/all_gather | solution.py:116
  7.3 133.1 %all-gather.6.cloned.1.call-start = ((), (), s32[]{:S(2)}) async-start(), calls=%async_computation.2 | async-start | bytes 2785280 | tf_op jit(solution)/shard_map/all_gather | solution.py:117
  25.1 9.4 %copy-start.7 = (s32[256]{0:T(256)S(1)}, s32[256]{0:T(256)}, u32[]{:S(2)}) copy-start(s32[256]{0:T(256)} %param.25) | copy-start | bytes 3076
  34.5 2.5 %copy-start.1 = (bf16[1,640,1280]{2,1,0:T(8,128)(2,1)S(1)}, bf16[1,640,1280]{2,1,0:T(8,128)(2,1)}, u32[]{:S(2)}) copy-start(bf16[1,640,1280]{2,1,0:T(8,128)(2,1)} %param.13) | copy-start | bytes 4915204
  120.6 1.4 copy-start.2
  124.1 0.9 copy-start.3
  125.0 2.6 %copy-start.8 = (pred[640]{0:T(1024)(128)(4,1)S(1)}, pred[640]{0:T(1024)(128)(4,1)}, u32[]{:S(2)}) copy-start(pred[640]{0:T(1024)(128)(4,1)} %iota_compare_fusion.2) | copy-start | bytes 1924
  127.6 12.7 %copy-start.4 = (bf16[64,1280]{1,0:T(8,128)(2,1)S(1)}, bf16[64,1280]{1,0:T(8,128)(2,1)}, u32[]{:S(2)}) copy-start(bf16[64,1280]{1,0:T(8,128)(2,1)} %gather_fusion.1) | copy-start | bytes 491524
  140.3 11.6 %copy-start.10 = (s32[16]{0:T(128)S(1)}, s32[16]{0:T(128)}, u32[]{:S(2)}) copy-start(s32[16]{0:T(128)} %select_reduce_fusion.2) | copy-start | bytes 196
  140.3 22.9 %copy-start.11 = (f32[1280]{0:T(1024)S(1)}, f32[1280]{0:T(1024)}, u32[]{:S(2)}) copy-start(f32[1280]{0:T(1024)} %param.17) | copy-start | bytes 15364
  147.5 12.2 %all-to-all-start = ((f32[1,64,1280]{2,0,1:T(1,128)}), f32[1,64,1280]{2,0,1:T(1,128)}, u32[]{:S(2)}, u32[]{:S(2)}) async-start(f32[1,64,1280]{2,0,1:T(1,128)} %copy.45), calls=%async_computation | async-start | bytes 655360 | tf_op jit(solution)/shard_map/all_to_all | solution.py:127
  163.3 2.6 %copy-start.5 = (bf16[1280,33]{0,1:T(8,128)(2,1)S(1)}, bf16[1280,33]{0,1:T(8,128)(2,1)}, u32[]{:S(2)}) copy-start(bf16[1280,33]{0,1:T(8,128)(2,1)} %param.19) | copy-start | bytes 253444
  163.3 2.6 %copy-start.9 = (f32[33]{0:T(128)S(1)}, f32[33]{0:T(128)}, u32[]{:S(2)}) copy-start(f32[33]{0:T(128)} %param.20) | copy-start | bytes 400
  163.3 2.9 %copy-start.6 = (s32[64]{0:T(128)S(1)}, s32[64]{0:T(128)}, u32[]{:S(2)}) copy-start(s32[64]{0:T(128)} %eq.57) | copy-start | bytes 772
Sparse Core Ops, SparseCore 0:
  9.8 77.3 all-gather.3
  89.6 50.6 all-gather.5
where the time goes:
time: 196 us; the launch traced here: 195 us
  waiting for transfers between devices  69.4 us (35%)
  local copies, waits for them, and re-layouts  49.3 us (25%)
  matrix products  21.6 us (11%)
  blocking collectives  20.2 us (10%)
  other arithmetic  16.1 us (8%)
  between operations  13.7 us (7%)
  starting transfers between devices  4.43 us (2%)
    all_gather x1, waiting for transfers between devices, on_device(): qkv_part = lax.all_gather(w_qkv, 'mp', axis=1, tiled=True)  49.6 us
    all_gather x1, blocking collectives, on_device(): everything = lax.all_gather(attention_logits, 'dp', axis=0, tiled=True)  20.2 us
    dot_general x1, local copies, waits for them, and re-layouts, on_device(): jnp.dot(normed.reshape(-1, feature), qkv_part.reshape(feature, -1), prefe...  15.1 us
    dot_general x1, matrix products, on_device(): jnp.dot(normed.reshape(-1, feature), qkv_part.reshape(feature, -1), prefe...  11.3 us
    all_gather x1, waiting for transfers between devices, on_device(): out_part = lax.all_gather(output_weight, 'mp', axis=1, tiled=True)  10.6 us
    gather x4, local copies, waits for them, and re-layouts, on_device(): targets = jnp.take_along_axis(seq_tokens[sequence], positions, axis=1)  10.2 us
    all_to_all x1, waiting for transfers between devices, on_device(): lax.all_to_all(lane_rows, 'mp', split_axis=1, concat_axis=0, tiled=True)  7.8 us
    gather x1, local copies, waits for them, and re-layouts, attend_projected(): projected[jnp.arange(copies)[:, None], positions, :, 0]  6.96 us
  transfers between devices with their start and end apart: 3, of which 3 were waited for; matrix products, arithmetic and copies ran while one was open for 37% of the time, Pallas kernels for 0%

commit v1 on v0

v1 whole, which is shorter than its diff:
```python
import numpy as np
import jax
import jax.numpy as jnp
from jax import lax
from jax.experimental import pallas as pl
from jax.experimental.pallas import tpu as pltpu
from jax.sharding import Mesh, PartitionSpec as P

epsilon = 1e-05
F32 = jnp.float32
BF16 = jnp.bfloat16
VMEM = pltpu.MemorySpace.VMEM
SMEM = pltpu.MemorySpace.SMEM


def rotary_tables(seq_span, head_size):
    half = head_size // 2
    power = (np.arange(half, dtype=np.float32) * np.float32(2.0 / head_size)).astype(np.float32)
    frequency = (np.float32(1.0) / np.power(np.float32(10000.0), power)).astype(np.float32)
    angles = (np.arange(seq_span, dtype=np.float32)[:, None] * frequency[None, :]).astype(np.float32)
    cosine = np.cos(angles.astype(np.float64)).astype(np.float32)
    sine = np.sin(angles.astype(np.float64)).astype(np.float32)
    cos_table = np.concatenate([cosine] * 4, axis=1)
    sin_table = np.concatenate([-sine, sine] * 2, axis=1)
    return cos_table, sin_table


def nt_dot(a, b):
    return lax.dot_general(a, b, (((1,), (1,)), ((), ())), preferred_element_type=F32)


def nn_dot(a, b, **options):
    return lax.dot_general(a, b, (((1,), (0,)), ((), ())), preferred_element_type=F32, **options)


def rotate(part, cos_table, sin_table, half):
    width = part.shape[1]
    lane = lax.broadcasted_iota(jnp.int32, part.shape, 1) % (2 * half)
    turned = jnp.where(
        lane < half,
        pltpu.roll(part, width - half, 1),
        pltpu.roll(part, half, 1),
    )
    return part * cos_table + turned * sin_table


def whole(space=VMEM):
    return pl.BlockSpec(memory_space=space)


def call(kernel, outs, n_smem, args, vmem=48 * 1024 * 1024):
    specs = [whole(SMEM)] * n_smem + [whole()] * (len(args) - n_smem)
    return pl.pallas_call(
        kernel,
        out_shape=outs,
        in_specs=specs,
        out_specs=jax.tree.map(lambda _: whole(), outs),
        compiler_params=pltpu.CompilerParams(vmem_limit_bytes=vmem),
    )(*args)


def prepare_kernel(
    index_ref, sequence_ref, length_ref, codes_ref, tokens_ref, states_ref, gain_ref,
    cos_ref, sin_ref,
    normed_ref, picked_ref, rows_ref, qcos_ref, qsin_ref, targets_ref,
):
    copy = index_ref[0]
    sequence = sequence_ref[copy]
    length = length_ref[sequence]
    codes_all = codes_ref[...]
    lane = lax.broadcasted_iota(jnp.int32, codes_all.shape, 1)
    codes = jnp.sum(jnp.where(lane == copy, codes_all, 0), axis=1, keepdims=True)
    quotient = jnp.floor(codes.astype(F32) / length.astype(F32)).astype(jnp.int32)
    positions = codes - quotient * length
    positions = jnp.where(positions < 0, positions + length, positions)
    positions = jnp.where(positions >= length, positions - length, positions)
    span = states_ref.shape[0]
    spot = lax.broadcasted_iota(jnp.int32, (codes.shape[0], span), 1)
    hit = spot == positions
    tokens = tokens_ref[pl.ds(sequence, 1), :]
    targets = jnp.sum(jnp.where(hit, tokens, 0), axis=1, keepdims=True)
    targets_ref[...] = jnp.broadcast_to(targets, targets_ref.shape)
    hot = hit.astype(F32)
    qcos_ref[...] = nn_dot(hot, cos_ref[...], precision=lax.Precision.HIGHEST)
    qsin_ref[...] = nn_dot(hot, sin_ref[...], precision=lax.Precision.HIGHEST)
    hot = hot.astype(BF16)
    block = 128
    gain = gain_ref[...]

    def step(i, carry):
        at = pl.multiple_of(i * block, block)
        values = states_ref[pl.ds(at, block), :].astype(F32)
        average = jnp.mean(values, axis=1, keepdims=True)
        centred = values - average
        variance = jnp.mean(centred * centred, axis=1, keepdims=True)
        normed_ref[pl.ds(at, block), :] = (
            centred * lax.rsqrt(variance + epsilon) * gain
        ).astype(BF16)
        return carry

    lax.fori_loop(0, span // block, step, 0)
    rows_ref[...] = nn_dot(hot, states_ref[...])
    picked_ref[...] = nn_dot(hot, normed_ref[...]).astype(BF16)


def keys_kernel(
    index_ref, sequence_ref, length_ref, core_ref, normed_ref, picked_ref, mine_refs, other_refs,
    cos_ref, sin_ref, qcos_ref, qsin_ref, probs_ref,
):
    half = 32
    length = length_ref[sequence_ref[index_ref[0]]]
    first = core_ref[0] == 0
    mine = jnp.concatenate([r[...] for r in mine_refs], axis=0)
    other = jnp.concatenate([r[...] for r in other_refs], axis=0)
    key_weight = jnp.where(first, mine, other)
    query_weight = jnp.where(first, other, mine)
    keys = nt_dot(normed_ref[...], key_weight)
    queries = nt_dot(picked_ref[...], query_weight) * 0.125
    pairs = keys.shape[1] // 128
    keys = jnp.concatenate(
        [rotate(keys[:, 128 * i : 128 * i + 128], cos_ref[...], sin_ref[...], half) for i in range(pairs)],
        axis=1,
    ).astype(BF16)
    queries = jnp.concatenate(
        [rotate(queries[:, 128 * i : 128 * i + 128], qcos_ref[...], qsin_ref[...], half) for i in range(pairs)],
        axis=1,
    ).astype(BF16)
    heads = keys.shape[1] // 64
    masks = queries.shape[0]
    spread = jnp.concatenate([queries] * heads, axis=0)
    row = lax.broadcasted_iota(jnp.int32, spread.shape, 0) // masks
    lane = lax.broadcasted_iota(jnp.int32, spread.shape, 1) // 64
    spread = jnp.where(row == lane, spread, jnp.zeros_like(spread))
    logits = nt_dot(spread, keys)
    alive = lax.broadcasted_iota(jnp.int32, logits.shape, 1) < length
    logits = jnp.where(alive, logits, -1e30)
    largest = jnp.max(logits, axis=1, keepdims=True)
    weights = jnp.exp(logits - largest)
    total = jnp.sum(weights, axis=1, keepdims=True)
    probs_ref[...] = (weights * (1.0 / total)).astype(BF16)


def values_kernel(core_ref, normed_ref, mine_refs, other_refs, values_ref, out_ref):
    first = core_ref[0] == 0
    mine = jnp.concatenate([r[...] for r in mine_refs], axis=0)
    other = jnp.concatenate([r[...] for r in other_refs], axis=0)
    value_weight = jnp.where(first, mine, other)
    out_ref[...] = jnp.where(first, other, mine)
    values_ref[...] = nt_dot(normed_ref[...], value_weight).astype(BF16)


def final_kernel(
    rows_ref, targets_ref, gain_ref, bias_ref, dense_ref, decoder_ref, probs_refs, values_refs,
    out_refs, scores_ref,
):
    masks = rows_ref.shape[0]
    residual = rows_ref[...]
    for column in range(len(values_refs)):
        probs = jnp.concatenate(
            [r[masks * column : masks * (column + 1), :] for r in probs_refs], axis=0
        )
        mixed = nn_dot(probs, values_refs[column][...])
        heads = mixed.shape[1] // 64
        lane = lax.broadcasted_iota(jnp.int32, (masks, mixed.shape[1]), 1) // 64
        context = jnp.zeros((masks, mixed.shape[1]), F32)
        for head in range(heads):
            context = jnp.where(lane == head, mixed[masks * head : masks * (head + 1), :], context)
        residual = residual + nn_dot(context.astype(BF16), out_refs[column][...])
    average = jnp.mean(residual, axis=1, keepdims=True)
    centred = residual - average
    variance = jnp.mean(centred * centred, axis=1, keepdims=True)
    normed = (centred * lax.rsqrt(variance + epsilon) * gain_ref[...]).astype(BF16)
    dense = nn_dot(normed, dense_ref[...])
    active = 0.5 * dense * (1.0 + lax.erf(dense * np.float32(0.5**0.5)))
    average = jnp.mean(active, axis=1, keepdims=True)
    centred = active - average
    variance = jnp.mean(centred * centred, axis=1, keepdims=True)
    headed = (centred * lax.rsqrt(variance + epsilon)).astype(BF16)
    logits = nt_dot(headed, decoder_ref[...]) + bias_ref[...]
    largest = jnp.max(logits, axis=1, keepdims=True)
    total = jnp.sum(jnp.exp(logits - largest), axis=1, keepdims=True)
    vocab = lax.broadcasted_iota(jnp.int32, logits.shape, 1)
    chosen = jnp.sum(jnp.where(vocab == targets_ref[:, 0:1], logits, 0.0), axis=1, keepdims=True)
    score = chosen - largest - jnp.log(total)
    row = lax.broadcasted_iota(jnp.int32, (masks, masks), 0)
    lane = lax.broadcasted_iota(jnp.int32, (masks, masks), 1)
    scores_ref[...] = jnp.sum(jnp.where(row == lane, score, 0.0), axis=0, keepdims=True)


def pull(array, axis, offset):
    size = lax.axis_size(axis)
    return lax.ppermute(array, axis, [((i + offset) % size, i) for i in range(size)])


def swap(array):
    return lax.ppermute(array, "core", [(0, 1), (1, 0)])


def gather_plane(block, first_axis, second_axis):
    near = [block] + [pull(block, first_axis, d) for d in (1, 2, 3)]
    near = jnp.concatenate(near, axis=0)
    half = near.shape[0] // 2
    ahead = pull(near, second_axis, 1)
    behind = pull(near, second_axis, 3)
    far = [pull(ahead[:half], second_axis, 1), pull(behind[half:], second_axis, 3)]
    return [[near], [ahead], [behind], far]


def on_device(
    hidden_states,
    ln_attn_gain,
    w_qkv,
    output_weight,
    ln_final_gain,
    dense_weight,
    decoder_weight,
    decoder_bias,
    seq_tokens,
    seq_lengths,
    copy_sequence,
    mask_code,
    copy_owner,
):
    _, seq_span, feature = hidden_states.shape
    head_size = output_weight.shape[0]
    masks = mask_code.shape[1]
    vocab = decoder_weight.shape[1]
    core = lax.axis_index("core")
    group = lax.axis_index(("z", "core"))
    member = lax.axis_index(("y", "x"))
    members = lax.axis_size(("y", "x"))
    groups = lax.axis_size(("z", "core"))
    copy = (group * members + member).astype(jnp.int32).reshape(1)
    core_at = core.astype(jnp.int32).reshape(1)

    turned = jnp.transpose(w_qkv[:, 0, :])
    query_weight = turned[:head_size]
    key_weight = turned[head_size : 2 * head_size]
    value_weight = turned[2 * head_size :]
    out_weight = output_weight[:, 0, :]
    first = core == 0
    key_side = gather_plane(jnp.where(first, key_weight, query_weight), "x", "y")
    value_side = gather_plane(jnp.where(first, value_weight, out_weight), "y", "x")

    cos_table, sin_table = (jnp.asarray(t) for t in rotary_tables(seq_span, head_size))
    shape = jax.ShapeDtypeStruct
    normed, picked, rows, qcos, qsin, targets = call(
        prepare_kernel,
        [
            shape((seq_span, feature), BF16),
            shape((masks, feature), BF16),
            shape((masks, feature), F32),
            shape((masks, 128), F32),
            shape((masks, 128), F32),
            shape((masks, 128), jnp.int32),
        ],
        3,
        (
            copy, copy_sequence, seq_lengths, mask_code.T, seq_tokens, hidden_states[0],
            ln_attn_gain.reshape(1, -1), cos_table, sin_table,
        ),
    )

    def keys_call(parts):
        others = [swap(p) for p in parts]
        n = len(parts)
        width = sum(p.shape[0] for p in parts)

        def kernel(a, b, c, d, e, f, *refs):
            keys_kernel(a, b, c, d, e, f, refs[:n], refs[n : 2 * n], *refs[2 * n :])

        return call(
            kernel,
            shape((masks * width // head_size, seq_span), BF16),
            4,
            (copy, copy_sequence, seq_lengths, core_at, normed, picked, *parts, *others,
             cos_table, sin_table, qcos, qsin),
        )

    def values_call(parts):
        others = [swap(p) for p in parts]
        n = len(parts)
        width = sum(p.shape[0] for p in parts)

        def kernel(a, b, *refs):
            values_kernel(a, b, refs[:n], refs[n : 2 * n], *refs[2 * n :])

        return call(
            kernel,
            [shape((seq_span, width), BF16), shape((width, feature), BF16)],
            1,
            (core_at, normed, *parts, *others),
        )

    order = (0, 1, 3, 2)
    probs = [keys_call(key_side[i]) for i in order]
    mixed = [values_call(value_side[i]) for i in order]
    values = [m[0] for m in mixed]
    outs = [m[1] for m in mixed]
    n = len(probs)

    def kernel(a, b, c, d, e, f, *refs):
        final_kernel(a, b, c, d, e, f, refs[:n], refs[n : 2 * n], refs[2 * n : 3 * n], refs[3 * n])

    scores = call(
        kernel,
        shape((1, masks), F32),
        0,
        (rows, targets, ln_final_gain.reshape(1, -1), decoder_bias.reshape(1, -1), dense_weight,
         decoder_weight.T, *probs, *values, *outs),
    )

    own = masks // members
    pieces = lax.all_to_all(scores.reshape(members, own), ("y", "x"), 0, 0, tiled=True)
    owners = lax.dynamic_slice_in_dim(copy_owner, group * members, members, 0)
    slots = jnp.arange(groups * members, dtype=jnp.int32).reshape(groups, members)
    placed = jnp.where(
        slots[:, :, None, None] == owners[None, None, :, None], pieces[None, None, :, :], 0.0
    )
    placed = jnp.sum(placed, axis=2).reshape(groups, members * own)
    arrived = lax.all_to_all(placed, ("z", "core"), 0, 0, tiled=True)
    return jnp.sum(arrived.reshape(groups, members, own), axis=0)


def solution(mesh):
    fine = Mesh(mesh.devices.reshape(8, 2, 4, 4), ("z", "core", "y", "x"))
    dp, mp = ("z", "core"), ("y", "x")
    placed = (
        P(("z", "core", "y", "x"), None, None),
        P(),
        P(None, mp, None),
        P(None, mp, None),
        P(),
        P(),
        P(),
        P(),
        P(),
        P(),
        P(),
        P(),
        P(),
    )
    return jax.shard_map(
        on_device, mesh=fine, in_specs=placed, out_specs=P(dp, mp), check_vma=False
    )
```

time: 196 us -> 114 us (0.58)
  waiting for transfers between devices: 69.4 us -> 25.4 us
  local copies, waits for them, and re-layouts: 49.3 us -> 12.8 us
  starting transfers between devices: 4.43 us -> 32 us
  Pallas kernels: 0 us -> 23.5 us
  matrix products: 21.6 us -> 0 us
  other arithmetic: 16.1 us -> 2.32 us
  between operations: 13.7 us -> 0.48 us
  blocking collectives: 20.2 us -> 17.4 us
    all_gather x2 -> x0, waiting for transfers between devices: 60.2 us -> none  [the longest x1 49.6 us: on_device(): qkv_part = lax.all_gather(w_qkv, 'mp', axis=1, tiled=True)]
    ppermute x0 -> x24, starting transfers between devices: none -> 27.8 us  [the longest x14 21.4 us: pull(): lax.ppermute(array, axis, [((i + offset) % size, i) for i in range(size)])]
    gather x10 -> x0, local copies, waits for them, and re-layouts: 24 us -> none  [the longest x4 10.2 us: on_device(): targets = jnp.take_along_axis(seq_tokens[sequence], positions, axis=1)]
    pallas_call x0 -> x10, Pallas kernels: none -> 23.5 us  [call(): pl.pallas_call(kernel, out_shape=outs, in_specs=specs, out_specs=jax.tree...]
    dot_general x5 -> x0, matrix products: 21.6 us -> none  [the longest x1 11.3 us: on_device(): jnp.dot(normed.reshape(-1, feature), qkv_part.reshape(feature, -1), prefe...]
    all_gather x1 -> x0, blocking collectives: 20.2 us -> none  [on_device(): everything = lax.all_gather(attention_logits, 'dp', axis=0, tiled=True)]
    ppermute x0 -> x24, waiting for transfers between devices: none -> 19.2 us  [the longest x14 19.2 us: pull(): lax.ppermute(array, axis, [((i + offset) % size, i) for i in range(size)])]
    all_to_all x0 -> x1, blocking collectives: none -> 17.4 us  [on_device(): arrived = lax.all_to_all(placed, ('z', 'core'), 0, 0, tiled=True)]
  transfers between devices with their start and end apart: 3 -> 25, of which waited for: 3 -> 8; matrix products, arithmetic and copies ran while one was open for 37% -> 2% of each run, Pallas kernels for 0% -> 15%
where the time goes in v1:
time: 114 us
  starting transfers between devices  32 us (28%)
  waiting for transfers between devices  25.4 us (22%)
  Pallas kernels  23.5 us (21%)
  blocking collectives  17.4 us (15%)
  local copies, waits for them, and re-layouts  12.8 us (11%)
  other arithmetic  2.32 us (2%)
    pallas_call x10, Pallas kernels, call(): pl.pallas_call(kernel, out_shape=outs, in_specs=specs, out_specs=jax.tree...  23.5 us
    ppermute x14, starting transfers between devices, pull(): lax.ppermute(array, axis, [((i + offset) % size, i) for i in range(size)])  21.4 us
    ppermute x14, waiting for transfers between devices, pull(): lax.ppermute(array, axis, [((i + offset) % size, i) for i in range(size)])  19.2 us
    all_to_all x1, blocking collectives, on_device(): arrived = lax.all_to_all(placed, ('z', 'core'), 0, 0, tiled=True)  17.4 us
    unnamed x56, local copies, waits for them, and re-layouts  8.48 us
    ppermute x10, starting transfers between devices, swap(): return lax.ppermute(array, 'core', [(0, 1), (1, 0)])  6.37 us
    all_to_all x1, waiting for transfers between devices, on_device(): lax.all_to_all(scores.reshape(members, own), ('y', 'x'), 0, 0, tiled=True)  6.15 us
    all_to_all x1, starting transfers between devices, on_device(): lax.all_to_all(scores.reshape(members, own), ('y', 'x'), 0, 0, tiled=True)  4.18 us
  transfers between devices with their start and end apart: 25, of which 8 were waited for; matrix products, arithmetic and copies ran while one was open for 2% of the time, Pallas kernels for 15%

profile of v1, /device:TPU:1, one launch (start us, length us, event | category | flops | bytes accessed | tf_op | source)
XLA Modules:
  0.0 113.8 jit_solution(1211482417147700055)
XLA Ops:
  0.0 1.2 %slice_select_fusion = (bf16[64,1280]{1,0:T(8,128)(2,1)S(1)}, bf16[64,1280]{1,0:T(8,128)(2,1)S(1)}) fusion(bf16[192,1280]{1,0:T(8,128)(2,1)} %bitcast.18, bf16[64,1,1280]{2,0,1:T(8,128)(2,1)} %param.18, pred[]{:T(512)S(6)} %eq.24), kind=kLoop, calls=%fused_computation.3 | loop fusion | flops 163840 | bytes 983041 | tf_op jit(solution)/shard_map/jit(_where)/select_n | solution.py:243
  1.2 3.6 %collective-permute-start.12 = (bf16[64,1280]{1,0:T(8,128)(2,1)S(1)}, bf16[64,1280]{1,0:T(8,128)(2,1)S(1)}, u32[]{:S(2)}, u32[]{:S(2)}) collective-permute-start(bf16[64,1280]{1,0:T(8,128)(2,1)S(1)} %get-tuple-element.33), channel_id=1, source_target_pairs={{4,0},{8,4},{12,8},{0,12},{5,1},{9,5},{13,9},{1,13},{6,2},{10,6},{... | collective-permute-start | bytes 491528 | tf_op jit(solution)/shard_map/ppermute | solution.py:192
  4.8 0.3 collective-permute-start.13
  5.2 0.7 collective-permute-start.14
  5.9 2.5 %collective-permute-start = (bf16[64,1280]{1,0:T(8,128)(2,1)S(1)}, bf16[64,1280]{1,0:T(8,128)(2,1)S(1)}, u32[]{:S(2)}, u32[]{:S(2)}) collective-permute-start(bf16[64,1280]{1,0:T(8,128)(2,1)S(1)} %get-tuple-element.34), channel_id=1, source_target_pairs={{1,0},{2,1},{3,2},{0,3},{5,4},{6,5},{7,6},{4,7},{9,8},{10,9},{11,1... | collective-permute-start | bytes 491528 | tf_op jit(solution)/shard_map/ppermute | solution.py:192
  8.4 0.5 collective-permute-start.1
  8.9 0.7 collective-permute-done.12
  9.6 2.9 %collective-permute-start.2 = (bf16[64,1280]{1,0:T(8,128)(2,1)S(1)}, bf16[64,1280]{1,0:T(8,128)(2,1)S(1)}, u32[]{:S(2)}, u32[]{:S(2)}) collective-permute-start(bf16[64,1280]{1,0:T(8,128)(2,1)S(1)} %get-tuple-element.34), channel_id=1, source_target_pairs={{3,0},{0,1},{1,2},{2,3},{7,4},{4,5},{5,6},{6,7},{11,8},{8,9},{9,10... | collective-permute-start | bytes 491528 | tf_op jit(solution)/shard_map/ppermute | solution.py:192
  12.4 3.5 %collective-permute-done.14 = bf16[64,1280]{1,0:T(8,128)(2,1)S(1)} collective-permute-done((bf16[64,1280]{1,0:T(8,128)(2,1)S(1)}, bf16[64,1280]{1,0:T(8,128)(2,1)S(1)}, u32[]{:S(2)}, u32[]{:S(2)}) %collective-permute-start.14) | collective-permute-done | bytes 163872 | tf_op jit(solution)/shard_map/ppermute | solution.py:192
  16.0 2.6 %collective-permute-start.16 = (bf16[256,1280]{1,0:T(8,128)(2,1)S(1)}, bf16[256,1280]{1,0:T(8,128)(2,1)}, u32[]{:S(2)}, u32[]{:S(2)}) collective-permute-start(bf16[256,1280]{1,0:T(8,128)(2,1)S(1)} %pad_maximum_fusion.1.refs_0_), channel_id=1, source_target_pairs={{1,0},{2,1},{3,2},{0,3},{5,4},{6,5},{7,6},{4,7},{9,8},{10,9},{11,1... | collective-permute-start | bytes 1966088 | tf_op jit(solution)/shard_map/ppermute | solution.py:192
  18.6 0.8 collective-permute-done.2
  19.6 1.0 collective-permute-start.7
  20.6 1.8 %collective-permute-start.4 = (bf16[256,1280]{1,0:T(8,128)(2,1)S(1)}, bf16[256,1280]{1,0:T(8,128)(2,1)S(1)}, u32[]{:S(2)}, u32[]{:S(2)}) collective-permute-start(bf16[256,1280]{1,0:T(8,128)(2,1)S(1)} %pad_maximum_fusion.refs_0_), channel_id=1, source_target_pairs={{4,0},{8,4},{12,8},{0,12},{5,1},{9,5},{13,9},{1,13},{6,2},{10,6},{... | collective-permute-start | bytes 1966088 | tf_op jit(solution)/shard_map/ppermute | solution.py:192
  22.3 1.6 %collective-permute-start.3 = (bf16[256,1280]{1,0:T(8,128)(2,1)S(1)}, bf16[256,1280]{1,0:T(8,128)(2,1)S(1)}, u32[]{:S(2)}, u32[]{:S(2)}) collective-permute-start(bf16[256,1280]{1,0:T(8,128)(2,1)S(1)} %pad_maximum_fusion.refs_0_), channel_id=1, source_target_pairs={{0,16},{16,0},{1,17},{17,1},{2,18},{18,2},{3,19},{19,3},{4,20},{20... | collective-permute-start | bytes 1966088 | tf_op jit(solution)/shard_map/ppermute | solution.py:196
  24.0 8.2 %collective-permute-done.16.refs_0_ = bf16[256,1280]{1,0:T(8,128)(2,1)} collective-permute-done((bf16[256,1280]{1,0:T(8,128)(2,1)S(1)}, bf16[256,1280]{1,0:T(8,128)(2,1)}, u32[]{:S(2)}, u32[]{:S(2)}) %collective-permute-start.16) | collective-permute-done | bytes 655392 | tf_op jit(solution)/shard_map/ppermute | solution.py:192
  32.2 1.3 %collective-permute-start.15 = (bf16[256,1280]{1,0:T(8,128)(2,1)S(1)}, bf16[256,1280]{1,0:T(8,128)(2,1)S(1)}, u32[]{:S(2)}, u32[]{:S(2)}) collective-permute-start(bf16[256,1280]{1,0:T(8,128)(2,1)S(1)} %pad_maximum_fusion.1.refs_0_), channel_id=1, source_target_pairs={{0,16},{16,0},{1,17},{17,1},{2,18},{18,2},{3,19},{19,3},{4,20},{20... | collective-permute-start | bytes 1966088 | tf_op jit(solution)/shard_map/ppermute | solution.py:196
  33.5 1.0 slice.33
  34.5 0.9 collective-permute-done.19.refs_0_
  35.4 2.7 %collective-permute-start.18 = (bf16[128,1280]{1,0:T(8,128)(2,1)S(1)}, bf16[128,1280]{1,0:T(8,128)(2,1)S(1)}, u32[]{:S(2)}, u32[]{:S(2)}) collective-permute-start(bf16[128,1280]{1,0:T(8,128)(2,1)S(1)} %slice.33), channel_id=1, source_target_pairs={{1,0},{2,1},{3,2},{0,3},{5,4},{6,5},{7,6},{4,7},{9,8},{10,9},{11,1... | collective-permute-start | bytes 983048 | tf_op jit(solution)/shard_map/ppermute | solution.py:192
  38.1 1.0 slice.34
  39.1 0.1 collective-permute-start.20
  39.3 0.1 collective-permute-start.8
  39.4 0.8 copy-done.3
  40.2 2.7 %collective-permute-start.6 = (bf16[128,1280]{1,0:T(8,128)(2,1)S(1)}, bf16[128,1280]{1,0:T(8,128)(2,1)}, u32[]{:S(2)}, u32[]{:S(2)}) collective-permute-start(bf16[128,1280]{1,0:T(8,128)(2,1)S(1)} %slice.30), channel_id=1, source_target_pairs={{4,0},{8,4},{12,8},{0,12},{5,1},{9,5},{13,9},{1,13},{6,2},{10,6},{... | collective-permute-start | bytes 983048 | tf_op jit(solution)/shard_map/ppermute | solution.py:192
  42.9 2.4 %collective-permute-done.18.refs_0_ = bf16[128,1280]{1,0:T(8,128)(2,1)S(1)} collective-permute-done((bf16[128,1280]{1,0:T(8,128)(2,1)S(1)}, bf16[128,1280]{1,0:T(8,128)(2,1)S(1)}, u32[]{:S(2)}, u32[]{:S(2)}) %collective-permute-start.18) | collective-permute-done | bytes 327712 | tf_op jit(solution)/shard_map/ppermute | solution.py:192
  45.3 0.8 collective-permute-start.21
  46.0 0.7 copy-done.7
  46.8 2.7 %collective-permute-done.20.refs_1_ = bf16[128,1280]{1,0:T(8,128)(2,1)S(1)} collective-permute-done((bf16[128,1280]{1,0:T(8,128)(2,1)S(1)}, bf16[128,1280]{1,0:T(8,128)(2,1)S(1)}, u32[]{:S(2)}, u32[]{:S(2)}) %collective-permute-start.20) | collective-permute-done | bytes 327712 | tf_op jit(solution)/shard_map/ppermute | solution.py:192
  49.4 1.1 collective-permute-start.22
  50.5 0.7 copy-done.9
  51.3 0.7 copy-done.15
  52.0 0.9 copy-done.5
  52.9 0.5 collective-permute-start.11
  53.4 0.7 copy-done.11
  54.1 0.5 collective-permute-start.17
  54.7 0.8 copy-done.13
  55.4 0.7 copy-done.17
  56.2 0.5 collective-permute-start.9
  56.7 0.1 dynamic_slice.3
  56.8 1.4 %copy-done.2 = bf16[1,640,1280]{2,1,0:T(8,128)(2,1)S(1)} copy-done((bf16[1,640,1280]{2,1,0:T(8,128)(2,1)S(1)}, bf16[1,640,1280]{2,1,0:T(8,128)(2,1)}, u32[]{:S(2)}) %copy-start.2) | copy-done | bytes 1638424
  58.3 3.3 %shard_map.145 = (bf16[640,1280]{1,0:T(8,128)(2,1)S(1)}, bf16[64,1280]{1,0:T(8,128)(2,1)S(1)}, f32[64,1280]{1,0:T(8,128)S(1)}, f32[64,128]{1,0:T(8,128)S(1)}, f3...) custom-call(s32[1]{0:T(128)} %bitcast.index_ref.a, s32[256]{0:T(256)S(1)} %copy-done.22, s32[24]{0:T(128)S(1)} %copy-done.23, ...), custom_call_target="tpu_custom_call" | custom-call | tf_op jit(solution)/shard_map/pallas_call | solution.py:53
  61.6 0.7 shard_map.150
  62.2 0.4 copy-done.4
  62.7 2.1 %shard_map.146.refs_0_ = bf16[256,640]{1,0:T(8,128)(2,1)S(1)} custom-call(s32[1]{0:T(128)} %bitcast.index_ref.a, s32[256]{0:T(256)S(1)} %copy-done.22, s32[24]{0:T(128)S(1)} %copy-done.23, s32[1]{0:T(128)} %bitcast.5.d.a, bf16[640,1280]{1,0:T(8,128)(2,1)S(1)} %get-tuple-element.21.e.b, bf16[64,1280]{1,0:T(8,128)(2,1)S(1)} %get-tuple-element.22.f, ...), custom_call_target="tpu_custom_call" | custom-call | tf_op jit(solution)/shard_map/pallas_call | solution.py:53
  64.9 0.6 shard_map.152
  65.5 0.3 copy-done.16
  65.8 0.1 copy-done.18
  65.9 2.6 %shard_map.148.refs_2_ = bf16[256,640]{1,0:T(8,128)(2,1)S(1)} custom-call(s32[1]{0:T(128)} %bitcast.index_ref.a, s32[256]{0:T(256)S(1)} %copy-done.22, s32[24]{0:T(128)S(1)} %copy-done.23, s32[1]{0:T(128)} %bitcast.5.d.a, bf16[640,1280]{1,0:T(8,128)(2,1)S(1)} %get-tuple-element.21.e.b, bf16[64,1280]{1,0:T(8,128)(2,1)S(1)} %get-tuple-element.22.f, ...), custom_call_target="tpu_custom_call" | custom-call | tf_op jit(solution)/shard_map/pallas_call | solution.py:53
  68.6 2.7 %shard_map.149.refs_3_ = bf16[256,640]{1,0:T(8,128)(2,1)S(1)} custom-call(s32[1]{0:T(128)} %bitcast.index_ref.a, s32[256]{0:T(256)S(1)} %copy-done.22, s32[24]{0:T(128)S(1)} %copy-done.23, s32[1]{0:T(128)} %bitcast.5.d.a, bf16[640,1280]{1,0:T(8,128)(2,1)S(1)} %get-tuple-element.21.e.b, bf16[64,1280]{1,0:T(8,128)(2,1)S(1)} %get-tuple-element.22.f, ...), custom_call_target="tpu_custom_call" | custom-call | tf_op jit(solution)/shard_map/pallas_call | solution.py:53
  71.3 2.7 %shard_map.147.refs_1_ = bf16[256,640]{1,0:T(8,128)(2,1)S(1)} custom-call(s32[1]{0:T(128)} %bitcast.index_ref.a, s32[256]{0:T(256)S(1)} %copy-done.22, s32[24]{0:T(128)S(1)} %copy-done.23, s32[1]{0:T(128)} %bitcast.5.d.a, bf16[640,1280]{1,0:T(8,128)(2,1)S(1)} %get-tuple-element.21.e.b, bf16[64,1280]{1,0:T(8,128)(2,1)S(1)} %get-tuple-element.22.f, ...), custom_call_target="tpu_custom_call" | custom-call | tf_op jit(solution)/shard_map/pallas_call | solution.py:53
  74.0 1.9 %shard_map.151 = (bf16[640,256]{1,0:T(8,128)(2,1)S(1)}, bf16[256,1280]{1,0:T(8,128)(2,1)S(1)}) custom-call(s32[1]{0:T(128)} %bitcast.5.d.a, bf16[640,1280]{1,0:T(8,128)(2,1)S(1)} %get-tuple-element.21.e.b, bf16[256,1280]{1,0:T(8,128)(2,1)} %collective-permute-done.16.refs_0_, bf16[256,1280]{1,0:T(8,128)(2,1)} %collective-permute-done.17.refs_1_), custom_call_target="tpu_custom_call" | custom-call | tf_op jit(solution)/shard_map/pallas_call | solution.py:53
  75.9 1.9 %shard_map.153 = (bf16[640,256]{1,0:T(8,128)(2,1)S(1)}, bf16[256,1280]{1,0:T(8,128)(2,1)S(1)}) custom-call(s32[1]{0:T(128)} %bitcast.5.d.a, bf16[640,1280]{1,0:T(8,128)(2,1)S(1)} %get-tuple-element.21.e.b, bf16[256,1280]{1,0:T(8,128)(2,1)} %collective-permute-done.19.refs_0_, bf16[256,1280]{1,0:T(8,128)(2,1)} %collective-permute-done.23.refs_1_), custom_call_target="tpu_custom_call" | custom-call | tf_op jit(solution)/shard_map/pallas_call | solution.py:53
  77.9 4.9 %shard_map.154 = f32[1,64]{1,0:T(1,128)S(1)} custom-call(f32[64,1280]{1,0:T(8,128)S(1)} %get-tuple-element.19.a, s32[64,128]{1,0:T(8,128)S(1)} %get-tuple-element.20.b, f32[1,1280]{1,0:T(1,128)S(1)} %reshape.46.c, f32[1,33]{1,0:T(1,128)S(1)} %bitcast.17, bf16[1280,1280]{1,0:T(8,128)(2,1)} %e.1, bf16[33,1280]{1,0:T(8,128)(2,1)S(1)} %bitcast.15, ...), custom_call_target="tpu_custom_call" | custom-call | tf_op jit(solution)/shard_map/pallas_call | solution.py:53
  82.8 0.5 broadcast.22
  83.3 0.7 reduce.5
  84.0 0.7 all_to_all.12
  84.7 4.2 %all-to-all-start = ((f32[16,1,4]{2,1,0:T(1,128)}), f32[16,1,4]{2,1,0:T(1,128)S(1)}, u32[]{:S(2)}, u32[]{:S(2)}) async-start(f32[16,1,4]{2,1,0:T(1,128)} %bitcast.10), calls=%async_computation | async-start | bytes 16384 | tf_op jit(solution)/shard_map/all_to_all | solution.py:314
  88.9 0.1 broadcast_compare_fusion
  89.0 6.1 %all-to-all-done = f32[16,1,4]{2,1,0:T(1,128)S(1)} async-done(((f32[16,1,4]{2,1,0:T(1,128)}), f32[16,1,4]{2,1,0:T(1,128)S(1)}, u32[]{:S(2)}, u32[]{:S(2)}) %all-to-all-start) | async-done | bytes 288 | tf_op jit(solution)/shard_map/all_to_all | solution.py:314
  95.2 0.2 select_reduce_fusion
  95.5 0.1 copy.29
  95.6 17.4 %all_to_all.18 = f32[16,1,64]{2,1,0:T(1,128)S(1)} all-to-all(f32[16,1,64]{2,1,0:T(1,128)S(1)} %copy.30), channel_id=1, replica_groups=mesh['z'=8,'core'=2,'y'=4,'x'=4] {'z','core'}, dimensions={0} | all-to-all | bytes 8192 | tf_op jit(solution)/shard_map/all_to_all | solution.py:321
  113.0 0.1 reduce_sum.22
  113.1 0.7 copy.31
  (75 shorter events, 0.5 us)
Async XLA Ops:
  1.2 8.4 %collective-permute-start.12 = (bf16[64,1280]{1,0:T(8,128)(2,1)S(1)}, bf16[64,1280]{1,0:T(8,128)(2,1)S(1)}, u32[]{:S(2)}, u32[]{:S(2)}) collective-permute-start(bf16[64,1280]{1,0:T(8,128)(2,1)S(1)} %get-tuple-element.33), channel_id=1, source_target_pairs={{4,0},{8,4},{12,8},{0,12},{5,1},{9,5},{13,9},{1,13},{6,2},{10,6},{... | collective-permute-start | bytes 491528 | tf_op jit(solution)/shard_map/ppermute | solution.py:192
  4.8 7.6 %collective-permute-start.13 = (bf16[64,1280]{1,0:T(8,128)(2,1)S(1)}, bf16[64,1280]{1,0:T(8,128)(2,1)S(1)}, u32[]{:S(2)}, u32[]{:S(2)}) collective-permute-start(bf16[64,1280]{1,0:T(8,128)(2,1)S(1)} %get-tuple-element.33), channel_id=1, source_target_pairs={{8,0},{12,4},{0,8},{4,12},{9,1},{13,5},{1,9},{5,13},{10,2},{14,6},... | collective-permute-start | bytes 491528 | tf_op jit(solution)/shard_map/ppermute | solution.py:192
  5.2 10.8 %collective-permute-start.14 = (bf16[64,1280]{1,0:T(8,128)(2,1)S(1)}, bf16[64,1280]{1,0:T(8,128)(2,1)S(1)}, u32[]{:S(2)}, u32[]{:S(2)}) collective-permute-start(bf16[64,1280]{1,0:T(8,128)(2,1)S(1)} %get-tuple-element.33), channel_id=1, source_target_pairs={{12,0},{0,4},{4,8},{8,12},{13,1},{1,5},{5,9},{9,13},{14,2},{2,6},{... | collective-permute-start | bytes 491528 | tf_op jit(solution)/shard_map/ppermute | solution.py:192
  5.9 12.7 %collective-permute-start = (bf16[64,1280]{1,0:T(8,128)(2,1)S(1)}, bf16[64,1280]{1,0:T(8,128)(2,1)S(1)}, u32[]{:S(2)}, u32[]{:S(2)}) collective-permute-start(bf16[64,1280]{1,0:T(8,128)(2,1)S(1)} %get-tuple-element.34), channel_id=1, source_target_pairs={{1,0},{2,1},{3,2},{0,3},{5,4},{6,5},{7,6},{4,7},{9,8},{10,9},{11,1... | collective-permute-start | bytes 491528 | tf_op jit(solution)/shard_map/ppermute | solution.py:192
  8.4 10.2 %collective-permute-start.1 = (bf16[64,1280]{1,0:T(8,128)(2,1)S(1)}, bf16[64,1280]{1,0:T(8,128)(2,1)S(1)}, u32[]{:S(2)}, u32[]{:S(2)}) collective-permute-start(bf16[64,1280]{1,0:T(8,128)(2,1)S(1)} %get-tuple-element.34), channel_id=1, source_target_pairs={{2,0},{3,1},{0,2},{1,3},{6,4},{7,5},{4,6},{5,7},{10,8},{11,9},{8,1... | collective-permute-start | bytes 491528 | tf_op jit(solution)/shard_map/ppermute | solution.py:192
  9.6 9.8 %collective-permute-start.2 = (bf16[64,1280]{1,0:T(8,128)(2,1)S(1)}, bf16[64,1280]{1,0:T(8,128)(2,1)S(1)}, u32[]{:S(2)}, u32[]{:S(2)}) collective-permute-start(bf16[64,1280]{1,0:T(8,128)(2,1)S(1)} %get-tuple-element.34), channel_id=1, source_target_pairs={{3,0},{0,1},{1,2},{2,3},{7,4},{4,5},{5,6},{6,7},{11,8},{8,9},{9,10... | collective-permute-start | bytes 491528 | tf_op jit(solution)/shard_map/ppermute | solution.py:192
  16.0 16.2 %collective-permute-start.16 = (bf16[256,1280]{1,0:T(8,128)(2,1)S(1)}, bf16[256,1280]{1,0:T(8,128)(2,1)}, u32[]{:S(2)}, u32[]{:S(2)}) collective-permute-start(bf16[256,1280]{1,0:T(8,128)(2,1)S(1)} %pad_maximum_fusion.1.refs_0_), channel_id=1, source_target_pairs={{1,0},{2,1},{3,2},{0,3},{5,4},{6,5},{7,6},{4,7},{9,8},{10,9},{11,1... | collective-permute-start | bytes 1966088 | tf_op jit(solution)/shard_map/ppermute | solution.py:192
  18.6 16.8 %collective-permute-start.19 = (bf16[256,1280]{1,0:T(8,128)(2,1)S(1)}, bf16[256,1280]{1,0:T(8,128)(2,1)}, u32[]{:S(2)}, u32[]{:S(2)}) collective-permute-start(bf16[256,1280]{1,0:T(8,128)(2,1)S(1)} %pad_maximum_fusion.1.refs_0_), channel_id=1, source_target_pairs={{3,0},{0,1},{1,2},{2,3},{7,4},{4,5},{5,6},{6,7},{11,8},{8,9},{9,10... | collective-permute-start | bytes 1966088 | tf_op jit(solution)/shard_map/ppermute | solution.py:192
  19.5 37.2 %copy-start.25 = (f32[1280]{0:T(1024)S(1)}, f32[1280]{0:T(1024)}, u32[]{:S(2)}) copy-start(f32[1280]{0:T(1024)} %param.16) | copy-start | bytes 15364
  19.5 37.2 %copy-start.26 = (f32[1280]{0:T(1024)S(1)}, f32[1280]{0:T(1024)}, u32[]{:S(2)}) copy-start(f32[1280]{0:T(1024)} %param.19) | copy-start | bytes 15364
  19.5 37.2 %copy-start.27 = (s32[256]{0:T(256)S(1)}, s32[256]{0:T(256)}, u32[]{:S(2)}) copy-start(s32[256]{0:T(256)} %param.27) | copy-start | bytes 3076
  19.5 37.3 %copy-start = (f32[640,128]{1,0:T(8,128)S(1)}, f32[640,128]{1,0:T(8,128)}, u32[]{:S(2)}) copy-start(f32[640,128]{1,0:T(8,128)} %constant.36.clone.cos_ref.refs_2_.refs_4_) | copy-start | bytes 983044
  19.5 37.3 %copy-start.1 = (f32[640,128]{1,0:T(8,128)S(1)}, f32[640,128]{1,0:T(8,128)}, u32[]{:S(2)}) copy-start(f32[640,128]{1,0:T(8,128)} %constant.37.clone.sin_ref.refs_3_.refs_5_) | copy-start | bytes 983044
  19.5 37.3 %copy-start.20 = (s32[256,64]{0,1:T(8,128)S(1)}, s32[256,64]{0,1:T(8,128)}, u32[]{:S(2)}) copy-start(s32[256,64]{0,1:T(8,128)} %param.26) | copy-start | bytes 196612
  19.5 37.2 %copy-start.21 = (s32[24,640]{1,0:T(8,128)S(1)}, s32[24,640]{1,0:T(8,128)}, u32[]{:S(2)}) copy-start(s32[24,640]{1,0:T(8,128)} %tokens_ref.1) | copy-start | bytes 184324
  19.6 37.2 %copy-start.22 = (s32[256]{0:T(256)S(1)}, s32[256]{0:T(256)}, u32[]{:S(2)}) copy-start(s32[256]{0:T(256)} %b.7) | copy-start | bytes 3076
  19.6 37.2 %copy-start.23 = (s32[24]{0:T(128)S(1)}, s32[24]{0:T(128)}, u32[]{:S(2)}) copy-start(s32[24]{0:T(128)} %c.7) | copy-start | bytes 292
  19.6 19.5 %collective-permute-start.7 = (bf16[256,1280]{1,0:T(8,128)(2,1)S(1)}, bf16[256,1280]{1,0:T(8,128)(2,1)S(1)}, u32[]{:S(2)}, u32[]{:S(2)}) collective-permute-start(bf16[256,1280]{1,0:T(8,128)(2,1)S(1)} %pad_maximum_fusion.refs_0_), channel_id=1, source_target_pairs={{12,0},{0,4},{4,8},{8,12},{13,1},{1,5},{5,9},{9,13},{14,2},{2,6},{... | collective-permute-start | bytes 1966088 | tf_op jit(solution)/shard_map/ppermute | solution.py:192
  20.6 18.7 %collective-permute-start.4 = (bf16[256,1280]{1,0:T(8,128)(2,1)S(1)}, bf16[256,1280]{1,0:T(8,128)(2,1)S(1)}, u32[]{:S(2)}, u32[]{:S(2)}) collective-permute-start(bf16[256,1280]{1,0:T(8,128)(2,1)S(1)} %pad_maximum_fusion.refs_0_), channel_id=1, source_target_pairs={{4,0},{8,4},{12,8},{0,12},{5,1},{9,5},{13,9},{1,13},{6,2},{10,6},{... | collective-permute-start | bytes 1966088 | tf_op jit(solution)/shard_map/ppermute | solution.py:192
  22.3 17.0 %collective-permute-start.3 = (bf16[256,1280]{1,0:T(8,128)(2,1)S(1)}, bf16[256,1280]{1,0:T(8,128)(2,1)S(1)}, u32[]{:S(2)}, u32[]{:S(2)}) collective-permute-start(bf16[256,1280]{1,0:T(8,128)(2,1)S(1)} %pad_maximum_fusion.refs_0_), channel_id=1, source_target_pairs={{0,16},{16,0},{1,17},{17,1},{2,18},{18,2},{3,19},{19,3},{4,20},{20... | collective-permute-start | bytes 1966088 | tf_op jit(solution)/shard_map/ppermute | solution.py:196
  32.2 19.8 %collective-permute-start.15 = (bf16[256,1280]{1,0:T(8,128)(2,1)S(1)}, bf16[256,1280]{1,0:T(8,128)(2,1)S(1)}, u32[]{:S(2)}, u32[]{:S(2)}) collective-permute-start(bf16[256,1280]{1,0:T(8,128)(2,1)S(1)} %pad_maximum_fusion.1.refs_0_), channel_id=1, source_target_pairs={{0,16},{16,0},{1,17},{17,1},{2,18},{18,2},{3,19},{19,3},{4,20},{20... | collective-permute-start | bytes 1966088 | tf_op jit(solution)/shard_map/ppermute | solution.py:196
  35.4 9.9 %collective-permute-start.18 = (bf16[128,1280]{1,0:T(8,128)(2,1)S(1)}, bf16[128,1280]{1,0:T(8,128)(2,1)S(1)}, u32[]{:S(2)}, u32[]{:S(2)}) collective-permute-start(bf16[128,1280]{1,0:T(8,128)(2,1)S(1)} %slice.33), channel_id=1, source_target_pairs={{1,0},{2,1},{3,2},{0,3},{5,4},{6,5},{7,6},{4,7},{9,8},{10,9},{11,1... | collective-permute-start | bytes 983048 | tf_op jit(solution)/shard_map/ppermute | solution.py:192
  39.1 10.3 %collective-permute-start.20 = (bf16[128,1280]{1,0:T(8,128)(2,1)S(1)}, bf16[128,1280]{1,0:T(8,128)(2,1)S(1)}, u32[]{:S(2)}, u32[]{:S(2)}) collective-permute-start(bf16[128,1280]{1,0:T(8,128)(2,1)S(1)} %slice.34), channel_id=1, source_target_pairs={{3,0},{0,1},{1,2},{2,3},{7,4},{4,5},{5,6},{6,7},{11,8},{8,9},{9,10... | collective-permute-start | bytes 983048 | tf_op jit(solution)/shard_map/ppermute | solution.py:192
  39.3 12.0 %collective-permute-start.8 = (bf16[128,1280]{1,0:T(8,128)(2,1)S(1)}, bf16[128,1280]{1,0:T(8,128)(2,1)S(1)}, u32[]{:S(2)}, u32[]{:S(2)}) collective-permute-start(bf16[128,1280]{1,0:T(8,128)(2,1)S(1)} %slice.31), channel_id=1, source_target_pairs={{12,0},{0,4},{4,8},{8,12},{13,1},{1,5},{5,9},{9,13},{14,2},{2,6},{... | collective-permute-start | bytes 983048 | tf_op jit(solution)/shard_map/ppermute | solution.py:192
  39.4 0.9 copy-start.3
  40.2 13.2 %collective-permute-start.6 = (bf16[128,1280]{1,0:T(8,128)(2,1)S(1)}, bf16[128,1280]{1,0:T(8,128)(2,1)}, u32[]{:S(2)}, u32[]{:S(2)}) collective-permute-start(bf16[128,1280]{1,0:T(8,128)(2,1)S(1)} %slice.30), channel_id=1, source_target_pairs={{4,0},{8,4},{12,8},{0,12},{5,1},{9,5},{13,9},{1,13},{6,2},{10,6},{... | collective-permute-start | bytes 983048 | tf_op jit(solution)/shard_map/ppermute | solution.py:192
  45.3 8.2 %collective-permute-start.21 = (bf16[128,1280]{1,0:T(8,128)(2,1)S(1)}, bf16[128,1280]{1,0:T(8,128)(2,1)S(1)}, u32[]{:S(2)}, u32[]{:S(2)}) collective-permute-start(bf16[128,1280]{1,0:T(8,128)(2,1)S(1)} %collective-permute-done.18.refs_0_), channel_id=1, source_target_pairs={{0,16},{16,0},{1,17},{17,1},{2,18},{18,2},{3,19},{19,3},{4,20},{20... | collective-permute-start | bytes 983048 | tf_op jit(solution)/shard_map/ppermute | solution.py:196
  46.0 0.7 copy-start.7
  49.4 5.2 %collective-permute-start.22 = (bf16[128,1280]{1,0:T(8,128)(2,1)S(1)}, bf16[128,1280]{1,0:T(8,128)(2,1)S(1)}, u32[]{:S(2)}, u32[]{:S(2)}) collective-permute-start(bf16[128,1280]{1,0:T(8,128)(2,1)S(1)} %collective-permute-done.20.refs_1_), channel_id=1, source_target_pairs={{0,16},{16,0},{1,17},{17,1},{2,18},{18,2},{3,19},{19,3},{4,20},{20... | collective-permute-start | bytes 983048 | tf_op jit(solution)/shard_map/ppermute | solution.py:196
  50.5 0.8 copy-start.9
  51.3 4.1 %collective-permute-start.10 = (bf16[128,1280]{1,0:T(8,128)(2,1)S(1)}, bf16[128,1280]{1,0:T(8,128)(2,1)S(1)}, u32[]{:S(2)}, u32[]{:S(2)}) collective-permute-start(bf16[128,1280]{1,0:T(8,128)(2,1)S(1)} %collective-permute-done.8.refs_1_), channel_id=1, source_target_pairs={{0,16},{16,0},{1,17},{17,1},{2,18},{18,2},{3,19},{19,3},{4,20},{20... | collective-permute-start | bytes 983048 | tf_op jit(solution)/shard_map/ppermute | solution.py:196
  51.3 0.7 copy-start.15
  52.0 0.9 copy-start.5
  52.9 15.7 %collective-permute-start.11 = (bf16[256,1280]{1,0:T(8,128)(2,1)S(1)}, bf16[256,1280]{1,0:T(8,128)(2,1)}, u32[]{:S(2)}, u32[]{:S(2)}) collective-permute-start(bf16[256,1280]{1,0:T(8,128)(2,1)S(1)} %collective-permute-done.7.refs_0_), channel_id=1, source_target_pairs={{0,16},{16,0},{1,17},{17,1},{2,18},{18,2},{3,19},{19,3},{4,20},{20... | collective-permute-start | bytes 1966088 | tf_op jit(solution)/shard_map/ppermute | solution.py:196
  53.4 17.9 %collective-permute-start.5 = (bf16[256,1280]{1,0:T(8,128)(2,1)S(1)}, bf16[256,1280]{1,0:T(8,128)(2,1)}, u32[]{:S(2)}, u32[]{:S(2)}) collective-permute-start(bf16[256,1280]{1,0:T(8,128)(2,1)S(1)} %collective-permute-done.4.refs_0_), channel_id=1, source_target_pairs={{0,16},{16,0},{1,17},{17,1},{2,18},{18,2},{3,19},{19,3},{4,20},{20... | collective-permute-start | bytes 1966088 | tf_op jit(solution)/shard_map/ppermute | solution.py:196
  53.4 0.7 copy-start.11
  54.1 19.8 %collective-permute-start.17 = (bf16[256,1280]{1,0:T(8,128)(2,1)}, bf16[256,1280]{1,0:T(8,128)(2,1)}, u32[]{:S(2)}, u32[]{:S(2)}) collective-permute-start(bf16[256,1280]{1,0:T(8,128)(2,1)} %collective-permute-done.16.refs_0_), channel_id=1, source_target_pairs={{0,16},{16,0},{1,17},{17,1},{2,18},{18,2},{3,19},{19,3},{4,20},{20... | collective-permute-start | bytes 1966088 | tf_op jit(solution)/shard_map/ppermute | solution.py:196
  54.7 0.8 copy-start.13
  55.4 20.5 %collective-permute-start.23 = (bf16[256,1280]{1,0:T(8,128)(2,1)}, bf16[256,1280]{1,0:T(8,128)(2,1)}, u32[]{:S(2)}, u32[]{:S(2)}) collective-permute-start(bf16[256,1280]{1,0:T(8,128)(2,1)} %collective-permute-done.19.refs_0_), channel_id=1, source_target_pairs={{0,16},{16,0},{1,17},{17,1},{2,18},{18,2},{3,19},{19,3},{4,20},{20... | collective-permute-start | bytes 1966088 | tf_op jit(solution)/shard_map/ppermute | solution.py:196
  55.4 0.7 copy-start.17
  56.2 9.4 %collective-permute-start.9 = (bf16[128,1280]{1,0:T(8,128)(2,1)}, bf16[128,1280]{1,0:T(8,128)(2,1)}, u32[]{:S(2)}, u32[]{:S(2)}) collective-permute-start(bf16[128,1280]{1,0:T(8,128)(2,1)} %collective-permute-done.6.refs_0_), channel_id=1, source_target_pairs={{0,16},{16,0},{1,17},{17,1},{2,18},{18,2},{3,19},{19,3},{4,20},{20... | collective-permute-start | bytes 983048 | tf_op jit(solution)/shard_map/ppermute | solution.py:196
  56.8 1.4 %copy-start.2 = (bf16[1,640,1280]{2,1,0:T(8,128)(2,1)S(1)}, bf16[1,640,1280]{2,1,0:T(8,128)(2,1)}, u32[]{:S(2)}) copy-start(bf16[1,640,1280]{2,1,0:T(8,128)(2,1)} %param.15) | copy-start | bytes 4915204
  58.3 3.3 %copy-start.6 = (bf16[256,1280]{1,0:T(8,128)(2,1)S(1)}, bf16[256,1280]{1,0:T(8,128)(2,1)}, u32[]{:S(2)}) copy-start(bf16[256,1280]{1,0:T(8,128)(2,1)} %copy-done.5) | copy-start | bytes 1966084
  61.6 1.1 copy-start.4
  62.7 2.2 %copy-start.8 = (bf16[128,1280]{1,0:T(8,128)(2,1)S(1)}, bf16[128,1280]{1,0:T(8,128)(2,1)}, u32[]{:S(2)}) copy-start(bf16[128,1280]{1,0:T(8,128)(2,1)} %copy-done.7) | copy-start | bytes 983044
  62.7 2.2 %copy-start.10 = (bf16[128,1280]{1,0:T(8,128)(2,1)S(1)}, bf16[128,1280]{1,0:T(8,128)(2,1)}, u32[]{:S(2)}) copy-start(bf16[128,1280]{1,0:T(8,128)(2,1)} %copy-done.9) | copy-start | bytes 983044
  62.7 2.2 %copy-start.12 = (bf16[128,1280]{1,0:T(8,128)(2,1)S(1)}, bf16[128,1280]{1,0:T(8,128)(2,1)}, u32[]{:S(2)}) copy-start(bf16[128,1280]{1,0:T(8,128)(2,1)} %copy-done.11) | copy-start | bytes 983044
  62.7 2.2 %copy-start.14 = (bf16[128,1280]{1,0:T(8,128)(2,1)S(1)}, bf16[128,1280]{1,0:T(8,128)(2,1)}, u32[]{:S(2)}) copy-start(bf16[128,1280]{1,0:T(8,128)(2,1)} %copy-done.13) | copy-start | bytes 983044
  64.9 1.0 copy-start.16
  64.9 1.1 copy-start.18
  75.9 2.0 %copy-start.19 = (bf16[1280,33]{0,1:T(8,128)(2,1)S(1)}, bf16[1280,33]{0,1:T(8,128)(2,1)}, u32[]{:S(2)}) copy-start(bf16[1280,33]{0,1:T(8,128)(2,1)} %param.21) | copy-start | bytes 253444
  75.9 2.0 %copy-start.24 = (f32[33]{0:T(128)S(1)}, f32[33]{0:T(128)}, u32[]{:S(2)}) copy-start(f32[33]{0:T(128)} %param.22) | copy-start | bytes 400
  84.7 10.4 %all-to-all-start = ((f32[16,1,4]{2,1,0:T(1,128)}), f32[16,1,4]{2,1,0:T(1,128)S(1)}, u32[]{:S(2)}, u32[]{:S(2)}) async-start(f32[16,1,4]{2,1,0:T(1,128)} %bitcast.10), calls=%async_computation | async-start | bytes 16384 | tf_op jit(solution)/shard_map/all_to_all | solution.py:314

commit v2 on v1

v2 whole, which is shorter than its diff:
```python
import numpy as np
import jax
import jax.numpy as jnp
from jax import lax
from jax.experimental import pallas as pl
from jax.experimental.pallas import tpu as pltpu
from jax.sharding import Mesh, PartitionSpec as P

epsilon = 1e-05
F32 = jnp.float32
BF16 = jnp.bfloat16


def rotary_tables(seq_span, head_size):
    half = head_size // 2
    power = (np.arange(half, dtype=np.float32) * np.float32(2.0 / head_size)).astype(np.float32)
    frequency = (np.float32(1.0) / np.power(np.float32(10000.0), power)).astype(np.float32)
    angles = (np.arange(seq_span, dtype=np.float32)[:, None] * frequency[None, :]).astype(np.float32)
    cosine = np.cos(angles.astype(np.float64)).astype(np.float32)
    sine = np.sin(angles.astype(np.float64)).astype(np.float32)
    cos_table = np.concatenate([cosine] * 4, axis=1)
    sin_table = np.concatenate([-sine, sine] * 2, axis=1)
    return cos_table, sin_table


def nt_dot(a, b):
    return lax.dot_general(a, b, (((1,), (1,)), ((), ())), preferred_element_type=F32)


def nn_dot(a, b, **options):
    return lax.dot_general(a, b, (((1,), (0,)), ((), ())), preferred_element_type=F32, **options)


def rotate(part, cos_table, sin_table, half):
    width = part.shape[1]
    lane = lax.broadcasted_iota(jnp.int32, part.shape, 1) % (2 * half)
    turned = jnp.where(
        lane < half,
        pltpu.roll(part, width - half, 1),
        pltpu.roll(part, half, 1),
    )
    return part * cos_table + turned * sin_table


def call(kernel, outs, n_smem, args, flops=0, exps=0, vmem=24 * 1024 * 1024):
    space = pltpu.MemorySpace
    specs = [pl.BlockSpec(memory_space=space.SMEM)] * n_smem
    specs += [pl.BlockSpec(memory_space=space.VMEM)] * (len(args) - n_smem)
    moved = sum(a.size * a.dtype.itemsize for a in list(args) + jax.tree.leaves(outs))
    return pl.pallas_call(
        kernel,
        out_shape=outs,
        in_specs=specs,
        out_specs=jax.tree.map(lambda _: pl.BlockSpec(memory_space=space.VMEM), outs),
        cost_estimate=pl.CostEstimate(flops=flops, transcendentals=exps, bytes_accessed=moved),
        compiler_params=pltpu.CompilerParams(vmem_limit_bytes=vmem),
    )(*args)


def copy_of(place_ref, core):
    return (place_ref[0] * 2 + core) * 16 + place_ref[2]


def prepare_kernel(
    place_ref, sequence_ref, length_ref, codes_ref, tokens_ref, mine_ref, other_ref, gain_ref,
    cos_ref, sin_ref,
    normed_ref, picked_ref, rows_ref, qcos_ref, qsin_ref, targets_ref,
):
    span = mine_ref.shape[0]
    masks = codes_ref.shape[0]
    gain = gain_ref[...]
    block = 128
    for states_ref, core in ((mine_ref, place_ref[1]), (other_ref, 1 - place_ref[1])):
        copy = copy_of(place_ref, core)
        sequence = sequence_ref[copy]
        length = length_ref[sequence]
        codes_all = codes_ref[...]
        lane = lax.broadcasted_iota(jnp.int32, codes_all.shape, 1)
        codes = jnp.sum(jnp.where(lane == copy, codes_all, 0), axis=1, keepdims=True)
        quotient = jnp.floor(codes.astype(F32) / length.astype(F32)).astype(jnp.int32)
        positions = codes - quotient * length
        positions = jnp.where(positions < 0, positions + length, positions)
        positions = jnp.where(positions >= length, positions - length, positions)
        hit = lax.broadcasted_iota(jnp.int32, (masks, span), 1) == positions
        tokens = tokens_ref[pl.ds(sequence, 1), :]
        targets = jnp.sum(jnp.where(hit, tokens, 0), axis=1, keepdims=True)
        base = pl.multiple_of(core * span, block)
        at_mask = pl.ds(pl.multiple_of(core * masks, masks), masks)
        targets_ref[at_mask, :] = jnp.broadcast_to(targets, (masks, targets_ref.shape[1]))
        hot = hit.astype(F32)
        qcos_ref[at_mask, :] = nn_dot(hot, cos_ref[...], precision=lax.Precision.HIGHEST)
        qsin_ref[at_mask, :] = nn_dot(hot, sin_ref[...], precision=lax.Precision.HIGHEST)
        hot = hot.astype(BF16)

        def step(i, carry):
            at = pl.multiple_of(i * block, block)
            values = states_ref[pl.ds(at, block), :].astype(F32)
            average = jnp.mean(values, axis=1, keepdims=True)
            centred = values - average
            variance = jnp.mean(centred * centred, axis=1, keepdims=True)
            normed_ref[pl.ds(base + at, block), :] = (
                centred * lax.rsqrt(variance + epsilon) * gain
            ).astype(BF16)
            return carry

        lax.fori_loop(0, span // block, step, 0)
        rows_ref[at_mask, :] = nn_dot(hot, states_ref[...])
        picked_ref[at_mask, :] = nn_dot(hot, normed_ref[pl.ds(base, span), :]).astype(BF16)


def keys_kernel(
    place_ref, sequence_ref, length_ref, normed_ref, picked_ref, cos_ref, sin_ref, qcos_ref,
    qsin_ref, block_refs, probs_ref,
):
    size = block_refs[0].shape[0] // 2
    span = normed_ref.shape[0] // 2
    masks = picked_ref.shape[0] // 2
    heads = len(block_refs)
    key_weight = jnp.concatenate([r[size:, :] for r in block_refs], axis=0)
    query_weight = jnp.concatenate([r[:size, :] for r in block_refs], axis=0)
    keys = nt_dot(normed_ref[...], key_weight)
    queries = nt_dot(picked_ref[...], query_weight) * 0.125
    for core in range(2):
        length = length_ref[sequence_ref[copy_of(place_ref, core)]]
        rows = slice(span * core, span * (core + 1))
        own = slice(masks * core, masks * (core + 1))
        turned_keys, turned_queries = [], []
        for i in range(heads // 2):
            lanes = slice(128 * i, 128 * (i + 1))
            turned_keys.append(rotate(keys[rows, lanes], cos_ref[...], sin_ref[...], size // 2))
            turned_queries.append(
                rotate(queries[own, lanes], qcos_ref[own, :], qsin_ref[own, :], size // 2)
            )
        key_rows = jnp.concatenate(turned_keys, axis=1).astype(BF16)
        query_rows = jnp.concatenate(turned_queries, axis=1).astype(BF16)
        spread = jnp.concatenate([query_rows] * heads, axis=0)
        row = lax.broadcasted_iota(jnp.int32, spread.shape, 0) // masks
        lane = lax.broadcasted_iota(jnp.int32, spread.shape, 1) // size
        spread = jnp.where(row == lane, spread, jnp.zeros_like(spread))
        logits = nt_dot(spread, key_rows)
        alive = lax.broadcasted_iota(jnp.int32, logits.shape, 1) < length
        logits = jnp.where(alive, logits, -1e30)
        largest = jnp.max(logits, axis=1, keepdims=True)
        weights = jnp.exp(logits - largest)
        total = jnp.sum(weights, axis=1, keepdims=True)
        probs_ref[core] = (weights * (1.0 / total)).astype(BF16)


def values_kernel(normed_ref, block_refs, values_ref):
    size = block_refs[0].shape[0] // 2
    weight = jnp.concatenate([r[:size, :] for r in block_refs], axis=0)
    values_ref[...] = nt_dot(normed_ref[...], weight).astype(BF16)


def mix_kernel(place_ref, probs_refs, values_refs, block_refs, partial_ref):
    right = place_ref[3] == 1
    own_probs, near_probs, far_probs = probs_refs
    size = block_refs[0].shape[0] // 2
    masks = own_probs.shape[1] // 2
    span = own_probs.shape[2]
    columns = ((0,), (1, 3), (2,))

    def rows_of(core, step, which):
        ref = (own_probs, near_probs, far_probs, near_probs)[step]
        start = masks * (which + (2 if step == 3 else 0))
        return ref[core, start : start + masks, :]

    contexts = []
    for core in range(2):
        parts = []
        for values_ref, group in zip(values_refs, columns):
            stack = []
            for column in group:
                which = (0, 1, 1, 0)[column]
                for i in range(2):
                    even = rows_of(core, (0, 2)[i], which)
                    odd = rows_of(core, (3, 1)[i], which)
                    if column % 2:
                        even, odd = odd, even
                    stack.append(jnp.where(right, even, odd))
            mixed = nn_dot(
                jnp.concatenate(stack, axis=0), values_ref[span * core : span * (core + 1), :]
            )
            lane = lax.broadcasted_iota(jnp.int32, (masks, mixed.shape[1]), 1) // size
            context = mixed[:masks, :]
            for head in range(1, len(stack)):
                context = jnp.where(
                    lane == head, mixed[masks * head : masks * (head + 1), :], context
                )
            parts.append(context.astype(BF16))
        contexts.append(jnp.concatenate(parts, axis=1))
    weight = jnp.concatenate([r[size:, :] for r in block_refs], axis=0)
    partial_ref[...] = nn_dot(jnp.concatenate(contexts, axis=0), weight)


def score_kernel(
    place_ref, owner_ref, rows_ref, mine_ref, other_ref, targets_ref, gain_ref, bias_ref,
    dense_ref, decoder_ref, placed_ref,
):
    residual = rows_ref[...] + (mine_ref[...] + other_ref[...])
    average = jnp.mean(residual, axis=1, keepdims=True)
    centred = residual - average
    variance = jnp.mean(centred * centred, axis=1, keepdims=True)
    normed = (centred * lax.rsqrt(variance + epsilon) * gain_ref[...]).astype(BF16)
    dense = nn_dot(normed, dense_ref[...])
    active = 0.5 * dense * (1.0 + lax.erf(dense * np.float32(0.5**0.5)))
    average = jnp.mean(active, axis=1, keepdims=True)
    centred = active - average
    variance = jnp.mean(centred * centred, axis=1, keepdims=True)
    headed = (centred * lax.rsqrt(variance + epsilon)).astype(BF16)
    logits = nt_dot(headed, decoder_ref[...]) + bias_ref[...]
    largest = jnp.max(logits, axis=1, keepdims=True)
    total = jnp.sum(jnp.exp(logits - largest), axis=1, keepdims=True)
    vocab = lax.broadcasted_iota(jnp.int32, logits.shape, 1)
    chosen = jnp.sum(jnp.where(vocab == targets_ref[:, 0:1], logits, 0.0), axis=1, keepdims=True)
    score = chosen - largest - jnp.log(total)
    masks = score.shape[0] // 2
    devices, width = placed_ref.shape
    member = lax.broadcasted_iota(jnp.int32, (devices, masks), 0) % 16
    part = lax.broadcasted_iota(jnp.int32, (devices, masks), 1) // 4
    take = (member == part).astype(F32)
    fits = (
        lax.broadcasted_iota(jnp.int32, (masks, width), 0) % 4
        == lax.broadcasted_iota(jnp.int32, (masks, width), 1) % 4
    )
    layer = lax.broadcasted_iota(jnp.int32, (devices, width), 0) // 16
    slot = lax.broadcasted_iota(jnp.int32, (devices, width), 1) // 4
    wanted = 16 * (2 * layer + place_ref[1]) + slot
    placed = jnp.zeros((devices, width), F32)
    for core in range(2):
        own = jnp.where(fits, score[masks * core : masks * (core + 1), :], 0.0)
        laid = nn_dot(take, own, precision=lax.Precision.HIGHEST)
        placed = jnp.where(wanted == owner_ref[copy_of(place_ref, core)], laid, placed)
    placed_ref[...] = placed


def pull(array, axis, offset):
    size = lax.axis_size(axis)
    return lax.ppermute(array, axis, [((i + offset) % size, i) for i in range(size)])


def swap(array):
    return lax.ppermute(array, "core", [(0, 1), (1, 0)])


def pull_right(array, axis, offset):
    pairs = []
    for core in range(2):
        for y in range(4):
            for x in range(4):
                if (x + y) % 2 == core:
                    to_y = (y - offset) % 4 if axis == "y" else y
                    to_x = (x - offset) % 4 if axis == "x" else x
                    pairs.append(((core * 4 + y) * 4 + x, (core * 4 + to_y) * 4 + to_x))
    return lax.ppermute(array, ("core", "y", "x"), pairs)


def gather_line(block, right, axis):
    behind = pull_right(block, axis, -1)
    ahead = pull_right(block, axis, 1)
    across = pull_right(block, axis, 2)
    return jnp.where(right, block, behind), jnp.where(right, across, ahead)


def gather_plane(low, high, axis):
    ahead_low = pull(low, axis, 1)
    behind_high = pull(high, axis, 3)
    ahead_high = pull(high, axis, 1)
    behind_low = pull(low, axis, 3)
    far_low = pull(ahead_low, axis, 1)
    far_high = pull(behind_high, axis, 3)
    return (
        (low, high),
        (ahead_low, ahead_high, behind_low, behind_high),
        (far_low, far_high),
    )


def on_device(
    hidden_states,
    ln_attn_gain,
    w_qkv,
    output_weight,
    ln_final_gain,
    dense_weight,
    decoder_weight,
    decoder_bias,
    seq_tokens,
    seq_lengths,
    copy_sequence,
    mask_code,
    copy_owner,
):
    _, span, feature = hidden_states.shape
    size = output_weight.shape[0]
    masks = mask_code.shape[1]
    core = lax.axis_index("core")
    member = lax.axis_index(("y", "x"))
    right = (lax.axis_index("x") + lax.axis_index("y")) % 2 == core
    place = jnp.stack([lax.axis_index("z"), core, member, right.astype(core.dtype)])
    place = place.astype(jnp.int32)

    turned = jnp.transpose(w_qkv[:, 0, :])
    key_block = turned[: 2 * size]
    value_block = jnp.concatenate([turned[2 * size :], output_weight[:, 0, :]], axis=0)
    key_low, key_high = gather_line(key_block, right, "x")
    value_low, value_high = gather_line(value_block, right, "y")
    key_groups = gather_plane(key_low, key_high, "y")
    value_groups = gather_plane(value_low, value_high, "x")
    states = hidden_states[0]
    states_other = swap(states)

    cos_table, sin_table = (jnp.asarray(t) for t in rotary_tables(span, size))
    shape = jax.ShapeDtypeStruct
    normed, picked, rows, qcos, qsin, targets = call(
        prepare_kernel,
        [
            shape((2 * span, feature), BF16),
            shape((2 * masks, feature), BF16),
            shape((2 * masks, feature), F32),
            shape((2 * masks, 128), F32),
            shape((2 * masks, 128), F32),
            shape((2 * masks, 128), jnp.int32),
        ],
        3,
        (
            place, copy_sequence, seq_lengths, mask_code.T, seq_tokens, states, states_other,
            ln_attn_gain.reshape(1, -1), cos_table, sin_table,
        ),
        flops=8 * masks * span * feature + 20 * span * feature,
    )

    def keys_call(blocks):
        heads = len(blocks)

        def kernel(*refs):
            keys_kernel(*refs[:9], refs[9 : 9 + heads], refs[9 + heads])

        return call(
            kernel,
            shape((2, heads * masks, span), BF16),
            3,
            (place, copy_sequence, seq_lengths, normed, picked, cos_table, sin_table, qcos, qsin,
             *blocks),
            flops=4 * span * feature * 256,
            exps=2 * heads * masks * span,
        )

    def values_call(blocks):
        heads = len(blocks)

        def kernel(*refs):
            values_kernel(refs[0], refs[1 : 1 + heads], refs[1 + heads])

        return call(
            kernel,
            shape((2 * span, heads * size), BF16),
            0,
            (normed, *blocks),
            flops=4 * span * feature * 256,
        )

    probs = [keys_call(blocks) for blocks in key_groups]
    values = [values_call(blocks) for blocks in value_groups]
    value_blocks = [b for group in value_groups for b in group]

    def kernel(*refs):
        mix_kernel(refs[0], refs[1:4], refs[4:7], refs[7:15], refs[15])

    partial = call(
        kernel,
        shape((2 * masks, feature), F32),
        1,
        (place, *probs, *values, *value_blocks),
        flops=4 * masks * feature * 8 * size,
    )
    placed = call(
        score_kernel,
        shape((128, 64), F32),
        2,
        (
            place, copy_owner, rows, partial, swap(partial), targets,
            ln_final_gain.reshape(1, -1), decoder_bias.reshape(1, -1), dense_weight,
            decoder_weight.T,
        ),
        flops=4 * masks * feature * feature,
    )
    arrived = lax.all_to_all(placed, ("z", "y", "x"), 0, 0, tiled=True)
    return jnp.sum(arrived, axis=0).reshape(16, 4)


def solution(mesh):
    fine = Mesh(mesh.devices.reshape(8, 2, 4, 4), ("z", "core", "y", "x"))
    dp, mp = ("z", "core"), ("y", "x")
    placed = (
        P(("z", "core", "y", "x"), None, None),
        P(),
        P(None, mp, None),
        P(None, mp, None),
        P(),
        P(),
        P(),
        P(),
        P(),
        P(),
        P(),
        P(),
        P(),
    )
    return jax.shard_map(
        on_device, mesh=fine, in_specs=placed, out_specs=P(dp, mp), check_vma=False
    )
```

time: 114 us -> 111 us (0.974)
  waiting for transfers between devices: 25.4 us -> 14.8 us
  blocking collectives: 17.4 us -> 26.2 us
  local copies, waits for them, and re-layouts: 12.8 us -> 5.12 us
  other arithmetic: 2.32 us -> 4.9 us
  starting transfers between devices: 32 us -> 34.4 us
    ppermute x14 -> x12, starting transfers between devices: 21.4 us -> 12.5 us  [pull(): lax.ppermute(array, axis, [((i + offset) % size, i) for i in range(size)])]
    ppermute x14 -> x12, waiting for transfers between devices: 19.2 us -> 10.4 us  [pull(): lax.ppermute(array, axis, [((i + offset) % size, i) for i in range(size)])]
    all_to_all x1, blocking collectives: 17.4 us -> 26.2 us  [on_device(): arrived = lax.all_to_all(placed, ('z', 'y', 'x'), 0, 0, tiled=True)]
    ppermute x10 -> x2, starting transfers between devices: 6.37 us -> 14.7 us  [swap(): return lax.ppermute(array, 'core', [(0, 1), (1, 0)])]
    ppermute x0 -> x6, starting transfers between devices: none -> 7.21 us  [pull_right(): return lax.ppermute(array, ('core', 'y', 'x'), pairs)]
    unnamed x56 -> x40, local copies, waits for them, and re-layouts: 8.48 us -> 1.56 us
    all_to_all x1 -> x0, waiting for transfers between devices: 6.15 us -> none  [on_device(): lax.all_to_all(scores.reshape(members, own), ('y', 'x'), 0, 0, tiled=True)]
    all_to_all x1 -> x0, starting transfers between devices: 4.18 us -> none  [on_device(): lax.all_to_all(scores.reshape(members, own), ('y', 'x'), 0, 0, tiled=True)]
  transfers between devices with their start and end apart: 25 -> 20, of which waited for: 8 -> 5; matrix products, arithmetic and copies ran while one was open for 2% -> 5% of each run, Pallas kernels for 15% -> 17%
where the time goes in v2:
time: 111 us; the launch traced here: 110 us
  starting transfers between devices  34.4 us (31%)
  blocking collectives  26.2 us (24%)
  Pallas kernels  24.2 us (22%)
  waiting for transfers between devices  14.8 us (13%)
  local copies, waits for them, and re-layouts  5.12 us (5%)
  other arithmetic  4.9 us (4%)
    all_to_all x1, blocking collectives, on_device(): arrived = lax.all_to_all(placed, ('z', 'y', 'x'), 0, 0, tiled=True)  26.2 us
    pallas_call x9, Pallas kernels, call(): pl.pallas_call(kernel, out_shape=outs, in_specs=specs, out_specs=jax.tree...  24.2 us
    ppermute x2, starting transfers between devices, swap(): return lax.ppermute(array, 'core', [(0, 1), (1, 0)])  14.7 us
    ppermute x12, starting transfers between devices, pull(): lax.ppermute(array, axis, [((i + offset) % size, i) for i in range(size)])  12.5 us
    ppermute x12, waiting for transfers between devices, pull(): lax.ppermute(array, axis, [((i + offset) % size, i) for i in range(size)])  10.4 us
    ppermute x6, starting transfers between devices, pull_right(): return lax.ppermute(array, ('core', 'y', 'x'), pairs)  7.21 us
    select_n x4, other arithmetic, gather_line(): return (jnp.where(right, block, behind), jnp.where(right, across, ahead))  3 us
    ppermute x6, waiting for transfers between devices, pull_right(): return lax.ppermute(array, ('core', 'y', 'x'), pairs)  2.68 us
  transfers between devices with their start and end apart: 20, of which 5 were waited for; matrix products, arithmetic and copies ran while one was open for 5% of the time, Pallas kernels for 17%

profile of v2, /device:TPU:1, one launch (start us, length us, event | category | flops | bytes accessed | tf_op | source)
XLA Modules:
  0.0 110.0 jit_solution(16029284947084987325)
XLA Ops:
  0.0 0.0 copy-start.3
  0.1 1.9 %slice.8 = bf16[128,1280]{1,0:T(8,128)(2,1)} slice(bf16[192,1280]{1,0:T(8,128)(2,1)} %bitcast.21), slice={[0:128], [0:1280]} | slice | bytes 655360 | tf_op jit(solution)/shard_map/slice | solution.py:304
  1.9 1.3 %collective-permute-start.1 = (bf16[128,1280]{1,0:T(8,128)(2,1)}, bf16[128,1280]{1,0:T(8,128)(2,1)}, u32[]{:S(2)}, u32[]{:S(2)}) collective-permute-start(bf16[128,1280]{1,0:T(8,128)(2,1)} %slice.8), channel_id=1, source_target_pairs={{0,1},{2,3},{5,6},{7,4},{8,9},{10,11},{13,14},{15,12},{17,18},{19,... | collective-permute-start | bytes 983048 | tf_op jit(solution)/shard_map/ppermute | solution.py:255
  3.2 0.7 collective-permute-start.2
  3.9 1.3 %collective-permute-start.3 = (bf16[128,1280]{1,0:T(8,128)(2,1)}, bf16[128,1280]{1,0:T(8,128)(2,1)}, u32[]{:S(2)}, u32[]{:S(2)}) collective-permute-start(bf16[128,1280]{1,0:T(8,128)(2,1)} %slice.8), channel_id=1, source_target_pairs={{0,3},{2,1},{5,4},{7,6},{8,11},{10,9},{13,12},{15,14},{17,16},{19,... | collective-permute-start | bytes 983048 | tf_op jit(solution)/shard_map/ppermute | solution.py:255
  5.2 0.9 slice.9
  6.2 1.7 %pad_maximum_fusion = bf16[128,1280]{1,0:T(8,128)(2,1)} fusion(bf16[64,1280]{1,0:T(8,128)(2,1)} %bitcast.24, bf16[64,1280]{1,0:T(8,128)(2,1)S(1)} %slice.9), kind=kLoop, calls=%fused_computation | loop fusion | flops 655360 | bytes 655360 | tf_op jit(solution)/shard_map/concatenate | solution.py:305
  7.8 1.3 %collective-permute-start.10 = (bf16[128,1280]{1,0:T(8,128)(2,1)}, bf16[128,1280]{1,0:T(8,128)(2,1)S(1)}, u32[]{:S(2)}, u32[]{:S(2)}) collective-permute-start(bf16[128,1280]{1,0:T(8,128)(2,1)} %pad_maximum_fusion), channel_id=1, source_target_pairs={{0,4},{2,6},{5,9},{7,11},{8,12},{10,14},{13,1},{15,3},{17,21},{19,... | collective-permute-start | bytes 983048 | tf_op jit(solution)/shard_map/ppermute | solution.py:255
  9.1 1.4 %collective-permute-start.11 = (bf16[128,1280]{1,0:T(8,128)(2,1)}, bf16[128,1280]{1,0:T(8,128)(2,1)}, u32[]{:S(2)}, u32[]{:S(2)}) collective-permute-start(bf16[128,1280]{1,0:T(8,128)(2,1)} %pad_maximum_fusion), channel_id=1, source_target_pairs={{0,8},{2,10},{5,13},{7,15},{8,0},{10,2},{13,5},{15,7},{17,25},{19,... | collective-permute-start | bytes 983048 | tf_op jit(solution)/shard_map/ppermute | solution.py:255
  10.5 0.8 collective-permute-done.1
  11.3 1.3 %collective-permute-start.12 = (bf16[128,1280]{1,0:T(8,128)(2,1)}, bf16[128,1280]{1,0:T(8,128)(2,1)S(1)}, u32[]{:S(2)}, u32[]{:S(2)}) collective-permute-start(bf16[128,1280]{1,0:T(8,128)(2,1)} %pad_maximum_fusion), channel_id=1, source_target_pairs={{0,12},{2,14},{5,1},{7,3},{8,4},{10,6},{13,9},{15,11},{17,29},{19,... | collective-permute-start | bytes 983048 | tf_op jit(solution)/shard_map/ppermute | solution.py:255
  12.6 1.1 %broadcast_select_fusion.3.refs_9_ = bf16[128,1280]{1,0:T(8,128)(2,1)S(1)} fusion(bf16[128,1280]{1,0:T(8,128)(2,1)} %collective-permute-done.1, pred[]{:T(512)S(6)} %eq.5, bf16[192,1280]{1,0:T(8,128)(2,1)} %bitcast.23), kind=kLoop, calls=%fused_computation.4 | loop fusion | flops 163840 | bytes 983041 | tf_op jit(solution)/shard_map/jit(_where)/select_n | solution.py:262
  13.7 0.0 collective-permute-done.2
  13.7 12.0 %collective-permute-start = (bf16[640,1280]{1,0:T(8,128)(2,1)}, bf16[640,1280]{1,0:T(8,128)(2,1)}, u32[]{:S(2)}, u32[]{:S(2)}) collective-permute-start(bf16[640,1280]{1,0:T(8,128)(2,1)} %bitcast.15), channel_id=1, source_target_pairs={{0,16},{16,0},{1,17},{17,1},{2,18},{18,2},{3,19},{19,3},{4,20},{20... | collective-permute-start | bytes 4915208 | tf_op jit(solution)/shard_map/ppermute | solution.py:243
  25.7 0.0 collective-permute-done.3
  25.7 0.0 collective-permute-start.4
  25.7 1.7 %broadcast_select_fusion.2.refs_10_ = bf16[128,1280]{1,0:T(8,128)(2,1)} fusion(bf16[128,1280]{1,0:T(8,128)(2,1)S(1)} %collective-permute-done.2, bf16[128,1280]{1,0:T(8,128)(2,1)} %collective-permute-done.3, pred[]{:T(512)S(6)} %eq.5), kind=kLoop, calls=%fused_computation.3 | loop fusion | flops 163840 | bytes 983041 | tf_op jit(solution)/shard_map/jit(_where)/select_n | solution.py:262
  27.5 0.0 collective-permute-done.10
  27.5 0.5 collective-permute-start.6
  28.0 0.1 broadcast_select_fusion.1.refs_1_.refs_7_
  28.1 2.2 %collective-permute-start.5 = (bf16[128,1280]{1,0:T(8,128)(2,1)}, bf16[128,1280]{1,0:T(8,128)(2,1)S(1)}, u32[]{:S(2)}, u32[]{:S(2)}) collective-permute-start(bf16[128,1280]{1,0:T(8,128)(2,1)} %broadcast_select_fusion.2.refs_10_), channel_id=1, source_target_pairs={{4,0},{8,4},{12,8},{0,12},{5,1},{9,5},{13,9},{1,13},{6,2},{10,6},{... | collective-permute-start | bytes 983048 | tf_op jit(solution)/shard_map/ppermute | solution.py:239
  30.3 1.9 %collective-permute-done.12 = bf16[128,1280]{1,0:T(8,128)(2,1)S(1)} collective-permute-done((bf16[128,1280]{1,0:T(8,128)(2,1)}, bf16[128,1280]{1,0:T(8,128)(2,1)S(1)}, u32[]{:S(2)}, u32[]{:S(2)}) %collective-permute-start.12) | collective-permute-done | bytes 327712 | tf_op jit(solution)/shard_map/ppermute | solution.py:255
  32.2 7.0 %collective-permute-done.4.refs_9_ = bf16[128,1280]{1,0:T(8,128)(2,1)} collective-permute-done((bf16[128,1280]{1,0:T(8,128)(2,1)S(1)}, bf16[128,1280]{1,0:T(8,128)(2,1)}, u32[]{:S(2)}, u32[]{:S(2)}) %collective-permute-start.4) | collective-permute-done | bytes 327712 | tf_op jit(solution)/shard_map/ppermute | solution.py:239
  39.2 2.1 %collective-permute-start.13 = (bf16[128,1280]{1,0:T(8,128)(2,1)S(1)}, bf16[128,1280]{1,0:T(8,128)(2,1)S(1)}, u32[]{:S(2)}, u32[]{:S(2)}) collective-permute-start(bf16[128,1280]{1,0:T(8,128)(2,1)S(1)} %broadcast_select_fusion.1.refs_1_.refs_7_), channel_id=1, source_target_pairs={{1,0},{2,1},{3,2},{0,3},{5,4},{6,5},{7,6},{4,7},{9,8},{10,9},{11,1... | collective-permute-start | bytes 983048 | tf_op jit(solution)/shard_map/ppermute | solution.py:239
  41.3 0.1 broadcast_select_fusion.refs_2_.refs_8_
  41.4 3.4 %collective-permute-done.5.refs_10_ = bf16[128,1280]{1,0:T(8,128)(2,1)S(1)} collective-permute-done((bf16[128,1280]{1,0:T(8,128)(2,1)}, bf16[128,1280]{1,0:T(8,128)(2,1)S(1)}, u32[]{:S(2)}, u32[]{:S(2)}) %collective-permute-start.5) | collective-permute-done | bytes 327712 | tf_op jit(solution)/shard_map/ppermute | solution.py:239
  44.8 0.7 copy-done.8
  45.5 0.0 collective-permute-start.16
  45.5 0.0 collective-permute-done.6.refs_11_
  45.5 0.7 copy-done.6
  46.2 2.8 %collective-permute-start.8 = (bf16[128,1280]{1,0:T(8,128)(2,1)}, bf16[128,1280]{1,0:T(8,128)(2,1)}, u32[]{:S(2)}, u32[]{:S(2)}) collective-permute-start(bf16[128,1280]{1,0:T(8,128)(2,1)} %collective-permute-done.4.refs_9_), channel_id=1, source_target_pairs={{4,0},{8,4},{12,8},{0,12},{5,1},{9,5},{13,9},{1,13},{6,2},{10,6},{... | collective-permute-start | bytes 983048 | tf_op jit(solution)/shard_map/ppermute | solution.py:239
  49.0 0.0 collective-permute-done.7.refs_12_
  49.0 0.0 collective-permute-start.9
  49.0 0.1 pad_add_fusion.place_ref.refs_0_
  49.1 1.9 %collective-permute-start.14 = (bf16[128,1280]{1,0:T(8,128)(2,1)S(1)}, bf16[128,1280]{1,0:T(8,128)(2,1)S(1)}, u32[]{:S(2)}, u32[]{:S(2)}) collective-permute-start(bf16[128,1280]{1,0:T(8,128)(2,1)S(1)} %broadcast_select_fusion.refs_2_.refs_8_), channel_id=1, source_target_pairs={{1,0},{2,1},{3,2},{0,3},{5,4},{6,5},{7,6},{4,7},{9,8},{10,9},{11,1... | collective-permute-start | bytes 983048 | tf_op jit(solution)/shard_map/ppermute | solution.py:239
  51.1 0.0 collective-permute-done.other_ref
  51.1 0.0 collective-permute-start.15
  51.2 6.6 %shard_map.145 = (bf16[1280,1280]{1,0:T(8,128)(2,1)S(1)}, bf16[128,1280]{1,0:T(8,128)(2,1)S(1)}, f32[128,1280]{1,0:T(8,128)S(1)}, f32[128,128]{1,0:T(8,128)S(1)}...) custom-call(s32[4]{0:T(128)S(1)} %pad_add_fusion.place_ref.refs_0_, s32[256]{0:T(256)S(1)} %copy-done.13, ...), custom_call_target="tpu_custom_call" | custom-call | flops 435814400 | bytes 8521840 | tf_op jit(solution)/shard_map/pallas_call | solution.py:50
  57.7 0.0 collective-permute-done.16.refs_4_.refs_12_
  57.8 2.9 %collective-permute-start.17 = (bf16[128,1280]{1,0:T(8,128)(2,1)S(1)}, bf16[128,1280]{1,0:T(8,128)(2,1)S(1)}, u32[]{:S(2)}, u32[]{:S(2)}) collective-permute-start(bf16[128,1280]{1,0:T(8,128)(2,1)S(1)} %collective-permute-done.13.refs_1_.refs_9_), channel_id=1, source_target_pairs={{1,0},{2,1},{3,2},{0,3},{5,4},{6,5},{7,6},{4,7},{9,8},{10,9},{11,1... | collective-permute-start | bytes 983048 | tf_op jit(solution)/shard_map/ppermute | solution.py:239
  60.7 0.0 collective-permute-done.8.refs_9_
  60.7 0.0 collective-permute-start.18
  60.7 1.0 shard_map.149.refs_4_
  61.7 2.9 %shard_map.146.refs_1_ = bf16[2,128,640]{2,1,0:T(8,128)(2,1)S(1)} custom-call(s32[4]{0:T(128)S(1)} %pad_add_fusion.place_ref.refs_0_, s32[256]{0:T(256)S(1)} %copy-done.13, s32[24]{0:T(128)S(1)} %copy-done.14, bf16[1280,1280]{1,0:T(8,128)(2,1)S(1)} %get-tuple-element.12.refs_3_.refs_0_, bf16[128,1280]{1,0:T(8,128)(2,1)S(1)} %get-tuple-element.13.refs_4_, ...), custom_call_target="tpu_custom_call" | custom-call | flops 838860800 | bytes 5375088 | tf_op jit(solution)/shard_map/pallas_call | solution.py:50
  64.6 3.4 %shard_map.147.refs_2_ = bf16[2,256,640]{2,1,0:T(8,128)(2,1)S(1)} custom-call(s32[4]{0:T(128)S(1)} %pad_add_fusion.place_ref.refs_0_, s32[256]{0:T(256)S(1)} %copy-done.13, s32[24]{0:T(128)S(1)} %copy-done.14, bf16[1280,1280]{1,0:T(8,128)(2,1)S(1)} %get-tuple-element.12.refs_3_.refs_0_, bf16[128,1280]{1,0:T(8,128)(2,1)S(1)} %get-tuple-element.13.refs_4_, ...), custom_call_target="tpu_custom_call" | custom-call | flops 838860800 | bytes 6358128 | tf_op jit(solution)/shard_map/pallas_call | solution.py:50
  68.0 0.0 collective-permute-done.9.refs_10_
  68.0 2.8 %shard_map.148.refs_3_ = bf16[2,128,640]{2,1,0:T(8,128)(2,1)S(1)} custom-call(s32[4]{0:T(128)S(1)} %pad_add_fusion.place_ref.refs_0_, s32[256]{0:T(256)S(1)} %copy-done.13, s32[24]{0:T(128)S(1)} %copy-done.14, bf16[1280,1280]{1,0:T(8,128)(2,1)S(1)} %get-tuple-element.12.refs_3_.refs_0_, bf16[128,1280]{1,0:T(8,128)(2,1)S(1)} %get-tuple-element.13.refs_4_, ...), custom_call_target="tpu_custom_call" | custom-call | flops 838860800 | bytes 5375088 | tf_op jit(solution)/shard_map/pallas_call | solution.py:50
  70.9 0.0 collective-permute-done.15.refs_3_.refs_11_
  70.9 2.0 %shard_map.150.refs_5_ = bf16[1280,256]{1,0:T(8,128)(2,1)S(1)} custom-call(bf16[1280,1280]{1,0:T(8,128)(2,1)S(1)} %get-tuple-element.12.refs_3_.refs_0_, bf16[128,1280]{1,0:T(8,128)(2,1)S(1)} %collective-permute-done.13.refs_1_.refs_9_, bf16[128,1280]{1,0:T(8,128)(2,1)S(1)} %collective-permute-done.14.refs_2_.refs_10_, ...), custom_call_target="tpu_custom_call" | custom-call | flops 838860800 | bytes 5242880 | tf_op jit(solution)/shard_map/pallas_call | solution.py:50
  72.9 0.0 collective-permute-done.18.refs_2_.refs_14_
  73.0 1.0 shard_map.151.refs_6_
  74.0 0.0 copy-start.19
  74.0 0.0 copy-start.2
  74.0 0.0 copy-start.10
  74.0 0.0 copy-start.15
  74.0 0.0 copy-start.16
  74.0 2.0 %shard_map.152.mine_ref = f32[128,1280]{1,0:T(8,128)S(1)} custom-call(s32[4]{0:T(128)S(1)} %pad_add_fusion.place_ref.refs_0_, bf16[2,128,640]{2,1,0:T(8,128)(2,1)S(1)} %shard_map.146.refs_1_, bf16[2,256,640]{2,1,0:T(8,128)(2,1)S(1)} %shard_map.147.refs_2_, bf16[2,128,640]{2,1,0:T(8,128)(2,1)S(1)} %shard_map.148.refs_3_, ...), custom_call_target="tpu_custom_call" | custom-call | flops 167772160 | bytes 5898256 | tf_op jit(solution)/shard_map/pallas_call | solution.py:50
  76.1 2.7 %collective-permute-start.19 = (f32[128,1280]{1,0:T(8,128)S(1)}, f32[128,1280]{1,0:T(8,128)S(1)}, u32[]{:S(2)}, u32[]{:S(2)}) collective-permute-start(f32[128,1280]{1,0:T(8,128)S(1)} %shard_map.152.mine_ref), channel_id=1, source_target_pairs={{0,16},{16,0},{1,17},{17,1},{2,18},{18,2},{3,19},{19,3},{4,20},{20... | collective-permute-start | bytes 1966088 | tf_op jit(solution)/shard_map/ppermute | solution.py:243
  78.8 1.7 %collective-permute-done.19.other_ref = f32[128,1280]{1,0:T(8,128)S(1)} collective-permute-done((f32[128,1280]{1,0:T(8,128)S(1)}, f32[128,1280]{1,0:T(8,128)S(1)}, u32[]{:S(2)}, u32[]{:S(2)}) %collective-permute-start.19) | collective-permute-done | bytes 655392 | tf_op jit(solution)/shard_map/ppermute | solution.py:243
  80.5 2.4 %shard_map.153 = f32[128,64]{1,0:T(8,128)S(1)} custom-call(s32[4]{0:T(128)S(1)} %pad_add_fusion.place_ref.refs_0_, s32[256]{0:T(256)S(1)} %copy-done.15, f32[128,1280]{1,0:T(8,128)S(1)} %get-tuple-element.11.rows_ref, f32[128,1280]{1,0:T(8,128)S(1)} %shard_map.152.mine_ref, f32[128,1280]{1,0:T(8,128)S(1)} %collective-permute-done.19.other_ref, ...), custom_call_target="tpu_custom_call" | custom-call | flops 419430400 | bytes 5431956 | tf_op jit(solution)/shard_map/pallas_call | solution.py:50
  82.9 26.2 %all_to_all.9 = f32[128,1,64]{2,1,0:T(1,128)S(1)} all-to-all(f32[128,1,64]{2,1,0:T(1,128)S(1)} %bitcast.17), channel_id=1, replica_groups=mesh['z'=8,'core'=2,'y'=4,'x'=4] {'z','y','x'}, dimensions={0} | all-to-all | bytes 65536 | tf_op jit(solution)/shard_map/all_to_all | solution.py:388
  109.1 0.2 reduce_sum.9
  109.2 0.1 reshape.17
  109.3 0.7 copy.19
  (39 shorter events, 0.1 us)
Async XLA Ops:
  0.0 51.1 %copy-start = (f32[640,128]{1,0:T(8,128)S(1)}, f32[640,128]{1,0:T(8,128)}, u32[]{:S(2)}) copy-start(f32[640,128]{1,0:T(8,128)} %constant.40.clone.cos_ref.refs_5_) | copy-start | bytes 983044
  0.0 51.1 %copy-start.1 = (f32[640,128]{1,0:T(8,128)S(1)}, f32[640,128]{1,0:T(8,128)}, u32[]{:S(2)}) copy-start(f32[640,128]{1,0:T(8,128)} %constant.41.clone.sin_ref.refs_6_) | copy-start | bytes 983044
  0.0 28.0 %copy-start.17 = (bf16[64,1,1280]{2,0,1:T(8,128)(2,1)S(1)}, bf16[64,1,1280]{2,0,1:T(8,128)(2,1)}, u32[]{:S(2)}) copy-start(bf16[64,1,1280]{2,0,1:T(8,128)(2,1)} %param.18) | copy-start | bytes 491524
  0.0 51.1 %copy-start.3 = (bf16[1,640,1280]{2,1,0:T(8,128)(2,1)S(1)}, bf16[1,640,1280]{2,1,0:T(8,128)(2,1)}, u32[]{:S(2)}) copy-start(bf16[1,640,1280]{2,1,0:T(8,128)(2,1)} %param.15) | copy-start | bytes 4915204
  0.0 49.1 %copy-start.18 = (f32[1280]{0:T(1024)S(1)}, f32[1280]{0:T(1024)}, u32[]{:S(2)}) copy-start(f32[1280]{0:T(1024)} %param.16) | copy-start | bytes 15364
  0.0 51.1 %copy-start.13 = (s32[256]{0:T(256)S(1)}, s32[256]{0:T(256)}, u32[]{:S(2)}) copy-start(s32[256]{0:T(256)} %refs_1_.5) | copy-start | bytes 3076
  0.0 51.1 %copy-start.14 = (s32[24]{0:T(128)S(1)}, s32[24]{0:T(128)}, u32[]{:S(2)}) copy-start(s32[24]{0:T(128)} %refs_2_.5) | copy-start | bytes 292
  0.1 51.1 %copy-start.11 = (s32[256,64]{0,1:T(8,128)S(1)}, s32[256,64]{0,1:T(8,128)}, u32[]{:S(2)}) copy-start(s32[256,64]{0,1:T(8,128)} %param.26) | copy-start | bytes 196612
  0.1 51.1 %copy-start.12 = (s32[24,640]{1,0:T(8,128)S(1)}, s32[24,640]{1,0:T(8,128)}, u32[]{:S(2)}) copy-start(s32[24,640]{1,0:T(8,128)} %tokens_ref.1) | copy-start | bytes 184324
  1.9 9.4 %collective-permute-start.1 = (bf16[128,1280]{1,0:T(8,128)(2,1)}, bf16[128,1280]{1,0:T(8,128)(2,1)}, u32[]{:S(2)}, u32[]{:S(2)}) collective-permute-start(bf16[128,1280]{1,0:T(8,128)(2,1)} %slice.8), channel_id=1, source_target_pairs={{0,1},{2,3},{5,6},{7,4},{8,9},{10,11},{13,14},{15,12},{17,18},{19,... | collective-permute-start | bytes 983048 | tf_op jit(solution)/shard_map/ppermute | solution.py:255
  3.2 10.5 %collective-permute-start.2 = (bf16[128,1280]{1,0:T(8,128)(2,1)}, bf16[128,1280]{1,0:T(8,128)(2,1)S(1)}, u32[]{:S(2)}, u32[]{:S(2)}) collective-permute-start(bf16[128,1280]{1,0:T(8,128)(2,1)} %slice.8), channel_id=1, source_target_pairs={{0,2},{2,0},{5,7},{7,5},{8,10},{10,8},{13,15},{15,13},{17,19},{19,... | collective-permute-start | bytes 983048 | tf_op jit(solution)/shard_map/ppermute | solution.py:255
  3.9 21.8 %collective-permute-start.3 = (bf16[128,1280]{1,0:T(8,128)(2,1)}, bf16[128,1280]{1,0:T(8,128)(2,1)}, u32[]{:S(2)}, u32[]{:S(2)}) collective-permute-start(bf16[128,1280]{1,0:T(8,128)(2,1)} %slice.8), channel_id=1, source_target_pairs={{0,3},{2,1},{5,4},{7,6},{8,11},{10,9},{13,12},{15,14},{17,16},{19,... | collective-permute-start | bytes 983048 | tf_op jit(solution)/shard_map/ppermute | solution.py:255
  7.8 19.7 %collective-permute-start.10 = (bf16[128,1280]{1,0:T(8,128)(2,1)}, bf16[128,1280]{1,0:T(8,128)(2,1)S(1)}, u32[]{:S(2)}, u32[]{:S(2)}) collective-permute-start(bf16[128,1280]{1,0:T(8,128)(2,1)} %pad_maximum_fusion), channel_id=1, source_target_pairs={{0,4},{2,6},{5,9},{7,11},{8,12},{10,14},{13,1},{15,3},{17,21},{19,... | collective-permute-start | bytes 983048 | tf_op jit(solution)/shard_map/ppermute | solution.py:255
  9.1 19.0 %collective-permute-start.11 = (bf16[128,1280]{1,0:T(8,128)(2,1)}, bf16[128,1280]{1,0:T(8,128)(2,1)}, u32[]{:S(2)}, u32[]{:S(2)}) collective-permute-start(bf16[128,1280]{1,0:T(8,128)(2,1)} %pad_maximum_fusion), channel_id=1, source_target_pairs={{0,8},{2,10},{5,13},{7,15},{8,0},{10,2},{13,5},{15,7},{17,25},{19,... | collective-permute-start | bytes 983048 | tf_op jit(solution)/shard_map/ppermute | solution.py:255
  11.3 20.9 %collective-permute-start.12 = (bf16[128,1280]{1,0:T(8,128)(2,1)}, bf16[128,1280]{1,0:T(8,128)(2,1)S(1)}, u32[]{:S(2)}, u32[]{:S(2)}) collective-permute-start(bf16[128,1280]{1,0:T(8,128)(2,1)} %pad_maximum_fusion), channel_id=1, source_target_pairs={{0,12},{2,14},{5,1},{7,3},{8,4},{10,6},{13,9},{15,11},{17,29},{19,... | collective-permute-start | bytes 983048 | tf_op jit(solution)/shard_map/ppermute | solution.py:255
  13.7 27.7 %copy-start.4 = (bf16[128,1280]{1,0:T(8,128)(2,1)}, bf16[128,1280]{1,0:T(8,128)(2,1)S(1)}, u32[]{:S(2)}) copy-start(bf16[128,1280]{1,0:T(8,128)(2,1)S(1)} %broadcast_select_fusion.3.refs_9_) | copy-start | bytes 983044
  13.7 37.3 %collective-permute-start = (bf16[640,1280]{1,0:T(8,128)(2,1)}, bf16[640,1280]{1,0:T(8,128)(2,1)}, u32[]{:S(2)}, u32[]{:S(2)}) collective-permute-start(bf16[640,1280]{1,0:T(8,128)(2,1)} %bitcast.15), channel_id=1, source_target_pairs={{0,16},{16,0},{1,17},{17,1},{2,18},{18,2},{3,19},{19,3},{4,20},{20... | collective-permute-start | bytes 4915208 | tf_op jit(solution)/shard_map/ppermute | solution.py:243
  25.7 13.5 %collective-permute-start.4 = (bf16[128,1280]{1,0:T(8,128)(2,1)S(1)}, bf16[128,1280]{1,0:T(8,128)(2,1)}, u32[]{:S(2)}, u32[]{:S(2)}) collective-permute-start(bf16[128,1280]{1,0:T(8,128)(2,1)S(1)} %broadcast_select_fusion.3.refs_9_), channel_id=1, source_target_pairs={{4,0},{8,4},{12,8},{0,12},{5,1},{9,5},{13,9},{1,13},{6,2},{10,6},{... | collective-permute-start | bytes 983048 | tf_op jit(solution)/shard_map/ppermute | solution.py:239
  27.5 18.0 %collective-permute-start.6 = (bf16[128,1280]{1,0:T(8,128)(2,1)S(1)}, bf16[128,1280]{1,0:T(8,128)(2,1)S(1)}, u32[]{:S(2)}, u32[]{:S(2)}) collective-permute-start(bf16[128,1280]{1,0:T(8,128)(2,1)S(1)} %broadcast_select_fusion.3.refs_9_), channel_id=1, source_target_pairs={{12,0},{0,4},{4,8},{8,12},{13,1},{1,5},{5,9},{9,13},{14,2},{2,6},{... | collective-permute-start | bytes 983048 | tf_op jit(solution)/shard_map/ppermute | solution.py:239
  28.1 16.7 %collective-permute-start.5 = (bf16[128,1280]{1,0:T(8,128)(2,1)}, bf16[128,1280]{1,0:T(8,128)(2,1)S(1)}, u32[]{:S(2)}, u32[]{:S(2)}) collective-permute-start(bf16[128,1280]{1,0:T(8,128)(2,1)} %broadcast_select_fusion.2.refs_10_), channel_id=1, source_target_pairs={{4,0},{8,4},{12,8},{0,12},{5,1},{9,5},{13,9},{1,13},{6,2},{10,6},{... | collective-permute-start | bytes 983048 | tf_op jit(solution)/shard_map/ppermute | solution.py:239
  32.2 16.8 %collective-permute-start.7 = (bf16[128,1280]{1,0:T(8,128)(2,1)}, bf16[128,1280]{1,0:T(8,128)(2,1)}, u32[]{:S(2)}, u32[]{:S(2)}) collective-permute-start(bf16[128,1280]{1,0:T(8,128)(2,1)} %broadcast_select_fusion.2.refs_10_), channel_id=1, source_target_pairs={{12,0},{0,4},{4,8},{8,12},{13,1},{1,5},{5,9},{9,13},{14,2},{2,6},{... | collective-permute-start | bytes 983048 | tf_op jit(solution)/shard_map/ppermute | solution.py:239
  39.2 9.9 %collective-permute-start.13 = (bf16[128,1280]{1,0:T(8,128)(2,1)S(1)}, bf16[128,1280]{1,0:T(8,128)(2,1)S(1)}, u32[]{:S(2)}, u32[]{:S(2)}) collective-permute-start(bf16[128,1280]{1,0:T(8,128)(2,1)S(1)} %broadcast_select_fusion.1.refs_1_.refs_7_), channel_id=1, source_target_pairs={{1,0},{2,1},{3,2},{0,3},{5,4},{6,5},{7,6},{4,7},{9,8},{10,9},{11,1... | collective-permute-start | bytes 983048 | tf_op jit(solution)/shard_map/ppermute | solution.py:239
  44.8 0.7 copy-start.8
  45.5 12.3 %collective-permute-start.16 = (bf16[128,1280]{1,0:T(8,128)(2,1)S(1)}, bf16[128,1280]{1,0:T(8,128)(2,1)}, u32[]{:S(2)}, u32[]{:S(2)}) collective-permute-start(bf16[128,1280]{1,0:T(8,128)(2,1)S(1)} %broadcast_select_fusion.refs_2_.refs_8_), channel_id=1, source_target_pairs={{3,0},{0,1},{1,2},{2,3},{7,4},{4,5},{5,6},{6,7},{11,8},{8,9},{9,10... | collective-permute-start | bytes 983048 | tf_op jit(solution)/shard_map/ppermute | solution.py:239
  45.5 0.7 copy-start.6
  46.2 14.4 %collective-permute-start.8 = (bf16[128,1280]{1,0:T(8,128)(2,1)}, bf16[128,1280]{1,0:T(8,128)(2,1)}, u32[]{:S(2)}, u32[]{:S(2)}) collective-permute-start(bf16[128,1280]{1,0:T(8,128)(2,1)} %collective-permute-done.4.refs_9_), channel_id=1, source_target_pairs={{4,0},{8,4},{12,8},{0,12},{5,1},{9,5},{13,9},{1,13},{6,2},{10,6},{... | collective-permute-start | bytes 983048 | tf_op jit(solution)/shard_map/ppermute | solution.py:239
  49.0 19.0 %collective-permute-start.9 = (bf16[128,1280]{1,0:T(8,128)(2,1)}, bf16[128,1280]{1,0:T(8,128)(2,1)S(1)}, u32[]{:S(2)}, u32[]{:S(2)}) collective-permute-start(bf16[128,1280]{1,0:T(8,128)(2,1)} %collective-permute-done.7.refs_12_), channel_id=1, source_target_pairs={{12,0},{0,4},{4,8},{8,12},{13,1},{1,5},{5,9},{9,13},{14,2},{2,6},{... | collective-permute-start | bytes 983048 | tf_op jit(solution)/shard_map/ppermute | solution.py:239
  49.1 21.7 %collective-permute-start.14 = (bf16[128,1280]{1,0:T(8,128)(2,1)S(1)}, bf16[128,1280]{1,0:T(8,128)(2,1)S(1)}, u32[]{:S(2)}, u32[]{:S(2)}) collective-permute-start(bf16[128,1280]{1,0:T(8,128)(2,1)S(1)} %broadcast_select_fusion.refs_2_.refs_8_), channel_id=1, source_target_pairs={{1,0},{2,1},{3,2},{0,3},{5,4},{6,5},{7,6},{4,7},{9,8},{10,9},{11,1... | collective-permute-start | bytes 983048 | tf_op jit(solution)/shard_map/ppermute | solution.py:239
  51.1 19.8 %collective-permute-start.15 = (bf16[128,1280]{1,0:T(8,128)(2,1)S(1)}, bf16[128,1280]{1,0:T(8,128)(2,1)S(1)}, u32[]{:S(2)}, u32[]{:S(2)}) collective-permute-start(bf16[128,1280]{1,0:T(8,128)(2,1)S(1)} %broadcast_select_fusion.1.refs_1_.refs_7_), channel_id=1, source_target_pairs={{3,0},{0,1},{1,2},{2,3},{7,4},{4,5},{5,6},{6,7},{11,8},{8,9},{9,10... | collective-permute-start | bytes 983048 | tf_op jit(solution)/shard_map/ppermute | solution.py:239
  51.1 10.6 %copy-start.5 = (bf16[128,1280]{1,0:T(8,128)(2,1)S(1)}, bf16[128,1280]{1,0:T(8,128)(2,1)}, u32[]{:S(2)}) copy-start(bf16[128,1280]{1,0:T(8,128)(2,1)} %copy-done.4) | copy-start | bytes 983044
  57.8 15.2 %collective-permute-start.17 = (bf16[128,1280]{1,0:T(8,128)(2,1)S(1)}, bf16[128,1280]{1,0:T(8,128)(2,1)S(1)}, u32[]{:S(2)}, u32[]{:S(2)}) collective-permute-start(bf16[128,1280]{1,0:T(8,128)(2,1)S(1)} %collective-permute-done.13.refs_1_.refs_9_), channel_id=1, source_target_pairs={{1,0},{2,1},{3,2},{0,3},{5,4},{6,5},{7,6},{4,7},{9,8},{10,9},{11,1... | collective-permute-start | bytes 983048 | tf_op jit(solution)/shard_map/ppermute | solution.py:239
  60.7 12.3 %collective-permute-start.18 = (bf16[128,1280]{1,0:T(8,128)(2,1)}, bf16[128,1280]{1,0:T(8,128)(2,1)S(1)}, u32[]{:S(2)}, u32[]{:S(2)}) collective-permute-start(bf16[128,1280]{1,0:T(8,128)(2,1)} %collective-permute-done.16.refs_4_.refs_12_), channel_id=1, source_target_pairs={{3,0},{0,1},{1,2},{2,3},{7,4},{4,5},{5,6},{6,7},{11,8},{8,9},{9,10... | collective-permute-start | bytes 983048 | tf_op jit(solution)/shard_map/ppermute | solution.py:239
  61.7 2.9 %copy-start.7 = (bf16[128,1280]{1,0:T(8,128)(2,1)S(1)}, bf16[128,1280]{1,0:T(8,128)(2,1)}, u32[]{:S(2)}) copy-start(bf16[128,1280]{1,0:T(8,128)(2,1)} %copy-done.6) | copy-start | bytes 983044
  61.7 2.9 %copy-start.9 = (bf16[128,1280]{1,0:T(8,128)(2,1)S(1)}, bf16[128,1280]{1,0:T(8,128)(2,1)}, u32[]{:S(2)}) copy-start(bf16[128,1280]{1,0:T(8,128)(2,1)} %copy-done.8) | copy-start | bytes 983044
  74.0 4.8 %copy-start.19 = (f32[1280]{0:T(1024)S(1)}, f32[1280]{0:T(1024)}, u32[]{:S(2)}) copy-start(f32[1280]{0:T(1024)} %param.19) | copy-start | bytes 15364
  74.0 6.5 %copy-start.2 = (bf16[1280,1280]{1,0:T(8,128)(2,1)S(1)}, bf16[1280,1280]{1,0:T(8,128)(2,1)}, u32[]{:S(2)}) copy-start(bf16[1280,1280]{1,0:T(8,128)(2,1)} %dense_ref.1) | copy-start | bytes 9830404
  74.0 6.5 %copy-start.10 = (bf16[1280,33]{0,1:T(8,128)(2,1)S(1)}, bf16[1280,33]{0,1:T(8,128)(2,1)}, u32[]{:S(2)}) copy-start(bf16[1280,33]{0,1:T(8,128)(2,1)} %param.21) | copy-start | bytes 253444
  74.0 6.5 %copy-start.15 = (s32[256]{0:T(256)S(1)}, s32[256]{0:T(256)}, u32[]{:S(2)}) copy-start(s32[256]{0:T(256)} %owner_ref.1) | copy-start | bytes 3076
  74.0 6.5 %copy-start.16 = (f32[33]{0:T(128)S(1)}, f32[33]{0:T(128)}, u32[]{:S(2)}) copy-start(f32[33]{0:T(128)} %param.22) | copy-start | bytes 400
  76.1 4.4 %collective-permute-start.19 = (f32[128,1280]{1,0:T(8,128)S(1)}, f32[128,1280]{1,0:T(8,128)S(1)}, u32[]{:S(2)}, u32[]{:S(2)}) collective-permute-start(f32[128,1280]{1,0:T(8,128)S(1)} %shard_map.152.mine_ref), channel_id=1, source_target_pairs={{0,16},{16,0},{1,17},{17,1},{2,18},{18,2},{3,19},{19,3},{4,20},{20... | collective-permute-start | bytes 1966088 | tf_op jit(solution)/shard_map/ppermute | solution.py:243

commit v3 on v2

v3 whole, which is shorter than its diff:
```python
import numpy as np
import jax
import jax.numpy as jnp
from jax import lax
from jax.experimental import pallas as pl
from jax.experimental.pallas import tpu as pltpu
from jax.sharding import Mesh, PartitionSpec as P

epsilon = 1e-05
F32 = jnp.float32
BF16 = jnp.bfloat16


def rotary_tables(seq_span, head_size):
    half = head_size // 2
    power = (np.arange(half, dtype=np.float32) * np.float32(2.0 / head_size)).astype(np.float32)
    frequency = (np.float32(1.0) / np.power(np.float32(10000.0), power)).astype(np.float32)
    angles = (np.arange(seq_span, dtype=np.float32)[:, None] * frequency[None, :]).astype(np.float32)
    cosine = np.cos(angles.astype(np.float64)).astype(np.float32)
    sine = np.sin(angles.astype(np.float64)).astype(np.float32)
    cos_table = np.concatenate([cosine] * 4, axis=1)
    sin_table = np.concatenate([-sine, sine] * 2, axis=1)
    return cos_table, sin_table


def nt_dot(a, b):
    return lax.dot_general(a, b, (((1,), (1,)), ((), ())), preferred_element_type=F32)


def nn_dot(a, b, **options):
    return lax.dot_general(a, b, (((1,), (0,)), ((), ())), preferred_element_type=F32, **options)


def rotate(part, cos_table, sin_table, half):
    width = part.shape[1]
    lane = lax.broadcasted_iota(jnp.int32, part.shape, 1) % (2 * half)
    turned = jnp.where(
        lane < half,
        pltpu.roll(part, width - half, 1),
        pltpu.roll(part, half, 1),
    )
    return part * cos_table + turned * sin_table


def call(kernel, outs, n_smem, args, flops=0, exps=0, vmem=24 * 1024 * 1024):
    space = pltpu.MemorySpace
    specs = [pl.BlockSpec(memory_space=space.SMEM)] * n_smem
    specs += [pl.BlockSpec(memory_space=space.VMEM)] * (len(args) - n_smem)
    moved = sum(a.size * a.dtype.itemsize for a in list(args) + jax.tree.leaves(outs))
    return pl.pallas_call(
        kernel,
        out_shape=outs,
        in_specs=specs,
        out_specs=jax.tree.map(lambda _: pl.BlockSpec(memory_space=space.VMEM), outs),
        cost_estimate=pl.CostEstimate(flops=flops, transcendentals=exps, bytes_accessed=moved),
        compiler_params=pltpu.CompilerParams(vmem_limit_bytes=vmem),
    )(*args)


def pack_kernel(turned_ref, out_ref, key_ref, value_ref, sems):
    size = out_ref.shape[0]
    copies = (
        pltpu.make_async_copy(turned_ref.at[: 2 * size], key_ref, sems.at[0]),
        pltpu.make_async_copy(turned_ref.at[2 * size :], value_ref.at[:size], sems.at[1]),
        pltpu.make_async_copy(out_ref, value_ref.at[size:], sems.at[2]),
    )
    for copy in copies:
        copy.start()
    for copy in copies:
        copy.wait()


def pack(turned, out_weight):
    size, feature = out_weight.shape
    anywhere = pl.BlockSpec(memory_space=pl.ANY)
    return pl.pallas_call(
        pack_kernel,
        out_shape=[jax.ShapeDtypeStruct((2 * size, feature), BF16)] * 2,
        in_specs=[anywhere] * 2,
        out_specs=[anywhere] * 2,
        scratch_shapes=[pltpu.SemaphoreType.DMA((3,))],
    )(turned, out_weight)


def copy_of(place_ref, core):
    return (place_ref[0] * 2 + core) * 16 + place_ref[2]


def prepare_kernel(
    mine, place_ref, sequence_ref, length_ref, codes_ref, tokens_ref, states_ref, gain_ref,
    cos_ref, sin_ref,
    normed_ref, picked_ref, rows_ref, qcos_ref, qsin_ref, targets_ref,
):
    span = states_ref.shape[0]
    masks = codes_ref.shape[0]
    gain = gain_ref[...]
    block = 128
    copy = copy_of(place_ref, place_ref[1] if mine else 1 - place_ref[1])
    sequence = sequence_ref[copy]
    length = length_ref[sequence]
    codes_all = codes_ref[...]
    lane = lax.broadcasted_iota(jnp.int32, codes_all.shape, 1)
    codes = jnp.sum(jnp.where(lane == copy, codes_all, 0), axis=1, keepdims=True)
    quotient = jnp.floor(codes.astype(F32) / length.astype(F32)).astype(jnp.int32)
    positions = codes - quotient * length
    positions = jnp.where(positions < 0, positions + length, positions)
    positions = jnp.where(positions >= length, positions - length, positions)
    hit = lax.broadcasted_iota(jnp.int32, (masks, span), 1) == positions
    tokens = tokens_ref[pl.ds(sequence, 1), :]
    targets = jnp.sum(jnp.where(hit, tokens, 0), axis=1, keepdims=True)
    targets_ref[...] = jnp.broadcast_to(targets, targets_ref.shape)
    hot = hit.astype(F32)
    qcos_ref[...] = nn_dot(hot, cos_ref[...], precision=lax.Precision.HIGHEST)
    qsin_ref[...] = nn_dot(hot, sin_ref[...], precision=lax.Precision.HIGHEST)
    hot = hot.astype(BF16)

    def step(i, carry):
        at = pl.multiple_of(i * block, block)
        values = states_ref[pl.ds(at, block), :].astype(F32)
        average = jnp.mean(values, axis=1, keepdims=True)
        centred = values - average
        variance = jnp.mean(centred * centred, axis=1, keepdims=True)
        normed_ref[pl.ds(at, block), :] = (
            centred * lax.rsqrt(variance + epsilon) * gain
        ).astype(BF16)
        return carry

    lax.fori_loop(0, span // block, step, 0)
    rows_ref[...] = nn_dot(hot, states_ref[...])
    picked_ref[...] = nn_dot(hot, normed_ref[...]).astype(BF16)


def keys_kernel(
    place_ref, sequence_ref, length_ref, normed_refs, picked_refs, cos_ref, sin_ref, qcos_refs,
    qsin_refs, block_refs, probs_ref,
):
    size = block_refs[0].shape[0] // 2
    masks = picked_refs[0].shape[0]
    heads = len(block_refs)
    key_weight = jnp.concatenate([r[size:, :] for r in block_refs], axis=0)
    query_weight = jnp.concatenate([r[:size, :] for r in block_refs], axis=0)
    cores = (place_ref[1], 1 - place_ref[1])
    for which in range(2):
        length = length_ref[sequence_ref[copy_of(place_ref, cores[which])]]
        keys = nt_dot(normed_refs[which][...], key_weight)
        queries = nt_dot(picked_refs[which][...], query_weight) * 0.125
        turned_keys, turned_queries = [], []
        for i in range(heads // 2):
            lanes = slice(128 * i, 128 * (i + 1))
            turned_keys.append(rotate(keys[:, lanes], cos_ref[...], sin_ref[...], size // 2))
            turned_queries.append(
                rotate(queries[:, lanes], qcos_refs[which][...], qsin_refs[which][...], size // 2)
            )
        key_rows = jnp.concatenate(turned_keys, axis=1).astype(BF16)
        query_rows = jnp.concatenate(turned_queries, axis=1).astype(BF16)
        spread = jnp.concatenate([query_rows] * heads, axis=0)
        row = lax.broadcasted_iota(jnp.int32, spread.shape, 0) // masks
        lane = lax.broadcasted_iota(jnp.int32, spread.shape, 1) // size
        spread = jnp.where(row == lane, spread, jnp.zeros_like(spread))
        logits = nt_dot(spread, key_rows)
        alive = lax.broadcasted_iota(jnp.int32, logits.shape, 1) < length
        logits = jnp.where(alive, logits, -1e30)
        largest = jnp.max(logits, axis=1, keepdims=True)
        weights = jnp.exp(logits - largest)
        total = jnp.sum(weights, axis=1, keepdims=True)
        probs_ref[which] = (weights * (1.0 / total)).astype(BF16)


def values_kernel(normed_refs, block_refs, values_ref):
    size = block_refs[0].shape[0] // 2
    weight = jnp.concatenate([r[:size, :] for r in block_refs], axis=0)
    for which in range(2):
        values_ref[which] = nt_dot(normed_refs[which][...], weight).astype(BF16)


def mix_kernel(place_ref, probs_refs, values_refs, block_refs, partial_ref):
    right = place_ref[3] == 1
    own_probs, near_probs, far_probs = probs_refs
    size = block_refs[0].shape[0] // 2
    masks = own_probs.shape[1] // 2
    columns = ((0,), (1, 3), (2,))

    def rows_of(core, step, which):
        ref = (own_probs, near_probs, far_probs, near_probs)[step]
        start = masks * (which + (2 if step == 3 else 0))
        return ref[core, start : start + masks, :]

    contexts = []
    for core in range(2):
        parts = []
        for values_ref, group in zip(values_refs, columns):
            stack = []
            for column in group:
                which = column // 2
                for i in range(2):
                    even = rows_of(core, (0, 2)[i], which)
                    odd = rows_of(core, (1, 3)[i], which)
                    if column % 2:
                        even, odd = odd, even
                    stack.append(jnp.where(right, even, odd))
            mixed = nn_dot(jnp.concatenate(stack, axis=0), values_ref[core])
            lane = lax.broadcasted_iota(jnp.int32, (masks, mixed.shape[1]), 1) // size
            context = mixed[:masks, :]
            for head in range(1, len(stack)):
                context = jnp.where(
                    lane == head, mixed[masks * head : masks * (head + 1), :], context
                )
            parts.append(context.astype(BF16))
        contexts.append(jnp.concatenate(parts, axis=1))
    weight = jnp.concatenate([r[size:, :] for r in block_refs], axis=0)
    partial_ref[...] = nn_dot(jnp.concatenate(contexts, axis=0), weight)


def score_kernel(
    place_ref, owner_ref, rows_refs, partial_ref, arrived_ref, targets_refs, gain_ref, bias_ref,
    dense_ref, decoder_ref, placed_ref,
):
    masks = rows_refs[0].shape[0]
    residual = jnp.concatenate(
        [
            rows_refs[0][...] + (partial_ref[:masks, :] + arrived_ref[masks:, :]),
            rows_refs[1][...] + (partial_ref[masks:, :] + arrived_ref[:masks, :]),
        ],
        axis=0,
    )
    targets = jnp.concatenate([r[:, 0:1] for r in targets_refs], axis=0)
    average = jnp.mean(residual, axis=1, keepdims=True)
    centred = residual - average
    variance = jnp.mean(centred * centred, axis=1, keepdims=True)
    normed = (centred * lax.rsqrt(variance + epsilon) * gain_ref[...]).astype(BF16)
    dense = nn_dot(normed, dense_ref[...])
    active = 0.5 * dense * (1.0 + lax.erf(dense * np.float32(0.5**0.5)))
    average = jnp.mean(active, axis=1, keepdims=True)
    centred = active - average
    variance = jnp.mean(centred * centred, axis=1, keepdims=True)
    headed = (centred * lax.rsqrt(variance + epsilon)).astype(BF16)
    logits = nt_dot(headed, decoder_ref[...]) + bias_ref[...]
    largest = jnp.max(logits, axis=1, keepdims=True)
    total = jnp.sum(jnp.exp(logits - largest), axis=1, keepdims=True)
    vocab = lax.broadcasted_iota(jnp.int32, logits.shape, 1)
    chosen = jnp.sum(jnp.where(vocab == targets, logits, 0.0), axis=1, keepdims=True)
    score = chosen - largest - jnp.log(total)
    devices, width = placed_ref.shape
    member = lax.broadcasted_iota(jnp.int32, (devices, masks), 0) % 16
    part = lax.broadcasted_iota(jnp.int32, (devices, masks), 1) // 4
    take = (member == part).astype(F32)
    fits = (
        lax.broadcasted_iota(jnp.int32, (masks, width), 0) % 4
        == lax.broadcasted_iota(jnp.int32, (masks, width), 1) % 4
    )
    layer = lax.broadcasted_iota(jnp.int32, (devices, width), 0) // 16
    slot = lax.broadcasted_iota(jnp.int32, (devices, width), 1) // 4
    wanted = 16 * (2 * layer + place_ref[1]) + slot
    placed = jnp.zeros((devices, width), F32)
    cores = (place_ref[1], 1 - place_ref[1])
    for which in range(2):
        own = jnp.where(fits, score[masks * which : masks * (which + 1), :], 0.0)
        laid = nn_dot(take, own, precision=lax.Precision.HIGHEST)
        placed = jnp.where(wanted == owner_ref[copy_of(place_ref, cores[which])], laid, placed)
    placed_ref[...] = placed


def pull(array, axis, offset):
    size = lax.axis_size(axis)
    return lax.ppermute(array, axis, [((i + offset) % size, i) for i in range(size)])


def swap(array):
    return lax.ppermute(array, "core", [(0, 1), (1, 0)])


def after(array, *others):
    return lax.optimization_barrier((array, *others))[0]


def gather_line(block, axis):
    near, far = [], []
    for core in range(2):
        for y in range(4):
            for x in range(4):
                def device(step):
                    to_y = (y + step) % 4 if axis == "y" else y
                    to_x = (x + step) % 4 if axis == "x" else x
                    return (((x + y) % 2) * 4 + to_y) * 4 + to_x

                source = (core * 4 + y) * 4 + x
                own = (x + y) % 2 == core
                near.append((source, device(-1 if own else 0)))
                far.append((source, device(1 if own else 2)))
    axes = ("core", "y", "x")
    return lax.ppermute(block, axes, near), lax.ppermute(block, axes, far)


def on_device(
    hidden_states,
    ln_attn_gain,
    w_qkv,
    output_weight,
    ln_final_gain,
    dense_weight,
    decoder_weight,
    decoder_bias,
    seq_tokens,
    seq_lengths,
    copy_sequence,
    mask_code,
    copy_owner,
):
    _, span, feature = hidden_states.shape
    size = output_weight.shape[0]
    masks = mask_code.shape[1]
    core = lax.axis_index("core")
    member = lax.axis_index(("y", "x"))
    right = (lax.axis_index("x") + lax.axis_index("y")) % 2 == core
    place = jnp.stack([lax.axis_index("z"), core, member, right.astype(core.dtype)])
    place = place.astype(jnp.int32)
    cos_table, sin_table = (jnp.asarray(t) for t in rotary_tables(span, size))
    shape = jax.ShapeDtypeStruct

    def prepare_call(mine, states):
        def kernel(*refs):
            prepare_kernel(mine, *refs)

        return call(
            kernel,
            [
                shape((span, feature), BF16),
                shape((masks, feature), BF16),
                shape((masks, feature), F32),
                shape((masks, 128), F32),
                shape((masks, 128), F32),
                shape((masks, 128), jnp.int32),
            ],
            3,
            (
                place, copy_sequence, seq_lengths, mask_code.T, seq_tokens, states,
                ln_attn_gain.reshape(1, -1), cos_table, sin_table,
            ),
            flops=4 * masks * span * feature + 10 * span * feature,
        )

    def keys_call(ready, blocks):
        heads = len(blocks)

        def kernel(*refs):
            keys_kernel(
                *refs[:3], refs[3:5], refs[5:7], *refs[7:9], refs[9:11], refs[11:13],
                refs[13 : 13 + heads], refs[13 + heads],
            )

        return call(
            kernel,
            shape((2, heads * masks, span), BF16),
            3,
            (place, copy_sequence, seq_lengths, *(r[0] for r in ready), *(r[1] for r in ready),
             cos_table, sin_table, *(r[3] for r in ready), *(r[4] for r in ready), *blocks),
            flops=4 * span * feature * 256,
            exps=2 * heads * masks * span,
        )

    def values_call(ready, blocks):
        heads = len(blocks)

        def kernel(*refs):
            values_kernel(refs[:2], refs[2 : 2 + heads], refs[2 + heads])

        return call(
            kernel,
            shape((2, span, heads * size), BF16),
            0,
            (*(r[0] for r in ready), *blocks),
            flops=4 * span * feature * 256,
        )

    states = hidden_states[0]
    key_block, value_block = pack(jnp.transpose(w_qkv[:, 0, :]), output_weight[:, 0, :])
    key_low, key_high = gather_line(key_block, "x")
    value_low, value_high = gather_line(value_block, "y")
    states_other = swap(states)
    mine = prepare_call(True, states)
    key_low, key_high = after(key_low, mine[0]), after(key_high, mine[0])
    value_low, value_high = after(value_low, mine[0]), after(value_high, mine[0])
    key_ahead = [pull(key_low, "y", 1)]
    key_behind = [pull(key_high, "y", 3)]
    value_ahead = [pull(value_low, "x", 1)]
    value_behind = [pull(value_high, "x", 3)]
    key_ahead.append(pull(key_high, "y", 1))
    key_behind.insert(0, pull(key_low, "y", 3))
    value_ahead.append(pull(value_high, "x", 1))
    value_behind.insert(0, pull(value_low, "x", 3))
    other = prepare_call(False, states_other)
    ready = (mine, other)
    own_probs = keys_call(ready, (key_low, key_high))
    key_far = (
        pull(after(key_ahead[0], own_probs), "y", 1),
        pull(after(key_behind[1], own_probs), "y", 3),
    )
    value_far = (
        pull(after(value_ahead[0], own_probs), "x", 1),
        pull(after(value_behind[1], own_probs), "x", 3),
    )
    own_values = values_call(ready, (value_low, value_high))
    near_probs = keys_call(ready, (*key_ahead, *key_behind))
    near_values = values_call(ready, (*value_ahead, *value_behind))
    key_far = tuple(after(b, near_probs, near_values) for b in key_far)
    far_probs = keys_call(ready, key_far)
    far_values = values_call(ready, value_far)
    probs = (own_probs, near_probs, far_probs)
    values = (own_values, near_values, far_values)
    value_blocks = (value_low, value_high, *value_ahead, *value_behind, *value_far)

    def mix(*refs):
        mix_kernel(refs[0], refs[1:4], refs[4:7], refs[7:15], refs[15])

    partial = call(
        mix,
        shape((2 * masks, feature), F32),
        1,
        (place, *probs, *values, *value_blocks),
        flops=4 * masks * feature * 8 * size,
    )

    def score(*refs):
        score_kernel(*refs[:2], refs[2:4], *refs[4:6], refs[6:8], *refs[8:])

    placed = call(
        score,
        shape((128, 64), F32),
        2,
        (
            place, copy_owner, mine[2], other[2], partial, swap(partial), mine[5], other[5],
            ln_final_gain.reshape(1, -1), decoder_bias.reshape(1, -1), dense_weight,
            decoder_weight.T,
        ),
        flops=4 * masks * feature * feature,
    )
    arrived = lax.all_to_all(placed, ("z", "y", "x"), 0, 0, tiled=True)
    return jnp.sum(arrived, axis=0).reshape(16, 4)


def solution(mesh):
    fine = Mesh(mesh.devices.reshape(8, 2, 4, 4), ("z", "core", "y", "x"))
    dp, mp = ("z", "core"), ("y", "x")
    placed = (
        P(("z", "core", "y", "x"), None, None),
        P(),
        P(None, mp, None),
        P(None, mp, None),
        P(),
        P(),
        P(),
        P(),
        P(),
        P(),
        P(),
        P(),
        P(),
    )
    return jax.shard_map(
        on_device, mesh=fine, in_specs=placed, out_specs=P(dp, mp), check_vma=False
    )
```

time: 111 us -> 113 us (1.018)
  Pallas kernels: 24.2 us -> 44.2 us
  starting transfers between devices: 34.4 us -> 22.7 us
  other arithmetic: 4.9 us -> 0.23 us
  local copies, waits for them, and re-layouts: 5.12 us -> 7.87 us
  blocking collectives: 26.2 us -> 24 us
    pallas_call x0 -> x1, Pallas kernels: none -> 21 us  [pack(): pl.pallas_call(pack_kernel, out_shape=[jax.ShapeDtypeStruct((2 * size, fe...]
    ppermute x2, starting transfers between devices: 14.7 us -> 6 us  [swap(): return lax.ppermute(array, 'core', [(0, 1), (1, 0)])]
    unnamed x40 -> x28, local copies, waits for them, and re-layouts: 1.56 us -> 6.42 us
    select_n x4 -> x0, other arithmetic: 3 us -> none  [gather_line(): return (jnp.where(right, block, behind), jnp.where(right, across, ahead))]
    slice x2 -> x0, local copies, waits for them, and re-layouts: 2.81 us -> none  [the longest x1 1.88 us: on_device(): key_block = turned[:2 * size]]
    ppermute x6 -> x4, waiting for transfers between devices: 2.68 us -> 0.01 us  [gather_line(): return (lax.ppermute(block, axes, near), lax.ppermute(block, axes, far))]
    ppermute x6 -> x4, starting transfers between devices: 7.21 us -> 4.99 us  [gather_line(): return (lax.ppermute(block, axes, near), lax.ppermute(block, axes, far))]
    all_to_all x1, blocking collectives: 26.2 us -> 24 us  [on_device(): arrived = lax.all_to_all(placed, ('z', 'y', 'x'), 0, 0, tiled=True)]
  transfers between devices with their start and end apart: 20 -> 18, of which waited for: 5 -> 4; matrix products, arithmetic and copies ran while one was open for 5% -> 1% of each run, Pallas kernels for 17% -> 35%
where the time goes in v3:
time: 113 us
  Pallas kernels  44.2 us (39%)
  blocking collectives  24 us (21%)
  starting transfers between devices  22.7 us (20%)
  waiting for transfers between devices  13.9 us (12%)
  local copies, waits for them, and re-layouts  7.87 us (7%)
    all_to_all x1, blocking collectives, on_device(): arrived = lax.all_to_all(placed, ('z', 'y', 'x'), 0, 0, tiled=True)  24 us
    pallas_call x10, Pallas kernels, call(): pl.pallas_call(kernel, out_shape=outs, in_specs=specs, out_specs=jax.tree...  23.2 us
    pallas_call x1, Pallas kernels, pack(): pl.pallas_call(pack_kernel, out_shape=[jax.ShapeDtypeStruct((2 * size, fe...  21 us
    ppermute x12, waiting for transfers between devices, pull(): lax.ppermute(array, axis, [((i + offset) % size, i) for i in range(size)])  12.2 us
    ppermute x12, starting transfers between devices, pull(): lax.ppermute(array, axis, [((i + offset) % size, i) for i in range(size)])  11.7 us
    unnamed x28, local copies, waits for them, and re-layouts  6.42 us
    ppermute x2, starting transfers between devices, swap(): return lax.ppermute(array, 'core', [(0, 1), (1, 0)])  6 us
    ppermute x4, starting transfers between devices, gather_line(): return (lax.ppermute(block, axes, near), lax.ppermute(block, axes, far))  4.99 us
  transfers between devices with their start and end apart: 18, of which 4 were waited for; matrix products, arithmetic and copies ran while one was open for 1% of the time, Pallas kernels for 35%

profile of v3, /device:TPU:1, one launch (start us, length us, event | category | flops | bytes accessed | tf_op | source)
XLA Modules:
  0.0 113.1 jit_solution(4774099455720247567)
XLA Ops:
  0.0 3.2 %collective-permute-start = (bf16[640,1280]{1,0:T(8,128)(2,1)}, bf16[640,1280]{1,0:T(8,128)(2,1)S(1)}, u32[]{:S(2)}, u32[]{:S(2)}) collective-permute-start(bf16[640,1280]{1,0:T(8,128)(2,1)} %bitcast.15), channel_id=1, source_target_pairs={{0,16},{16,0},{1,17},{17,1},{2,18},{18,2},{3,19},{19,3},{4,20},{20... | collective-permute-start | bytes 4915208 | tf_op jit(solution)/shard_map/ppermute | solution.py:269
  3.2 21.0 %shard_map.147 = (bf16[128,1280]{1,0:T(8,128)(2,1)}, bf16[128,1280]{1,0:T(8,128)(2,1)}) custom-call(bf16[192,1280]{1,0:T(8,128)(2,1)} %bitcast.22, bf16[64,1280]{1,0:T(8,128)(2,1)} %bitcast.23), custom_call_target="tpu_custom_call" | custom-call | tf_op jit(solution)/shard_map/pallas_call | solution.py:76
  24.2 0.1 collective-permute-start.1
  24.3 1.4 %collective-permute-start.2 = (bf16[128,1280]{1,0:T(8,128)(2,1)}, bf16[128,1280]{1,0:T(8,128)(2,1)S(1)}, u32[]{:S(2)}, u32[]{:S(2)}) collective-permute-start(bf16[128,1280]{1,0:T(8,128)(2,1)} %get-tuple-element.39), channel_id=1, source_target_pairs={{0,1},{1,19},{2,3},{3,17},{4,22},{5,6},{6,20},{7,4},{8,9},{9,27},{... | collective-permute-start | bytes 983048 | tf_op jit(solution)/shard_map/ppermute | solution.py:291
  25.7 0.0 collective-permute-start.8
  25.8 3.5 %collective-permute-start.10 = (bf16[128,1280]{1,0:T(8,128)(2,1)}, bf16[128,1280]{1,0:T(8,128)(2,1)S(1)}, u32[]{:S(2)}, u32[]{:S(2)}) collective-permute-start(bf16[128,1280]{1,0:T(8,128)(2,1)} %get-tuple-element.43), channel_id=1, source_target_pairs={{0,4},{1,25},{2,6},{3,27},{4,28},{5,9},{6,30},{7,11},{8,12},{9,17}... | collective-permute-start | bytes 983048 | tf_op jit(solution)/shard_map/ppermute | solution.py:291
  29.2 0.7 reshape.15.refs_6_
  29.9 0.1 pad_add_fusion.refs_0_
  30.0 1.0 copy-done
  31.0 1.0 copy-done.2
  32.0 1.4 %copy-done.5 = bf16[1,640,1280]{2,1,0:T(8,128)(2,1)S(1)} copy-done((bf16[1,640,1280]{2,1,0:T(8,128)(2,1)S(1)}, bf16[1,640,1280]{2,1,0:T(8,128)(2,1)}, u32[]{:S(2)}) %copy-start.5) | copy-done | bytes 1638424
  33.4 0.8 copy-done.6
  34.2 0.8 copy-done.7
  35.1 0.7 copy-done.9
  35.7 0.7 copy-done.10
  36.4 3.3 %shard_map.145 = (bf16[640,1280]{1,0:T(8,128)(2,1)S(1)}, bf16[64,1280]{1,0:T(8,128)(2,1)S(1)}, f32[64,1280]{1,0:T(8,128)S(1)}, f32[64,128]{1,0:T(8,128)S(1)}, f3...) custom-call(s32[4]{0:T(128)S(1)} %pad_add_fusion.refs_0_, s32[256]{0:T(256)S(1)} %copy-done.9, s32[24]{0:T(128)S(1)} %copy-done.10, ...), custom_call_target="tpu_custom_call" | custom-call | flops 217907200 | bytes 4655216 | tf_op jit(solution)/shard_map/pallas_call | solution.py:50
  39.7 0.0 copy-start.3
  39.7 0.0 collective-permute-done.1.refs_13_
  39.7 0.1 collective-permute-start.3
  39.8 0.0 collective-permute-done.2.refs_14_
  39.8 2.9 %collective-permute-start.4 = (bf16[128,1280]{1,0:T(8,128)(2,1)S(1)}, bf16[128,1280]{1,0:T(8,128)(2,1)S(1)}, u32[]{:S(2)}, u32[]{:S(2)}) collective-permute-start(bf16[128,1280]{1,0:T(8,128)(2,1)S(1)} %collective-permute-done.2.refs_14_), channel_id=1, source_target_pairs={{4,0},{8,4},{12,8},{0,12},{5,1},{9,5},{13,9},{1,13},{6,2},{10,6},{... | collective-permute-start | bytes 983048 | tf_op jit(solution)/shard_map/ppermute | solution.py:265
  42.7 0.0 collective-permute-done.8.refs_2_.refs_7_
  42.7 0.0 collective-permute-start.6
  42.7 0.0 collective-permute-done.10.refs_3_.refs_8_
  42.7 1.9 %collective-permute-start.9 = (bf16[128,1280]{1,0:T(8,128)(2,1)S(1)}, bf16[128,1280]{1,0:T(8,128)(2,1)S(1)}, u32[]{:S(2)}, u32[]{:S(2)}) collective-permute-start(bf16[128,1280]{1,0:T(8,128)(2,1)S(1)} %collective-permute-done.8.refs_2_.refs_7_), channel_id=1, source_target_pairs={{1,0},{2,1},{3,2},{0,3},{5,4},{6,5},{7,6},{4,7},{9,8},{10,9},{11,1... | collective-permute-start | bytes 983048 | tf_op jit(solution)/shard_map/ppermute | solution.py:265
  44.6 4.7 %collective-permute-done.3.refs_13_ = bf16[128,1280]{1,0:T(8,128)(2,1)S(1)} collective-permute-done((bf16[128,1280]{1,0:T(8,128)(2,1)S(1)}, bf16[128,1280]{1,0:T(8,128)(2,1)S(1)}, u32[]{:S(2)}, u32[]{:S(2)}) %collective-permute-start.3) | collective-permute-done | bytes 327712 | tf_op jit(solution)/shard_map/ppermute | solution.py:265
  49.3 0.0 collective-permute-start.13
  49.3 7.0 %collective-permute-done.4.refs_14_ = bf16[128,1280]{1,0:T(8,128)(2,1)S(1)} collective-permute-done((bf16[128,1280]{1,0:T(8,128)(2,1)S(1)}, bf16[128,1280]{1,0:T(8,128)(2,1)S(1)}, u32[]{:S(2)}, u32[]{:S(2)}) %collective-permute-start.4) | collective-permute-done | bytes 327712 | tf_op jit(solution)/shard_map/ppermute | solution.py:265
  56.3 0.7 collective-permute-start.5
  57.1 0.0 collective-permute-done.refs_5_
  57.1 0.7 collective-permute-start.11
  57.8 3.3 %shard_map.146 = (bf16[640,1280]{1,0:T(8,128)(2,1)S(1)}, bf16[64,1280]{1,0:T(8,128)(2,1)S(1)}, f32[64,1280]{1,0:T(8,128)S(1)}, f32[64,128]{1,0:T(8,128)S(1)}, f3...) custom-call(s32[4]{0:T(128)S(1)} %pad_add_fusion.refs_0_, s32[256]{0:T(256)S(1)} %copy-done.9, s32[24]{0:T(128)S(1)} %copy-done.10, ...), custom_call_target="tpu_custom_call" | custom-call | flops 217907200 | bytes 4655216 | tf_op jit(solution)/shard_map/pallas_call | solution.py:50
  61.1 0.0 collective-permute-done.6.refs_16_
  61.1 0.9 collective-permute-start.12
  61.9 3.1 %shard_map.148.refs_1_ = bf16[2,128,640]{2,1,0:T(8,128)(2,1)S(1)} custom-call(s32[4]{0:T(128)S(1)} %pad_add_fusion.refs_0_, s32[256]{0:T(256)S(1)} %copy-done.9, s32[24]{0:T(128)S(1)} %copy-done.10, bf16[640,1280]{1,0:T(8,128)(2,1)S(1)} %get-tuple-element.31.refs_3_.refs_0_, bf16[640,1280]{1,0:T(8,128)(2,1)S(1)} %get-tuple-element.32.refs_4_.refs_1_, ...), custom_call_target="tpu_custom_call" | custom-call | flops 838860800 | bytes 5375088 | tf_op jit(solution)/shard_map/pallas_call | solution.py:50
  65.0 0.0 collective-permute-done.9.refs_2_.refs_9_
  65.0 2.0 %collective-permute-start.7 = (bf16[128,1280]{1,0:T(8,128)(2,1)S(1)}, bf16[128,1280]{1,0:T(8,128)(2,1)S(1)}, u32[]{:S(2)}, u32[]{:S(2)}) collective-permute-start(bf16[128,1280]{1,0:T(8,128)(2,1)S(1)} %collective-permute-done.3.refs_13_), channel_id=1, source_target_pairs={{4,0},{8,4},{12,8},{0,12},{5,1},{9,5},{13,9},{1,13},{6,2},{10,6},{... | collective-permute-start | bytes 983048 | tf_op jit(solution)/shard_map/ppermute | solution.py:265
  67.0 0.0 collective-permute-done.13.refs_5_.refs_12_
  67.0 0.0 collective-permute-start.14
  67.0 0.0 collective-permute-done.5.refs_15_
  67.0 2.5 %collective-permute-start.15 = (bf16[128,1280]{1,0:T(8,128)(2,1)S(1)}, bf16[128,1280]{1,0:T(8,128)(2,1)S(1)}, u32[]{:S(2)}, u32[]{:S(2)}) collective-permute-start(bf16[128,1280]{1,0:T(8,128)(2,1)S(1)} %collective-permute-done.9.refs_2_.refs_9_), channel_id=1, source_target_pairs={{1,0},{2,1},{3,2},{0,3},{5,4},{6,5},{7,6},{4,7},{9,8},{10,9},{11,1... | collective-permute-start | bytes 983048 | tf_op jit(solution)/shard_map/ppermute | solution.py:265
  69.6 0.0 collective-permute-start.16
  69.6 1.0 shard_map.152.refs_4_
  70.6 3.6 %shard_map.149.refs_2_ = bf16[2,256,640]{2,1,0:T(8,128)(2,1)S(1)} custom-call(s32[4]{0:T(128)S(1)} %pad_add_fusion.refs_0_, s32[256]{0:T(256)S(1)} %copy-done.9, s32[24]{0:T(128)S(1)} %copy-done.10, bf16[640,1280]{1,0:T(8,128)(2,1)S(1)} %get-tuple-element.31.refs_3_.refs_0_, bf16[640,1280]{1,0:T(8,128)(2,1)S(1)} %get-tuple-element.32.refs_4_.refs_1_, ...), custom_call_target="tpu_custom_call" | custom-call | flops 838860800 | bytes 6358128 | tf_op jit(solution)/shard_map/pallas_call | solution.py:50
  74.2 0.0 collective-permute-done.12.refs_4_.refs_11_
  74.2 1.0 shard_map.150.refs_5_
  75.2 0.0 collective-permute-done.7.refs_13_
  75.2 0.5 collective-permute-done.14.refs_14_
  75.7 3.1 %shard_map.151.refs_3_ = bf16[2,128,640]{2,1,0:T(8,128)(2,1)S(1)} custom-call(s32[4]{0:T(128)S(1)} %pad_add_fusion.refs_0_, s32[256]{0:T(256)S(1)} %copy-done.9, s32[24]{0:T(128)S(1)} %copy-done.10, bf16[640,1280]{1,0:T(8,128)(2,1)S(1)} %get-tuple-element.31.refs_3_.refs_0_, bf16[640,1280]{1,0:T(8,128)(2,1)S(1)} %get-tuple-element.32.refs_4_.refs_1_, ...), custom_call_target="tpu_custom_call" | custom-call | flops 838860800 | bytes 5375088 | tf_op jit(solution)/shard_map/pallas_call | solution.py:50
  78.8 0.0 collective-permute-done.15.refs_2_.refs_13_
  78.8 1.0 shard_map.153.refs_6_
  79.8 0.0 copy-start.13
  79.8 0.0 copy-start.4
  79.8 0.0 copy-start.8
  79.9 0.0 copy-start.11
  79.9 0.0 copy-start.12
  79.9 1.4 %shard_map.154.refs_4_ = f32[128,1280]{1,0:T(8,128)S(1)} custom-call(s32[4]{0:T(128)S(1)} %pad_add_fusion.refs_0_, bf16[2,128,640]{2,1,0:T(8,128)(2,1)S(1)} %shard_map.148.refs_1_, bf16[2,256,640]{2,1,0:T(8,128)(2,1)S(1)} %shard_map.149.refs_2_, bf16[2,128,640]{2,1,0:T(8,128)(2,1)S(1)} %shard_map.151.refs_3_, bf16[2,640,128]{2,1,0:T(8,128)(2,1)S(1)} %shard_map.152.refs_4_, ...), custom_call_target="tpu_custom_call" | custom-call | flops 167772160 | bytes 5898256 | tf_op jit(solution)/shard_map/pallas_call | solution.py:50
  81.3 2.8 %collective-permute-start.17 = (f32[128,1280]{1,0:T(8,128)S(1)}, f32[128,1280]{1,0:T(8,128)S(1)}, u32[]{:S(2)}, u32[]{:S(2)}) collective-permute-start(f32[128,1280]{1,0:T(8,128)S(1)} %shard_map.154.refs_4_), channel_id=1, source_target_pairs={{0,16},{16,0},{1,17},{17,1},{2,18},{18,2},{3,19},{19,3},{4,20},{20... | collective-permute-start | bytes 1966088 | tf_op jit(solution)/shard_map/ppermute | solution.py:269
  84.1 1.7 %collective-permute-done.17.refs_5_ = f32[128,1280]{1,0:T(8,128)S(1)} collective-permute-done((f32[128,1280]{1,0:T(8,128)S(1)}, f32[128,1280]{1,0:T(8,128)S(1)}, u32[]{:S(2)}, u32[]{:S(2)}) %collective-permute-start.17) | collective-permute-done | bytes 655392 | tf_op jit(solution)/shard_map/ppermute | solution.py:269
  85.8 2.4 %shard_map.155 = f32[128,64]{1,0:T(8,128)S(1)} custom-call(s32[4]{0:T(128)S(1)} %pad_add_fusion.refs_0_, s32[256]{0:T(256)S(1)} %copy-done.11, f32[64,1280]{1,0:T(8,128)S(1)} %get-tuple-element.29.refs_2_, f32[64,1280]{1,0:T(8,128)S(1)} %get-tuple-element.30.refs_3_, f32[128,1280]{1,0:T(8,128)S(1)} %shard_map.154.refs_4_, ...), custom_call_target="tpu_custom_call" | custom-call | flops 419430400 | bytes 5431956 | tf_op jit(solution)/shard_map/pallas_call | solution.py:50
  88.2 24.0 %all_to_all.9 = f32[128,1,64]{2,1,0:T(1,128)S(1)} all-to-all(f32[128,1,64]{2,1,0:T(1,128)S(1)} %bitcast.17), channel_id=1, replica_groups=mesh['z'=8,'core'=2,'y'=4,'x'=4] {'z','y','x'}, dimensions={0} | all-to-all | bytes 65536 | tf_op jit(solution)/shard_map/all_to_all | solution.py:437
  112.2 0.2 reduce_sum.9
  112.4 0.1 reshape.18
  112.4 0.7 copy.19
  (18 shorter events, 0.0 us)
Async XLA Ops:
  0.0 57.8 %copy-start.1 = (f32[640,128]{1,0:T(8,128)S(1)}, f32[640,128]{1,0:T(8,128)}, u32[]{:S(2)}) copy-start(f32[640,128]{1,0:T(8,128)} %constant.40.clone.refs_7_) | copy-start | bytes 983044
  0.0 57.1 %collective-permute-start = (bf16[640,1280]{1,0:T(8,128)(2,1)}, bf16[640,1280]{1,0:T(8,128)(2,1)S(1)}, u32[]{:S(2)}, u32[]{:S(2)}) collective-permute-start(bf16[640,1280]{1,0:T(8,128)(2,1)} %bitcast.15), channel_id=1, source_target_pairs={{0,16},{16,0},{1,17},{17,1},{2,18},{18,2},{3,19},{19,3},{4,20},{20... | collective-permute-start | bytes 4915208 | tf_op jit(solution)/shard_map/ppermute | solution.py:269
  24.2 15.5 %collective-permute-start.1 = (bf16[128,1280]{1,0:T(8,128)(2,1)}, bf16[128,1280]{1,0:T(8,128)(2,1)S(1)}, u32[]{:S(2)}, u32[]{:S(2)}) collective-permute-start(bf16[128,1280]{1,0:T(8,128)(2,1)} %get-tuple-element.39), channel_id=1, source_target_pairs={{0,3},{1,17},{2,1},{3,19},{4,20},{5,4},{6,22},{7,6},{8,11},{9,25},... | collective-permute-start | bytes 983048 | tf_op jit(solution)/shard_map/ppermute | solution.py:291
  24.3 15.5 %collective-permute-start.2 = (bf16[128,1280]{1,0:T(8,128)(2,1)}, bf16[128,1280]{1,0:T(8,128)(2,1)S(1)}, u32[]{:S(2)}, u32[]{:S(2)}) collective-permute-start(bf16[128,1280]{1,0:T(8,128)(2,1)} %get-tuple-element.39), channel_id=1, source_target_pairs={{0,1},{1,19},{2,3},{3,17},{4,22},{5,6},{6,20},{7,4},{8,9},{9,27},{... | collective-permute-start | bytes 983048 | tf_op jit(solution)/shard_map/ppermute | solution.py:291
  25.7 17.0 %collective-permute-start.8 = (bf16[128,1280]{1,0:T(8,128)(2,1)}, bf16[128,1280]{1,0:T(8,128)(2,1)S(1)}, u32[]{:S(2)}, u32[]{:S(2)}) collective-permute-start(bf16[128,1280]{1,0:T(8,128)(2,1)} %get-tuple-element.43), channel_id=1, source_target_pairs={{0,12},{1,17},{2,14},{3,19},{4,20},{5,1},{6,22},{7,3},{8,4},{9,25}... | collective-permute-start | bytes 983048 | tf_op jit(solution)/shard_map/ppermute | solution.py:291
  25.8 17.0 %collective-permute-start.10 = (bf16[128,1280]{1,0:T(8,128)(2,1)}, bf16[128,1280]{1,0:T(8,128)(2,1)S(1)}, u32[]{:S(2)}, u32[]{:S(2)}) collective-permute-start(bf16[128,1280]{1,0:T(8,128)(2,1)} %get-tuple-element.43), channel_id=1, source_target_pairs={{0,4},{1,25},{2,6},{3,27},{4,28},{5,9},{6,30},{7,11},{8,12},{9,17}... | collective-permute-start | bytes 983048 | tf_op jit(solution)/shard_map/ppermute | solution.py:291
  30.0 1.0 copy-start
  31.0 1.0 copy-start.2
  32.0 1.4 %copy-start.5 = (bf16[1,640,1280]{2,1,0:T(8,128)(2,1)S(1)}, bf16[1,640,1280]{2,1,0:T(8,128)(2,1)}, u32[]{:S(2)}) copy-start(bf16[1,640,1280]{2,1,0:T(8,128)(2,1)} %param.15) | copy-start | bytes 4915204
  33.4 0.8 copy-start.6
  34.2 0.8 copy-start.7
  35.1 0.7 copy-start.9
  35.7 0.7 copy-start.10
  39.7 22.2 %copy-start.3 = (f32[640,128]{1,0:T(8,128)S(1)}, f32[640,128]{1,0:T(8,128)}, u32[]{:S(2)}) copy-start(f32[640,128]{1,0:T(8,128)} %constant.41.clone.refs_8_) | copy-start | bytes 983044
  39.7 9.6 %collective-permute-start.3 = (bf16[128,1280]{1,0:T(8,128)(2,1)S(1)}, bf16[128,1280]{1,0:T(8,128)(2,1)S(1)}, u32[]{:S(2)}, u32[]{:S(2)}) collective-permute-start(bf16[128,1280]{1,0:T(8,128)(2,1)S(1)} %collective-permute-done.1.refs_13_), channel_id=1, source_target_pairs={{4,0},{8,4},{12,8},{0,12},{5,1},{9,5},{13,9},{1,13},{6,2},{10,6},{... | collective-permute-start | bytes 983048 | tf_op jit(solution)/shard_map/ppermute | solution.py:265
  39.8 16.5 %collective-permute-start.4 = (bf16[128,1280]{1,0:T(8,128)(2,1)S(1)}, bf16[128,1280]{1,0:T(8,128)(2,1)S(1)}, u32[]{:S(2)}, u32[]{:S(2)}) collective-permute-start(bf16[128,1280]{1,0:T(8,128)(2,1)S(1)} %collective-permute-done.2.refs_14_), channel_id=1, source_target_pairs={{4,0},{8,4},{12,8},{0,12},{5,1},{9,5},{13,9},{1,13},{6,2},{10,6},{... | collective-permute-start | bytes 983048 | tf_op jit(solution)/shard_map/ppermute | solution.py:265
  42.7 18.4 %collective-permute-start.6 = (bf16[128,1280]{1,0:T(8,128)(2,1)S(1)}, bf16[128,1280]{1,0:T(8,128)(2,1)S(1)}, u32[]{:S(2)}, u32[]{:S(2)}) collective-permute-start(bf16[128,1280]{1,0:T(8,128)(2,1)S(1)} %collective-permute-done.2.refs_14_), channel_id=1, source_target_pairs={{12,0},{0,4},{4,8},{8,12},{13,1},{1,5},{5,9},{9,13},{14,2},{2,6},{... | collective-permute-start | bytes 983048 | tf_op jit(solution)/shard_map/ppermute | solution.py:265
  42.7 22.3 %collective-permute-start.9 = (bf16[128,1280]{1,0:T(8,128)(2,1)S(1)}, bf16[128,1280]{1,0:T(8,128)(2,1)S(1)}, u32[]{:S(2)}, u32[]{:S(2)}) collective-permute-start(bf16[128,1280]{1,0:T(8,128)(2,1)S(1)} %collective-permute-done.8.refs_2_.refs_7_), channel_id=1, source_target_pairs={{1,0},{2,1},{3,2},{0,3},{5,4},{6,5},{7,6},{4,7},{9,8},{10,9},{11,1... | collective-permute-start | bytes 983048 | tf_op jit(solution)/shard_map/ppermute | solution.py:265
  49.3 17.7 %collective-permute-start.13 = (bf16[128,1280]{1,0:T(8,128)(2,1)S(1)}, bf16[128,1280]{1,0:T(8,128)(2,1)S(1)}, u32[]{:S(2)}, u32[]{:S(2)}) collective-permute-start(bf16[128,1280]{1,0:T(8,128)(2,1)S(1)} %collective-permute-done.10.refs_3_.refs_8_), channel_id=1, source_target_pairs={{3,0},{0,1},{1,2},{2,3},{7,4},{4,5},{5,6},{6,7},{11,8},{8,9},{9,10... | collective-permute-start | bytes 983048 | tf_op jit(solution)/shard_map/ppermute | solution.py:265
  56.3 10.7 %collective-permute-start.5 = (bf16[128,1280]{1,0:T(8,128)(2,1)S(1)}, bf16[128,1280]{1,0:T(8,128)(2,1)S(1)}, u32[]{:S(2)}, u32[]{:S(2)}) collective-permute-start(bf16[128,1280]{1,0:T(8,128)(2,1)S(1)} %collective-permute-done.1.refs_13_), channel_id=1, source_target_pairs={{12,0},{0,4},{4,8},{8,12},{13,1},{1,5},{5,9},{9,13},{14,2},{2,6},{... | collective-permute-start | bytes 983048 | tf_op jit(solution)/shard_map/ppermute | solution.py:265
  57.1 12.5 %collective-permute-start.11 = (bf16[128,1280]{1,0:T(8,128)(2,1)S(1)}, bf16[128,1280]{1,0:T(8,128)(2,1)S(1)}, u32[]{:S(2)}, u32[]{:S(2)}) collective-permute-start(bf16[128,1280]{1,0:T(8,128)(2,1)S(1)} %collective-permute-done.10.refs_3_.refs_8_), channel_id=1, source_target_pairs={{1,0},{2,1},{3,2},{0,3},{5,4},{6,5},{7,6},{4,7},{9,8},{10,9},{11,1... | collective-permute-start | bytes 983048 | tf_op jit(solution)/shard_map/ppermute | solution.py:265
  61.1 13.1 %collective-permute-start.12 = (bf16[128,1280]{1,0:T(8,128)(2,1)S(1)}, bf16[128,1280]{1,0:T(8,128)(2,1)S(1)}, u32[]{:S(2)}, u32[]{:S(2)}) collective-permute-start(bf16[128,1280]{1,0:T(8,128)(2,1)S(1)} %collective-permute-done.8.refs_2_.refs_7_), channel_id=1, source_target_pairs={{3,0},{0,1},{1,2},{2,3},{7,4},{4,5},{5,6},{6,7},{11,8},{8,9},{9,10... | collective-permute-start | bytes 983048 | tf_op jit(solution)/shard_map/ppermute | solution.py:265
  65.0 10.2 %collective-permute-start.7 = (bf16[128,1280]{1,0:T(8,128)(2,1)S(1)}, bf16[128,1280]{1,0:T(8,128)(2,1)S(1)}, u32[]{:S(2)}, u32[]{:S(2)}) collective-permute-start(bf16[128,1280]{1,0:T(8,128)(2,1)S(1)} %collective-permute-done.3.refs_13_), channel_id=1, source_target_pairs={{4,0},{8,4},{12,8},{0,12},{5,1},{9,5},{13,9},{1,13},{6,2},{10,6},{... | collective-permute-start | bytes 983048 | tf_op jit(solution)/shard_map/ppermute | solution.py:265
  67.0 8.7 %collective-permute-start.14 = (bf16[128,1280]{1,0:T(8,128)(2,1)S(1)}, bf16[128,1280]{1,0:T(8,128)(2,1)S(1)}, u32[]{:S(2)}, u32[]{:S(2)}) collective-permute-start(bf16[128,1280]{1,0:T(8,128)(2,1)S(1)} %collective-permute-done.6.refs_16_), channel_id=1, source_target_pairs={{12,0},{0,4},{4,8},{8,12},{13,1},{1,5},{5,9},{9,13},{14,2},{2,6},{... | collective-permute-start | bytes 983048 | tf_op jit(solution)/shard_map/ppermute | solution.py:265
  67.0 11.7 %collective-permute-start.15 = (bf16[128,1280]{1,0:T(8,128)(2,1)S(1)}, bf16[128,1280]{1,0:T(8,128)(2,1)S(1)}, u32[]{:S(2)}, u32[]{:S(2)}) collective-permute-start(bf16[128,1280]{1,0:T(8,128)(2,1)S(1)} %collective-permute-done.9.refs_2_.refs_9_), channel_id=1, source_target_pairs={{1,0},{2,1},{3,2},{0,3},{5,4},{6,5},{7,6},{4,7},{9,8},{10,9},{11,1... | collective-permute-start | bytes 983048 | tf_op jit(solution)/shard_map/ppermute | solution.py:265
  69.6 9.2 %collective-permute-start.16 = (bf16[128,1280]{1,0:T(8,128)(2,1)S(1)}, bf16[128,1280]{1,0:T(8,128)(2,1)S(1)}, u32[]{:S(2)}, u32[]{:S(2)}) collective-permute-start(bf16[128,1280]{1,0:T(8,128)(2,1)S(1)} %collective-permute-done.13.refs_5_.refs_12_), channel_id=1, source_target_pairs={{3,0},{0,1},{1,2},{2,3},{7,4},{4,5},{5,6},{6,7},{11,8},{8,9},{9,10... | collective-permute-start | bytes 983048 | tf_op jit(solution)/shard_map/ppermute | solution.py:265
  79.8 4.3 %copy-start.13 = (f32[1280]{0:T(1024)S(1)}, f32[1280]{0:T(1024)}, u32[]{:S(2)}) copy-start(f32[1280]{0:T(1024)} %param.19) | copy-start | bytes 15364
  79.8 6.0 %copy-start.4 = (bf16[1280,1280]{1,0:T(8,128)(2,1)S(1)}, bf16[1280,1280]{1,0:T(8,128)(2,1)}, u32[]{:S(2)}) copy-start(bf16[1280,1280]{1,0:T(8,128)(2,1)} %refs_10_.1) | copy-start | bytes 9830404
  79.8 6.0 %copy-start.8 = (bf16[1280,33]{0,1:T(8,128)(2,1)S(1)}, bf16[1280,33]{0,1:T(8,128)(2,1)}, u32[]{:S(2)}) copy-start(bf16[1280,33]{0,1:T(8,128)(2,1)} %param.21) | copy-start | bytes 253444
  79.9 6.0 %copy-start.11 = (s32[256]{0:T(256)S(1)}, s32[256]{0:T(256)}, u32[]{:S(2)}) copy-start(s32[256]{0:T(256)} %refs_1_.11) | copy-start | bytes 3076
  79.9 6.0 %copy-start.12 = (f32[33]{0:T(128)S(1)}, f32[33]{0:T(128)}, u32[]{:S(2)}) copy-start(f32[33]{0:T(128)} %param.22) | copy-start | bytes 400
  81.3 4.5 %collective-permute-start.17 = (f32[128,1280]{1,0:T(8,128)S(1)}, f32[128,1280]{1,0:T(8,128)S(1)}, u32[]{:S(2)}, u32[]{:S(2)}) collective-permute-start(f32[128,1280]{1,0:T(8,128)S(1)} %shard_map.154.refs_4_), channel_id=1, source_target_pairs={{0,16},{16,0},{1,17},{17,1},{2,18},{18,2},{3,19},{19,3},{4,20},{20... | collective-permute-start | bytes 1966088 | tf_op jit(solution)/shard_map/ppermute | solution.py:269

commit v4 on v3

--- a/solution.py
+++ b/solution.py
@@ -20,7 +20,7 @@
     sine = np.sin(angles.astype(np.float64)).astype(np.float32)
     cos_table = np.concatenate([cosine] * 4, axis=1)
     sin_table = np.concatenate([-sine, sine] * 2, axis=1)
-    return cos_table, sin_table
+    return np.concatenate([cos_table, sin_table], axis=1)
 
 
 def nt_dot(a, b):
@@ -31,7 +31,8 @@
     return lax.dot_general(a, b, (((1,), (0,)), ((), ())), preferred_element_type=F32, **options)
 
 
-def rotate(part, cos_table, sin_table, half):
+def rotate(part, table, half):
+    cos_table, sin_table = table[:, :128], table[:, 128:]
     width = part.shape[1]
     lane = lax.broadcasted_iota(jnp.int32, part.shape, 1) % (2 * half)
     turned = jnp.where(
@@ -42,16 +43,20 @@
     return part * cos_table + turned * sin_table
 
 
-def call(kernel, outs, n_smem, args, flops=0, exps=0, vmem=24 * 1024 * 1024):
-    space = pltpu.MemorySpace
-    specs = [pl.BlockSpec(memory_space=space.SMEM)] * n_smem
-    specs += [pl.BlockSpec(memory_space=space.VMEM)] * (len(args) - n_smem)
+IN_PLACE = pl.BlockSpec(memory_space=pltpu.MemorySpace.HBM)
+ON_CHIP = pl.BlockSpec(memory_space=pltpu.MemorySpace.VMEM)
+
+
+def call(kernel, outs, args, n_any=0, scratch=(), flops=0, exps=0, vmem=24 * 1024 * 1024):
     moved = sum(a.size * a.dtype.itemsize for a in list(args) + jax.tree.leaves(outs))
+    place = pltpu.with_memory_space_constraint
+    args = [place(a, pltpu.HBM) if i < n_any else a for i, a in enumerate(args)]
     return pl.pallas_call(
         kernel,
         out_shape=outs,
-        in_specs=specs,
-        out_specs=jax.tree.map(lambda _: pl.BlockSpec(memory_space=space.VMEM), outs),
+        in_specs=[IN_PLACE] * n_any + [ON_CHIP] * (len(args) - n_any),
+        out_specs=jax.tree.map(lambda _: ON_CHIP, outs),
+        scratch_shapes=list(scratch),
         cost_estimate=pl.CostEstimate(flops=flops, transcendentals=exps, bytes_accessed=moved),
         compiler_params=pltpu.CompilerParams(vmem_limit_bytes=vmem),
     )(*args)
@@ -72,47 +77,74 @@
 
 def pack(turned, out_weight):
     size, feature = out_weight.shape
-    anywhere = pl.BlockSpec(memory_space=pl.ANY)
-    return pl.pallas_call(
+    return call(
         pack_kernel,
-        out_shape=[jax.ShapeDtypeStruct((2 * size, feature), BF16)] * 2,
-        in_specs=[anywhere] * 2,
-        out_specs=[anywhere] * 2,
-        scratch_shapes=[pltpu.SemaphoreType.DMA((3,))],
-    )(turned, out_weight)
-
-
-def copy_of(place_ref, core):
-    return (place_ref[0] * 2 + core) * 16 + place_ref[2]
-
-
-def prepare_kernel(
-    mine, place_ref, sequence_ref, length_ref, codes_ref, tokens_ref, states_ref, gain_ref,
-    cos_ref, sin_ref,
-    normed_ref, picked_ref, rows_ref, qcos_ref, qsin_ref, targets_ref,
-):
+        [jax.ShapeDtypeStruct((2 * size, feature), BF16)] * 2,
+        (turned, out_weight),
+        n_any=2,
+        scratch=[pltpu.SemaphoreType.DMA((3,))],
+    )
+
+
+def first(mask, values):
+    picked = jnp.sum(jnp.where(mask, values, 0), axis=1, keepdims=True)
+    return jnp.sum(picked, axis=0, keepdims=True)
+
+
+def prepare_kernel(mine, *refs):
+    n = 8 if mine else 7
+    sources, refs = refs[:n], refs[n:]
+    if not mine:
+        states_ref, refs = refs[0], refs[1:]
+    normed_ref, picked_ref, rows_ref, qtable_ref, meta_ref = refs[:5]
+    refs = refs[5:]
+    if mine:
+        table_ref, refs = refs[0], refs[1:]
+    scratch, sems = refs[:-1], refs[-1]
+    if mine:
+        targets = (*scratch[:6], table_ref, scratch[6])
+        states_ref = scratch[6]
+    else:
+        targets = scratch
+        table_ref = scratch[6]
+    copies = [
+        pltpu.make_async_copy(source, target, sems.at[i])
+        for i, (source, target) in enumerate(zip(sources, targets))
+    ]
+    for copy in copies:
+        copy.start()
+    for copy in copies:
+        copy.wait()
+    sequence_ref, length_ref, owner_ref, codes_ref, tokens_ref, gain_ref = targets[:6]
     span = states_ref.shape[0]
     masks = codes_ref.shape[0]
-    gain = gain_ref[...]
-    block = 128
-    copy = copy_of(place_ref, place_ref[1] if mine else 1 - place_ref[1])
-    sequence = sequence_ref[copy]
-    length = length_ref[sequence]
-    codes_all = codes_ref[...]
-    lane = lax.broadcasted_iota(jnp.int32, codes_all.shape, 1)
-    codes = jnp.sum(jnp.where(lane == copy, codes_all, 0), axis=1, keepdims=True)
+    core = lax.axis_index("core")
+    core = core if mine else 1 - core
+    copy = ((lax.axis_index("z") * 2 + core) * 4 + lax.axis_index("y")) * 4 + lax.axis_index("x")
+
+    def numbers(count):
+        return lax.broadcasted_iota(jnp.int32, (1, count), 1)
+
+    own = numbers(codes_ref.shape[1]) == copy
+    sequence = first(own, sequence_ref[...].reshape(1, -1))
+    owner = first(own, owner_ref[...].reshape(1, -1))
+    length = first(numbers(length_ref.shape[0]) == sequence, length_ref[...].reshape(1, -1))
+    codes = jnp.sum(jnp.where(own, codes_ref[...], 0), axis=1, keepdims=True)
     quotient = jnp.floor(codes.astype(F32) / length.astype(F32)).astype(jnp.int32)
     positions = codes - quotient * length
     positions = jnp.where(positions < 0, positions + length, positions)
     positions = jnp.where(positions >= length, positions - length, positions)
     hit = lax.broadcasted_iota(jnp.int32, (masks, span), 1) == positions
-    tokens = tokens_ref[pl.ds(sequence, 1), :]
+    line = lax.broadcasted_iota(jnp.int32, tokens_ref.shape, 0)
+    tokens = jnp.sum(jnp.where(line == sequence, tokens_ref[...], 0), axis=0, keepdims=True)
     targets = jnp.sum(jnp.where(hit, tokens, 0), axis=1, keepdims=True)
-    targets_ref[...] = jnp.broadcast_to(targets, targets_ref.shape)
+    lane = lax.broadcasted_iota(jnp.int32, meta_ref.shape, 1)
+    meta_ref[...] = jnp.where(lane == 0, targets, jnp.where(lane == 1, length, owner))
     hot = hit.astype(F32)
-    qcos_ref[...] = nn_dot(hot, cos_ref[...], precision=lax.Precision.HIGHEST)
-    qsin_ref[...] = nn_dot(hot, sin_ref[...], precision=lax.Precision.HIGHEST)
+    qtable_ref[...] = nn_dot(hot, table_ref[...], precision=lax.Precision.HIGHEST)
     hot = hot.astype(BF16)
+    gain = gain_ref[...].reshape(1, -1)
+    block = 128
 
     def step(i, carry):
         at = pl.multiple_of(i * block, block)
@@ -131,25 +163,23 @@
 
 
 def keys_kernel(
-    place_ref, sequence_ref, length_ref, normed_refs, picked_refs, cos_ref, sin_ref, qcos_refs,
-    qsin_refs, block_refs, probs_ref,
+    table_ref, normed_refs, picked_refs, qtable_refs, meta_refs, block_refs, probs_ref
 ):
     size = block_refs[0].shape[0] // 2
     masks = picked_refs[0].shape[0]
     heads = len(block_refs)
     key_weight = jnp.concatenate([r[size:, :] for r in block_refs], axis=0)
     query_weight = jnp.concatenate([r[:size, :] for r in block_refs], axis=0)
-    cores = (place_ref[1], 1 - place_ref[1])
     for which in range(2):
-        length = length_ref[sequence_ref[copy_of(place_ref, cores[which])]]
+        length = meta_refs[which][0:1, 1:2]
         keys = nt_dot(normed_refs[which][...], key_weight)
         queries = nt_dot(picked_refs[which][...], query_weight) * 0.125
         turned_keys, turned_queries = [], []
         for i in range(heads // 2):
             lanes = slice(128 * i, 128 * (i + 1))
-            turned_keys.append(rotate(keys[:, lanes], cos_ref[...], sin_ref[...], size // 2))
+            turned_keys.append(rotate(keys[:, lanes], table_ref[...], size // 2))
             turned_queries.append(
-                rotate(queries[:, lanes], qcos_refs[which][...], qsin_refs[which][...], size // 2)
+                rotate(queries[:, lanes], qtable_refs[which][...], size // 2)
             )
         key_rows = jnp.concatenate(turned_keys, axis=1).astype(BF16)
         query_rows = jnp.concatenate(turned_queries, axis=1).astype(BF16)
@@ -173,8 +203,8 @@
         values_ref[which] = nt_dot(normed_refs[which][...], weight).astype(BF16)
 
 
-def mix_kernel(place_ref, probs_refs, values_refs, block_refs, partial_ref):
-    right = place_ref[3] == 1
+def mix_kernel(probs_refs, values_refs, block_refs, partial_ref):
+    right = (lax.axis_index("x") + lax.axis_index("y")) % 2 == lax.axis_index("core")
     own_probs, near_probs, far_probs = probs_refs
     size = block_refs[0].shape[0] // 2
     masks = own_probs.shape[1] // 2
@@ -212,8 +242,8 @@
 
 
 def score_kernel(
-    place_ref, owner_ref, rows_refs, partial_ref, arrived_ref, targets_refs, gain_ref, bias_ref,
-    dense_ref, decoder_ref, placed_ref,
+    rows_refs, partial_ref, arrived_ref, meta_refs, gain_ref, bias_ref, dense_ref, decoder_ref,
+    placed_ref,
 ):
     masks = rows_refs[0].shape[0]
     residual = jnp.concatenate(
@@ -223,7 +253,7 @@
         ],
         axis=0,
     )
-    targets = jnp.concatenate([r[:, 0:1] for r in targets_refs], axis=0)
+    targets = jnp.concatenate([r[:, 0:1] for r in meta_refs], axis=0)
     average = jnp.mean(residual, axis=1, keepdims=True)
     centred = residual - average
     variance = jnp.mean(centred * centred, axis=1, keepdims=True)
@@ -250,13 +280,12 @@
     )
     layer = lax.broadcasted_iota(jnp.int32, (devices, width), 0) // 16
     slot = lax.broadcasted_iota(jnp.int32, (devices, width), 1) // 4
-    wanted = 16 * (2 * layer + place_ref[1]) + slot
+    wanted = 16 * (2 * layer + lax.axis_index("core")) + slot
     placed = jnp.zeros((devices, width), F32)
-    cores = (place_ref[1], 1 - place_ref[1])
     for which in range(2):
         own = jnp.where(fits, score[masks * which : masks * (which + 1), :], 0.0)
         laid = nn_dot(take, own, precision=lax.Precision.HIGHEST)
-        placed = jnp.where(wanted == owner_ref[copy_of(place_ref, cores[which])], laid, placed)
+        placed = jnp.where(wanted == meta_refs[which][0:1, 2:3], laid, placed)
     placed_ref[...] = placed
 
 
@@ -309,33 +338,35 @@
     _, span, feature = hidden_states.shape
     size = output_weight.shape[0]
     masks = mask_code.shape[1]
-    core = lax.axis_index("core")
-    member = lax.axis_index(("y", "x"))
-    right = (lax.axis_index("x") + lax.axis_index("y")) % 2 == core
-    place = jnp.stack([lax.axis_index("z"), core, member, right.astype(core.dtype)])
-    place = place.astype(jnp.int32)
-    cos_table, sin_table = (jnp.asarray(t) for t in rotary_tables(span, size))
+    table = jnp.asarray(rotary_tables(span, size))
     shape = jax.ShapeDtypeStruct
 
-    def prepare_call(mine, states):
+    def prepare_call(mine, states, table):
+        small = [copy_sequence, seq_lengths, copy_owner, mask_code.T, seq_tokens, ln_attn_gain]
+        outs = [
+            shape((span, feature), BF16),
+            shape((masks, feature), BF16),
+            shape((masks, feature), F32),
+            shape((masks, 256), F32),
+            shape((masks, 128), jnp.int32),
+        ]
+        args = [*small, table, states]
+        scratch = [pltpu.VMEM(a.shape, a.dtype) for a in small]
+        if mine:
+            outs.append(shape(table.shape, F32))
+            scratch.append(pltpu.VMEM(states.shape, states.dtype))
+        else:
+            scratch.append(pltpu.VMEM(table.shape, table.dtype))
+
         def kernel(*refs):
             prepare_kernel(mine, *refs)
 
         return call(
             kernel,
-            [
-                shape((span, feature), BF16),
-                shape((masks, feature), BF16),
-                shape((masks, feature), F32),
-                shape((masks, 128), F32),
-                shape((masks, 128), F32),
-                shape((masks, 128), jnp.int32),
-            ],
-            3,
-            (
-                place, copy_sequence, seq_lengths, mask_code.T, seq_tokens, states,
-                ln_attn_gain.reshape(1, -1), cos_table, sin_table,
-            ),
+            outs,
+            args,
+            n_any=8 if mine else 7,
+            scratch=[*scratch, pltpu.SemaphoreType.DMA((8,))],
             flops=4 * masks * span * feature + 10 * span * feature,
         )
 
@@ -344,16 +375,15 @@
 
         def kernel(*refs):
             keys_kernel(
-                *refs[:3], refs[3:5], refs[5:7], *refs[7:9], refs[9:11], refs[11:13],
-                refs[13 : 13 + heads], refs[13 + heads],
+                refs[0], refs[1:3], refs[3:5], refs[5:7], refs[7:9], refs[9 : 9 + heads],
+                refs[9 + heads],
             )
 
+        per_copy = [r[i] for i in (0, 1, 3, 4) for r in ready]
         return call(
             kernel,
             shape((2, heads * masks, span), BF16),
-            3,
-            (place, copy_sequence, seq_lengths, *(r[0] for r in ready), *(r[1] for r in ready),
-             cos_table, sin_table, *(r[3] for r in ready), *(r[4] for r in ready), *blocks),
+            (ready[0][5], *per_copy, *blocks),
             flops=4 * span * feature * 256,
             exps=2 * heads * masks * span,
         )
@@ -367,7 +397,6 @@
         return call(
             kernel,
             shape((2, span, heads * size), BF16),
-            0,
             (*(r[0] for r in ready), *blocks),
             flops=4 * span * feature * 256,
         )
@@ -377,58 +406,56 @@
     key_low, key_high = gather_line(key_block, "x")
     value_low, value_high = gather_line(value_block, "y")
     states_other = swap(states)
-    mine = prepare_call(True, states)
-    key_low, key_high = after(key_low, mine[0]), after(key_high, mine[0])
-    value_low, value_high = after(value_low, mine[0]), after(value_high, mine[0])
-    key_ahead = [pull(key_low, "y", 1)]
-    key_behind = [pull(key_high, "y", 3)]
-    value_ahead = [pull(value_low, "x", 1)]
-    value_behind = [pull(value_high, "x", 3)]
-    key_ahead.append(pull(key_high, "y", 1))
-    key_behind.insert(0, pull(key_low, "y", 3))
-    value_ahead.append(pull(value_high, "x", 1))
-    value_behind.insert(0, pull(value_low, "x", 3))
-    other = prepare_call(False, states_other)
+    mine = prepare_call(True, states, table)
+    key_ahead_low = pull(after(key_low, mine[0]), "y", 1)
+    key_behind_high = pull(after(key_high, mine[0]), "y", 3)
+    value_ahead_low = pull(after(value_low, mine[0]), "x", 1)
+    value_behind_high = pull(after(value_high, mine[0]), "x", 3)
+    other = prepare_call(False, after(states_other, mine[0]), table)
     ready = (mine, other)
+    key_ahead_high = pull(after(key_high, key_ahead_low, other[0]), "y", 1)
+    key_behind_low = pull(after(key_low, key_behind_high, other[0]), "y", 3)
+    value_ahead_high = pull(after(value_high, value_ahead_low, other[0]), "x", 1)
+    value_behind_low = pull(after(value_low, value_behind_high, other[0]), "x", 3)
     own_probs = keys_call(ready, (key_low, key_high))
+    own_values = values_call(ready, (value_low, value_high))
     key_far = (
-        pull(after(key_ahead[0], own_probs), "y", 1),
-        pull(after(key_behind[1], own_probs), "y", 3),
+        pull(after(key_ahead_low, key_ahead_high, own_probs, own_values), "y", 1),
+        pull(after(key_behind_high, key_behind_low, own_probs, own_values), "y", 3),
     )
     value_far = (
-        pull(after(value_ahead[0], own_probs), "x", 1),
-        pull(after(value_behind[1], own_probs), "x", 3),
-    )
-    own_values = values_call(ready, (value_low, value_high))
-    near_probs = keys_call(ready, (*key_ahead, *key_behind))
-    near_values = values_call(ready, (*value_ahead, *value_behind))
+        pull(after(value_ahead_low, value_ahead_high, own_probs, own_values), "x", 1),
+        pull(after(value_behind_high, value_behind_low, own_probs, own_values), "x", 3),
+    )
+    key_near = (key_ahead_low, key_ahead_high, key_behind_low, key_behind_high)
+    value_near = (value_ahead_low, value_ahead_high, value_behind_low, value_behind_high)
+    near_probs = keys_call(ready, key_near)
+    near_values = values_call(ready, value_near)
     key_far = tuple(after(b, near_probs, near_values) for b in key_far)
     far_probs = keys_call(ready, key_far)
     far_values = values_call(ready, value_far)
     probs = (own_probs, near_probs, far_probs)
     values = (own_values, near_values, far_values)
-    value_blocks = (value_low, value_high, *value_ahead, *value_behind, *value_far)
+    value_blocks = (value_low, value_high, *value_near, *value_far)
 
     def mix(*refs):
-        mix_kernel(refs[0], refs[1:4], refs[4:7], refs[7:15], refs[15])
+        mix_kernel(refs[:3], refs[3:6], refs[6:14], refs[14])
 
     partial = call(
         mix,
         shape((2 * masks, feature), F32),
-        1,
-        (place, *probs, *values, *value_blocks),
+        (*probs, *values, *value_blocks),
         flops=4 * masks * feature * 8 * size,
     )
 
     def score(*refs):
-        score_kernel(*refs[:2], refs[2:4], *refs[4:6], refs[6:8], *refs[8:])
+        score_kernel(refs[:2], *refs[2:4], refs[4:6], *refs[6:])
 
     placed = call(
         score,
         shape((128, 64), F32),
-        2,
         (
-            place, copy_owner, mine[2], other[2], partial, swap(partial), mine[5], other[5],
+            mine[2], other[2], partial, swap(partial), mine[4], other[4],
             ln_final_gain.reshape(1, -1), decoder_bias.reshape(1, -1), dense_weight,
             decoder_weight.T,
         ),

time: 113 us -> 80.9 us (0.72)
  Pallas kernels: 44.2 us -> 24.1 us
  waiting for transfers between devices: 13.9 us -> 3.76 us
  local copies, waits for them, and re-layouts: 7.87 us -> 0.78 us
  starting transfers between devices: 22.7 us -> 27.9 us
    pallas_call x11, Pallas kernels: 44.2 us -> 24.1 us  [call(): pl.pallas_call(kernel, out_shape=outs, in_specs=[IN_PLACE] * n_any + [ON_...]
    ppermute x12, waiting for transfers between devices: 12.2 us -> 2.03 us  [pull(): lax.ppermute(array, axis, [((i + offset) % size, i) for i in range(size)])]
    unnamed x28 -> x8, local copies, waits for them, and re-layouts: 6.42 us -> 0.03 us
    ppermute x12, starting transfers between devices: 11.7 us -> 16.2 us  [pull(): lax.ppermute(array, axis, [((i + offset) % size, i) for i in range(size)])]
  transfers between devices with their start and end apart: 18 -> 18, of which waited for: 4 -> 3; matrix products, arithmetic and copies ran while one was open for 1% -> 0% of each run, Pallas kernels for 35% -> 25%
where the time goes in v4:
time: 80.9 us; the launch traced here: 80.7 us
  starting transfers between devices  27.9 us (34%)
  Pallas kernels  24.1 us (30%)
  blocking collectives  23.8 us (29%)
  waiting for transfers between devices  3.76 us (5%)
    pallas_call x11, Pallas kernels, call(): pl.pallas_call(kernel, out_shape=outs, in_specs=[IN_PLACE] * n_any + [ON_...  24.1 us
    all_to_all x1, blocking collectives, on_device(): arrived = lax.all_to_all(placed, ('z', 'y', 'x'), 0, 0, tiled=True)  23.8 us
    ppermute x12, starting transfers between devices, pull(): lax.ppermute(array, axis, [((i + offset) % size, i) for i in range(size)])  16.2 us
    ppermute x2, starting transfers between devices, swap(): return lax.ppermute(array, 'core', [(0, 1), (1, 0)])  6.72 us
    ppermute x4, starting transfers between devices, gather_line(): return (lax.ppermute(block, axes, near), lax.ppermute(block, axes, far))  4.99 us
    ppermute x12, waiting for transfers between devices, pull(): lax.ppermute(array, axis, [((i + offset) % size, i) for i in range(size)])  2.03 us
    ppermute x2, waiting for transfers between devices, swap(): return lax.ppermute(array, 'core', [(0, 1), (1, 0)])  1.72 us
  transfers between devices with their start and end apart: 18, of which 3 were waited for; matrix products, arithmetic and copies ran while one was open for 0% of the time, Pallas kernels for 25%

profile of v4, /device:TPU:1, one launch (start us, length us, event | category | flops | bytes accessed | tf_op | source)
XLA Modules:
  0.0 80.7 jit_solution(3224720595178111867)
XLA Ops:
  0.0 3.2 %collective-permute-start = (bf16[640,1280]{1,0:T(8,128)(2,1)}, bf16[640,1280]{1,0:T(8,128)(2,1)S(1)}, u32[]{:S(2)}, u32[]{:S(2)}) collective-permute-start(bf16[640,1280]{1,0:T(8,128)(2,1)} %bitcast.14), channel_id=1, source_target_pairs={{0,16},{16,0},{1,17},{17,1},{2,18},{18,2},{3,19},{19,3},{4,20},{20... | collective-permute-start | bytes 4915208 | tf_op jit(solution)/shard_map/ppermute | solution.py:298
  3.2 1.1 %shard_map.138 = (bf16[128,1280]{1,0:T(8,128)(2,1)S(1)}, bf16[128,1280]{1,0:T(8,128)(2,1)S(1)}) custom-call(bf16[192,1280]{1,0:T(8,128)(2,1)} %bitcast.16, bf16[64,1280]{1,0:T(8,128)(2,1)} %bitcast.19), custom_call_target="tpu_custom_call" | custom-call | bytes 1310720 | tf_op jit(solution)/shard_map/pallas_call | solution.py:54
  4.4 0.1 collective-permute-start.1
  4.5 1.4 %collective-permute-start.2 = (bf16[128,1280]{1,0:T(8,128)(2,1)S(1)}, bf16[128,1280]{1,0:T(8,128)(2,1)S(1)}, u32[]{:S(2)}, u32[]{:S(2)}) collective-permute-start(bf16[128,1280]{1,0:T(8,128)(2,1)S(1)} %get-tuple-element.45), channel_id=1, source_target_pairs={{0,1},{1,19},{2,3},{3,17},{4,22},{5,6},{6,20},{7,4},{8,9},{9,27},{... | collective-permute-start | bytes 983048 | tf_op jit(solution)/shard_map/ppermute | solution.py:320
  5.9 0.0 collective-permute-start.7
  5.9 3.5 %collective-permute-start.8 = (bf16[128,1280]{1,0:T(8,128)(2,1)S(1)}, bf16[128,1280]{1,0:T(8,128)(2,1)S(1)}, u32[]{:S(2)}, u32[]{:S(2)}) collective-permute-start(bf16[128,1280]{1,0:T(8,128)(2,1)S(1)} %get-tuple-element.50), channel_id=1, source_target_pairs={{0,4},{1,25},{2,6},{3,27},{4,28},{5,9},{6,30},{7,11},{8,12},{9,17}... | collective-permute-start | bytes 983048 | tf_op jit(solution)/shard_map/ppermute | solution.py:320
  9.4 4.9 %shard_map.136 = (bf16[640,1280]{1,0:T(8,128)(2,1)S(1)}, bf16[64,1280]{1,0:T(8,128)(2,1)S(1)}, f32[64,1280]{1,0:T(8,128)S(1)}, f32[64,256]{1,0:T(8,128)S(1)}, s3...) custom-call(s32[256]{0:T(256)} %refs_0_.3, s32[24]{0:T(128)} %refs_1_.3, s32[256]{0:T(256)} %refs_2_.3, s32[64,256]{1,0:T(8,128)} %bitcast.17, ...), custom_call_target="tpu_custom_call" | custom-call | flops 217907200 | bytes 5311584 | tf_op jit(solution)/shard_map/pallas_call | solution.py:54
  14.2 0.0 collective-permute-done.1.refs_9_
  14.2 1.2 %collective-permute-start.3 = (bf16[128,1280]{1,0:T(8,128)(2,1)S(1)}, bf16[128,1280]{1,0:T(8,128)(2,1)S(1)}, u32[]{:S(2)}, u32[]{:S(2)}) collective-permute-start(bf16[128,1280]{1,0:T(8,128)(2,1)S(1)} %collective-permute-done.1.refs_9_), channel_id=1, source_target_pairs={{4,0},{8,4},{12,8},{0,12},{5,1},{9,5},{13,9},{1,13},{6,2},{10,6},{... | collective-permute-start | bytes 983048 | tf_op jit(solution)/shard_map/ppermute | solution.py:294
  15.5 0.0 collective-permute-done.2.refs_10_
  15.5 0.3 collective-permute-start.5
  15.8 0.0 collective-permute-done.7.refs_2_.refs_6_
  15.8 3.2 %collective-permute-start.10 = (bf16[128,1280]{1,0:T(8,128)(2,1)S(1)}, bf16[128,1280]{1,0:T(8,128)(2,1)S(1)}, u32[]{:S(2)}, u32[]{:S(2)}) collective-permute-start(bf16[128,1280]{1,0:T(8,128)(2,1)S(1)} %collective-permute-done.7.refs_2_.refs_6_), channel_id=1, source_target_pairs={{1,0},{2,1},{3,2},{0,3},{5,4},{6,5},{7,6},{4,7},{9,8},{10,9},{11,1... | collective-permute-start | bytes 983048 | tf_op jit(solution)/shard_map/ppermute | solution.py:294
  19.0 0.0 collective-permute-done.8.refs_3_.refs_7_
  19.0 0.0 collective-permute-start.12
  19.0 0.0 collective-permute-done.refs_7_
  19.0 4.4 %shard_map.137 = (bf16[640,1280]{1,0:T(8,128)(2,1)S(1)}, bf16[64,1280]{1,0:T(8,128)(2,1)S(1)}, f32[64,1280]{1,0:T(8,128)S(1)}, f32[64,256]{1,0:T(8,128)S(1)}, s32[64,128]{1,0:T(8,128)S(1)}) custom-call(s32[256]{0:T(256)} %refs_0_.3, s32[24]{0:T(128)} %refs_1_.3, s32[256]{0:T(256)} %refs_2_.3, s32[64,256]{1,0:T(8,128)} %bitcast.18, s32[24,640]{1,0:T(8,128)} %refs_4_.3, ...), custom_call_target="tpu_custom_call" | custom-call | flops 217907200 | bytes 4656224 | tf_op jit(solution)/shard_map/pallas_call | solution.py:54
  23.4 0.4 collective-permute-done.3.refs_9_
  23.8 2.7 %collective-permute-start.4 = (bf16[128,1280]{1,0:T(8,128)(2,1)S(1)}, bf16[128,1280]{1,0:T(8,128)(2,1)S(1)}, u32[]{:S(2)}, u32[]{:S(2)}) collective-permute-start(bf16[128,1280]{1,0:T(8,128)(2,1)S(1)} %collective-permute-done.2.refs_10_), channel_id=1, source_target_pairs={{4,0},{8,4},{12,8},{0,12},{5,1},{9,5},{13,9},{1,13},{6,2},{10,6},{... | collective-permute-start | bytes 983048 | tf_op jit(solution)/shard_map/ppermute | solution.py:294
  26.5 0.0 collective-permute-done.5.refs_12_
  26.5 0.0 collective-permute-start.6
  26.5 0.0 collective-permute-done.10.refs_2_.refs_8_
  26.5 3.0 %collective-permute-start.11 = (bf16[128,1280]{1,0:T(8,128)(2,1)S(1)}, bf16[128,1280]{1,0:T(8,128)(2,1)S(1)}, u32[]{:S(2)}, u32[]{:S(2)}) collective-permute-start(bf16[128,1280]{1,0:T(8,128)(2,1)S(1)} %collective-permute-done.8.refs_3_.refs_7_), channel_id=1, source_target_pairs={{1,0},{2,1},{3,2},{0,3},{5,4},{6,5},{7,6},{4,7},{9,8},{10,9},{11,1... | collective-permute-start | bytes 983048 | tf_op jit(solution)/shard_map/ppermute | solution.py:294
  29.5 0.0 collective-permute-done.12.refs_5_.refs_11_
  29.5 0.0 collective-permute-start.13
  29.5 1.0 %shard_map.141.refs_3_ = bf16[2,640,128]{2,1,0:T(8,128)(2,1)S(1)} custom-call(bf16[640,1280]{1,0:T(8,128)(2,1)S(1)} %get-tuple-element.34.refs_1_.refs_0_, bf16[640,1280]{1,0:T(8,128)(2,1)S(1)} %get-tuple-element.38.refs_2_.refs_1_, bf16[128,1280]{1,0:T(8,128)(2,1)S(1)} %collective-permute-done.7.refs_2_.refs_6_, ...), custom_call_target="tpu_custom_call" | custom-call | flops 838860800 | bytes 4259840 | tf_op jit(solution)/shard_map/pallas_call | solution.py:54
  30.5 2.5 %shard_map.139.refs_0_ = bf16[2,128,640]{2,1,0:T(8,128)(2,1)S(1)} custom-call(f32[640,256]{1,0:T(8,128)S(1)} %get-tuple-element.37.refs_0_, bf16[640,1280]{1,0:T(8,128)(2,1)S(1)} %get-tuple-element.34.refs_1_.refs_0_, bf16[640,1280]{1,0:T(8,128)(2,1)S(1)} %get-tuple-element.38.refs_2_.refs_1_, bf16[64,1280]{1,0:T(8,128)(2,1)S(1)} %get-tuple-element.39.refs_3_, ...), custom_call_target="tpu_custom_call" | custom-call | flops 838860800 | bytes 5439488 | tf_op jit(solution)/shard_map/pallas_call | solution.py:54
  33.0 0.0 collective-permute-done.4.refs_10_
  33.0 3.0 %collective-permute-start.9 = (bf16[128,1280]{1,0:T(8,128)(2,1)S(1)}, bf16[128,1280]{1,0:T(8,128)(2,1)S(1)}, u32[]{:S(2)}, u32[]{:S(2)}) collective-permute-start(bf16[128,1280]{1,0:T(8,128)(2,1)S(1)} %collective-permute-done.3.refs_9_), channel_id=1, source_target_pairs={{4,0},{8,4},{12,8},{0,12},{5,1},{9,5},{13,9},{1,13},{6,2},{10,6},{... | collective-permute-start | bytes 983048 | tf_op jit(solution)/shard_map/ppermute | solution.py:294
  36.1 0.0 collective-permute-done.6.refs_11_
  36.1 0.0 collective-permute-start.14
  36.1 0.0 collective-permute-done.11.refs_3_.refs_9_
  36.1 2.8 %collective-permute-start.15 = (bf16[128,1280]{1,0:T(8,128)(2,1)S(1)}, bf16[128,1280]{1,0:T(8,128)(2,1)S(1)}, u32[]{:S(2)}, u32[]{:S(2)}) collective-permute-start(bf16[128,1280]{1,0:T(8,128)(2,1)S(1)} %collective-permute-done.10.refs_2_.refs_8_), channel_id=1, source_target_pairs={{1,0},{2,1},{3,2},{0,3},{5,4},{6,5},{7,6},{4,7},{9,8},{10,9},{11,1... | collective-permute-start | bytes 983048 | tf_op jit(solution)/shard_map/ppermute | solution.py:294
  38.8 0.0 collective-permute-done.13.refs_4_.refs_10_
  38.8 0.0 collective-permute-start.16
  38.8 3.0 %shard_map.140.refs_1_ = bf16[2,256,640]{2,1,0:T(8,128)(2,1)S(1)} custom-call(f32[640,256]{1,0:T(8,128)S(1)} %get-tuple-element.37.refs_0_, bf16[640,1280]{1,0:T(8,128)(2,1)S(1)} %get-tuple-element.34.refs_1_.refs_0_, bf16[640,1280]{1,0:T(8,128)(2,1)S(1)} %get-tuple-element.38.refs_2_.refs_1_, bf16[64,1280]{1,0:T(8,128)(2,1)S(1)} %get-tuple-element.39.refs_3_, ...), custom_call_target="tpu_custom_call" | custom-call | flops 838860800 | bytes 6422528 | tf_op jit(solution)/shard_map/pallas_call | solution.py:54
  41.8 1.0 %shard_map.142.refs_4_ = bf16[2,640,256]{2,1,0:T(8,128)(2,1)S(1)} custom-call(bf16[640,1280]{1,0:T(8,128)(2,1)S(1)} %get-tuple-element.34.refs_1_.refs_0_, bf16[640,1280]{1,0:T(8,128)(2,1)S(1)} %get-tuple-element.38.refs_2_.refs_1_, bf16[128,1280]{1,0:T(8,128)(2,1)S(1)} %collective-permute-done.10.refs_2_.refs_8_, ...), custom_call_target="tpu_custom_call" | custom-call | flops 838860800 | bytes 5242880 | tf_op jit(solution)/shard_map/pallas_call | solution.py:54
  42.9 0.0 collective-permute-done.9.refs_9_
  42.9 1.6 %collective-permute-done.14.refs_10_ = bf16[128,1280]{1,0:T(8,128)(2,1)S(1)} collective-permute-done((bf16[128,1280]{1,0:T(8,128)(2,1)S(1)}, bf16[128,1280]{1,0:T(8,128)(2,1)S(1)}, u32[]{:S(2)}, u32[]{:S(2)}) %collective-permute-start.14) | collective-permute-done | bytes 327712 | tf_op jit(solution)/shard_map/ppermute | solution.py:294
  44.5 2.5 %shard_map.143.refs_2_ = bf16[2,128,640]{2,1,0:T(8,128)(2,1)S(1)} custom-call(f32[640,256]{1,0:T(8,128)S(1)} %get-tuple-element.37.refs_0_, bf16[640,1280]{1,0:T(8,128)(2,1)S(1)} %get-tuple-element.34.refs_1_.refs_0_, bf16[640,1280]{1,0:T(8,128)(2,1)S(1)} %get-tuple-element.38.refs_2_.refs_1_, bf16[64,1280]{1,0:T(8,128)(2,1)S(1)} %get-tuple-element.39.refs_3_, ...), custom_call_target="tpu_custom_call" | custom-call | flops 838860800 | bytes 5439488 | tf_op jit(solution)/shard_map/pallas_call | solution.py:54
  47.0 0.0 collective-permute-done.15.refs_2_.refs_12_
  47.0 0.0 collective-permute-done.16.refs_3_.refs_13_
  47.0 1.0 %shard_map.144.refs_5_ = bf16[2,640,128]{2,1,0:T(8,128)(2,1)S(1)} custom-call(bf16[640,1280]{1,0:T(8,128)(2,1)S(1)} %get-tuple-element.34.refs_1_.refs_0_, bf16[640,1280]{1,0:T(8,128)(2,1)S(1)} %get-tuple-element.38.refs_2_.refs_1_, bf16[128,1280]{1,0:T(8,128)(2,1)S(1)} %collective-permute-done.15.refs_2_.refs_12_, ...), custom_call_target="tpu_custom_call" | custom-call | flops 838860800 | bytes 4259840 | tf_op jit(solution)/shard_map/pallas_call | solution.py:54
  48.0 0.0 copy-start.3
  48.0 0.0 copy-start
  48.0 0.0 copy-start.1
  48.0 0.0 copy-start.2
  48.0 0.9 %shard_map.145.refs_2_ = f32[128,1280]{1,0:T(8,128)S(1)} custom-call(bf16[2,128,640]{2,1,0:T(8,128)(2,1)S(1)} %shard_map.139.refs_0_, bf16[2,256,640]{2,1,0:T(8,128)(2,1)S(1)} %shard_map.140.refs_1_, bf16[2,128,640]{2,1,0:T(8,128)(2,1)S(1)} %shard_map.143.refs_2_, bf16[2,640,128]{2,1,0:T(8,128)(2,1)S(1)} %shard_map.141.refs_3_, ...), custom_call_target="tpu_custom_call" | custom-call | flops 167772160 | bytes 5898240 | tf_op jit(solution)/shard_map/pallas_call | solution.py:54
  49.0 3.5 %collective-permute-start.17 = (f32[128,1280]{1,0:T(8,128)S(1)}, f32[128,1280]{1,0:T(8,128)S(1)}, u32[]{:S(2)}, u32[]{:S(2)}) collective-permute-start(f32[128,1280]{1,0:T(8,128)S(1)} %shard_map.145.refs_2_), channel_id=1, source_target_pairs={{0,16},{16,0},{1,17},{17,1},{2,18},{18,2},{3,19},{19,3},{4,20},{20... | collective-permute-start | bytes 1966088 | tf_op jit(solution)/shard_map/ppermute | solution.py:298
  52.4 0.0 copy-done.3
  52.5 1.7 %collective-permute-done.17.refs_3_ = f32[128,1280]{1,0:T(8,128)S(1)} collective-permute-done((f32[128,1280]{1,0:T(8,128)S(1)}, f32[128,1280]{1,0:T(8,128)S(1)}, u32[]{:S(2)}, u32[]{:S(2)}) %collective-permute-start.17) | collective-permute-done | bytes 655392 | tf_op jit(solution)/shard_map/ppermute | solution.py:298
  54.2 0.0 copy-done
  54.2 0.0 copy-done.1
  54.2 0.0 copy-done.2
  54.2 1.8 %shard_map.146 = f32[128,64]{1,0:T(8,128)S(1)} custom-call(f32[64,1280]{1,0:T(8,128)S(1)} %get-tuple-element.33.refs_0_, f32[64,1280]{1,0:T(8,128)S(1)} %get-tuple-element.36.refs_1_, f32[128,1280]{1,0:T(8,128)S(1)} %shard_map.145.refs_2_, f32[128,1280]{1,0:T(8,128)S(1)} %collective-permute-done.17.refs_3_, s32[64,128]{1,0:T(8,128)S(1)} %get-tuple-element.43.refs_7_.refs_4_, ...), custom_call_target="tpu_custom_call" | custom-call | flops 419430400 | bytes 5430916 | tf_op jit(solution)/shard_map/pallas_call | solution.py:54
  56.0 23.8 %all_to_all.9 = f32[128,1,64]{2,1,0:T(1,128)S(1)} all-to-all(f32[128,1,64]{2,1,0:T(1,128)S(1)} %bitcast.11), channel_id=1, replica_groups=mesh['z'=8,'core'=2,'y'=4,'x'=4] {'z','y','x'}, dimensions={0} | all-to-all | bytes 65536 | tf_op jit(solution)/shard_map/all_to_all | solution.py:464
  79.8 0.2 reduce_sum.9
  79.9 0.1 reshape.13
  80.0 0.7 copy.18
  (1 shorter events, 0.0 us)
Async XLA Ops:
  0.0 19.0 %collective-permute-start = (bf16[640,1280]{1,0:T(8,128)(2,1)}, bf16[640,1280]{1,0:T(8,128)(2,1)S(1)}, u32[]{:S(2)}, u32[]{:S(2)}) collective-permute-start(bf16[640,1280]{1,0:T(8,128)(2,1)} %bitcast.14), channel_id=1, source_target_pairs={{0,16},{16,0},{1,17},{17,1},{2,18},{18,2},{3,19},{19,3},{4,20},{20... | collective-permute-start | bytes 4915208 | tf_op jit(solution)/shard_map/ppermute | solution.py:298
  4.4 9.9 %collective-permute-start.1 = (bf16[128,1280]{1,0:T(8,128)(2,1)S(1)}, bf16[128,1280]{1,0:T(8,128)(2,1)S(1)}, u32[]{:S(2)}, u32[]{:S(2)}) collective-permute-start(bf16[128,1280]{1,0:T(8,128)(2,1)S(1)} %get-tuple-element.45), channel_id=1, source_target_pairs={{0,3},{1,17},{2,1},{3,19},{4,20},{5,4},{6,22},{7,6},{8,11},{9,25},... | collective-permute-start | bytes 983048 | tf_op jit(solution)/shard_map/ppermute | solution.py:320
  4.5 11.0 %collective-permute-start.2 = (bf16[128,1280]{1,0:T(8,128)(2,1)S(1)}, bf16[128,1280]{1,0:T(8,128)(2,1)S(1)}, u32[]{:S(2)}, u32[]{:S(2)}) collective-permute-start(bf16[128,1280]{1,0:T(8,128)(2,1)S(1)} %get-tuple-element.45), channel_id=1, source_target_pairs={{0,1},{1,19},{2,3},{3,17},{4,22},{5,6},{6,20},{7,4},{8,9},{9,27},{... | collective-permute-start | bytes 983048 | tf_op jit(solution)/shard_map/ppermute | solution.py:320
  5.9 9.9 %collective-permute-start.7 = (bf16[128,1280]{1,0:T(8,128)(2,1)S(1)}, bf16[128,1280]{1,0:T(8,128)(2,1)S(1)}, u32[]{:S(2)}, u32[]{:S(2)}) collective-permute-start(bf16[128,1280]{1,0:T(8,128)(2,1)S(1)} %get-tuple-element.50), channel_id=1, source_target_pairs={{0,12},{1,17},{2,14},{3,19},{4,20},{5,1},{6,22},{7,3},{8,4},{9,25}... | collective-permute-start | bytes 983048 | tf_op jit(solution)/shard_map/ppermute | solution.py:320
  5.9 13.1 %collective-permute-start.8 = (bf16[128,1280]{1,0:T(8,128)(2,1)S(1)}, bf16[128,1280]{1,0:T(8,128)(2,1)S(1)}, u32[]{:S(2)}, u32[]{:S(2)}) collective-permute-start(bf16[128,1280]{1,0:T(8,128)(2,1)S(1)} %get-tuple-element.50), channel_id=1, source_target_pairs={{0,4},{1,25},{2,6},{3,27},{4,28},{5,9},{6,30},{7,11},{8,12},{9,17}... | collective-permute-start | bytes 983048 | tf_op jit(solution)/shard_map/ppermute | solution.py:320
  14.2 9.6 %collective-permute-start.3 = (bf16[128,1280]{1,0:T(8,128)(2,1)S(1)}, bf16[128,1280]{1,0:T(8,128)(2,1)S(1)}, u32[]{:S(2)}, u32[]{:S(2)}) collective-permute-start(bf16[128,1280]{1,0:T(8,128)(2,1)S(1)} %collective-permute-done.1.refs_9_), channel_id=1, source_target_pairs={{4,0},{8,4},{12,8},{0,12},{5,1},{9,5},{13,9},{1,13},{6,2},{10,6},{... | collective-permute-start | bytes 983048 | tf_op jit(solution)/shard_map/ppermute | solution.py:294
  15.5 11.0 %collective-permute-start.5 = (bf16[128,1280]{1,0:T(8,128)(2,1)S(1)}, bf16[128,1280]{1,0:T(8,128)(2,1)S(1)}, u32[]{:S(2)}, u32[]{:S(2)}) collective-permute-start(bf16[128,1280]{1,0:T(8,128)(2,1)S(1)} %collective-permute-done.2.refs_10_), channel_id=1, source_target_pairs={{12,0},{0,4},{4,8},{8,12},{13,1},{1,5},{5,9},{9,13},{14,2},{2,6},{... | collective-permute-start | bytes 983048 | tf_op jit(solution)/shard_map/ppermute | solution.py:294
  15.8 10.7 %collective-permute-start.10 = (bf16[128,1280]{1,0:T(8,128)(2,1)S(1)}, bf16[128,1280]{1,0:T(8,128)(2,1)S(1)}, u32[]{:S(2)}, u32[]{:S(2)}) collective-permute-start(bf16[128,1280]{1,0:T(8,128)(2,1)S(1)} %collective-permute-done.7.refs_2_.refs_6_), channel_id=1, source_target_pairs={{1,0},{2,1},{3,2},{0,3},{5,4},{6,5},{7,6},{4,7},{9,8},{10,9},{11,1... | collective-permute-start | bytes 983048 | tf_op jit(solution)/shard_map/ppermute | solution.py:294
  19.0 10.5 %collective-permute-start.12 = (bf16[128,1280]{1,0:T(8,128)(2,1)S(1)}, bf16[128,1280]{1,0:T(8,128)(2,1)S(1)}, u32[]{:S(2)}, u32[]{:S(2)}) collective-permute-start(bf16[128,1280]{1,0:T(8,128)(2,1)S(1)} %collective-permute-done.8.refs_3_.refs_7_), channel_id=1, source_target_pairs={{3,0},{0,1},{1,2},{2,3},{7,4},{4,5},{5,6},{6,7},{11,8},{8,9},{9,10... | collective-permute-start | bytes 983048 | tf_op jit(solution)/shard_map/ppermute | solution.py:294
  23.8 9.2 %collective-permute-start.4 = (bf16[128,1280]{1,0:T(8,128)(2,1)S(1)}, bf16[128,1280]{1,0:T(8,128)(2,1)S(1)}, u32[]{:S(2)}, u32[]{:S(2)}) collective-permute-start(bf16[128,1280]{1,0:T(8,128)(2,1)S(1)} %collective-permute-done.2.refs_10_), channel_id=1, source_target_pairs={{4,0},{8,4},{12,8},{0,12},{5,1},{9,5},{13,9},{1,13},{6,2},{10,6},{... | collective-permute-start | bytes 983048 | tf_op jit(solution)/shard_map/ppermute | solution.py:294
  26.5 9.6 %collective-permute-start.6 = (bf16[128,1280]{1,0:T(8,128)(2,1)S(1)}, bf16[128,1280]{1,0:T(8,128)(2,1)S(1)}, u32[]{:S(2)}, u32[]{:S(2)}) collective-permute-start(bf16[128,1280]{1,0:T(8,128)(2,1)S(1)} %collective-permute-done.1.refs_9_), channel_id=1, source_target_pairs={{12,0},{0,4},{4,8},{8,12},{13,1},{1,5},{5,9},{9,13},{14,2},{2,6},{... | collective-permute-start | bytes 983048 | tf_op jit(solution)/shard_map/ppermute | solution.py:294
  26.5 9.6 %collective-permute-start.11 = (bf16[128,1280]{1,0:T(8,128)(2,1)S(1)}, bf16[128,1280]{1,0:T(8,128)(2,1)S(1)}, u32[]{:S(2)}, u32[]{:S(2)}) collective-permute-start(bf16[128,1280]{1,0:T(8,128)(2,1)S(1)} %collective-permute-done.8.refs_3_.refs_7_), channel_id=1, source_target_pairs={{1,0},{2,1},{3,2},{0,3},{5,4},{6,5},{7,6},{4,7},{9,8},{10,9},{11,1... | collective-permute-start | bytes 983048 | tf_op jit(solution)/shard_map/ppermute | solution.py:294
  29.5 9.4 %collective-permute-start.13 = (bf16[128,1280]{1,0:T(8,128)(2,1)S(1)}, bf16[128,1280]{1,0:T(8,128)(2,1)S(1)}, u32[]{:S(2)}, u32[]{:S(2)}) collective-permute-start(bf16[128,1280]{1,0:T(8,128)(2,1)S(1)} %collective-permute-done.7.refs_2_.refs_6_), channel_id=1, source_target_pairs={{3,0},{0,1},{1,2},{2,3},{7,4},{4,5},{5,6},{6,7},{11,8},{8,9},{9,10... | collective-permute-start | bytes 983048 | tf_op jit(solution)/shard_map/ppermute | solution.py:294
  33.0 9.9 %collective-permute-start.9 = (bf16[128,1280]{1,0:T(8,128)(2,1)S(1)}, bf16[128,1280]{1,0:T(8,128)(2,1)S(1)}, u32[]{:S(2)}, u32[]{:S(2)}) collective-permute-start(bf16[128,1280]{1,0:T(8,128)(2,1)S(1)} %collective-permute-done.3.refs_9_), channel_id=1, source_target_pairs={{4,0},{8,4},{12,8},{0,12},{5,1},{9,5},{13,9},{1,13},{6,2},{10,6},{... | collective-permute-start | bytes 983048 | tf_op jit(solution)/shard_map/ppermute | solution.py:294
  36.1 8.4 %collective-permute-start.14 = (bf16[128,1280]{1,0:T(8,128)(2,1)S(1)}, bf16[128,1280]{1,0:T(8,128)(2,1)S(1)}, u32[]{:S(2)}, u32[]{:S(2)}) collective-permute-start(bf16[128,1280]{1,0:T(8,128)(2,1)S(1)} %collective-permute-done.5.refs_12_), channel_id=1, source_target_pairs={{12,0},{0,4},{4,8},{8,12},{13,1},{1,5},{5,9},{9,13},{14,2},{2,6},{... | collective-permute-start | bytes 983048 | tf_op jit(solution)/shard_map/ppermute | solution.py:294
  36.1 10.9 %collective-permute-start.15 = (bf16[128,1280]{1,0:T(8,128)(2,1)S(1)}, bf16[128,1280]{1,0:T(8,128)(2,1)S(1)}, u32[]{:S(2)}, u32[]{:S(2)}) collective-permute-start(bf16[128,1280]{1,0:T(8,128)(2,1)S(1)} %collective-permute-done.10.refs_2_.refs_8_), channel_id=1, source_target_pairs={{1,0},{2,1},{3,2},{0,3},{5,4},{6,5},{7,6},{4,7},{9,8},{10,9},{11,1... | collective-permute-start | bytes 983048 | tf_op jit(solution)/shard_map/ppermute | solution.py:294
  38.8 8.2 %collective-permute-start.16 = (bf16[128,1280]{1,0:T(8,128)(2,1)S(1)}, bf16[128,1280]{1,0:T(8,128)(2,1)S(1)}, u32[]{:S(2)}, u32[]{:S(2)}) collective-permute-start(bf16[128,1280]{1,0:T(8,128)(2,1)S(1)} %collective-permute-done.12.refs_5_.refs_11_), channel_id=1, source_target_pairs={{3,0},{0,1},{1,2},{2,3},{7,4},{4,5},{5,6},{6,7},{11,8},{8,9},{9,10... | collective-permute-start | bytes 983048 | tf_op jit(solution)/shard_map/ppermute | solution.py:294
  48.0 4.5 %copy-start.3 = (f32[1280]{0:T(1024)S(1)}, f32[1280]{0:T(1024)}, u32[]{:S(2)}) copy-start(f32[1280]{0:T(1024)} %param.18) | copy-start | bytes 15364
  48.0 6.2 %copy-start = (bf16[1280,1280]{1,0:T(8,128)(2,1)S(1)}, bf16[1280,1280]{1,0:T(8,128)(2,1)}, u32[]{:S(2)}) copy-start(bf16[1280,1280]{1,0:T(8,128)(2,1)} %refs_8_.1) | copy-start | bytes 9830404
  48.0 6.2 %copy-start.1 = (bf16[1280,33]{0,1:T(8,128)(2,1)S(1)}, bf16[1280,33]{0,1:T(8,128)(2,1)}, u32[]{:S(2)}) copy-start(bf16[1280,33]{0,1:T(8,128)(2,1)} %param.20) | copy-start | bytes 253444
  48.0 6.2 %copy-start.2 = (f32[33]{0:T(128)S(1)}, f32[33]{0:T(128)}, u32[]{:S(2)}) copy-start(f32[33]{0:T(128)} %param.21) | copy-start | bytes 400
  49.0 5.2 %collective-permute-start.17 = (f32[128,1280]{1,0:T(8,128)S(1)}, f32[128,1280]{1,0:T(8,128)S(1)}, u32[]{:S(2)}, u32[]{:S(2)}) collective-permute-start(f32[128,1280]{1,0:T(8,128)S(1)} %shard_map.145.refs_2_), channel_id=1, source_target_pairs={{0,16},{16,0},{1,17},{17,1},{2,18},{18,2},{3,19},{19,3},{4,20},{20... | collective-permute-start | bytes 1966088 | tf_op jit(solution)/shard_map/ppermute | solution.py:298

commit v5 on v4

--- a/solution.py
+++ b/solution.py
@@ -18,9 +18,14 @@
     angles = (np.arange(seq_span, dtype=np.float32)[:, None] * frequency[None, :]).astype(np.float32)
     cosine = np.cos(angles.astype(np.float64)).astype(np.float32)
     sine = np.sin(angles.astype(np.float64)).astype(np.float32)
-    cos_table = np.concatenate([cosine] * 4, axis=1)
-    sin_table = np.concatenate([-sine, sine] * 2, axis=1)
-    return np.concatenate([cos_table, sin_table], axis=1)
+    wide = np.concatenate([cosine] * 4 + [-sine, sine] * 2, axis=1)
+    rest = np.concatenate([cosine, sine], axis=1)
+    parts = []
+    for _ in range(3):
+        parts.append(rest.astype(BF16))
+        rest = rest - parts[-1].astype(np.float32)
+    parts.append(np.zeros_like(parts[0]))
+    return wide, np.concatenate(parts, axis=1)
 
 
 def nt_dot(a, b):
@@ -91,41 +96,61 @@
     return jnp.sum(picked, axis=0, keepdims=True)
 
 
-def prepare_kernel(mine, *refs):
-    n = 8 if mine else 7
-    sources, refs = refs[:n], refs[n:]
-    if not mine:
-        states_ref, refs = refs[0], refs[1:]
-    normed_ref, picked_ref, rows_ref, qtable_ref, meta_ref = refs[:5]
-    refs = refs[5:]
-    if mine:
-        table_ref, refs = refs[0], refs[1:]
-    scratch, sems = refs[:-1], refs[-1]
-    if mine:
-        targets = (*scratch[:6], table_ref, scratch[6])
-        states_ref = scratch[6]
-    else:
-        targets = scratch
-        table_ref = scratch[6]
+def norm_rows(values, gain):
+    average = jnp.mean(values, axis=1, keepdims=True)
+    centred = values - average
+    variance = jnp.mean(centred * centred, axis=1, keepdims=True)
+    return (centred * lax.rsqrt(variance + epsilon) * gain).astype(BF16)
+
+
+def prepare_kernel(mine, small_refs, pick_ref, states_from, table_from, out_refs, scratch, sems):
+    normed_ref, picked_ref, rows_ref, qtable_ref, meta_ref = out_refs[:5]
     copies = [
         pltpu.make_async_copy(source, target, sems.at[i])
-        for i, (source, target) in enumerate(zip(sources, targets))
+        for i, (source, target) in enumerate(zip((*small_refs, pick_ref), scratch))
     ]
-    for copy in copies:
+    late = []
+    if mine:
+        states_ref = scratch[7]
+        late = [
+            pltpu.make_async_copy(states_from, states_ref, sems.at[7]),
+            pltpu.make_async_copy(table_from, out_refs[5], sems.at[8]),
+        ]
+    else:
+        states_ref = states_from
+    for copy in (*copies, *late):
         copy.start()
-    for copy in copies:
-        copy.wait()
-    sequence_ref, length_ref, owner_ref, codes_ref, tokens_ref, gain_ref = targets[:6]
-    span = states_ref.shape[0]
+    sequence_ref, length_ref, owner_ref, codes_ref, tokens_ref, gain_ref, pick_ref = scratch[:7]
+    span, feature = normed_ref.shape
     masks = codes_ref.shape[0]
     core = lax.axis_index("core")
     core = core if mine else 1 - core
-    copy = ((lax.axis_index("z") * 2 + core) * 4 + lax.axis_index("y")) * 4 + lax.axis_index("x")
+    copy_id = (
+        (lax.axis_index("z") * 2 + core) * 4 + lax.axis_index("y")
+    ) * 4 + lax.axis_index("x")
+    copies[5].wait()
+    block = 16
+
+    def norm_all():
+        gain = gain_ref[...].reshape(1, -1)
+
+        def step(i, carry):
+            at = pl.multiple_of(i * block, block)
+            values = states_ref[pl.ds(at, block), :].astype(F32)
+            normed_ref[pl.ds(at, block), :] = norm_rows(values, gain)
+            return carry
+
+        lax.fori_loop(0, span // block, step, 0, unroll=20)
+
+    if not mine:
+        norm_all()
+    for copy in (*copies[:5], copies[6]):
+        copy.wait()
 
     def numbers(count):
         return lax.broadcasted_iota(jnp.int32, (1, count), 1)
 
-    own = numbers(codes_ref.shape[1]) == copy
+    own = numbers(codes_ref.shape[1]) == copy_id
     sequence = first(own, sequence_ref[...].reshape(1, -1))
     owner = first(own, owner_ref[...].reshape(1, -1))
     length = first(numbers(length_ref.shape[0]) == sequence, length_ref[...].reshape(1, -1))
@@ -140,47 +165,42 @@
     targets = jnp.sum(jnp.where(hit, tokens, 0), axis=1, keepdims=True)
     lane = lax.broadcasted_iota(jnp.int32, meta_ref.shape, 1)
     meta_ref[...] = jnp.where(lane == 0, targets, jnp.where(lane == 1, length, owner))
-    hot = hit.astype(F32)
-    qtable_ref[...] = nn_dot(hot, table_ref[...], precision=lax.Precision.HIGHEST)
-    hot = hot.astype(BF16)
-    gain = gain_ref[...].reshape(1, -1)
-    block = 128
-
-    def step(i, carry):
-        at = pl.multiple_of(i * block, block)
-        values = states_ref[pl.ds(at, block), :].astype(F32)
-        average = jnp.mean(values, axis=1, keepdims=True)
-        centred = values - average
-        variance = jnp.mean(centred * centred, axis=1, keepdims=True)
-        normed_ref[pl.ds(at, block), :] = (
-            centred * lax.rsqrt(variance + epsilon) * gain
-        ).astype(BF16)
-        return carry
-
-    lax.fori_loop(0, span // block, step, 0)
-    rows_ref[...] = nn_dot(hot, states_ref[...])
-    picked_ref[...] = nn_dot(hot, normed_ref[...]).astype(BF16)
-
-
-def keys_kernel(
-    table_ref, normed_refs, picked_refs, qtable_refs, meta_refs, block_refs, probs_ref
-):
-    size = block_refs[0].shape[0] // 2
+    hot = hit.astype(F32).astype(BF16)
+    picks = nn_dot(hot, pick_ref[...])
+    wide = picks.shape[1] // 4
+    picks = picks[:, :wide] + picks[:, wide : 2 * wide] + picks[:, 2 * wide : 3 * wide]
+    cosine, sine = picks[:, : wide // 2], picks[:, wide // 2 :]
+    qtable_ref[...] = jnp.concatenate([cosine] * 4 + [-sine, sine] * 2, axis=1)
+    for copy in late:
+        copy.wait()
+    if mine:
+        norm_all()
+    rows = nn_dot(hot, states_ref[...])
+    rows_ref[...] = rows
+    picked_ref[...] = norm_rows(rows, gain_ref[...].reshape(1, -1))
+
+
+def attend(table_ref, normed_refs, picked_refs, qtable_refs, meta_refs, key_refs, value_refs):
+    size = key_refs[0].shape[0] // 2
     masks = picked_refs[0].shape[0]
-    heads = len(block_refs)
-    key_weight = jnp.concatenate([r[size:, :] for r in block_refs], axis=0)
-    query_weight = jnp.concatenate([r[:size, :] for r in block_refs], axis=0)
+    heads = len(key_refs)
+    width = heads * size
+    weight = jnp.concatenate(
+        [r[size:, :] for r in key_refs] + [r[:size, :] for r in value_refs], axis=0
+    )
+    query_weight = jnp.concatenate([r[:size, :] for r in key_refs], axis=0)
+    picked = jnp.concatenate([r[...] for r in picked_refs], axis=0)
+    queries = nt_dot(picked, query_weight) * 0.125
+    results = []
     for which in range(2):
         length = meta_refs[which][0:1, 1:2]
-        keys = nt_dot(normed_refs[which][...], key_weight)
-        queries = nt_dot(picked_refs[which][...], query_weight) * 0.125
+        projected = nt_dot(normed_refs[which][...], weight)
+        own = queries[masks * which : masks * (which + 1), :]
         turned_keys, turned_queries = [], []
         for i in range(heads // 2):
             lanes = slice(128 * i, 128 * (i + 1))
-            turned_keys.append(rotate(keys[:, lanes], table_ref[...], size // 2))
-            turned_queries.append(
-                rotate(queries[:, lanes], qtable_refs[which][...], size // 2)
-            )
+            turned_keys.append(rotate(projected[:, lanes], table_ref[...], size // 2))
+            turned_queries.append(rotate(own[:, lanes], qtable_refs[which][...], size // 2))
         key_rows = jnp.concatenate(turned_keys, axis=1).astype(BF16)
         query_rows = jnp.concatenate(turned_queries, axis=1).astype(BF16)
         spread = jnp.concatenate([query_rows] * heads, axis=0)
@@ -193,42 +213,51 @@
         largest = jnp.max(logits, axis=1, keepdims=True)
         weights = jnp.exp(logits - largest)
         total = jnp.sum(weights, axis=1, keepdims=True)
-        probs_ref[which] = (weights * (1.0 / total)).astype(BF16)
-
-
-def values_kernel(normed_refs, block_refs, values_ref):
-    size = block_refs[0].shape[0] // 2
-    weight = jnp.concatenate([r[:size, :] for r in block_refs], axis=0)
-    for which in range(2):
-        values_ref[which] = nt_dot(normed_refs[which][...], weight).astype(BF16)
-
-
-def mix_kernel(probs_refs, values_refs, block_refs, partial_ref):
+        probs = (weights * (1.0 / total)).astype(BF16)
+        results.append((probs, projected[:, width:].astype(BF16)))
+    return results
+
+
+def attend_kernel(*refs):
+    inputs, (probs_ref, values_ref) = refs[:-2], refs[-2:]
+    for which, (probs, values) in enumerate(attend(*inputs)):
+        probs_ref[which] = probs
+        values_ref[which] = values
+
+
+def mix_kernel(probs_refs, values_refs, block_refs, inputs, partial_ref):
+    last = attend(*inputs)
     right = (lax.axis_index("x") + lax.axis_index("y")) % 2 == lax.axis_index("core")
-    own_probs, near_probs, far_probs = probs_refs
+    own_probs, near_probs = probs_refs
     size = block_refs[0].shape[0] // 2
     masks = own_probs.shape[1] // 2
-    columns = ((0,), (1, 3), (2,))
-
-    def rows_of(core, step, which):
-        ref = (own_probs, near_probs, far_probs, near_probs)[step]
+
+    def rows_of(copy, step, which):
         start = masks * (which + (2 if step == 3 else 0))
-        return ref[core, start : start + masks, :]
+        if step == 2:
+            return last[copy][0][start : start + masks, :]
+        ref = near_probs if step % 2 else own_probs
+        return ref[copy, start : start + masks, :]
 
     contexts = []
-    for core in range(2):
+    for copy in range(2):
         parts = []
-        for values_ref, group in zip(values_refs, columns):
+        groups = (
+            (values_refs[0][copy], (0,)),
+            (values_refs[1][copy], (1, 3)),
+            (last[copy][1], (2,)),
+        )
+        for values, columns in groups:
             stack = []
-            for column in group:
+            for column in columns:
                 which = column // 2
                 for i in range(2):
-                    even = rows_of(core, (0, 2)[i], which)
-                    odd = rows_of(core, (1, 3)[i], which)
+                    even = rows_of(copy, (0, 2)[i], which)
+                    odd = rows_of(copy, (1, 3)[i], which)
                     if column % 2:
                         even, odd = odd, even
                     stack.append(jnp.where(right, even, odd))
-            mixed = nn_dot(jnp.concatenate(stack, axis=0), values_ref[core])
+            mixed = nn_dot(jnp.concatenate(stack, axis=0), values)
             lane = lax.broadcasted_iota(jnp.int32, (masks, mixed.shape[1]), 1) // size
             context = mixed[:masks, :]
             for head in range(1, len(stack)):
@@ -338,10 +367,10 @@
     _, span, feature = hidden_states.shape
     size = output_weight.shape[0]
     masks = mask_code.shape[1]
-    table = jnp.asarray(rotary_tables(span, size))
+    table, pick_table = (jnp.asarray(t) for t in rotary_tables(span, size))
     shape = jax.ShapeDtypeStruct
 
-    def prepare_call(mine, states, table):
+    def prepare_call(mine, states):
         small = [copy_sequence, seq_lengths, copy_owner, mask_code.T, seq_tokens, ln_attn_gain]
         outs = [
             shape((span, feature), BF16),
@@ -350,55 +379,53 @@
             shape((masks, 256), F32),
             shape((masks, 128), jnp.int32),
         ]
-        args = [*small, table, states]
-        scratch = [pltpu.VMEM(a.shape, a.dtype) for a in small]
+        args = [*small, pick_table, table, states] if mine else [*small, pick_table, states]
+        scratch = [pltpu.VMEM(a.shape, a.dtype) for a in (*small, pick_table)]
         if mine:
             outs.append(shape(table.shape, F32))
             scratch.append(pltpu.VMEM(states.shape, states.dtype))
-        else:
-            scratch.append(pltpu.VMEM(table.shape, table.dtype))
+        n, m = len(args), len(outs)
 
         def kernel(*refs):
-            prepare_kernel(mine, *refs)
+            prepare_kernel(
+                mine, refs[:6], refs[6], refs[n - 1], refs[7], refs[n : n + m], refs[n + m : -1],
+                refs[-1],
+            )
 
         return call(
             kernel,
             outs,
             args,
-            n_any=8 if mine else 7,
-            scratch=[*scratch, pltpu.SemaphoreType.DMA((8,))],
+            n_any=9 if mine else 7,
+            scratch=[*scratch, pltpu.SemaphoreType.DMA((9,))],
             flops=4 * masks * span * feature + 10 * span * feature,
         )
 
-    def keys_call(ready, blocks):
-        heads = len(blocks)
+    def attend_args(ready, key_blocks, value_blocks):
+        per_copy = [r[i] for i in (0, 1, 3, 4) for r in ready]
+        return (ready[0][5], *per_copy, *key_blocks, *value_blocks)
+
+    def attend_refs(refs, heads):
+        return (
+            refs[0], refs[1:3], refs[3:5], refs[5:7], refs[7:9], refs[9 : 9 + heads],
+            refs[9 + heads : 9 + 2 * heads],
+        )
+
+    def attend_call(ready, key_blocks, value_blocks):
+        heads = len(key_blocks)
 
         def kernel(*refs):
-            keys_kernel(
-                refs[0], refs[1:3], refs[3:5], refs[5:7], refs[7:9], refs[9 : 9 + heads],
-                refs[9 + heads],
-            )
-
-        per_copy = [r[i] for i in (0, 1, 3, 4) for r in ready]
+            attend_kernel(*attend_refs(refs, heads), *refs[-2:])
+
         return call(
             kernel,
-            shape((2, heads * masks, span), BF16),
-            (ready[0][5], *per_copy, *blocks),
-            flops=4 * span * feature * 256,
+            [
+                shape((2, heads * masks, span), BF16),
+                shape((2, span, heads * size), BF16),
+            ],
+            attend_args(ready, key_blocks, value_blocks),
+            flops=4 * span * feature * heads * 128,
             exps=2 * heads * masks * span,
-        )
-
-    def values_call(ready, blocks):
-        heads = len(blocks)
-
-        def kernel(*refs):
-            values_kernel(refs[:2], refs[2 : 2 + heads], refs[2 + heads])
-
-        return call(
-            kernel,
-            shape((2, span, heads * size), BF16),
-            (*(r[0] for r in ready), *blocks),
-            flops=4 * span * feature * 256,
         )
 
     states = hidden_states[0]
@@ -406,19 +433,18 @@
     key_low, key_high = gather_line(key_block, "x")
     value_low, value_high = gather_line(value_block, "y")
     states_other = swap(states)
-    mine = prepare_call(True, states, table)
+    mine = prepare_call(True, states)
     key_ahead_low = pull(after(key_low, mine[0]), "y", 1)
     key_behind_high = pull(after(key_high, mine[0]), "y", 3)
     value_ahead_low = pull(after(value_low, mine[0]), "x", 1)
     value_behind_high = pull(after(value_high, mine[0]), "x", 3)
-    other = prepare_call(False, after(states_other, mine[0]), table)
+    other = prepare_call(False, after(states_other, mine[0]))
     ready = (mine, other)
     key_ahead_high = pull(after(key_high, key_ahead_low, other[0]), "y", 1)
     key_behind_low = pull(after(key_low, key_behind_high, other[0]), "y", 3)
     value_ahead_high = pull(after(value_high, value_ahead_low, other[0]), "x", 1)
     value_behind_low = pull(after(value_low, value_behind_high, other[0]), "x", 3)
-    own_probs = keys_call(ready, (key_low, key_high))
-    own_values = values_call(ready, (value_low, value_high))
+    own_probs, own_values = attend_call(ready, (key_low, key_high), (value_low, value_high))
     key_far = (
         pull(after(key_ahead_low, key_ahead_high, own_probs, own_values), "y", 1),
         pull(after(key_behind_high, key_behind_low, own_probs, own_values), "y", 3),
@@ -429,23 +455,24 @@
     )
     key_near = (key_ahead_low, key_ahead_high, key_behind_low, key_behind_high)
     value_near = (value_ahead_low, value_ahead_high, value_behind_low, value_behind_high)
-    near_probs = keys_call(ready, key_near)
-    near_values = values_call(ready, value_near)
-    key_far = tuple(after(b, near_probs, near_values) for b in key_far)
-    far_probs = keys_call(ready, key_far)
-    far_values = values_call(ready, value_far)
-    probs = (own_probs, near_probs, far_probs)
-    values = (own_values, near_values, far_values)
-    value_blocks = (value_low, value_high, *value_near, *value_far)
+    near_probs, near_values = attend_call(ready, key_near, value_near)
+    key_far = tuple(after(b, near_probs) for b in key_far)
+    value_blocks = (value_low, value_high, *value_near)
 
     def mix(*refs):
-        mix_kernel(refs[:3], refs[3:6], refs[6:14], refs[14])
+        mix_kernel(
+            refs[0:2], refs[2:4], (*refs[4:10], *refs[-3:-1]), attend_refs(refs[10:], 2), refs[-1]
+        )
 
     partial = call(
         mix,
         shape((2 * masks, feature), F32),
-        (*probs, *values, *value_blocks),
-        flops=4 * masks * feature * 8 * size,
+        (
+            own_probs, near_probs, own_values, near_values, *value_blocks,
+            *attend_args(ready, key_far, value_far),
+        ),
+        flops=4 * span * feature * 256 + 4 * masks * feature * 8 * size,
+        exps=4 * masks * span,
     )
 
     def score(*refs):

time: 80.9 us -> 82.5 us (1.020)
  Pallas kernels: 24.1 us -> 17.9 us
  waiting for transfers between devices: 3.76 us -> 9.53 us
  starting transfers between devices: 27.9 us -> 30.2 us
    pallas_call x11 -> x7, Pallas kernels: 24.1 us -> 17.9 us  [call(): pl.pallas_call(kernel, out_shape=outs, in_specs=[IN_PLACE] * n_any + [ON_...]
    ppermute x12, waiting for transfers between devices: 2.03 us -> 7.44 us  [pull(): lax.ppermute(array, axis, [((i + offset) % size, i) for i in range(size)])]
    ppermute x12, starting transfers between devices: 16.2 us -> 19.4 us  [pull(): lax.ppermute(array, axis, [((i + offset) % size, i) for i in range(size)])]
    ppermute x2, starting transfers between devices: 6.72 us -> 5.84 us  [swap(): return lax.ppermute(array, 'core', [(0, 1), (1, 0)])]
  transfers between devices with their start and end apart: 18 -> 18, of which waited for: 3 -> 7; matrix products, arithmetic and copies ran while one was open for 0% -> 0% of each run, Pallas kernels for 25% -> 16%
where the time goes in v5:
time: 82.5 us; the launch traced here: 82.3 us
  starting transfers between devices  30.2 us (37%)
  blocking collectives  23.6 us (29%)
  Pallas kernels  17.9 us (22%)
  waiting for transfers between devices  9.53 us (12%)
    all_to_all x1, blocking collectives, on_device(): arrived = lax.all_to_all(placed, ('z', 'y', 'x'), 0, 0, tiled=True)  23.6 us
    ppermute x12, starting transfers between devices, pull(): lax.ppermute(array, axis, [((i + offset) % size, i) for i in range(size)])  19.4 us
    pallas_call x7, Pallas kernels, call(): pl.pallas_call(kernel, out_shape=outs, in_specs=[IN_PLACE] * n_any + [ON_...  17.9 us
    ppermute x12, waiting for transfers between devices, pull(): lax.ppermute(array, axis, [((i + offset) % size, i) for i in range(size)])  7.44 us
    ppermute x2, starting transfers between devices, swap(): return lax.ppermute(array, 'core', [(0, 1), (1, 0)])  5.84 us
    ppermute x4, starting transfers between devices, gather_line(): return (lax.ppermute(block, axes, near), lax.ppermute(block, axes, far))  4.99 us
    ppermute x2, waiting for transfers between devices, swap(): return lax.ppermute(array, 'core', [(0, 1), (1, 0)])  1.72 us
  transfers between devices with their start and end apart: 18, of which 7 were waited for; matrix products, arithmetic and copies ran while one was open for 0% of the time, Pallas kernels for 16%

profile of v5, /device:TPU:1, one launch (start us, length us, event | category | flops | bytes accessed | tf_op | source)
XLA Modules:
  0.0 82.3 jit_solution(11936677311097778042)
XLA Ops:
  0.0 3.2 %collective-permute-start = (bf16[640,1280]{1,0:T(8,128)(2,1)}, bf16[640,1280]{1,0:T(8,128)(2,1)S(1)}, u32[]{:S(2)}, u32[]{:S(2)}) collective-permute-start(bf16[640,1280]{1,0:T(8,128)(2,1)} %bitcast.14), channel_id=1, source_target_pairs={{0,16},{16,0},{1,17},{17,1},{2,18},{18,2},{3,19},{19,3},{4,20},{20... | collective-permute-start | bytes 4915208 | tf_op jit(solution)/shard_map/ppermute | solution.py:327
  3.2 1.1 %shard_map.147 = (bf16[128,1280]{1,0:T(8,128)(2,1)S(1)}, bf16[128,1280]{1,0:T(8,128)(2,1)S(1)}) custom-call(bf16[192,1280]{1,0:T(8,128)(2,1)} %bitcast.16, bf16[64,1280]{1,0:T(8,128)(2,1)} %bitcast.19), custom_call_target="tpu_custom_call" | custom-call | bytes 1310720 | tf_op jit(solution)/shard_map/pallas_call | solution.py:59
  4.4 0.1 collective-permute-start.1
  4.5 1.4 %collective-permute-start.2 = (bf16[128,1280]{1,0:T(8,128)(2,1)S(1)}, bf16[128,1280]{1,0:T(8,128)(2,1)S(1)}, u32[]{:S(2)}, u32[]{:S(2)}) collective-permute-start(bf16[128,1280]{1,0:T(8,128)(2,1)S(1)} %get-tuple-element.49), channel_id=1, source_target_pairs={{0,1},{1,19},{2,3},{3,17},{4,22},{5,6},{6,20},{7,4},{8,9},{9,27},{... | collective-permute-start | bytes 983048 | tf_op jit(solution)/shard_map/ppermute | solution.py:349
  5.9 0.0 collective-permute-start.3
  5.9 3.5 %collective-permute-start.4 = (bf16[128,1280]{1,0:T(8,128)(2,1)S(1)}, bf16[128,1280]{1,0:T(8,128)(2,1)S(1)}, u32[]{:S(2)}, u32[]{:S(2)}) collective-permute-start(bf16[128,1280]{1,0:T(8,128)(2,1)S(1)} %get-tuple-element.50), channel_id=1, source_target_pairs={{0,4},{1,25},{2,6},{3,27},{4,28},{5,9},{6,30},{7,11},{8,12},{9,17}... | collective-permute-start | bytes 983048 | tf_op jit(solution)/shard_map/ppermute | solution.py:349
  9.4 3.5 %shard_map.145 = (bf16[640,1280]{1,0:T(8,128)(2,1)S(1)}, bf16[64,1280]{1,0:T(8,128)(2,1)S(1)}, f32[64,1280]{1,0:T(8,128)S(1)}, f32[64,256]{1,0:T(8,128)S(1)}, s3...) custom-call(s32[256]{0:T(256)} %refs_0_.3, s32[24]{0:T(128)} %refs_1_.3, s32[256]{0:T(256)} %refs_2_.3, s32[64,256]{1,0:T(8,128)} %bitcast.17, ...), custom_call_target="tpu_custom_call" | custom-call | flops 217907200 | bytes 5639264 | tf_op jit(solution)/shard_map/pallas_call | solution.py:59
  12.8 0.4 collective-permute-done.1.refs_9_
  13.2 2.3 %collective-permute-start.5 = (bf16[128,1280]{1,0:T(8,128)(2,1)S(1)}, bf16[128,1280]{1,0:T(8,128)(2,1)S(1)}, u32[]{:S(2)}, u32[]{:S(2)}) collective-permute-start(bf16[128,1280]{1,0:T(8,128)(2,1)S(1)} %collective-permute-done.1.refs_9_), channel_id=1, source_target_pairs={{4,0},{8,4},{12,8},{0,12},{5,1},{9,5},{13,9},{1,13},{6,2},{10,6},{... | collective-permute-start | bytes 983048 | tf_op jit(solution)/shard_map/ppermute | solution.py:323
  15.5 0.0 collective-permute-done.2.refs_10_
  15.5 0.3 collective-permute-start.7
  15.7 0.0 collective-permute-done.3.refs_11_.refs_4_
  15.8 3.2 %collective-permute-start.9 = (bf16[128,1280]{1,0:T(8,128)(2,1)S(1)}, bf16[128,1280]{1,0:T(8,128)(2,1)S(1)}, u32[]{:S(2)}, u32[]{:S(2)}) collective-permute-start(bf16[128,1280]{1,0:T(8,128)(2,1)S(1)} %collective-permute-done.3.refs_11_.refs_4_), channel_id=1, source_target_pairs={{1,0},{2,1},{3,2},{0,3},{5,4},{6,5},{7,6},{4,7},{9,8},{10,9},{11,1... | collective-permute-start | bytes 983048 | tf_op jit(solution)/shard_map/ppermute | solution.py:323
  19.0 0.0 collective-permute-done.4.refs_12_.refs_5_
  19.0 0.0 collective-permute-start.11
  19.0 0.0 collective-permute-done.refs_7_
  19.0 2.8 %shard_map.146 = (bf16[640,1280]{1,0:T(8,128)(2,1)S(1)}, bf16[64,1280]{1,0:T(8,128)(2,1)S(1)}, f32[64,1280]{1,0:T(8,128)S(1)}, f32[64,256]{1,0:T(8,128)S(1)}, s32[64,128]{1,0:T(8,128)S(1)}) custom-call(s32[256]{0:T(256)} %refs_0_.3, s32[24]{0:T(128)} %refs_1_.3, s32[256]{0:T(256)} %refs_2_.3, s32[64,256]{1,0:T(8,128)} %bitcast.18, s32[24,640]{1,0:T(8,128)} %refs_4_.3, ...), custom_call_target="tpu_custom_call" | custom-call | flops 217907200 | bytes 4328544 | tf_op jit(solution)/shard_map/pallas_call | solution.py:59
  21.8 1.3 %collective-permute-done.5.refs_9_ = bf16[128,1280]{1,0:T(8,128)(2,1)S(1)} collective-permute-done((bf16[128,1280]{1,0:T(8,128)(2,1)S(1)}, bf16[128,1280]{1,0:T(8,128)(2,1)S(1)}, u32[]{:S(2)}, u32[]{:S(2)}) %collective-permute-start.5) | collective-permute-done | bytes 327712 | tf_op jit(solution)/shard_map/ppermute | solution.py:323
  23.1 3.4 %collective-permute-start.6 = (bf16[128,1280]{1,0:T(8,128)(2,1)S(1)}, bf16[128,1280]{1,0:T(8,128)(2,1)S(1)}, u32[]{:S(2)}, u32[]{:S(2)}) collective-permute-start(bf16[128,1280]{1,0:T(8,128)(2,1)S(1)} %collective-permute-done.2.refs_10_), channel_id=1, source_target_pairs={{4,0},{8,4},{12,8},{0,12},{5,1},{9,5},{13,9},{1,13},{6,2},{10,6},{... | collective-permute-start | bytes 983048 | tf_op jit(solution)/shard_map/ppermute | solution.py:323
  26.5 0.0 collective-permute-done.7.refs_12_
  26.5 0.0 collective-permute-start.8
  26.5 0.0 collective-permute-done.9.refs_13_.refs_6_
  26.5 3.0 %collective-permute-start.10 = (bf16[128,1280]{1,0:T(8,128)(2,1)S(1)}, bf16[128,1280]{1,0:T(8,128)(2,1)S(1)}, u32[]{:S(2)}, u32[]{:S(2)}) collective-permute-start(bf16[128,1280]{1,0:T(8,128)(2,1)S(1)} %collective-permute-done.4.refs_12_.refs_5_), channel_id=1, source_target_pairs={{1,0},{2,1},{3,2},{0,3},{5,4},{6,5},{7,6},{4,7},{9,8},{10,9},{11,1... | collective-permute-start | bytes 983048 | tf_op jit(solution)/shard_map/ppermute | solution.py:323
  29.5 0.0 collective-permute-done.11.refs_16_.refs_9_
  29.5 0.0 collective-permute-start.12
  29.5 2.5 %shard_map.148 = (bf16[2,128,640]{2,1,0:T(8,128)(2,1)S(1)}, bf16[2,640,128]{2,1,0:T(8,128)(2,1)S(1)}) custom-call(f32[640,256]{1,0:T(8,128)S(1)} %get-tuple-element.41.refs_0_.refs_10_, bf16[640,1280]{1,0:T(8,128)(2,1)S(1)} %get-tuple-element.38.refs_1_.refs_11_, bf16[640,1280]{1,0:T(8,128)(2,1)S(1)} %get-tuple-element.42.refs_2_.refs_12_, ...), custom_call_target="tpu_custom_call" | custom-call | flops 838860800 | bytes 6422528 | tf_op jit(solution)/shard_map/pallas_call | solution.py:59
  32.0 0.3 collective-permute-done.6.refs_10_
  32.3 3.4 %collective-permute-start.13 = (bf16[128,1280]{1,0:T(8,128)(2,1)S(1)}, bf16[128,1280]{1,0:T(8,128)(2,1)S(1)}, u32[]{:S(2)}, u32[]{:S(2)}) collective-permute-start(bf16[128,1280]{1,0:T(8,128)(2,1)S(1)} %collective-permute-done.5.refs_9_), channel_id=1, source_target_pairs={{4,0},{8,4},{12,8},{0,12},{5,1},{9,5},{13,9},{1,13},{6,2},{10,6},{... | collective-permute-start | bytes 983048 | tf_op jit(solution)/shard_map/ppermute | solution.py:323
  35.7 0.0 collective-permute-done.8.refs_11_
  35.7 0.0 collective-permute-start.14
  35.7 0.0 collective-permute-done.10.refs_14_.refs_7_
  35.7 3.8 %collective-permute-start.15 = (bf16[128,1280]{1,0:T(8,128)(2,1)S(1)}, bf16[128,1280]{1,0:T(8,128)(2,1)S(1)}, u32[]{:S(2)}, u32[]{:S(2)}) collective-permute-start(bf16[128,1280]{1,0:T(8,128)(2,1)S(1)} %collective-permute-done.9.refs_13_.refs_6_), channel_id=1, source_target_pairs={{1,0},{2,1},{3,2},{0,3},{5,4},{6,5},{7,6},{4,7},{9,8},{10,9},{11,1... | collective-permute-start | bytes 983048 | tf_op jit(solution)/shard_map/ppermute | solution.py:323
  39.5 0.0 collective-permute-done.12.refs_15_.refs_8_
  39.5 0.0 collective-permute-start.16
  39.5 3.0 %shard_map.149 = (bf16[2,256,640]{2,1,0:T(8,128)(2,1)S(1)}, bf16[2,640,256]{2,1,0:T(8,128)(2,1)S(1)}) custom-call(f32[640,256]{1,0:T(8,128)S(1)} %get-tuple-element.41.refs_0_.refs_10_, bf16[640,1280]{1,0:T(8,128)(2,1)S(1)} %get-tuple-element.38.refs_1_.refs_11_, bf16[640,1280]{1,0:T(8,128)(2,1)S(1)} %get-tuple-element.42.refs_2_.refs_12_, ...), custom_call_target="tpu_custom_call" | custom-call | flops 1677721600 | bytes 8388608 | tf_op jit(solution)/shard_map/pallas_call | solution.py:59
  42.5 0.0 collective-permute-done.13.refs_19_
  42.5 1.2 %collective-permute-done.14.refs_20_ = bf16[128,1280]{1,0:T(8,128)(2,1)S(1)} collective-permute-done((bf16[128,1280]{1,0:T(8,128)(2,1)S(1)}, bf16[128,1280]{1,0:T(8,128)(2,1)S(1)}, u32[]{:S(2)}, u32[]{:S(2)}) %collective-permute-start.14) | collective-permute-done | bytes 327712 | tf_op jit(solution)/shard_map/ppermute | solution.py:323
  43.7 1.5 %collective-permute-done.15.refs_21_ = bf16[128,1280]{1,0:T(8,128)(2,1)S(1)} collective-permute-done((bf16[128,1280]{1,0:T(8,128)(2,1)S(1)}, bf16[128,1280]{1,0:T(8,128)(2,1)S(1)}, u32[]{:S(2)}, u32[]{:S(2)}) %collective-permute-start.15) | collective-permute-done | bytes 327712 | tf_op jit(solution)/shard_map/ppermute | solution.py:323
  45.2 3.1 %collective-permute-done.16.refs_22_ = bf16[128,1280]{1,0:T(8,128)(2,1)S(1)} collective-permute-done((bf16[128,1280]{1,0:T(8,128)(2,1)S(1)}, bf16[128,1280]{1,0:T(8,128)(2,1)S(1)}, u32[]{:S(2)}, u32[]{:S(2)}) %collective-permute-start.16) | collective-permute-done | bytes 327712 | tf_op jit(solution)/shard_map/ppermute | solution.py:323
  48.3 0.0 copy-start.3
  48.3 0.0 copy-start
  48.3 0.0 copy-start.1
  48.3 0.0 copy-start.2
  48.3 3.3 %shard_map.150.refs_2_ = f32[128,1280]{1,0:T(8,128)S(1)} custom-call(bf16[2,128,640]{2,1,0:T(8,128)(2,1)S(1)} %get-tuple-element.51.refs_0_, bf16[2,256,640]{2,1,0:T(8,128)(2,1)S(1)} %get-tuple-element.60.refs_1_, bf16[2,640,128]{2,1,0:T(8,128)(2,1)S(1)} %get-tuple-element.61.refs_2_, bf16[2,640,256]{2,1,0:T(8,128)(2,1)S(1)} %get-tuple-element.62.refs_3_, ...), custom_call_target="tpu_custom_call" | custom-call | flops 1006632960 | bytes 10354688 | tf_op jit(solution)/shard_map/pallas_call | solution.py:59
  51.6 2.6 %collective-permute-start.17 = (f32[128,1280]{1,0:T(8,128)S(1)}, f32[128,1280]{1,0:T(8,128)S(1)}, u32[]{:S(2)}, u32[]{:S(2)}) collective-permute-start(f32[128,1280]{1,0:T(8,128)S(1)} %shard_map.150.refs_2_), channel_id=1, source_target_pairs={{0,16},{16,0},{1,17},{17,1},{2,18},{18,2},{3,19},{19,3},{4,20},{20... | collective-permute-start | bytes 1966088 | tf_op jit(solution)/shard_map/ppermute | solution.py:327
  54.2 0.0 copy-done.3
  54.2 1.7 %collective-permute-done.17.refs_3_ = f32[128,1280]{1,0:T(8,128)S(1)} collective-permute-done((f32[128,1280]{1,0:T(8,128)S(1)}, f32[128,1280]{1,0:T(8,128)S(1)}, u32[]{:S(2)}, u32[]{:S(2)}) %collective-permute-start.17) | collective-permute-done | bytes 655392 | tf_op jit(solution)/shard_map/ppermute | solution.py:327
  56.0 0.0 copy-done
  56.0 0.0 copy-done.1
  56.0 0.0 copy-done.2
  56.0 1.8 %shard_map.151 = f32[128,64]{1,0:T(8,128)S(1)} custom-call(f32[64,1280]{1,0:T(8,128)S(1)} %get-tuple-element.37.refs_0_, f32[64,1280]{1,0:T(8,128)S(1)} %get-tuple-element.40.refs_1_, f32[128,1280]{1,0:T(8,128)S(1)} %shard_map.150.refs_2_, f32[128,1280]{1,0:T(8,128)S(1)} %collective-permute-done.17.refs_3_, ...), custom_call_target="tpu_custom_call" | custom-call | flops 419430400 | bytes 5430916 | tf_op jit(solution)/shard_map/pallas_call | solution.py:59
  57.8 23.6 %all_to_all.9 = f32[128,1,64]{2,1,0:T(1,128)S(1)} all-to-all(f32[128,1,64]{2,1,0:T(1,128)S(1)} %bitcast.11), channel_id=1, replica_groups=mesh['z'=8,'core'=2,'y'=4,'x'=4] {'z','y','x'}, dimensions={0} | all-to-all | bytes 65536 | tf_op jit(solution)/shard_map/all_to_all | solution.py:491
  81.4 0.2 reduce_sum.9
  81.5 0.1 reshape.13
  81.6 0.7 copy.19
  (1 shorter events, 0.0 us)
Async XLA Ops:
  0.0 19.0 %collective-permute-start = (bf16[640,1280]{1,0:T(8,128)(2,1)}, bf16[640,1280]{1,0:T(8,128)(2,1)S(1)}, u32[]{:S(2)}, u32[]{:S(2)}) collective-permute-start(bf16[640,1280]{1,0:T(8,128)(2,1)} %bitcast.14), channel_id=1, source_target_pairs={{0,16},{16,0},{1,17},{17,1},{2,18},{18,2},{3,19},{19,3},{4,20},{20... | collective-permute-start | bytes 4915208 | tf_op jit(solution)/shard_map/ppermute | solution.py:327
  4.4 8.8 %collective-permute-start.1 = (bf16[128,1280]{1,0:T(8,128)(2,1)S(1)}, bf16[128,1280]{1,0:T(8,128)(2,1)S(1)}, u32[]{:S(2)}, u32[]{:S(2)}) collective-permute-start(bf16[128,1280]{1,0:T(8,128)(2,1)S(1)} %get-tuple-element.49), channel_id=1, source_target_pairs={{0,3},{1,17},{2,1},{3,19},{4,20},{5,4},{6,22},{7,6},{8,11},{9,25},... | collective-permute-start | bytes 983048 | tf_op jit(solution)/shard_map/ppermute | solution.py:349
  4.5 11.0 %collective-permute-start.2 = (bf16[128,1280]{1,0:T(8,128)(2,1)S(1)}, bf16[128,1280]{1,0:T(8,128)(2,1)S(1)}, u32[]{:S(2)}, u32[]{:S(2)}) collective-permute-start(bf16[128,1280]{1,0:T(8,128)(2,1)S(1)} %get-tuple-element.49), channel_id=1, source_target_pairs={{0,1},{1,19},{2,3},{3,17},{4,22},{5,6},{6,20},{7,4},{8,9},{9,27},{... | collective-permute-start | bytes 983048 | tf_op jit(solution)/shard_map/ppermute | solution.py:349
  5.9 9.9 %collective-permute-start.3 = (bf16[128,1280]{1,0:T(8,128)(2,1)S(1)}, bf16[128,1280]{1,0:T(8,128)(2,1)S(1)}, u32[]{:S(2)}, u32[]{:S(2)}) collective-permute-start(bf16[128,1280]{1,0:T(8,128)(2,1)S(1)} %get-tuple-element.50), channel_id=1, source_target_pairs={{0,12},{1,17},{2,14},{3,19},{4,20},{5,1},{6,22},{7,3},{8,4},{9,25}... | collective-permute-start | bytes 983048 | tf_op jit(solution)/shard_map/ppermute | solution.py:349
  5.9 13.1 %collective-permute-start.4 = (bf16[128,1280]{1,0:T(8,128)(2,1)S(1)}, bf16[128,1280]{1,0:T(8,128)(2,1)S(1)}, u32[]{:S(2)}, u32[]{:S(2)}) collective-permute-start(bf16[128,1280]{1,0:T(8,128)(2,1)S(1)} %get-tuple-element.50), channel_id=1, source_target_pairs={{0,4},{1,25},{2,6},{3,27},{4,28},{5,9},{6,30},{7,11},{8,12},{9,17}... | collective-permute-start | bytes 983048 | tf_op jit(solution)/shard_map/ppermute | solution.py:349
  13.2 9.9 %collective-permute-start.5 = (bf16[128,1280]{1,0:T(8,128)(2,1)S(1)}, bf16[128,1280]{1,0:T(8,128)(2,1)S(1)}, u32[]{:S(2)}, u32[]{:S(2)}) collective-permute-start(bf16[128,1280]{1,0:T(8,128)(2,1)S(1)} %collective-permute-done.1.refs_9_), channel_id=1, source_target_pairs={{4,0},{8,4},{12,8},{0,12},{5,1},{9,5},{13,9},{1,13},{6,2},{10,6},{... | collective-permute-start | bytes 983048 | tf_op jit(solution)/shard_map/ppermute | solution.py:323
  15.5 11.0 %collective-permute-start.7 = (bf16[128,1280]{1,0:T(8,128)(2,1)S(1)}, bf16[128,1280]{1,0:T(8,128)(2,1)S(1)}, u32[]{:S(2)}, u32[]{:S(2)}) collective-permute-start(bf16[128,1280]{1,0:T(8,128)(2,1)S(1)} %collective-permute-done.2.refs_10_), channel_id=1, source_target_pairs={{12,0},{0,4},{4,8},{8,12},{13,1},{1,5},{5,9},{9,13},{14,2},{2,6},{... | collective-permute-start | bytes 983048 | tf_op jit(solution)/shard_map/ppermute | solution.py:323
  15.8 10.7 %collective-permute-start.9 = (bf16[128,1280]{1,0:T(8,128)(2,1)S(1)}, bf16[128,1280]{1,0:T(8,128)(2,1)S(1)}, u32[]{:S(2)}, u32[]{:S(2)}) collective-permute-start(bf16[128,1280]{1,0:T(8,128)(2,1)S(1)} %collective-permute-done.3.refs_11_.refs_4_), channel_id=1, source_target_pairs={{1,0},{2,1},{3,2},{0,3},{5,4},{6,5},{7,6},{4,7},{9,8},{10,9},{11,1... | collective-permute-start | bytes 983048 | tf_op jit(solution)/shard_map/ppermute | solution.py:323
  19.0 10.5 %collective-permute-start.11 = (bf16[128,1280]{1,0:T(8,128)(2,1)S(1)}, bf16[128,1280]{1,0:T(8,128)(2,1)S(1)}, u32[]{:S(2)}, u32[]{:S(2)}) collective-permute-start(bf16[128,1280]{1,0:T(8,128)(2,1)S(1)} %collective-permute-done.4.refs_12_.refs_5_), channel_id=1, source_target_pairs={{3,0},{0,1},{1,2},{2,3},{7,4},{4,5},{5,6},{6,7},{11,8},{8,9},{9,10... | collective-permute-start | bytes 983048 | tf_op jit(solution)/shard_map/ppermute | solution.py:323
  23.1 9.2 %collective-permute-start.6 = (bf16[128,1280]{1,0:T(8,128)(2,1)S(1)}, bf16[128,1280]{1,0:T(8,128)(2,1)S(1)}, u32[]{:S(2)}, u32[]{:S(2)}) collective-permute-start(bf16[128,1280]{1,0:T(8,128)(2,1)S(1)} %collective-permute-done.2.refs_10_), channel_id=1, source_target_pairs={{4,0},{8,4},{12,8},{0,12},{5,1},{9,5},{13,9},{1,13},{6,2},{10,6},{... | collective-permute-start | bytes 983048 | tf_op jit(solution)/shard_map/ppermute | solution.py:323
  26.5 9.2 %collective-permute-start.8 = (bf16[128,1280]{1,0:T(8,128)(2,1)S(1)}, bf16[128,1280]{1,0:T(8,128)(2,1)S(1)}, u32[]{:S(2)}, u32[]{:S(2)}) collective-permute-start(bf16[128,1280]{1,0:T(8,128)(2,1)S(1)} %collective-permute-done.1.refs_9_), channel_id=1, source_target_pairs={{12,0},{0,4},{4,8},{8,12},{13,1},{1,5},{5,9},{9,13},{14,2},{2,6},{... | collective-permute-start | bytes 983048 | tf_op jit(solution)/shard_map/ppermute | solution.py:323
  26.5 9.2 %collective-permute-start.10 = (bf16[128,1280]{1,0:T(8,128)(2,1)S(1)}, bf16[128,1280]{1,0:T(8,128)(2,1)S(1)}, u32[]{:S(2)}, u32[]{:S(2)}) collective-permute-start(bf16[128,1280]{1,0:T(8,128)(2,1)S(1)} %collective-permute-done.4.refs_12_.refs_5_), channel_id=1, source_target_pairs={{1,0},{2,1},{3,2},{0,3},{5,4},{6,5},{7,6},{4,7},{9,8},{10,9},{11,1... | collective-permute-start | bytes 983048 | tf_op jit(solution)/shard_map/ppermute | solution.py:323
  29.5 10.0 %collective-permute-start.12 = (bf16[128,1280]{1,0:T(8,128)(2,1)S(1)}, bf16[128,1280]{1,0:T(8,128)(2,1)S(1)}, u32[]{:S(2)}, u32[]{:S(2)}) collective-permute-start(bf16[128,1280]{1,0:T(8,128)(2,1)S(1)} %collective-permute-done.3.refs_11_.refs_4_), channel_id=1, source_target_pairs={{3,0},{0,1},{1,2},{2,3},{7,4},{4,5},{5,6},{6,7},{11,8},{8,9},{9,10... | collective-permute-start | bytes 983048 | tf_op jit(solution)/shard_map/ppermute | solution.py:323
  32.3 10.2 %collective-permute-start.13 = (bf16[128,1280]{1,0:T(8,128)(2,1)S(1)}, bf16[128,1280]{1,0:T(8,128)(2,1)S(1)}, u32[]{:S(2)}, u32[]{:S(2)}) collective-permute-start(bf16[128,1280]{1,0:T(8,128)(2,1)S(1)} %collective-permute-done.5.refs_9_), channel_id=1, source_target_pairs={{4,0},{8,4},{12,8},{0,12},{5,1},{9,5},{13,9},{1,13},{6,2},{10,6},{... | collective-permute-start | bytes 983048 | tf_op jit(solution)/shard_map/ppermute | solution.py:323
  35.7 8.0 %collective-permute-start.14 = (bf16[128,1280]{1,0:T(8,128)(2,1)S(1)}, bf16[128,1280]{1,0:T(8,128)(2,1)S(1)}, u32[]{:S(2)}, u32[]{:S(2)}) collective-permute-start(bf16[128,1280]{1,0:T(8,128)(2,1)S(1)} %collective-permute-done.7.refs_12_), channel_id=1, source_target_pairs={{12,0},{0,4},{4,8},{8,12},{13,1},{1,5},{5,9},{9,13},{14,2},{2,6},{... | collective-permute-start | bytes 983048 | tf_op jit(solution)/shard_map/ppermute | solution.py:323
  35.7 9.5 %collective-permute-start.15 = (bf16[128,1280]{1,0:T(8,128)(2,1)S(1)}, bf16[128,1280]{1,0:T(8,128)(2,1)S(1)}, u32[]{:S(2)}, u32[]{:S(2)}) collective-permute-start(bf16[128,1280]{1,0:T(8,128)(2,1)S(1)} %collective-permute-done.9.refs_13_.refs_6_), channel_id=1, source_target_pairs={{1,0},{2,1},{3,2},{0,3},{5,4},{6,5},{7,6},{4,7},{9,8},{10,9},{11,1... | collective-permute-start | bytes 983048 | tf_op jit(solution)/shard_map/ppermute | solution.py:323
  39.5 8.8 %collective-permute-start.16 = (bf16[128,1280]{1,0:T(8,128)(2,1)S(1)}, bf16[128,1280]{1,0:T(8,128)(2,1)S(1)}, u32[]{:S(2)}, u32[]{:S(2)}) collective-permute-start(bf16[128,1280]{1,0:T(8,128)(2,1)S(1)} %collective-permute-done.11.refs_16_.refs_9_), channel_id=1, source_target_pairs={{3,0},{0,1},{1,2},{2,3},{7,4},{4,5},{5,6},{6,7},{11,8},{8,9},{9,10... | collective-permute-start | bytes 983048 | tf_op jit(solution)/shard_map/ppermute | solution.py:323
  48.3 5.9 %copy-start.3 = (f32[1280]{0:T(1024)S(1)}, f32[1280]{0:T(1024)}, u32[]{:S(2)}) copy-start(f32[1280]{0:T(1024)} %param.19) | copy-start | bytes 15364
  48.3 7.6 %copy-start = (bf16[1280,1280]{1,0:T(8,128)(2,1)S(1)}, bf16[1280,1280]{1,0:T(8,128)(2,1)}, u32[]{:S(2)}) copy-start(bf16[1280,1280]{1,0:T(8,128)(2,1)} %refs_8_.1) | copy-start | bytes 9830404
  48.3 7.6 %copy-start.1 = (bf16[1280,33]{0,1:T(8,128)(2,1)S(1)}, bf16[1280,33]{0,1:T(8,128)(2,1)}, u32[]{:S(2)}) copy-start(bf16[1280,33]{0,1:T(8,128)(2,1)} %param.21) | copy-start | bytes 253444
  48.3 7.6 %copy-start.2 = (f32[33]{0:T(128)S(1)}, f32[33]{0:T(128)}, u32[]{:S(2)}) copy-start(f32[33]{0:T(128)} %param.22) | copy-start | bytes 400
  51.6 4.3 %collective-permute-start.17 = (f32[128,1280]{1,0:T(8,128)S(1)}, f32[128,1280]{1,0:T(8,128)S(1)}, u32[]{:S(2)}, u32[]{:S(2)}) collective-permute-start(f32[128,1280]{1,0:T(8,128)S(1)} %shard_map.150.refs_2_), channel_id=1, source_target_pairs={{0,16},{16,0},{1,17},{17,1},{2,18},{18,2},{3,19},{19,3},{4,20},{20... | collective-permute-start | bytes 1966088 | tf_op jit(solution)/shard_map/ppermute | solution.py:327

commit v6 on v5

--- a/solution.py
+++ b/solution.py
@@ -433,30 +433,33 @@
     key_low, key_high = gather_line(key_block, "x")
     value_low, value_high = gather_line(value_block, "y")
     states_other = swap(states)
-    mine = prepare_call(True, states)
-    key_ahead_low = pull(after(key_low, mine[0]), "y", 1)
-    key_behind_high = pull(after(key_high, mine[0]), "y", 3)
-    value_ahead_low = pull(after(value_low, mine[0]), "x", 1)
-    value_behind_high = pull(after(value_high, mine[0]), "x", 3)
-    other = prepare_call(False, after(states_other, mine[0]))
+    key_ahead_low = pull(key_low, "y", 1)
+    key_behind_high = pull(key_high, "y", 3)
+    value_ahead_low = pull(value_low, "x", 1)
+    value_behind_high = pull(value_high, "x", 3)
+    mine = prepare_call(True, after(states, key_low, key_high, value_low, value_high))
+    key_ahead_high = pull(after(key_high, key_ahead_low, mine[0]), "y", 1)
+    key_behind_low = pull(after(key_low, key_behind_high, mine[0]), "y", 3)
+    value_ahead_high = pull(after(value_high, value_ahead_low, mine[0]), "x", 1)
+    value_behind_low = pull(after(value_low, value_behind_high, mine[0]), "x", 3)
+    first_round = (key_ahead_low, key_behind_high, value_ahead_low, value_behind_high)
+    other = prepare_call(False, after(states_other, mine[0], *first_round))
     ready = (mine, other)
-    key_ahead_high = pull(after(key_high, key_ahead_low, other[0]), "y", 1)
-    key_behind_low = pull(after(key_low, key_behind_high, other[0]), "y", 3)
-    value_ahead_high = pull(after(value_high, value_ahead_low, other[0]), "x", 1)
-    value_behind_low = pull(after(value_low, value_behind_high, other[0]), "x", 3)
-    own_probs, own_values = attend_call(ready, (key_low, key_high), (value_low, value_high))
     key_far = (
-        pull(after(key_ahead_low, key_ahead_high, own_probs, own_values), "y", 1),
-        pull(after(key_behind_high, key_behind_low, own_probs, own_values), "y", 3),
+        pull(after(key_ahead_low, key_ahead_high, other[0]), "y", 1),
+        pull(after(key_behind_high, key_behind_low, other[0]), "y", 3),
     )
     value_far = (
-        pull(after(value_ahead_low, value_ahead_high, own_probs, own_values), "x", 1),
-        pull(after(value_behind_high, value_behind_low, own_probs, own_values), "x", 3),
-    )
+        pull(after(value_ahead_low, value_ahead_high, other[0]), "x", 1),
+        pull(after(value_behind_high, value_behind_low, other[0]), "x", 3),
+    )
+    second_round = (key_ahead_high, key_behind_low, value_ahead_high, value_behind_low)
+    own_key = after(key_low, *second_round)
+    own_probs, own_values = attend_call(ready, (own_key, key_high), (value_low, value_high))
     key_near = (key_ahead_low, key_ahead_high, key_behind_low, key_behind_high)
     value_near = (value_ahead_low, value_ahead_high, value_behind_low, value_behind_high)
     near_probs, near_values = attend_call(ready, key_near, value_near)
-    key_far = tuple(after(b, near_probs) for b in key_far)
+    key_far = tuple(after(b, own_probs, near_probs) for b in key_far)
     value_blocks = (value_low, value_high, *value_near)
 
     def mix(*refs):

time: 82.5 us -> 82.5 us (level)
    ppermute x12, waiting for transfers between devices: 7.44 us -> 3.52 us  [pull(): lax.ppermute(array, axis, [((i + offset) % size, i) for i in range(size)])]
    ppermute x4, waiting for transfers between devices: 0.38 us -> 3.85 us  [gather_line(): return (lax.ppermute(block, axes, near), lax.ppermute(block, axes, far))]
  transfers between devices with their start and end apart: 18 -> 18, of which waited for: 7 -> 4; matrix products, arithmetic and copies ran while one was open for 0% -> 0% of each run, Pallas kernels for 16% -> 16%
where the time goes in v6:
time: 82.5 us; the launch traced here: 82.3 us
  starting transfers between devices  30.2 us (37%)
  blocking collectives  24.1 us (29%)
  Pallas kernels  17.9 us (22%)
  waiting for transfers between devices  9.09 us (11%)
    all_to_all x1, blocking collectives, on_device(): arrived = lax.all_to_all(placed, ('z', 'y', 'x'), 0, 0, tiled=True)  24.1 us
    ppermute x12, starting transfers between devices, pull(): lax.ppermute(array, axis, [((i + offset) % size, i) for i in range(size)])  18.9 us
    pallas_call x7, Pallas kernels, call(): pl.pallas_call(kernel, out_shape=outs, in_specs=[IN_PLACE] * n_any + [ON_...  17.9 us
    ppermute x2, starting transfers between devices, swap(): return lax.ppermute(array, 'core', [(0, 1), (1, 0)])  6.28 us
    ppermute x4, starting transfers between devices, gather_line(): return (lax.ppermute(block, axes, near), lax.ppermute(block, axes, far))  4.99 us
    ppermute x4, waiting for transfers between devices, gather_line(): return (lax.ppermute(block, axes, near), lax.ppermute(block, axes, far))  3.85 us
    ppermute x12, waiting for transfers between devices, pull(): lax.ppermute(array, axis, [((i + offset) % size, i) for i in range(size)])  3.52 us
    ppermute x2, waiting for transfers between devices, swap(): return lax.ppermute(array, 'core', [(0, 1), (1, 0)])  1.72 us
  transfers between devices with their start and end apart: 18, of which 4 were waited for; matrix products, arithmetic and copies ran while one was open for 0% of the time, Pallas kernels for 16%

profile of v6, /device:TPU:1, one launch (start us, length us, event | category | flops | bytes accessed | tf_op | source)
XLA Modules:
  0.0 82.3 jit_solution(7696712756341523416)
XLA Ops:
  0.0 3.2 %collective-permute-start.4 = (bf16[640,1280]{1,0:T(8,128)(2,1)}, bf16[640,1280]{1,0:T(8,128)(2,1)S(1)}, u32[]{:S(2)}, u32[]{:S(2)}) collective-permute-start(bf16[640,1280]{1,0:T(8,128)(2,1)} %bitcast.14), channel_id=1, source_target_pairs={{0,16},{16,0},{1,17},{17,1},{2,18},{18,2},{3,19},{19,3},{4,20},{20... | collective-permute-start | bytes 4915208 | tf_op jit(solution)/shard_map/ppermute | solution.py:327
  3.2 1.1 %shard_map.145 = (bf16[128,1280]{1,0:T(8,128)(2,1)S(1)}, bf16[128,1280]{1,0:T(8,128)(2,1)S(1)}) custom-call(bf16[192,1280]{1,0:T(8,128)(2,1)} %bitcast.16, bf16[64,1280]{1,0:T(8,128)(2,1)} %bitcast.19), custom_call_target="tpu_custom_call" | custom-call | bytes 1310720 | tf_op jit(solution)/shard_map/pallas_call | solution.py:59
  4.4 0.1 collective-permute-start
  4.5 1.4 %collective-permute-start.1 = (bf16[128,1280]{1,0:T(8,128)(2,1)S(1)}, bf16[128,1280]{1,0:T(8,128)(2,1)S(1)}, u32[]{:S(2)}, u32[]{:S(2)}) collective-permute-start(bf16[128,1280]{1,0:T(8,128)(2,1)S(1)} %get-tuple-element.35), channel_id=1, source_target_pairs={{0,1},{1,19},{2,3},{3,17},{4,22},{5,6},{6,20},{7,4},{8,9},{9,27},{... | collective-permute-start | bytes 983048 | tf_op jit(solution)/shard_map/ppermute | solution.py:349
  5.9 0.0 collective-permute-start.2
  5.9 3.5 %collective-permute-start.3 = (bf16[128,1280]{1,0:T(8,128)(2,1)S(1)}, bf16[128,1280]{1,0:T(8,128)(2,1)S(1)}, u32[]{:S(2)}, u32[]{:S(2)}) collective-permute-start(bf16[128,1280]{1,0:T(8,128)(2,1)S(1)} %get-tuple-element.36), channel_id=1, source_target_pairs={{0,4},{1,25},{2,6},{3,27},{4,28},{5,9},{6,30},{7,11},{8,12},{9,17}... | collective-permute-start | bytes 983048 | tf_op jit(solution)/shard_map/ppermute | solution.py:349
  9.4 3.8 %collective-permute-done.refs_9_ = bf16[128,1280]{1,0:T(8,128)(2,1)S(1)} collective-permute-done((bf16[128,1280]{1,0:T(8,128)(2,1)S(1)}, bf16[128,1280]{1,0:T(8,128)(2,1)S(1)}, u32[]{:S(2)}, u32[]{:S(2)}) %collective-permute-start) | collective-permute-done | bytes 327712 | tf_op jit(solution)/shard_map/ppermute | solution.py:349
  13.2 2.3 %collective-permute-start.5 = (bf16[128,1280]{1,0:T(8,128)(2,1)S(1)}, bf16[128,1280]{1,0:T(8,128)(2,1)S(1)}, u32[]{:S(2)}, u32[]{:S(2)}) collective-permute-start(bf16[128,1280]{1,0:T(8,128)(2,1)S(1)} %collective-permute-done.refs_9_), channel_id=1, source_target_pairs={{4,0},{8,4},{12,8},{0,12},{5,1},{9,5},{13,9},{1,13},{6,2},{10,6},{... | collective-permute-start | bytes 983048 | tf_op jit(solution)/shard_map/ppermute | solution.py:323
  15.5 0.0 collective-permute-done.1.refs_10_
  15.5 0.3 collective-permute-start.6
  15.7 0.0 collective-permute-done.2.refs_11_.refs_4_
  15.8 3.2 %collective-permute-start.7 = (bf16[128,1280]{1,0:T(8,128)(2,1)S(1)}, bf16[128,1280]{1,0:T(8,128)(2,1)S(1)}, u32[]{:S(2)}, u32[]{:S(2)}) collective-permute-start(bf16[128,1280]{1,0:T(8,128)(2,1)S(1)} %collective-permute-done.2.refs_11_.refs_4_), channel_id=1, source_target_pairs={{1,0},{2,1},{3,2},{0,3},{5,4},{6,5},{7,6},{4,7},{9,8},{10,9},{11,1... | collective-permute-start | bytes 983048 | tf_op jit(solution)/shard_map/ppermute | solution.py:323
  19.0 0.0 collective-permute-done.3.refs_12_.refs_5_
  19.0 0.0 collective-permute-start.8
  19.0 3.5 %shard_map.146 = (bf16[640,1280]{1,0:T(8,128)(2,1)S(1)}, bf16[64,1280]{1,0:T(8,128)(2,1)S(1)}, f32[64,1280]{1,0:T(8,128)S(1)}, f32[64,256]{1,0:T(8,128)S(1)}, s3...) custom-call(s32[256]{0:T(256)} %refs_0_.3, s32[24]{0:T(128)} %refs_1_.3, s32[256]{0:T(256)} %refs_2_.3, s32[64,256]{1,0:T(8,128)} %bitcast.17, ...), custom_call_target="tpu_custom_call" | custom-call | flops 217907200 | bytes 5639264 | tf_op jit(solution)/shard_map/pallas_call | solution.py:59
  22.4 0.6 collective-permute-done.5.refs_9_
  23.1 3.4 %collective-permute-start.9 = (bf16[128,1280]{1,0:T(8,128)(2,1)S(1)}, bf16[128,1280]{1,0:T(8,128)(2,1)S(1)}, u32[]{:S(2)}, u32[]{:S(2)}) collective-permute-start(bf16[128,1280]{1,0:T(8,128)(2,1)S(1)} %collective-permute-done.1.refs_10_), channel_id=1, source_target_pairs={{4,0},{8,4},{12,8},{0,12},{5,1},{9,5},{13,9},{1,13},{6,2},{10,6},{... | collective-permute-start | bytes 983048 | tf_op jit(solution)/shard_map/ppermute | solution.py:323
  26.5 0.0 collective-permute-done.6.refs_12_
  26.5 0.0 collective-permute-start.10
  26.5 0.0 collective-permute-done.7.refs_13_.refs_6_
  26.5 3.0 %collective-permute-start.11 = (bf16[128,1280]{1,0:T(8,128)(2,1)S(1)}, bf16[128,1280]{1,0:T(8,128)(2,1)S(1)}, u32[]{:S(2)}, u32[]{:S(2)}) collective-permute-start(bf16[128,1280]{1,0:T(8,128)(2,1)S(1)} %collective-permute-done.3.refs_12_.refs_5_), channel_id=1, source_target_pairs={{1,0},{2,1},{3,2},{0,3},{5,4},{6,5},{7,6},{4,7},{9,8},{10,9},{11,1... | collective-permute-start | bytes 983048 | tf_op jit(solution)/shard_map/ppermute | solution.py:323
  29.5 0.0 collective-permute-done.8.refs_16_.refs_9_
  29.5 0.0 collective-permute-start.12
  29.5 0.0 collective-permute-done.4.refs_7_
  29.5 2.8 %shard_map.147 = (bf16[640,1280]{1,0:T(8,128)(2,1)S(1)}, bf16[64,1280]{1,0:T(8,128)(2,1)S(1)}, f32[64,1280]{1,0:T(8,128)S(1)}, f32[64,256]{1,0:T(8,128)S(1)}, s32[64,128]{1,0:T(8,128)S(1)}) custom-call(s32[256]{0:T(256)} %refs_0_.3, s32[24]{0:T(128)} %refs_1_.3, s32[256]{0:T(256)} %refs_2_.3, s32[64,256]{1,0:T(8,128)} %bitcast.18, s32[24,640]{1,0:T(8,128)} %refs_4_.3, ...), custom_call_target="tpu_custom_call" | custom-call | flops 217907200 | bytes 4328544 | tf_op jit(solution)/shard_map/pallas_call | solution.py:59
  32.3 0.0 collective-permute-done.9.refs_10_
  32.3 3.4 %collective-permute-start.13 = (bf16[128,1280]{1,0:T(8,128)(2,1)S(1)}, bf16[128,1280]{1,0:T(8,128)(2,1)S(1)}, u32[]{:S(2)}, u32[]{:S(2)}) collective-permute-start(bf16[128,1280]{1,0:T(8,128)(2,1)S(1)} %collective-permute-done.5.refs_9_), channel_id=1, source_target_pairs={{4,0},{8,4},{12,8},{0,12},{5,1},{9,5},{13,9},{1,13},{6,2},{10,6},{... | collective-permute-start | bytes 983048 | tf_op jit(solution)/shard_map/ppermute | solution.py:323
  35.7 0.0 collective-permute-done.10.refs_11_
  35.7 0.0 collective-permute-start.14
  35.7 0.0 collective-permute-done.11.refs_14_.refs_7_
  35.7 3.4 %collective-permute-start.15 = (bf16[128,1280]{1,0:T(8,128)(2,1)S(1)}, bf16[128,1280]{1,0:T(8,128)(2,1)S(1)}, u32[]{:S(2)}, u32[]{:S(2)}) collective-permute-start(bf16[128,1280]{1,0:T(8,128)(2,1)S(1)} %collective-permute-done.7.refs_13_.refs_6_), channel_id=1, source_target_pairs={{1,0},{2,1},{3,2},{0,3},{5,4},{6,5},{7,6},{4,7},{9,8},{10,9},{11,1... | collective-permute-start | bytes 983048 | tf_op jit(solution)/shard_map/ppermute | solution.py:323
  39.1 0.0 collective-permute-done.12.refs_15_.refs_8_
  39.1 0.0 collective-permute-start.16
  39.1 2.5 %shard_map.148 = (bf16[2,128,640]{2,1,0:T(8,128)(2,1)S(1)}, bf16[2,640,128]{2,1,0:T(8,128)(2,1)S(1)}) custom-call(f32[640,256]{1,0:T(8,128)S(1)} %get-tuple-element.42.refs_0_.refs_10_, bf16[640,1280]{1,0:T(8,128)(2,1)S(1)} %get-tuple-element.39.refs_1_.refs_11_, bf16[640,1280]{1,0:T(8,128)(2,1)S(1)} %get-tuple-element.43.refs_2_.refs_12_, ...), custom_call_target="tpu_custom_call" | custom-call | flops 838860800 | bytes 6422528 | tf_op jit(solution)/shard_map/pallas_call | solution.py:59
  41.6 3.0 %shard_map.149 = (bf16[2,256,640]{2,1,0:T(8,128)(2,1)S(1)}, bf16[2,640,256]{2,1,0:T(8,128)(2,1)S(1)}) custom-call(f32[640,256]{1,0:T(8,128)S(1)} %get-tuple-element.42.refs_0_.refs_10_, bf16[640,1280]{1,0:T(8,128)(2,1)S(1)} %get-tuple-element.39.refs_1_.refs_11_, bf16[640,1280]{1,0:T(8,128)(2,1)S(1)} %get-tuple-element.43.refs_2_.refs_12_, ...), custom_call_target="tpu_custom_call" | custom-call | flops 1677721600 | bytes 8388608 | tf_op jit(solution)/shard_map/pallas_call | solution.py:59
  44.6 0.0 collective-permute-done.13.refs_19_
  44.6 0.0 collective-permute-done.14.refs_20_
  44.6 0.0 collective-permute-done.15.refs_21_
  44.6 2.9 %collective-permute-done.16.refs_22_ = bf16[128,1280]{1,0:T(8,128)(2,1)S(1)} collective-permute-done((bf16[128,1280]{1,0:T(8,128)(2,1)S(1)}, bf16[128,1280]{1,0:T(8,128)(2,1)S(1)}, u32[]{:S(2)}, u32[]{:S(2)}) %collective-permute-start.16) | collective-permute-done | bytes 327712 | tf_op jit(solution)/shard_map/ppermute | solution.py:323
  47.5 0.0 copy-start.3
  47.5 0.0 copy-start
  47.5 0.0 copy-start.1
  47.5 0.0 copy-start.2
  47.5 3.3 %shard_map.150.refs_2_ = f32[128,1280]{1,0:T(8,128)S(1)} custom-call(bf16[2,128,640]{2,1,0:T(8,128)(2,1)S(1)} %get-tuple-element.55.refs_0_, bf16[2,256,640]{2,1,0:T(8,128)(2,1)S(1)} %get-tuple-element.56.refs_1_, bf16[2,640,128]{2,1,0:T(8,128)(2,1)S(1)} %get-tuple-element.57.refs_2_, bf16[2,640,256]{2,1,0:T(8,128)(2,1)S(1)} %get-tuple-element.58.refs_3_, ...), custom_call_target="tpu_custom_call" | custom-call | flops 1006632960 | bytes 10354688 | tf_op jit(solution)/shard_map/pallas_call | solution.py:59
  50.8 3.0 %collective-permute-start.17 = (f32[128,1280]{1,0:T(8,128)S(1)}, f32[128,1280]{1,0:T(8,128)S(1)}, u32[]{:S(2)}, u32[]{:S(2)}) collective-permute-start(f32[128,1280]{1,0:T(8,128)S(1)} %shard_map.150.refs_2_), channel_id=1, source_target_pairs={{0,16},{16,0},{1,17},{17,1},{2,18},{18,2},{3,19},{19,3},{4,20},{20... | collective-permute-start | bytes 1966088 | tf_op jit(solution)/shard_map/ppermute | solution.py:327
  53.8 0.0 copy-done.3
  53.8 1.7 %collective-permute-done.17.refs_3_ = f32[128,1280]{1,0:T(8,128)S(1)} collective-permute-done((f32[128,1280]{1,0:T(8,128)S(1)}, f32[128,1280]{1,0:T(8,128)S(1)}, u32[]{:S(2)}, u32[]{:S(2)}) %collective-permute-start.17) | collective-permute-done | bytes 655392 | tf_op jit(solution)/shard_map/ppermute | solution.py:327
  55.5 0.0 copy-done
  55.5 0.0 copy-done.1
  55.5 0.0 copy-done.2
  55.5 1.8 %shard_map.151 = f32[128,64]{1,0:T(8,128)S(1)} custom-call(f32[64,1280]{1,0:T(8,128)S(1)} %get-tuple-element.38.refs_0_, f32[64,1280]{1,0:T(8,128)S(1)} %get-tuple-element.41.refs_1_, f32[128,1280]{1,0:T(8,128)S(1)} %shard_map.150.refs_2_, f32[128,1280]{1,0:T(8,128)S(1)} %collective-permute-done.17.refs_3_, ...), custom_call_target="tpu_custom_call" | custom-call | flops 419430400 | bytes 5430916 | tf_op jit(solution)/shard_map/pallas_call | solution.py:59
  57.3 24.1 %all_to_all.9 = f32[128,1,64]{2,1,0:T(1,128)S(1)} all-to-all(f32[128,1,64]{2,1,0:T(1,128)S(1)} %bitcast.11), channel_id=1, replica_groups=mesh['z'=8,'core'=2,'y'=4,'x'=4] {'z','y','x'}, dimensions={0} | all-to-all | bytes 65536 | tf_op jit(solution)/shard_map/all_to_all | solution.py:494
  81.4 0.2 reduce_sum.9
  81.5 0.1 reshape.13
  81.6 0.7 copy.19
  (1 shorter events, 0.0 us)
Async XLA Ops:
  0.0 29.5 %collective-permute-start.4 = (bf16[640,1280]{1,0:T(8,128)(2,1)}, bf16[640,1280]{1,0:T(8,128)(2,1)S(1)}, u32[]{:S(2)}, u32[]{:S(2)}) collective-permute-start(bf16[640,1280]{1,0:T(8,128)(2,1)} %bitcast.14), channel_id=1, source_target_pairs={{0,16},{16,0},{1,17},{17,1},{2,18},{18,2},{3,19},{19,3},{4,20},{20... | collective-permute-start | bytes 4915208 | tf_op jit(solution)/shard_map/ppermute | solution.py:327
  4.4 8.8 %collective-permute-start = (bf16[128,1280]{1,0:T(8,128)(2,1)S(1)}, bf16[128,1280]{1,0:T(8,128)(2,1)S(1)}, u32[]{:S(2)}, u32[]{:S(2)}) collective-permute-start(bf16[128,1280]{1,0:T(8,128)(2,1)S(1)} %get-tuple-element.35), channel_id=1, source_target_pairs={{0,3},{1,17},{2,1},{3,19},{4,20},{5,4},{6,22},{7,6},{8,11},{9,25},... | collective-permute-start | bytes 983048 | tf_op jit(solution)/shard_map/ppermute | solution.py:349
  4.5 11.0 %collective-permute-start.1 = (bf16[128,1280]{1,0:T(8,128)(2,1)S(1)}, bf16[128,1280]{1,0:T(8,128)(2,1)S(1)}, u32[]{:S(2)}, u32[]{:S(2)}) collective-permute-start(bf16[128,1280]{1,0:T(8,128)(2,1)S(1)} %get-tuple-element.35), channel_id=1, source_target_pairs={{0,1},{1,19},{2,3},{3,17},{4,22},{5,6},{6,20},{7,4},{8,9},{9,27},{... | collective-permute-start | bytes 983048 | tf_op jit(solution)/shard_map/ppermute | solution.py:349
  5.9 9.9 %collective-permute-start.2 = (bf16[128,1280]{1,0:T(8,128)(2,1)S(1)}, bf16[128,1280]{1,0:T(8,128)(2,1)S(1)}, u32[]{:S(2)}, u32[]{:S(2)}) collective-permute-start(bf16[128,1280]{1,0:T(8,128)(2,1)S(1)} %get-tuple-element.36), channel_id=1, source_target_pairs={{0,12},{1,17},{2,14},{3,19},{4,20},{5,1},{6,22},{7,3},{8,4},{9,25}... | collective-permute-start | bytes 983048 | tf_op jit(solution)/shard_map/ppermute | solution.py:349
  5.9 13.1 %collective-permute-start.3 = (bf16[128,1280]{1,0:T(8,128)(2,1)S(1)}, bf16[128,1280]{1,0:T(8,128)(2,1)S(1)}, u32[]{:S(2)}, u32[]{:S(2)}) collective-permute-start(bf16[128,1280]{1,0:T(8,128)(2,1)S(1)} %get-tuple-element.36), channel_id=1, source_target_pairs={{0,4},{1,25},{2,6},{3,27},{4,28},{5,9},{6,30},{7,11},{8,12},{9,17}... | collective-permute-start | bytes 983048 | tf_op jit(solution)/shard_map/ppermute | solution.py:349
  13.2 9.9 %collective-permute-start.5 = (bf16[128,1280]{1,0:T(8,128)(2,1)S(1)}, bf16[128,1280]{1,0:T(8,128)(2,1)S(1)}, u32[]{:S(2)}, u32[]{:S(2)}) collective-permute-start(bf16[128,1280]{1,0:T(8,128)(2,1)S(1)} %collective-permute-done.refs_9_), channel_id=1, source_target_pairs={{4,0},{8,4},{12,8},{0,12},{5,1},{9,5},{13,9},{1,13},{6,2},{10,6},{... | collective-permute-start | bytes 983048 | tf_op jit(solution)/shard_map/ppermute | solution.py:323
  15.5 11.0 %collective-permute-start.6 = (bf16[128,1280]{1,0:T(8,128)(2,1)S(1)}, bf16[128,1280]{1,0:T(8,128)(2,1)S(1)}, u32[]{:S(2)}, u32[]{:S(2)}) collective-permute-start(bf16[128,1280]{1,0:T(8,128)(2,1)S(1)} %collective-permute-done.1.refs_10_), channel_id=1, source_target_pairs={{12,0},{0,4},{4,8},{8,12},{13,1},{1,5},{5,9},{9,13},{14,2},{2,6},{... | collective-permute-start | bytes 983048 | tf_op jit(solution)/shard_map/ppermute | solution.py:323
  15.8 10.7 %collective-permute-start.7 = (bf16[128,1280]{1,0:T(8,128)(2,1)S(1)}, bf16[128,1280]{1,0:T(8,128)(2,1)S(1)}, u32[]{:S(2)}, u32[]{:S(2)}) collective-permute-start(bf16[128,1280]{1,0:T(8,128)(2,1)S(1)} %collective-permute-done.2.refs_11_.refs_4_), channel_id=1, source_target_pairs={{1,0},{2,1},{3,2},{0,3},{5,4},{6,5},{7,6},{4,7},{9,8},{10,9},{11,1... | collective-permute-start | bytes 983048 | tf_op jit(solution)/shard_map/ppermute | solution.py:323
  19.0 10.5 %collective-permute-start.8 = (bf16[128,1280]{1,0:T(8,128)(2,1)S(1)}, bf16[128,1280]{1,0:T(8,128)(2,1)S(1)}, u32[]{:S(2)}, u32[]{:S(2)}) collective-permute-start(bf16[128,1280]{1,0:T(8,128)(2,1)S(1)} %collective-permute-done.3.refs_12_.refs_5_), channel_id=1, source_target_pairs={{3,0},{0,1},{1,2},{2,3},{7,4},{4,5},{5,6},{6,7},{11,8},{8,9},{9,10... | collective-permute-start | bytes 983048 | tf_op jit(solution)/shard_map/ppermute | solution.py:323
  23.1 9.2 %collective-permute-start.9 = (bf16[128,1280]{1,0:T(8,128)(2,1)S(1)}, bf16[128,1280]{1,0:T(8,128)(2,1)S(1)}, u32[]{:S(2)}, u32[]{:S(2)}) collective-permute-start(bf16[128,1280]{1,0:T(8,128)(2,1)S(1)} %collective-permute-done.1.refs_10_), channel_id=1, source_target_pairs={{4,0},{8,4},{12,8},{0,12},{5,1},{9,5},{13,9},{1,13},{6,2},{10,6},{... | collective-permute-start | bytes 983048 | tf_op jit(solution)/shard_map/ppermute | solution.py:323
  26.5 9.2 %collective-permute-start.10 = (bf16[128,1280]{1,0:T(8,128)(2,1)S(1)}, bf16[128,1280]{1,0:T(8,128)(2,1)S(1)}, u32[]{:S(2)}, u32[]{:S(2)}) collective-permute-start(bf16[128,1280]{1,0:T(8,128)(2,1)S(1)} %collective-permute-done.refs_9_), channel_id=1, source_target_pairs={{12,0},{0,4},{4,8},{8,12},{13,1},{1,5},{5,9},{9,13},{14,2},{2,6},{... | collective-permute-start | bytes 983048 | tf_op jit(solution)/shard_map/ppermute | solution.py:323
  26.5 9.2 %collective-permute-start.11 = (bf16[128,1280]{1,0:T(8,128)(2,1)S(1)}, bf16[128,1280]{1,0:T(8,128)(2,1)S(1)}, u32[]{:S(2)}, u32[]{:S(2)}) collective-permute-start(bf16[128,1280]{1,0:T(8,128)(2,1)S(1)} %collective-permute-done.3.refs_12_.refs_5_), channel_id=1, source_target_pairs={{1,0},{2,1},{3,2},{0,3},{5,4},{6,5},{7,6},{4,7},{9,8},{10,9},{11,1... | collective-permute-start | bytes 983048 | tf_op jit(solution)/shard_map/ppermute | solution.py:323
  29.5 9.6 %collective-permute-start.12 = (bf16[128,1280]{1,0:T(8,128)(2,1)S(1)}, bf16[128,1280]{1,0:T(8,128)(2,1)S(1)}, u32[]{:S(2)}, u32[]{:S(2)}) collective-permute-start(bf16[128,1280]{1,0:T(8,128)(2,1)S(1)} %collective-permute-done.2.refs_11_.refs_4_), channel_id=1, source_target_pairs={{3,0},{0,1},{1,2},{2,3},{7,4},{4,5},{5,6},{6,7},{11,8},{8,9},{9,10... | collective-permute-start | bytes 983048 | tf_op jit(solution)/shard_map/ppermute | solution.py:323
  32.3 12.3 %collective-permute-start.13 = (bf16[128,1280]{1,0:T(8,128)(2,1)S(1)}, bf16[128,1280]{1,0:T(8,128)(2,1)S(1)}, u32[]{:S(2)}, u32[]{:S(2)}) collective-permute-start(bf16[128,1280]{1,0:T(8,128)(2,1)S(1)} %collective-permute-done.5.refs_9_), channel_id=1, source_target_pairs={{4,0},{8,4},{12,8},{0,12},{5,1},{9,5},{13,9},{1,13},{6,2},{10,6},{... | collective-permute-start | bytes 983048 | tf_op jit(solution)/shard_map/ppermute | solution.py:323
  35.7 8.9 %collective-permute-start.14 = (bf16[128,1280]{1,0:T(8,128)(2,1)S(1)}, bf16[128,1280]{1,0:T(8,128)(2,1)S(1)}, u32[]{:S(2)}, u32[]{:S(2)}) collective-permute-start(bf16[128,1280]{1,0:T(8,128)(2,1)S(1)} %collective-permute-done.6.refs_12_), channel_id=1, source_target_pairs={{12,0},{0,4},{4,8},{8,12},{13,1},{1,5},{5,9},{9,13},{14,2},{2,6},{... | collective-permute-start | bytes 983048 | tf_op jit(solution)/shard_map/ppermute | solution.py:323
  35.7 8.9 %collective-permute-start.15 = (bf16[128,1280]{1,0:T(8,128)(2,1)S(1)}, bf16[128,1280]{1,0:T(8,128)(2,1)S(1)}, u32[]{:S(2)}, u32[]{:S(2)}) collective-permute-start(bf16[128,1280]{1,0:T(8,128)(2,1)S(1)} %collective-permute-done.7.refs_13_.refs_6_), channel_id=1, source_target_pairs={{1,0},{2,1},{3,2},{0,3},{5,4},{6,5},{7,6},{4,7},{9,8},{10,9},{11,1... | collective-permute-start | bytes 983048 | tf_op jit(solution)/shard_map/ppermute | solution.py:323
  39.1 8.4 %collective-permute-start.16 = (bf16[128,1280]{1,0:T(8,128)(2,1)S(1)}, bf16[128,1280]{1,0:T(8,128)(2,1)S(1)}, u32[]{:S(2)}, u32[]{:S(2)}) collective-permute-start(bf16[128,1280]{1,0:T(8,128)(2,1)S(1)} %collective-permute-done.8.refs_16_.refs_9_), channel_id=1, source_target_pairs={{3,0},{0,1},{1,2},{2,3},{7,4},{4,5},{5,6},{6,7},{11,8},{8,9},{9,10... | collective-permute-start | bytes 983048 | tf_op jit(solution)/shard_map/ppermute | solution.py:323
  47.5 6.3 %copy-start.3 = (f32[1280]{0:T(1024)S(1)}, f32[1280]{0:T(1024)}, u32[]{:S(2)}) copy-start(f32[1280]{0:T(1024)} %param.19) | copy-start | bytes 15364
  47.5 8.1 %copy-start = (bf16[1280,1280]{1,0:T(8,128)(2,1)S(1)}, bf16[1280,1280]{1,0:T(8,128)(2,1)}, u32[]{:S(2)}) copy-start(bf16[1280,1280]{1,0:T(8,128)(2,1)} %refs_8_.1) | copy-start | bytes 9830404
  47.5 8.1 %copy-start.1 = (bf16[1280,33]{0,1:T(8,128)(2,1)S(1)}, bf16[1280,33]{0,1:T(8,128)(2,1)}, u32[]{:S(2)}) copy-start(bf16[1280,33]{0,1:T(8,128)(2,1)} %param.21) | copy-start | bytes 253444
  47.5 8.1 %copy-start.2 = (f32[33]{0:T(128)S(1)}, f32[33]{0:T(128)}, u32[]{:S(2)}) copy-start(f32[33]{0:T(128)} %param.22) | copy-start | bytes 400
  50.8 4.8 %collective-permute-start.17 = (f32[128,1280]{1,0:T(8,128)S(1)}, f32[128,1280]{1,0:T(8,128)S(1)}, u32[]{:S(2)}, u32[]{:S(2)}) collective-permute-start(f32[128,1280]{1,0:T(8,128)S(1)} %shard_map.150.refs_2_), channel_id=1, source_target_pairs={{0,16},{16,0},{1,17},{17,1},{2,18},{18,2},{3,19},{19,3},{4,20},{20... | collective-permute-start | bytes 1966088 | tf_op jit(solution)/shard_map/ppermute | solution.py:327

commit v7 on v6

--- a/solution.py
+++ b/solution.py
@@ -225,49 +225,66 @@
         values_ref[which] = values
 
 
-def mix_kernel(probs_refs, values_refs, block_refs, inputs, partial_ref):
-    last = attend(*inputs)
+def mix_columns(columns, probs, values, masks, size):
     right = (lax.axis_index("x") + lax.axis_index("y")) % 2 == lax.axis_index("core")
-    own_probs, near_probs = probs_refs
+
+    def rows_of(step, which):
+        start = masks * (which + (2 if step == 3 else 0))
+        return probs[(0, 1, 2, 1)[step]](start, start + masks)
+
+    stack = []
+    for column in columns:
+        which = column // 2
+        for i in range(2):
+            even = rows_of((0, 2)[i], which)
+            odd = rows_of((1, 3)[i], which)
+            if column % 2:
+                even, odd = odd, even
+            stack.append(jnp.where(right, even, odd))
+    mixed = nn_dot(jnp.concatenate(stack, axis=0), values)
+    lane = lax.broadcasted_iota(jnp.int32, (masks, mixed.shape[1]), 1) // size
+    context = mixed[:masks, :]
+    for head in range(1, len(stack)):
+        context = jnp.where(lane == head, mixed[masks * head : masks * (head + 1), :], context)
+    return context.astype(BF16)
+
+
+def rows_reader(ref, copy):
+    return lambda start, end: ref[copy, start:end, :]
+
+
+def first_mix_kernel(probs_refs, values_refs, block_refs, inputs, probs_ref, partial_ref):
     size = block_refs[0].shape[0] // 2
-    masks = own_probs.shape[1] // 2
-
-    def rows_of(copy, step, which):
-        start = masks * (which + (2 if step == 3 else 0))
-        if step == 2:
-            return last[copy][0][start : start + masks, :]
-        ref = near_probs if step % 2 else own_probs
-        return ref[copy, start : start + masks, :]
-
+    masks = probs_refs[0].shape[1] // 2
+    for copy, (probs, _) in enumerate(attend(*inputs)):
+        probs_ref[copy] = probs
     contexts = []
     for copy in range(2):
-        parts = []
-        groups = (
-            (values_refs[0][copy], (0,)),
-            (values_refs[1][copy], (1, 3)),
-            (last[copy][1], (2,)),
+        readers = [rows_reader(r, copy) for r in (*probs_refs, probs_ref)]
+        contexts.append(
+            jnp.concatenate(
+                [
+                    mix_columns(columns, readers, ref[copy], masks, size)
+                    for columns, ref in zip(((0,), (1, 3)), values_refs)
+                ],
+                axis=1,
+            )
         )
-        for values, columns in groups:
-            stack = []
-            for column in columns:
-                which = column // 2
-                for i in range(2):
-                    even = rows_of(copy, (0, 2)[i], which)
-                    odd = rows_of(copy, (1, 3)[i], which)
-                    if column % 2:
-                        even, odd = odd, even
-                    stack.append(jnp.where(right, even, odd))
-            mixed = nn_dot(jnp.concatenate(stack, axis=0), values)
-            lane = lax.broadcasted_iota(jnp.int32, (masks, mixed.shape[1]), 1) // size
-            context = mixed[:masks, :]
-            for head in range(1, len(stack)):
-                context = jnp.where(
-                    lane == head, mixed[masks * head : masks * (head + 1), :], context
-                )
-            parts.append(context.astype(BF16))
-        contexts.append(jnp.concatenate(parts, axis=1))
     weight = jnp.concatenate([r[size:, :] for r in block_refs], axis=0)
     partial_ref[...] = nn_dot(jnp.concatenate(contexts, axis=0), weight)
+
+
+def last_mix_kernel(probs_refs, normed_refs, block_refs, sum_ref, partial_ref):
+    size = block_refs[0].shape[0] // 2
+    masks = probs_refs[0].shape[1] // 2
+    value_weight = jnp.concatenate([r[:size, :] for r in block_refs], axis=0)
+    contexts = []
+    for copy in range(2):
+        readers = [rows_reader(r, copy) for r in probs_refs]
+        values = nt_dot(normed_refs[copy][...], value_weight).astype(BF16)
+        contexts.append(mix_columns((2,), readers, values, masks, size))
+    weight = jnp.concatenate([r[size:, :] for r in block_refs], axis=0)
+    partial_ref[...] = sum_ref[...] + nn_dot(jnp.concatenate(contexts, axis=0), weight)
 
 
 def score_kernel(
@@ -405,17 +422,18 @@
         per_copy = [r[i] for i in (0, 1, 3, 4) for r in ready]
         return (ready[0][5], *per_copy, *key_blocks, *value_blocks)
 
-    def attend_refs(refs, heads):
+    def attend_refs(refs, heads, value_heads):
+        keys_at = 9 + heads
         return (
-            refs[0], refs[1:3], refs[3:5], refs[5:7], refs[7:9], refs[9 : 9 + heads],
-            refs[9 + heads : 9 + 2 * heads],
+            refs[0], refs[1:3], refs[3:5], refs[5:7], refs[7:9], refs[9:keys_at],
+            refs[keys_at : keys_at + value_heads],
         )
 
     def attend_call(ready, key_blocks, value_blocks):
         heads = len(key_blocks)
 
         def kernel(*refs):
-            attend_kernel(*attend_refs(refs, heads), *refs[-2:])
+            attend_kernel(*attend_refs(refs, heads, heads), *refs[-2:])
 
         return call(
             kernel,
@@ -462,20 +480,31 @@
     key_far = tuple(after(b, own_probs, near_probs) for b in key_far)
     value_blocks = (value_low, value_high, *value_near)
 
-    def mix(*refs):
-        mix_kernel(
-            refs[0:2], refs[2:4], (*refs[4:10], *refs[-3:-1]), attend_refs(refs[10:], 2), refs[-1]
+    def first_mix(*refs):
+        first_mix_kernel(
+            refs[0:2], refs[2:4], refs[4:10], attend_refs(refs[10:], 2, 0), *refs[-2:]
         )
 
-    partial = call(
-        mix,
-        shape((2 * masks, feature), F32),
+    far_probs, first_sum = call(
+        first_mix,
+        [shape((2, 2 * masks, span), BF16), shape((2 * masks, feature), F32)],
         (
             own_probs, near_probs, own_values, near_values, *value_blocks,
-            *attend_args(ready, key_far, value_far),
+            *attend_args(ready, key_far, ()),
         ),
-        flops=4 * span * feature * 256 + 4 * masks * feature * 8 * size,
+        flops=4 * span * feature * 256 + 4 * masks * feature * 6 * size,
         exps=4 * masks * span,
+    )
+    value_far = tuple(after(b, far_probs) for b in value_far)
+
+    def last_mix(*refs):
+        last_mix_kernel(refs[:3], refs[3:5], refs[5:7], *refs[7:])
+
+    partial = call(
+        last_mix,
+        shape((2 * masks, feature), F32),
+        (own_probs, near_probs, far_probs, mine[0], other[0], *value_far, first_sum),
+        flops=4 * span * feature * 256 + 4 * masks * feature * 2 * size,
     )
 
     def score(*refs):

time: 82.5 us -> 83.5 us (1.012)
  waiting for transfers between devices: 9.09 us -> 6.22 us
  Pallas kernels: 17.9 us -> 20.3 us
  blocking collectives: 24.1 us -> 25.9 us
    ppermute x12, waiting for transfers between devices: 3.52 us -> 0.64 us  [pull(): lax.ppermute(array, axis, [((i + offset) % size, i) for i in range(size)])]
    pallas_call x7 -> x8, Pallas kernels: 17.9 us -> 20.3 us  [call(): pl.pallas_call(kernel, out_shape=outs, in_specs=[IN_PLACE] * n_any + [ON_...]
    all_to_all x1, blocking collectives: 24.1 us -> 25.9 us  [on_device(): arrived = lax.all_to_all(placed, ('z', 'y', 'x'), 0, 0, tiled=True)]
  transfers between devices with their start and end apart: 18 -> 18, of which waited for: 4 -> 3; matrix products, arithmetic and copies ran while one was open for 0% -> 0% of each run, Pallas kernels for 16% -> 19%
where the time goes in v7:
time: 83.5 us; the launch traced here: 83.3 us
  starting transfers between devices  29.9 us (36%)
  blocking collectives  25.9 us (31%)
  Pallas kernels  20.3 us (24%)
  waiting for transfers between devices  6.22 us (7%)
    all_to_all x1, blocking collectives, on_device(): arrived = lax.all_to_all(placed, ('z', 'y', 'x'), 0, 0, tiled=True)  25.9 us
    pallas_call x8, Pallas kernels, call(): pl.pallas_call(kernel, out_shape=outs, in_specs=[IN_PLACE] * n_any + [ON_...  20.3 us
    ppermute x12, starting transfers between devices, pull(): lax.ppermute(array, axis, [((i + offset) % size, i) for i in range(size)])  18.9 us
    ppermute x2, starting transfers between devices, swap(): return lax.ppermute(array, 'core', [(0, 1), (1, 0)])  6.02 us
    ppermute x4, starting transfers between devices, gather_line(): return (lax.ppermute(block, axes, near), lax.ppermute(block, axes, far))  4.99 us
    ppermute x4, waiting for transfers between devices, gather_line(): return (lax.ppermute(block, axes, near), lax.ppermute(block, axes, far))  3.85 us
    ppermute x2, waiting for transfers between devices, swap(): return lax.ppermute(array, 'core', [(0, 1), (1, 0)])  1.72 us
  transfers between devices with their start and end apart: 18, of which 3 were waited for; matrix products, arithmetic and copies ran while one was open for 0% of the time, Pallas kernels for 19%

profile of v7, /device:TPU:1, one launch (start us, length us, event | category | flops | bytes accessed | tf_op | source)
XLA Modules:
  0.0 83.3 jit_solution(17620446063856154925)
XLA Ops:
  0.0 3.2 %collective-permute-start.4 = (bf16[640,1280]{1,0:T(8,128)(2,1)}, bf16[640,1280]{1,0:T(8,128)(2,1)S(1)}, u32[]{:S(2)}, u32[]{:S(2)}) collective-permute-start(bf16[640,1280]{1,0:T(8,128)(2,1)} %bitcast.14), channel_id=1, source_target_pairs={{0,16},{16,0},{1,17},{17,1},{2,18},{18,2},{3,19},{19,3},{4,20},{20... | collective-permute-start | bytes 4915208 | tf_op jit(solution)/shard_map/ppermute | solution.py:344
  3.2 1.1 %shard_map.145 = (bf16[128,1280]{1,0:T(8,128)(2,1)S(1)}, bf16[128,1280]{1,0:T(8,128)(2,1)S(1)}) custom-call(bf16[192,1280]{1,0:T(8,128)(2,1)} %bitcast.16, bf16[64,1280]{1,0:T(8,128)(2,1)} %bitcast.19), custom_call_target="tpu_custom_call" | custom-call | bytes 1310720 | tf_op jit(solution)/shard_map/pallas_call | solution.py:59
  4.4 0.1 collective-permute-start
  4.5 1.4 %collective-permute-start.1 = (bf16[128,1280]{1,0:T(8,128)(2,1)S(1)}, bf16[128,1280]{1,0:T(8,128)(2,1)S(1)}, u32[]{:S(2)}, u32[]{:S(2)}) collective-permute-start(bf16[128,1280]{1,0:T(8,128)(2,1)S(1)} %get-tuple-element.39), channel_id=1, source_target_pairs={{0,1},{1,19},{2,3},{3,17},{4,22},{5,6},{6,20},{7,4},{8,9},{9,27},{... | collective-permute-start | bytes 983048 | tf_op jit(solution)/shard_map/ppermute | solution.py:366
  5.9 0.0 collective-permute-start.2
  5.9 3.5 %collective-permute-start.3 = (bf16[128,1280]{1,0:T(8,128)(2,1)S(1)}, bf16[128,1280]{1,0:T(8,128)(2,1)S(1)}, u32[]{:S(2)}, u32[]{:S(2)}) collective-permute-start(bf16[128,1280]{1,0:T(8,128)(2,1)S(1)} %get-tuple-element.40), channel_id=1, source_target_pairs={{0,4},{1,25},{2,6},{3,27},{4,28},{5,9},{6,30},{7,11},{8,12},{9,17}... | collective-permute-start | bytes 983048 | tf_op jit(solution)/shard_map/ppermute | solution.py:366
  9.4 3.8 %collective-permute-done.refs_9_ = bf16[128,1280]{1,0:T(8,128)(2,1)S(1)} collective-permute-done((bf16[128,1280]{1,0:T(8,128)(2,1)S(1)}, bf16[128,1280]{1,0:T(8,128)(2,1)S(1)}, u32[]{:S(2)}, u32[]{:S(2)}) %collective-permute-start) | collective-permute-done | bytes 327712 | tf_op jit(solution)/shard_map/ppermute | solution.py:366
  13.2 2.3 %collective-permute-start.5 = (bf16[128,1280]{1,0:T(8,128)(2,1)S(1)}, bf16[128,1280]{1,0:T(8,128)(2,1)S(1)}, u32[]{:S(2)}, u32[]{:S(2)}) collective-permute-start(bf16[128,1280]{1,0:T(8,128)(2,1)S(1)} %collective-permute-done.refs_9_), channel_id=1, source_target_pairs={{4,0},{8,4},{12,8},{0,12},{5,1},{9,5},{13,9},{1,13},{6,2},{10,6},{... | collective-permute-start | bytes 983048 | tf_op jit(solution)/shard_map/ppermute | solution.py:340
  15.5 0.0 collective-permute-done.1.refs_10_
  15.5 0.3 collective-permute-start.6
  15.7 0.0 collective-permute-done.2.refs_11_.refs_4_
  15.8 3.2 %collective-permute-start.7 = (bf16[128,1280]{1,0:T(8,128)(2,1)S(1)}, bf16[128,1280]{1,0:T(8,128)(2,1)S(1)}, u32[]{:S(2)}, u32[]{:S(2)}) collective-permute-start(bf16[128,1280]{1,0:T(8,128)(2,1)S(1)} %collective-permute-done.2.refs_11_.refs_4_), channel_id=1, source_target_pairs={{1,0},{2,1},{3,2},{0,3},{5,4},{6,5},{7,6},{4,7},{9,8},{10,9},{11,1... | collective-permute-start | bytes 983048 | tf_op jit(solution)/shard_map/ppermute | solution.py:340
  19.0 0.0 collective-permute-done.3.refs_12_.refs_5_
  19.0 0.0 collective-permute-start.8
  19.0 3.5 %shard_map.146 = (bf16[640,1280]{1,0:T(8,128)(2,1)S(1)}, bf16[64,1280]{1,0:T(8,128)(2,1)S(1)}, f32[64,1280]{1,0:T(8,128)S(1)}, f32[64,256]{1,0:T(8,128)S(1)}, s3...) custom-call(s32[256]{0:T(256)} %refs_0_.3, s32[24]{0:T(128)} %refs_1_.3, s32[256]{0:T(256)} %refs_2_.3, s32[64,256]{1,0:T(8,128)} %bitcast.17, ...), custom_call_target="tpu_custom_call" | custom-call | flops 217907200 | bytes 5639264 | tf_op jit(solution)/shard_map/pallas_call | solution.py:59
  22.4 0.6 collective-permute-done.5.refs_9_
  23.1 3.4 %collective-permute-start.9 = (bf16[128,1280]{1,0:T(8,128)(2,1)S(1)}, bf16[128,1280]{1,0:T(8,128)(2,1)S(1)}, u32[]{:S(2)}, u32[]{:S(2)}) collective-permute-start(bf16[128,1280]{1,0:T(8,128)(2,1)S(1)} %collective-permute-done.1.refs_10_), channel_id=1, source_target_pairs={{4,0},{8,4},{12,8},{0,12},{5,1},{9,5},{13,9},{1,13},{6,2},{10,6},{... | collective-permute-start | bytes 983048 | tf_op jit(solution)/shard_map/ppermute | solution.py:340
  26.5 0.0 collective-permute-done.6.refs_12_
  26.5 0.0 collective-permute-start.10
  26.5 0.0 collective-permute-done.7.refs_13_.refs_6_
  26.5 3.0 %collective-permute-start.11 = (bf16[128,1280]{1,0:T(8,128)(2,1)S(1)}, bf16[128,1280]{1,0:T(8,128)(2,1)S(1)}, u32[]{:S(2)}, u32[]{:S(2)}) collective-permute-start(bf16[128,1280]{1,0:T(8,128)(2,1)S(1)} %collective-permute-done.3.refs_12_.refs_5_), channel_id=1, source_target_pairs={{1,0},{2,1},{3,2},{0,3},{5,4},{6,5},{7,6},{4,7},{9,8},{10,9},{11,1... | collective-permute-start | bytes 983048 | tf_op jit(solution)/shard_map/ppermute | solution.py:340
  29.5 0.0 collective-permute-done.8.refs_16_.refs_9_
  29.5 0.0 collective-permute-start.12
  29.5 0.0 collective-permute-done.4.refs_7_
  29.5 2.8 %shard_map.147 = (bf16[640,1280]{1,0:T(8,128)(2,1)S(1)}, bf16[64,1280]{1,0:T(8,128)(2,1)S(1)}, f32[64,1280]{1,0:T(8,128)S(1)}, f32[64,256]{1,0:T(8,128)S(1)}, s32[64,128]{1,0:T(8,128)S(1)}) custom-call(s32[256]{0:T(256)} %refs_0_.3, s32[24]{0:T(128)} %refs_1_.3, s32[256]{0:T(256)} %refs_2_.3, s32[64,256]{1,0:T(8,128)} %bitcast.18, s32[24,640]{1,0:T(8,128)} %refs_4_.3, ...), custom_call_target="tpu_custom_call" | custom-call | flops 217907200 | bytes 4328544 | tf_op jit(solution)/shard_map/pallas_call | solution.py:59
  32.3 0.0 collective-permute-done.9.refs_10_
  32.3 3.4 %collective-permute-start.13 = (bf16[128,1280]{1,0:T(8,128)(2,1)S(1)}, bf16[128,1280]{1,0:T(8,128)(2,1)S(1)}, u32[]{:S(2)}, u32[]{:S(2)}) collective-permute-start(bf16[128,1280]{1,0:T(8,128)(2,1)S(1)} %collective-permute-done.5.refs_9_), channel_id=1, source_target_pairs={{4,0},{8,4},{12,8},{0,12},{5,1},{9,5},{13,9},{1,13},{6,2},{10,6},{... | collective-permute-start | bytes 983048 | tf_op jit(solution)/shard_map/ppermute | solution.py:340
  35.7 0.0 collective-permute-done.10.refs_11_
  35.7 0.0 collective-permute-start.14
  35.7 0.0 collective-permute-done.11.refs_14_.refs_7_
  35.7 3.4 %collective-permute-start.15 = (bf16[128,1280]{1,0:T(8,128)(2,1)S(1)}, bf16[128,1280]{1,0:T(8,128)(2,1)S(1)}, u32[]{:S(2)}, u32[]{:S(2)}) collective-permute-start(bf16[128,1280]{1,0:T(8,128)(2,1)S(1)} %collective-permute-done.7.refs_13_.refs_6_), channel_id=1, source_target_pairs={{1,0},{2,1},{3,2},{0,3},{5,4},{6,5},{7,6},{4,7},{9,8},{10,9},{11,1... | collective-permute-start | bytes 983048 | tf_op jit(solution)/shard_map/ppermute | solution.py:340
  39.1 0.0 collective-permute-done.12.refs_15_.refs_8_
  39.1 0.0 collective-permute-start.16
  39.1 2.5 %shard_map.148 = (bf16[2,128,640]{2,1,0:T(8,128)(2,1)S(1)}, bf16[2,640,128]{2,1,0:T(8,128)(2,1)S(1)}) custom-call(f32[640,256]{1,0:T(8,128)S(1)} %get-tuple-element.46.refs_0_.refs_10_, bf16[640,1280]{1,0:T(8,128)(2,1)S(1)} %get-tuple-element.43.refs_1_.refs_11_.refs_3_, bf16[640,1280]{1,0:T(8,128)(2,1)S(1)} %get-tuple-element.47.refs_2_.refs_12_.refs_4_, ...), custom_call_target="tpu_custom_call" | custom-call | flops 838860800 | bytes 6422528 | tf_op jit(solution)/shard_map/pallas_call | solution.py:59
  41.6 3.0 %shard_map.149 = (bf16[2,256,640]{2,1,0:T(8,128)(2,1)S(1)}, bf16[2,640,256]{2,1,0:T(8,128)(2,1)S(1)}) custom-call(f32[640,256]{1,0:T(8,128)S(1)} %get-tuple-element.46.refs_0_.refs_10_, bf16[640,1280]{1,0:T(8,128)(2,1)S(1)} %get-tuple-element.43.refs_1_.refs_11_.refs_3_, bf16[640,1280]{1,0:T(8,128)(2,1)S(1)} %get-tuple-element.47.refs_2_.refs_12_.refs_4_, ...), custom_call_target="tpu_custom_call" | custom-call | flops 1677721600 | bytes 8388608 | tf_op jit(solution)/shard_map/pallas_call | solution.py:59
  44.6 0.0 collective-permute-done.13.refs_19_
  44.6 0.0 collective-permute-done.14.refs_20_
  44.6 3.3 %shard_map.150 = (bf16[2,128,640]{2,1,0:T(8,128)(2,1)S(1)}, f32[128,1280]{1,0:T(8,128)S(1)}) custom-call(bf16[2,128,640]{2,1,0:T(8,128)(2,1)S(1)} %get-tuple-element.59.refs_0_, bf16[2,256,640]{2,1,0:T(8,128)(2,1)S(1)} %get-tuple-element.60.refs_1_, bf16[2,640,128]{2,1,0:T(8,128)(2,1)S(1)} %get-tuple-element.61.refs_2_, ...), custom_call_target="tpu_custom_call" | custom-call | flops 964689920 | bytes 10027008 | tf_op jit(solution)/shard_map/pallas_call | solution.py:59
  47.9 0.0 collective-permute-done.15.refs_5_
  47.9 0.0 collective-permute-done.16.refs_6_
  47.9 0.0 copy-start.3
  47.9 0.0 copy-start
  47.9 0.0 copy-start.1
  47.9 0.0 copy-start.2
  47.9 2.3 %shard_map.151.refs_2_ = f32[128,1280]{1,0:T(8,128)S(1)} custom-call(bf16[2,128,640]{2,1,0:T(8,128)(2,1)S(1)} %get-tuple-element.59.refs_0_, bf16[2,256,640]{2,1,0:T(8,128)(2,1)S(1)} %get-tuple-element.60.refs_1_, bf16[2,128,640]{2,1,0:T(8,128)(2,1)S(1)} %get-tuple-element.67.refs_2_, bf16[640,1280]{1,0:T(8,128)(2,1)S(1)} %get-tuple-element.43.refs_1_.refs_11_.refs_3_, ...), custom_call_target="tpu_custom_call" | custom-call | flops 880803840 | bytes 6553600 | tf_op jit(solution)/shard_map/pallas_call | solution.py:59
  50.3 2.8 %collective-permute-start.17 = (f32[128,1280]{1,0:T(8,128)S(1)}, f32[128,1280]{1,0:T(8,128)S(1)}, u32[]{:S(2)}, u32[]{:S(2)}) collective-permute-start(f32[128,1280]{1,0:T(8,128)S(1)} %shard_map.151.refs_2_), channel_id=1, source_target_pairs={{0,16},{16,0},{1,17},{17,1},{2,18},{18,2},{3,19},{19,3},{4,20},{20... | collective-permute-start | bytes 1966088 | tf_op jit(solution)/shard_map/ppermute | solution.py:344
  53.1 0.0 copy-done.3
  53.1 1.7 %collective-permute-done.17.refs_3_ = f32[128,1280]{1,0:T(8,128)S(1)} collective-permute-done((f32[128,1280]{1,0:T(8,128)S(1)}, f32[128,1280]{1,0:T(8,128)S(1)}, u32[]{:S(2)}, u32[]{:S(2)}) %collective-permute-start.17) | collective-permute-done | bytes 655392 | tf_op jit(solution)/shard_map/ppermute | solution.py:344
  54.8 0.0 copy-done
  54.8 0.0 copy-done.1
  54.8 0.0 copy-done.2
  54.8 1.8 %shard_map.152 = f32[128,64]{1,0:T(8,128)S(1)} custom-call(f32[64,1280]{1,0:T(8,128)S(1)} %get-tuple-element.42.refs_0_, f32[64,1280]{1,0:T(8,128)S(1)} %get-tuple-element.45.refs_1_, f32[128,1280]{1,0:T(8,128)S(1)} %shard_map.151.refs_2_, f32[128,1280]{1,0:T(8,128)S(1)} %collective-permute-done.17.refs_3_, ...), custom_call_target="tpu_custom_call" | custom-call | flops 419430400 | bytes 5430916 | tf_op jit(solution)/shard_map/pallas_call | solution.py:59
  56.6 25.9 %all_to_all.9 = f32[128,1,64]{2,1,0:T(1,128)S(1)} all-to-all(f32[128,1,64]{2,1,0:T(1,128)S(1)} %bitcast.11), channel_id=1, replica_groups=mesh['z'=8,'core'=2,'y'=4,'x'=4] {'z','y','x'}, dimensions={0} | all-to-all | bytes 65536 | tf_op jit(solution)/shard_map/all_to_all | solution.py:523
  82.4 0.2 reduce_sum.9
  82.6 0.1 reshape.13
  82.7 0.7 copy.19
  (1 shorter events, 0.0 us)
Async XLA Ops:
  0.0 29.5 %collective-permute-start.4 = (bf16[640,1280]{1,0:T(8,128)(2,1)}, bf16[640,1280]{1,0:T(8,128)(2,1)S(1)}, u32[]{:S(2)}, u32[]{:S(2)}) collective-permute-start(bf16[640,1280]{1,0:T(8,128)(2,1)} %bitcast.14), channel_id=1, source_target_pairs={{0,16},{16,0},{1,17},{17,1},{2,18},{18,2},{3,19},{19,3},{4,20},{20... | collective-permute-start | bytes 4915208 | tf_op jit(solution)/shard_map/ppermute | solution.py:344
  4.4 8.8 %collective-permute-start = (bf16[128,1280]{1,0:T(8,128)(2,1)S(1)}, bf16[128,1280]{1,0:T(8,128)(2,1)S(1)}, u32[]{:S(2)}, u32[]{:S(2)}) collective-permute-start(bf16[128,1280]{1,0:T(8,128)(2,1)S(1)} %get-tuple-element.39), channel_id=1, source_target_pairs={{0,3},{1,17},{2,1},{3,19},{4,20},{5,4},{6,22},{7,6},{8,11},{9,25},... | collective-permute-start | bytes 983048 | tf_op jit(solution)/shard_map/ppermute | solution.py:366
  4.5 11.0 %collective-permute-start.1 = (bf16[128,1280]{1,0:T(8,128)(2,1)S(1)}, bf16[128,1280]{1,0:T(8,128)(2,1)S(1)}, u32[]{:S(2)}, u32[]{:S(2)}) collective-permute-start(bf16[128,1280]{1,0:T(8,128)(2,1)S(1)} %get-tuple-element.39), channel_id=1, source_target_pairs={{0,1},{1,19},{2,3},{3,17},{4,22},{5,6},{6,20},{7,4},{8,9},{9,27},{... | collective-permute-start | bytes 983048 | tf_op jit(solution)/shard_map/ppermute | solution.py:366
  5.9 9.9 %collective-permute-start.2 = (bf16[128,1280]{1,0:T(8,128)(2,1)S(1)}, bf16[128,1280]{1,0:T(8,128)(2,1)S(1)}, u32[]{:S(2)}, u32[]{:S(2)}) collective-permute-start(bf16[128,1280]{1,0:T(8,128)(2,1)S(1)} %get-tuple-element.40), channel_id=1, source_target_pairs={{0,12},{1,17},{2,14},{3,19},{4,20},{5,1},{6,22},{7,3},{8,4},{9,25}... | collective-permute-start | bytes 983048 | tf_op jit(solution)/shard_map/ppermute | solution.py:366
  5.9 13.1 %collective-permute-start.3 = (bf16[128,1280]{1,0:T(8,128)(2,1)S(1)}, bf16[128,1280]{1,0:T(8,128)(2,1)S(1)}, u32[]{:S(2)}, u32[]{:S(2)}) collective-permute-start(bf16[128,1280]{1,0:T(8,128)(2,1)S(1)} %get-tuple-element.40), channel_id=1, source_target_pairs={{0,4},{1,25},{2,6},{3,27},{4,28},{5,9},{6,30},{7,11},{8,12},{9,17}... | collective-permute-start | bytes 983048 | tf_op jit(solution)/shard_map/ppermute | solution.py:366
  13.2 9.9 %collective-permute-start.5 = (bf16[128,1280]{1,0:T(8,128)(2,1)S(1)}, bf16[128,1280]{1,0:T(8,128)(2,1)S(1)}, u32[]{:S(2)}, u32[]{:S(2)}) collective-permute-start(bf16[128,1280]{1,0:T(8,128)(2,1)S(1)} %collective-permute-done.refs_9_), channel_id=1, source_target_pairs={{4,0},{8,4},{12,8},{0,12},{5,1},{9,5},{13,9},{1,13},{6,2},{10,6},{... | collective-permute-start | bytes 983048 | tf_op jit(solution)/shard_map/ppermute | solution.py:340
  15.5 11.0 %collective-permute-start.6 = (bf16[128,1280]{1,0:T(8,128)(2,1)S(1)}, bf16[128,1280]{1,0:T(8,128)(2,1)S(1)}, u32[]{:S(2)}, u32[]{:S(2)}) collective-permute-start(bf16[128,1280]{1,0:T(8,128)(2,1)S(1)} %collective-permute-done.1.refs_10_), channel_id=1, source_target_pairs={{12,0},{0,4},{4,8},{8,12},{13,1},{1,5},{5,9},{9,13},{14,2},{2,6},{... | collective-permute-start | bytes 983048 | tf_op jit(solution)/shard_map/ppermute | solution.py:340
  15.8 10.7 %collective-permute-start.7 = (bf16[128,1280]{1,0:T(8,128)(2,1)S(1)}, bf16[128,1280]{1,0:T(8,128)(2,1)S(1)}, u32[]{:S(2)}, u32[]{:S(2)}) collective-permute-start(bf16[128,1280]{1,0:T(8,128)(2,1)S(1)} %collective-permute-done.2.refs_11_.refs_4_), channel_id=1, source_target_pairs={{1,0},{2,1},{3,2},{0,3},{5,4},{6,5},{7,6},{4,7},{9,8},{10,9},{11,1... | collective-permute-start | bytes 983048 | tf_op jit(solution)/shard_map/ppermute | solution.py:340
  19.0 10.5 %collective-permute-start.8 = (bf16[128,1280]{1,0:T(8,128)(2,1)S(1)}, bf16[128,1280]{1,0:T(8,128)(2,1)S(1)}, u32[]{:S(2)}, u32[]{:S(2)}) collective-permute-start(bf16[128,1280]{1,0:T(8,128)(2,1)S(1)} %collective-permute-done.3.refs_12_.refs_5_), channel_id=1, source_target_pairs={{3,0},{0,1},{1,2},{2,3},{7,4},{4,5},{5,6},{6,7},{11,8},{8,9},{9,10... | collective-permute-start | bytes 983048 | tf_op jit(solution)/shard_map/ppermute | solution.py:340
  23.1 9.2 %collective-permute-start.9 = (bf16[128,1280]{1,0:T(8,128)(2,1)S(1)}, bf16[128,1280]{1,0:T(8,128)(2,1)S(1)}, u32[]{:S(2)}, u32[]{:S(2)}) collective-permute-start(bf16[128,1280]{1,0:T(8,128)(2,1)S(1)} %collective-permute-done.1.refs_10_), channel_id=1, source_target_pairs={{4,0},{8,4},{12,8},{0,12},{5,1},{9,5},{13,9},{1,13},{6,2},{10,6},{... | collective-permute-start | bytes 983048 | tf_op jit(solution)/shard_map/ppermute | solution.py:340
  26.5 9.2 %collective-permute-start.10 = (bf16[128,1280]{1,0:T(8,128)(2,1)S(1)}, bf16[128,1280]{1,0:T(8,128)(2,1)S(1)}, u32[]{:S(2)}, u32[]{:S(2)}) collective-permute-start(bf16[128,1280]{1,0:T(8,128)(2,1)S(1)} %collective-permute-done.refs_9_), channel_id=1, source_target_pairs={{12,0},{0,4},{4,8},{8,12},{13,1},{1,5},{5,9},{9,13},{14,2},{2,6},{... | collective-permute-start | bytes 983048 | tf_op jit(solution)/shard_map/ppermute | solution.py:340
  26.5 9.2 %collective-permute-start.11 = (bf16[128,1280]{1,0:T(8,128)(2,1)S(1)}, bf16[128,1280]{1,0:T(8,128)(2,1)S(1)}, u32[]{:S(2)}, u32[]{:S(2)}) collective-permute-start(bf16[128,1280]{1,0:T(8,128)(2,1)S(1)} %collective-permute-done.3.refs_12_.refs_5_), channel_id=1, source_target_pairs={{1,0},{2,1},{3,2},{0,3},{5,4},{6,5},{7,6},{4,7},{9,8},{10,9},{11,1... | collective-permute-start | bytes 983048 | tf_op jit(solution)/shard_map/ppermute | solution.py:340
  29.5 9.6 %collective-permute-start.12 = (bf16[128,1280]{1,0:T(8,128)(2,1)S(1)}, bf16[128,1280]{1,0:T(8,128)(2,1)S(1)}, u32[]{:S(2)}, u32[]{:S(2)}) collective-permute-start(bf16[128,1280]{1,0:T(8,128)(2,1)S(1)} %collective-permute-done.2.refs_11_.refs_4_), channel_id=1, source_target_pairs={{3,0},{0,1},{1,2},{2,3},{7,4},{4,5},{5,6},{6,7},{11,8},{8,9},{9,10... | collective-permute-start | bytes 983048 | tf_op jit(solution)/shard_map/ppermute | solution.py:340
  32.3 12.3 %collective-permute-start.13 = (bf16[128,1280]{1,0:T(8,128)(2,1)S(1)}, bf16[128,1280]{1,0:T(8,128)(2,1)S(1)}, u32[]{:S(2)}, u32[]{:S(2)}) collective-permute-start(bf16[128,1280]{1,0:T(8,128)(2,1)S(1)} %collective-permute-done.5.refs_9_), channel_id=1, source_target_pairs={{4,0},{8,4},{12,8},{0,12},{5,1},{9,5},{13,9},{1,13},{6,2},{10,6},{... | collective-permute-start | bytes 983048 | tf_op jit(solution)/shard_map/ppermute | solution.py:340
  35.7 8.9 %collective-permute-start.14 = (bf16[128,1280]{1,0:T(8,128)(2,1)S(1)}, bf16[128,1280]{1,0:T(8,128)(2,1)S(1)}, u32[]{:S(2)}, u32[]{:S(2)}) collective-permute-start(bf16[128,1280]{1,0:T(8,128)(2,1)S(1)} %collective-permute-done.6.refs_12_), channel_id=1, source_target_pairs={{12,0},{0,4},{4,8},{8,12},{13,1},{1,5},{5,9},{9,13},{14,2},{2,6},{... | collective-permute-start | bytes 983048 | tf_op jit(solution)/shard_map/ppermute | solution.py:340
  35.7 12.2 %collective-permute-start.15 = (bf16[128,1280]{1,0:T(8,128)(2,1)S(1)}, bf16[128,1280]{1,0:T(8,128)(2,1)S(1)}, u32[]{:S(2)}, u32[]{:S(2)}) collective-permute-start(bf16[128,1280]{1,0:T(8,128)(2,1)S(1)} %collective-permute-done.7.refs_13_.refs_6_), channel_id=1, source_target_pairs={{1,0},{2,1},{3,2},{0,3},{5,4},{6,5},{7,6},{4,7},{9,8},{10,9},{11,1... | collective-permute-start | bytes 983048 | tf_op jit(solution)/shard_map/ppermute | solution.py:340
  39.1 8.8 %collective-permute-start.16 = (bf16[128,1280]{1,0:T(8,128)(2,1)S(1)}, bf16[128,1280]{1,0:T(8,128)(2,1)S(1)}, u32[]{:S(2)}, u32[]{:S(2)}) collective-permute-start(bf16[128,1280]{1,0:T(8,128)(2,1)S(1)} %collective-permute-done.8.refs_16_.refs_9_), channel_id=1, source_target_pairs={{3,0},{0,1},{1,2},{2,3},{7,4},{4,5},{5,6},{6,7},{11,8},{8,9},{9,10... | collective-permute-start | bytes 983048 | tf_op jit(solution)/shard_map/ppermute | solution.py:340
  47.9 5.2 %copy-start.3 = (f32[1280]{0:T(1024)S(1)}, f32[1280]{0:T(1024)}, u32[]{:S(2)}) copy-start(f32[1280]{0:T(1024)} %param.19) | copy-start | bytes 15364
  47.9 6.9 %copy-start = (bf16[1280,1280]{1,0:T(8,128)(2,1)S(1)}, bf16[1280,1280]{1,0:T(8,128)(2,1)}, u32[]{:S(2)}) copy-start(bf16[1280,1280]{1,0:T(8,128)(2,1)} %refs_8_.1) | copy-start | bytes 9830404
  47.9 6.9 %copy-start.1 = (bf16[1280,33]{0,1:T(8,128)(2,1)S(1)}, bf16[1280,33]{0,1:T(8,128)(2,1)}, u32[]{:S(2)}) copy-start(bf16[1280,33]{0,1:T(8,128)(2,1)} %param.21) | copy-start | bytes 253444
  47.9 6.9 %copy-start.2 = (f32[33]{0:T(128)S(1)}, f32[33]{0:T(128)}, u32[]{:S(2)}) copy-start(f32[33]{0:T(128)} %param.22) | copy-start | bytes 400
  50.3 4.5 %collective-permute-start.17 = (f32[128,1280]{1,0:T(8,128)S(1)}, f32[128,1280]{1,0:T(8,128)S(1)}, u32[]{:S(2)}, u32[]{:S(2)}) collective-permute-start(f32[128,1280]{1,0:T(8,128)S(1)} %shard_map.151.refs_2_), channel_id=1, source_target_pairs={{0,16},{16,0},{1,17},{17,1},{2,18},{18,2},{3,19},{19,3},{4,20},{20... | collective-permute-start | bytes 1966088 | tf_op jit(solution)/shard_map/ppermute | solution.py:344

commit v8 on v7

--- a/solution.py
+++ b/solution.py
@@ -253,38 +253,59 @@
     return lambda start, end: ref[copy, start:end, :]
 
 
-def first_mix_kernel(probs_refs, values_refs, block_refs, inputs, probs_ref, partial_ref):
+def probs_kernel(*refs):
+    inputs, probs_ref = refs[:-1], refs[-1]
+    for which, (probs, _) in enumerate(attend(*inputs)):
+        probs_ref[which] = probs
+
+
+def mix_kernel(probs_refs, values_refs, normed_refs, far_refs, block_refs, partial_ref):
     size = block_refs[0].shape[0] // 2
     masks = probs_refs[0].shape[1] // 2
-    for copy, (probs, _) in enumerate(attend(*inputs)):
-        probs_ref[copy] = probs
+    value_weight = jnp.concatenate([r[:size, :] for r in far_refs], axis=0)
     contexts = []
     for copy in range(2):
-        readers = [rows_reader(r, copy) for r in (*probs_refs, probs_ref)]
+        readers = [rows_reader(r, copy) for r in probs_refs]
+        far = nt_dot(normed_refs[copy][...], value_weight).astype(BF16)
+        values = (values_refs[0][copy], values_refs[1][copy], far)
         contexts.append(
             jnp.concatenate(
                 [
-                    mix_columns(columns, readers, ref[copy], masks, size)
-                    for columns, ref in zip(((0,), (1, 3)), values_refs)
+                    mix_columns(columns, readers, value, masks, size)
+                    for columns, value in zip(((0,), (1, 3), (2,)), values)
                 ],
                 axis=1,
             )
         )
-    weight = jnp.concatenate([r[size:, :] for r in block_refs], axis=0)
+    weight = jnp.concatenate([r[size:, :] for r in (*block_refs, *far_refs)], axis=0)
     partial_ref[...] = nn_dot(jnp.concatenate(contexts, axis=0), weight)
 
 
-def last_mix_kernel(probs_refs, normed_refs, block_refs, sum_ref, partial_ref):
-    size = block_refs[0].shape[0] // 2
-    masks = probs_refs[0].shape[1] // 2
-    value_weight = jnp.concatenate([r[:size, :] for r in block_refs], axis=0)
-    contexts = []
-    for copy in range(2):
-        readers = [rows_reader(r, copy) for r in probs_refs]
-        values = nt_dot(normed_refs[copy][...], value_weight).astype(BF16)
-        contexts.append(mix_columns((2,), readers, values, masks, size))
-    weight = jnp.concatenate([r[size:, :] for r in block_refs], axis=0)
-    partial_ref[...] = sum_ref[...] + nn_dot(jnp.concatenate(contexts, axis=0), weight)
+def join_kernel(low_ref, high_ref, line_ref):
+    rows = low_ref.shape[0]
+    line_ref[:rows, :] = low_ref[...]
+    line_ref[rows:, :] = high_ref[...]
+
+
+def join(low, high):
+    line = jax.ShapeDtypeStruct((2 * low.shape[0], low.shape[1]), low.dtype)
+    return call(join_kernel, line, (low, high))
+
+
+def split_kernel(ahead_ref, behind_ref, low_ref, high_ref):
+    rows = low_ref.shape[0]
+    low_ref[...] = ahead_ref[:rows, :]
+    high_ref[...] = behind_ref[rows:, :]
+
+
+def split(ahead, behind):
+    half = jax.ShapeDtypeStruct((ahead.shape[0] // 2, ahead.shape[1]), ahead.dtype)
+    return call(split_kernel, [half, half], (ahead, behind))
+
+
+def halves(ref):
+    rows = ref.shape[0] // 2
+    return ref.at[:rows], ref.at[rows:]
 
 
 def score_kernel(
@@ -422,26 +443,26 @@
         per_copy = [r[i] for i in (0, 1, 3, 4) for r in ready]
         return (ready[0][5], *per_copy, *key_blocks, *value_blocks)
 
-    def attend_refs(refs, heads, value_heads):
-        keys_at = 9 + heads
-        return (
-            refs[0], refs[1:3], refs[3:5], refs[5:7], refs[7:9], refs[9:keys_at],
-            refs[keys_at : keys_at + value_heads],
-        )
-
-    def attend_call(ready, key_blocks, value_blocks):
-        heads = len(key_blocks)
+    def attend_refs(refs, keys, values):
+        return (refs[0], refs[1:3], refs[3:5], refs[5:7], refs[7:9], keys, values)
+
+    def attend_call(ready, key_lines, value_lines):
+        count = len(key_lines)
 
         def kernel(*refs):
-            attend_kernel(*attend_refs(refs, heads, heads), *refs[-2:])
-
+            lines = [halves(r) for r in refs[9:-2]]
+            keys = [h for line in lines[:count] for h in line]
+            values = [h for line in lines[count:] for h in line]
+            attend_kernel(*attend_refs(refs, keys, values), *refs[-2:])
+
+        heads = 2 * count
         return call(
             kernel,
             [
                 shape((2, heads * masks, span), BF16),
                 shape((2, span, heads * size), BF16),
             ],
-            attend_args(ready, key_blocks, value_blocks),
+            attend_args(ready, key_lines, value_lines),
             flops=4 * span * feature * heads * 128,
             exps=2 * heads * masks * span,
         )
@@ -451,60 +472,50 @@
     key_low, key_high = gather_line(key_block, "x")
     value_low, value_high = gather_line(value_block, "y")
     states_other = swap(states)
-    key_ahead_low = pull(key_low, "y", 1)
-    key_behind_high = pull(key_high, "y", 3)
-    value_ahead_low = pull(value_low, "x", 1)
-    value_behind_high = pull(value_high, "x", 3)
-    mine = prepare_call(True, after(states, key_low, key_high, value_low, value_high))
-    key_ahead_high = pull(after(key_high, key_ahead_low, mine[0]), "y", 1)
-    key_behind_low = pull(after(key_low, key_behind_high, mine[0]), "y", 3)
-    value_ahead_high = pull(after(value_high, value_ahead_low, mine[0]), "x", 1)
-    value_behind_low = pull(after(value_low, value_behind_high, mine[0]), "x", 3)
-    first_round = (key_ahead_low, key_behind_high, value_ahead_low, value_behind_high)
-    other = prepare_call(False, after(states_other, mine[0], *first_round))
+    key_line = join(key_low, key_high)
+    key_ahead = pull(key_line, "y", 1)
+    key_behind = pull(key_line, "y", 3)
+    value_line = join(value_low, value_high)
+    value_ahead = pull(value_line, "x", 1)
+    value_behind = pull(value_line, "x", 3)
+    mine = prepare_call(True, after(states, key_line, value_line))
+    other = prepare_call(False, after(states_other, mine[0]))
     ready = (mine, other)
-    key_far = (
-        pull(after(key_ahead_low, key_ahead_high, other[0]), "y", 1),
-        pull(after(key_behind_high, key_behind_low, other[0]), "y", 3),
-    )
-    value_far = (
-        pull(after(value_ahead_low, value_ahead_high, other[0]), "x", 1),
-        pull(after(value_behind_high, value_behind_low, other[0]), "x", 3),
-    )
-    second_round = (key_ahead_high, key_behind_low, value_ahead_high, value_behind_low)
-    own_key = after(key_low, *second_round)
-    own_probs, own_values = attend_call(ready, (own_key, key_high), (value_low, value_high))
-    key_near = (key_ahead_low, key_ahead_high, key_behind_low, key_behind_high)
-    value_near = (value_ahead_low, value_ahead_high, value_behind_low, value_behind_high)
-    near_probs, near_values = attend_call(ready, key_near, value_near)
-    key_far = tuple(after(b, own_probs, near_probs) for b in key_far)
-    value_blocks = (value_low, value_high, *value_near)
-
-    def first_mix(*refs):
-        first_mix_kernel(
-            refs[0:2], refs[2:4], refs[4:10], attend_refs(refs[10:], 2, 0), *refs[-2:]
-        )
-
-    far_probs, first_sum = call(
-        first_mix,
-        [shape((2, 2 * masks, span), BF16), shape((2 * masks, feature), F32)],
+    own_probs, own_values = attend_call(ready, (key_line,), (value_line,))
+    key_parts = split(after(key_ahead, own_probs), after(key_behind, own_probs))
+    key_far = (pull(key_parts[0], "y", 1), pull(key_parts[1], "y", 3))
+    value_parts = split(after(value_ahead, own_probs), after(value_behind, own_probs))
+    value_far = (pull(value_parts[0], "x", 1), pull(value_parts[1], "x", 3))
+    near_probs, near_values = attend_call(
+        ready, (key_ahead, key_behind), (value_ahead, value_behind)
+    )
+    key_far = tuple(after(b, near_probs) for b in key_far)
+    far_args = attend_args(ready, key_far, ())
+
+    def far_kernel(*refs):
+        probs_kernel(*attend_refs(refs, refs[9:11], ()), refs[-1])
+
+    far_probs = call(
+        far_kernel,
+        shape((2, 2 * masks, span), BF16),
+        far_args,
+        flops=4 * span * feature * 256,
+        exps=4 * masks * span,
+    )
+    value_far = tuple(after(b, far_probs) for b in value_far)
+
+    def mix(*refs):
+        blocks = [h for r in refs[9:12] for h in halves(r)]
+        mix_kernel(refs[:3], refs[3:5], refs[5:7], refs[7:9], blocks, refs[12])
+
+    partial = call(
+        mix,
+        shape((2 * masks, feature), F32),
         (
-            own_probs, near_probs, own_values, near_values, *value_blocks,
-            *attend_args(ready, key_far, ()),
+            own_probs, near_probs, far_probs, own_values, near_values, mine[0], other[0],
+            *value_far, value_line, value_ahead, value_behind,
         ),
-        flops=4 * span * feature * 256 + 4 * masks * feature * 6 * size,
-        exps=4 * masks * span,
-    )
-    value_far = tuple(after(b, far_probs) for b in value_far)
-
-    def last_mix(*refs):
-        last_mix_kernel(refs[:3], refs[3:5], refs[5:7], *refs[7:])
-
-    partial = call(
-        last_mix,
-        shape((2 * masks, feature), F32),
-        (own_probs, near_probs, far_probs, mine[0], other[0], *value_far, first_sum),
-        flops=4 * span * feature * 256 + 4 * masks * feature * 2 * size,
+        flops=4 * span * feature * 256 + 4 * masks * feature * 8 * size,
     )
 
     def score(*refs):

time: 83.5 us -> 79.1 us (0.947)
  starting transfers between devices: 29.9 us -> 17.6 us
  waiting for transfers between devices: 6.22 us -> 18.4 us
  blocking collectives: 25.9 us -> 22.2 us
    ppermute x12 -> x8, starting transfers between devices: 18.9 us -> 7.82 us  [pull(): lax.ppermute(array, axis, [((i + offset) % size, i) for i in range(size)])]
    ppermute x12 -> x8, waiting for transfers between devices: 0.64 us -> 11.6 us  [pull(): lax.ppermute(array, axis, [((i + offset) % size, i) for i in range(size)])]
    all_to_all x1, blocking collectives: 25.9 us -> 22.2 us  [on_device(): arrived = lax.all_to_all(placed, ('z', 'y', 'x'), 0, 0, tiled=True)]
    ppermute x2, starting transfers between devices: 6.02 us -> 4.76 us  [swap(): return lax.ppermute(array, 'core', [(0, 1), (1, 0)])]
    ppermute x4, waiting for transfers between devices: 3.85 us -> 5.04 us  [gather_line(): return (lax.ppermute(block, axes, near), lax.ppermute(block, axes, far))]
    pallas_call x8 -> x12, Pallas kernels: 20.3 us -> 19.6 us  [call(): pl.pallas_call(kernel, out_shape=outs, in_specs=[IN_PLACE] * n_any + [ON_...]
  transfers between devices with their start and end apart: 18 -> 14, of which waited for: 3 -> 7; matrix products, arithmetic and copies ran while one was open for 0% -> 0% of each run, Pallas kernels for 19% -> 20%
where the time goes in v8:
time: 79.1 us; the launch traced here: 78.9 us
  blocking collectives  22.2 us (28%)
  Pallas kernels  19.6 us (25%)
  waiting for transfers between devices  18.4 us (23%)
  starting transfers between devices  17.6 us (22%)
    all_to_all x1, blocking collectives, on_device(): arrived = lax.all_to_all(placed, ('z', 'y', 'x'), 0, 0, tiled=True)  22.2 us
    pallas_call x12, Pallas kernels, call(): pl.pallas_call(kernel, out_shape=outs, in_specs=[IN_PLACE] * n_any + [ON_...  19.6 us
    ppermute x8, waiting for transfers between devices, pull(): lax.ppermute(array, axis, [((i + offset) % size, i) for i in range(size)])  11.6 us
    ppermute x8, starting transfers between devices, pull(): lax.ppermute(array, axis, [((i + offset) % size, i) for i in range(size)])  7.82 us
    ppermute x4, waiting for transfers between devices, gather_line(): return (lax.ppermute(block, axes, near), lax.ppermute(block, axes, far))  5.04 us
    ppermute x4, starting transfers between devices, gather_line(): return (lax.ppermute(block, axes, near), lax.ppermute(block, axes, far))  4.99 us
    ppermute x2, starting transfers between devices, swap(): return lax.ppermute(array, 'core', [(0, 1), (1, 0)])  4.76 us
    ppermute x2, waiting for transfers between devices, swap(): return lax.ppermute(array, 'core', [(0, 1), (1, 0)])  1.72 us
  transfers between devices with their start and end apart: 14, of which 7 were waited for; matrix products, arithmetic and copies ran while one was open for 0% of the time, Pallas kernels for 20%

profile of v8, /device:TPU:1, one launch (start us, length us, event | category | flops | bytes accessed | tf_op | source)
XLA Modules:
  0.0 78.9 jit_solution(15164820295686270913)
XLA Ops:
  0.0 3.2 %collective-permute-start.4 = (bf16[640,1280]{1,0:T(8,128)(2,1)}, bf16[640,1280]{1,0:T(8,128)(2,1)S(1)}, u32[]{:S(2)}, u32[]{:S(2)}) collective-permute-start(bf16[640,1280]{1,0:T(8,128)(2,1)} %bitcast.14), channel_id=1, source_target_pairs={{0,16},{16,0},{1,17},{17,1},{2,18},{18,2},{3,19},{19,3},{4,20},{20... | collective-permute-start | bytes 4915208 | tf_op jit(solution)/shard_map/ppermute | solution.py:365
  3.2 1.1 %shard_map.145 = (bf16[128,1280]{1,0:T(8,128)(2,1)S(1)}, bf16[128,1280]{1,0:T(8,128)(2,1)S(1)}) custom-call(bf16[192,1280]{1,0:T(8,128)(2,1)} %bitcast.16, bf16[64,1280]{1,0:T(8,128)(2,1)} %bitcast.19), custom_call_target="tpu_custom_call" | custom-call | bytes 1310720 | tf_op jit(solution)/shard_map/pallas_call | solution.py:59
  4.4 0.1 collective-permute-start
  4.5 1.4 %collective-permute-start.1 = (bf16[128,1280]{1,0:T(8,128)(2,1)S(1)}, bf16[128,1280]{1,0:T(8,128)(2,1)S(1)}, u32[]{:S(2)}, u32[]{:S(2)}) collective-permute-start(bf16[128,1280]{1,0:T(8,128)(2,1)S(1)} %get-tuple-element.36), channel_id=1, source_target_pairs={{0,1},{1,19},{2,3},{3,17},{4,22},{5,6},{6,20},{7,4},{8,9},{9,27},{... | collective-permute-start | bytes 983048 | tf_op jit(solution)/shard_map/ppermute | solution.py:387
  5.9 0.0 collective-permute-start.2
  5.9 3.5 %collective-permute-start.3 = (bf16[128,1280]{1,0:T(8,128)(2,1)S(1)}, bf16[128,1280]{1,0:T(8,128)(2,1)S(1)}, u32[]{:S(2)}, u32[]{:S(2)}) collective-permute-start(bf16[128,1280]{1,0:T(8,128)(2,1)S(1)} %get-tuple-element.37), channel_id=1, source_target_pairs={{0,4},{1,25},{2,6},{3,27},{4,28},{5,9},{6,30},{7,11},{8,12},{9,17}... | collective-permute-start | bytes 983048 | tf_op jit(solution)/shard_map/ppermute | solution.py:387
  9.4 3.8 %collective-permute-done.low_ref = bf16[128,1280]{1,0:T(8,128)(2,1)S(1)} collective-permute-done((bf16[128,1280]{1,0:T(8,128)(2,1)S(1)}, bf16[128,1280]{1,0:T(8,128)(2,1)S(1)}, u32[]{:S(2)}, u32[]{:S(2)}) %collective-permute-start) | collective-permute-done | bytes 327712 | tf_op jit(solution)/shard_map/ppermute | solution.py:387
  13.2 1.2 %collective-permute-done.1.high_ref = bf16[128,1280]{1,0:T(8,128)(2,1)S(1)} collective-permute-done((bf16[128,1280]{1,0:T(8,128)(2,1)S(1)}, bf16[128,1280]{1,0:T(8,128)(2,1)S(1)}, u32[]{:S(2)}, u32[]{:S(2)}) %collective-permute-start.1) | collective-permute-done | bytes 327712 | tf_op jit(solution)/shard_map/ppermute | solution.py:387
  14.4 2.9 %collective-permute-start.5 = (bf16[256,1280]{1,0:T(8,128)(2,1)S(1)}, bf16[256,1280]{1,0:T(8,128)(2,1)S(1)}, u32[]{:S(2)}, u32[]{:S(2)}) collective-permute-start(bf16[256,1280]{1,0:T(8,128)(2,1)S(1)} %shard_map.146.refs_9_), channel_id=1, source_target_pairs={{4,0},{8,4},{12,8},{0,12},{5,1},{9,5},{13,9},{1,13},{6,2},{10,6},{... | collective-permute-start | bytes 1966088 | tf_op jit(solution)/shard_map/ppermute | solution.py:361
  17.3 0.0 collective-permute-start.6
  17.3 0.0 collective-permute-done.2.low_ref
  17.3 0.0 collective-permute-done.3.high_ref
  17.4 1.8 %collective-permute-start.7 = (bf16[256,1280]{1,0:T(8,128)(2,1)S(1)}, bf16[256,1280]{1,0:T(8,128)(2,1)S(1)}, u32[]{:S(2)}, u32[]{:S(2)}) collective-permute-start(bf16[256,1280]{1,0:T(8,128)(2,1)S(1)} %shard_map.147.refs_10_.refs_9_), channel_id=1, source_target_pairs={{1,0},{2,1},{3,2},{0,3},{5,4},{6,5},{7,6},{4,7},{9,8},{10,9},{11,1... | collective-permute-start | bytes 1966088 | tf_op jit(solution)/shard_map/ppermute | solution.py:361
  19.1 0.0 collective-permute-start.8
  19.1 3.5 %shard_map.148 = (bf16[640,1280]{1,0:T(8,128)(2,1)S(1)}, bf16[64,1280]{1,0:T(8,128)(2,1)S(1)}, f32[64,1280]{1,0:T(8,128)S(1)}, f32[64,256]{1,0:T(8,128)S(1)}, s3...) custom-call(s32[256]{0:T(256)} %refs_0_.3, s32[24]{0:T(128)} %refs_1_.3, s32[256]{0:T(256)} %refs_2_.3, s32[64,256]{1,0:T(8,128)} %bitcast.17, ...), custom_call_target="tpu_custom_call" | custom-call | flops 217907200 | bytes 5639264 | tf_op jit(solution)/shard_map/pallas_call | solution.py:59
  22.6 0.0 collective-permute-done.4.refs_7_
  22.6 2.8 %shard_map.149 = (bf16[640,1280]{1,0:T(8,128)(2,1)S(1)}, bf16[64,1280]{1,0:T(8,128)(2,1)S(1)}, f32[64,1280]{1,0:T(8,128)S(1)}, f32[64,256]{1,0:T(8,128)S(1)}, s32[64,128]{1,0:T(8,128)S(1)}) custom-call(s32[256]{0:T(256)} %refs_0_.3, s32[24]{0:T(128)} %refs_1_.3, s32[256]{0:T(256)} %refs_2_.3, s32[64,256]{1,0:T(8,128)} %bitcast.18, s32[24,640]{1,0:T(8,128)} %refs_4_.3, ...), custom_call_target="tpu_custom_call" | custom-call | flops 217907200 | bytes 4328544 | tf_op jit(solution)/shard_map/pallas_call | solution.py:59
  25.4 2.5 %shard_map.150 = (bf16[2,128,640]{2,1,0:T(8,128)(2,1)S(1)}, bf16[2,640,128]{2,1,0:T(8,128)(2,1)S(1)}) custom-call(f32[640,256]{1,0:T(8,128)S(1)} %get-tuple-element.43.refs_0_, bf16[640,1280]{1,0:T(8,128)(2,1)S(1)} %get-tuple-element.40.refs_1_.refs_5_, bf16[640,1280]{1,0:T(8,128)(2,1)S(1)} %get-tuple-element.44.refs_2_.refs_6_, ...), custom_call_target="tpu_custom_call" | custom-call | flops 838860800 | bytes 6422528 | tf_op jit(solution)/shard_map/pallas_call | solution.py:59
  27.9 3.1 %collective-permute-done.5.refs_9_.ahead_ref = bf16[256,1280]{1,0:T(8,128)(2,1)S(1)} collective-permute-done((bf16[256,1280]{1,0:T(8,128)(2,1)S(1)}, bf16[256,1280]{1,0:T(8,128)(2,1)S(1)}, u32[]{:S(2)}, u32[]{:S(2)}) %collective-permute-start.5) | collective-permute-done | bytes 655392 | tf_op jit(solution)/shard_map/ppermute | solution.py:361
  31.0 4.1 %collective-permute-done.6.refs_10_.behind_ref = bf16[256,1280]{1,0:T(8,128)(2,1)S(1)} collective-permute-done((bf16[256,1280]{1,0:T(8,128)(2,1)S(1)}, bf16[256,1280]{1,0:T(8,128)(2,1)S(1)}, u32[]{:S(2)}, u32[]{:S(2)}) %collective-permute-start.6) | collective-permute-done | bytes 655392 | tf_op jit(solution)/shard_map/ppermute | solution.py:361
  35.1 0.1 collective-permute-start.9
  35.2 1.5 %collective-permute-start.10 = (bf16[128,1280]{1,0:T(8,128)(2,1)S(1)}, bf16[128,1280]{1,0:T(8,128)(2,1)S(1)}, u32[]{:S(2)}, u32[]{:S(2)}) collective-permute-start(bf16[128,1280]{1,0:T(8,128)(2,1)S(1)} %get-tuple-element.57), channel_id=1, source_target_pairs={{12,0},{0,4},{4,8},{8,12},{13,1},{1,5},{5,9},{9,13},{14,2},{2,6},{... | collective-permute-start | bytes 983048 | tf_op jit(solution)/shard_map/ppermute | solution.py:361
  36.7 0.0 collective-permute-done.7.refs_11_.ahead_ref.refs_10_
  36.7 0.0 collective-permute-done.8.refs_12_.behind_ref.refs_11_
  36.7 1.6 %collective-permute-start.11 = (bf16[128,1280]{1,0:T(8,128)(2,1)S(1)}, bf16[128,1280]{1,0:T(8,128)(2,1)S(1)}, u32[]{:S(2)}, u32[]{:S(2)}) collective-permute-start(bf16[128,1280]{1,0:T(8,128)(2,1)S(1)} %get-tuple-element.63), channel_id=1, source_target_pairs={{1,0},{2,1},{3,2},{0,3},{5,4},{6,5},{7,6},{4,7},{9,8},{10,9},{11,1... | collective-permute-start | bytes 983048 | tf_op jit(solution)/shard_map/ppermute | solution.py:361
  38.4 0.0 collective-permute-start.12
  38.4 3.0 %shard_map.151 = (bf16[2,256,640]{2,1,0:T(8,128)(2,1)S(1)}, bf16[2,640,256]{2,1,0:T(8,128)(2,1)S(1)}) custom-call(f32[640,256]{1,0:T(8,128)S(1)} %get-tuple-element.43.refs_0_, bf16[640,1280]{1,0:T(8,128)(2,1)S(1)} %get-tuple-element.40.refs_1_.refs_5_, bf16[640,1280]{1,0:T(8,128)(2,1)S(1)} %get-tuple-element.44.refs_2_.refs_6_, ...), custom_call_target="tpu_custom_call" | custom-call | flops 1677721600 | bytes 8388608 | tf_op jit(solution)/shard_map/pallas_call | solution.py:59
  41.4 3.0 %collective-permute-done.9.refs_9_ = bf16[128,1280]{1,0:T(8,128)(2,1)S(1)} collective-permute-done((bf16[128,1280]{1,0:T(8,128)(2,1)S(1)}, bf16[128,1280]{1,0:T(8,128)(2,1)S(1)}, u32[]{:S(2)}, u32[]{:S(2)}) %collective-permute-start.9) | collective-permute-done | bytes 327712 | tf_op jit(solution)/shard_map/ppermute | solution.py:361
  44.3 1.5 %collective-permute-done.10.refs_10_ = bf16[128,1280]{1,0:T(8,128)(2,1)S(1)} collective-permute-done((bf16[128,1280]{1,0:T(8,128)(2,1)S(1)}, bf16[128,1280]{1,0:T(8,128)(2,1)S(1)}, u32[]{:S(2)}, u32[]{:S(2)}) %collective-permute-start.10) | collective-permute-done | bytes 327712 | tf_op jit(solution)/shard_map/ppermute | solution.py:361
  45.8 2.4 %shard_map.153.refs_2_ = bf16[2,128,640]{2,1,0:T(8,128)(2,1)S(1)} custom-call(f32[640,256]{1,0:T(8,128)S(1)} %get-tuple-element.43.refs_0_, bf16[640,1280]{1,0:T(8,128)(2,1)S(1)} %get-tuple-element.40.refs_1_.refs_5_, bf16[640,1280]{1,0:T(8,128)(2,1)S(1)} %get-tuple-element.44.refs_2_.refs_6_, bf16[64,1280]{1,0:T(8,128)(2,1)S(1)} %get-tuple-element.45.refs_3_, ...), custom_call_target="tpu_custom_call" | custom-call | flops 838860800 | bytes 5439488 | tf_op jit(solution)/shard_map/pallas_call | solution.py:59
  48.2 0.0 collective-permute-done.11.refs_7_
  48.2 0.0 collective-permute-done.12.refs_8_
  48.2 0.0 copy-start.3
  48.3 0.0 copy-start
  48.3 0.0 copy-start.1
  48.3 0.0 copy-start.2
  48.3 2.4 %shard_map.155.refs_2_ = f32[128,1280]{1,0:T(8,128)S(1)} custom-call(bf16[2,128,640]{2,1,0:T(8,128)(2,1)S(1)} %get-tuple-element.51.refs_0_, bf16[2,256,640]{2,1,0:T(8,128)(2,1)S(1)} %get-tuple-element.52.refs_1_, bf16[2,128,640]{2,1,0:T(8,128)(2,1)S(1)} %shard_map.153.refs_2_, bf16[2,640,128]{2,1,0:T(8,128)(2,1)S(1)} %get-tuple-element.59.refs_3_, ...), custom_call_target="tpu_custom_call" | custom-call | flops 1006632960 | bytes 8847360 | tf_op jit(solution)/shard_map/pallas_call | solution.py:59
  50.7 1.5 %collective-permute-start.13 = (f32[128,1280]{1,0:T(8,128)S(1)}, f32[128,1280]{1,0:T(8,128)S(1)}, u32[]{:S(2)}, u32[]{:S(2)}) collective-permute-start(f32[128,1280]{1,0:T(8,128)S(1)} %shard_map.155.refs_2_), channel_id=1, source_target_pairs={{0,16},{16,0},{1,17},{17,1},{2,18},{18,2},{3,19},{19,3},{4,20},{20... | collective-permute-start | bytes 1966088 | tf_op jit(solution)/shard_map/ppermute | solution.py:365
  52.2 0.0 copy-done.3
  52.2 1.7 %collective-permute-done.13.refs_3_ = f32[128,1280]{1,0:T(8,128)S(1)} collective-permute-done((f32[128,1280]{1,0:T(8,128)S(1)}, f32[128,1280]{1,0:T(8,128)S(1)}, u32[]{:S(2)}, u32[]{:S(2)}) %collective-permute-start.13) | collective-permute-done | bytes 655392 | tf_op jit(solution)/shard_map/ppermute | solution.py:365
  53.9 0.0 copy-done
  54.0 0.0 copy-done.1
  54.0 0.0 copy-done.2
  54.0 1.8 %shard_map.156 = f32[128,64]{1,0:T(8,128)S(1)} custom-call(f32[64,1280]{1,0:T(8,128)S(1)} %get-tuple-element.39.refs_0_, f32[64,1280]{1,0:T(8,128)S(1)} %get-tuple-element.42.refs_1_, f32[128,1280]{1,0:T(8,128)S(1)} %shard_map.155.refs_2_, f32[128,1280]{1,0:T(8,128)S(1)} %collective-permute-done.13.refs_3_, s32[64,128]{1,0:T(8,128)S(1)} %get-tuple-element.49.refs_7_.refs_4_, ...), custom_call_target="tpu_custom_call" | custom-call | flops 419430400 | bytes 5430916 | tf_op jit(solution)/shard_map/pallas_call | solution.py:59
  55.7 22.2 %all_to_all.9 = f32[128,1,64]{2,1,0:T(1,128)S(1)} all-to-all(f32[128,1,64]{2,1,0:T(1,128)S(1)} %bitcast.11), channel_id=1, replica_groups=mesh['z'=8,'core'=2,'y'=4,'x'=4] {'z','y','x'}, dimensions={0} | all-to-all | bytes 65536 | tf_op jit(solution)/shard_map/all_to_all | solution.py:534
  78.0 0.2 reduce_sum.9
  78.1 0.1 reshape.13
  78.2 0.7 copy.19
  (5 shorter events, 0.2 us)
Async XLA Ops:
  0.0 22.6 %collective-permute-start.4 = (bf16[640,1280]{1,0:T(8,128)(2,1)}, bf16[640,1280]{1,0:T(8,128)(2,1)S(1)}, u32[]{:S(2)}, u32[]{:S(2)}) collective-permute-start(bf16[640,1280]{1,0:T(8,128)(2,1)} %bitcast.14), channel_id=1, source_target_pairs={{0,16},{16,0},{1,17},{17,1},{2,18},{18,2},{3,19},{19,3},{4,20},{20... | collective-permute-start | bytes 4915208 | tf_op jit(solution)/shard_map/ppermute | solution.py:365
  4.4 8.8 %collective-permute-start = (bf16[128,1280]{1,0:T(8,128)(2,1)S(1)}, bf16[128,1280]{1,0:T(8,128)(2,1)S(1)}, u32[]{:S(2)}, u32[]{:S(2)}) collective-permute-start(bf16[128,1280]{1,0:T(8,128)(2,1)S(1)} %get-tuple-element.36), channel_id=1, source_target_pairs={{0,3},{1,17},{2,1},{3,19},{4,20},{5,4},{6,22},{7,6},{8,11},{9,25},... | collective-permute-start | bytes 983048 | tf_op jit(solution)/shard_map/ppermute | solution.py:387
  4.5 9.9 %collective-permute-start.1 = (bf16[128,1280]{1,0:T(8,128)(2,1)S(1)}, bf16[128,1280]{1,0:T(8,128)(2,1)S(1)}, u32[]{:S(2)}, u32[]{:S(2)}) collective-permute-start(bf16[128,1280]{1,0:T(8,128)(2,1)S(1)} %get-tuple-element.36), channel_id=1, source_target_pairs={{0,1},{1,19},{2,3},{3,17},{4,22},{5,6},{6,20},{7,4},{8,9},{9,27},{... | collective-permute-start | bytes 983048 | tf_op jit(solution)/shard_map/ppermute | solution.py:387
  5.9 11.4 %collective-permute-start.2 = (bf16[128,1280]{1,0:T(8,128)(2,1)S(1)}, bf16[128,1280]{1,0:T(8,128)(2,1)S(1)}, u32[]{:S(2)}, u32[]{:S(2)}) collective-permute-start(bf16[128,1280]{1,0:T(8,128)(2,1)S(1)} %get-tuple-element.37), channel_id=1, source_target_pairs={{0,12},{1,17},{2,14},{3,19},{4,20},{5,1},{6,22},{7,3},{8,4},{9,25}... | collective-permute-start | bytes 983048 | tf_op jit(solution)/shard_map/ppermute | solution.py:387
  5.9 11.4 %collective-permute-start.3 = (bf16[128,1280]{1,0:T(8,128)(2,1)S(1)}, bf16[128,1280]{1,0:T(8,128)(2,1)S(1)}, u32[]{:S(2)}, u32[]{:S(2)}) collective-permute-start(bf16[128,1280]{1,0:T(8,128)(2,1)S(1)} %get-tuple-element.37), channel_id=1, source_target_pairs={{0,4},{1,25},{2,6},{3,27},{4,28},{5,9},{6,30},{7,11},{8,12},{9,17}... | collective-permute-start | bytes 983048 | tf_op jit(solution)/shard_map/ppermute | solution.py:387
  14.4 16.6 %collective-permute-start.5 = (bf16[256,1280]{1,0:T(8,128)(2,1)S(1)}, bf16[256,1280]{1,0:T(8,128)(2,1)S(1)}, u32[]{:S(2)}, u32[]{:S(2)}) collective-permute-start(bf16[256,1280]{1,0:T(8,128)(2,1)S(1)} %shard_map.146.refs_9_), channel_id=1, source_target_pairs={{4,0},{8,4},{12,8},{0,12},{5,1},{9,5},{13,9},{1,13},{6,2},{10,6},{... | collective-permute-start | bytes 1966088 | tf_op jit(solution)/shard_map/ppermute | solution.py:361
  17.3 17.8 %collective-permute-start.6 = (bf16[256,1280]{1,0:T(8,128)(2,1)S(1)}, bf16[256,1280]{1,0:T(8,128)(2,1)S(1)}, u32[]{:S(2)}, u32[]{:S(2)}) collective-permute-start(bf16[256,1280]{1,0:T(8,128)(2,1)S(1)} %shard_map.146.refs_9_), channel_id=1, source_target_pairs={{12,0},{0,4},{4,8},{8,12},{13,1},{1,5},{5,9},{9,13},{14,2},{2,6},{... | collective-permute-start | bytes 1966088 | tf_op jit(solution)/shard_map/ppermute | solution.py:361
  17.4 19.3 %collective-permute-start.7 = (bf16[256,1280]{1,0:T(8,128)(2,1)S(1)}, bf16[256,1280]{1,0:T(8,128)(2,1)S(1)}, u32[]{:S(2)}, u32[]{:S(2)}) collective-permute-start(bf16[256,1280]{1,0:T(8,128)(2,1)S(1)} %shard_map.147.refs_10_.refs_9_), channel_id=1, source_target_pairs={{1,0},{2,1},{3,2},{0,3},{5,4},{6,5},{7,6},{4,7},{9,8},{10,9},{11,1... | collective-permute-start | bytes 1966088 | tf_op jit(solution)/shard_map/ppermute | solution.py:361
  19.1 17.5 %collective-permute-start.8 = (bf16[256,1280]{1,0:T(8,128)(2,1)S(1)}, bf16[256,1280]{1,0:T(8,128)(2,1)S(1)}, u32[]{:S(2)}, u32[]{:S(2)}) collective-permute-start(bf16[256,1280]{1,0:T(8,128)(2,1)S(1)} %shard_map.147.refs_10_.refs_9_), channel_id=1, source_target_pairs={{3,0},{0,1},{1,2},{2,3},{7,4},{4,5},{5,6},{6,7},{11,8},{8,9},{9,10... | collective-permute-start | bytes 1966088 | tf_op jit(solution)/shard_map/ppermute | solution.py:361
  35.1 9.2 %collective-permute-start.9 = (bf16[128,1280]{1,0:T(8,128)(2,1)S(1)}, bf16[128,1280]{1,0:T(8,128)(2,1)S(1)}, u32[]{:S(2)}, u32[]{:S(2)}) collective-permute-start(bf16[128,1280]{1,0:T(8,128)(2,1)S(1)} %get-tuple-element.55), channel_id=1, source_target_pairs={{4,0},{8,4},{12,8},{0,12},{5,1},{9,5},{13,9},{1,13},{6,2},{10,6},{... | collective-permute-start | bytes 983048 | tf_op jit(solution)/shard_map/ppermute | solution.py:361
  35.2 10.6 %collective-permute-start.10 = (bf16[128,1280]{1,0:T(8,128)(2,1)S(1)}, bf16[128,1280]{1,0:T(8,128)(2,1)S(1)}, u32[]{:S(2)}, u32[]{:S(2)}) collective-permute-start(bf16[128,1280]{1,0:T(8,128)(2,1)S(1)} %get-tuple-element.57), channel_id=1, source_target_pairs={{12,0},{0,4},{4,8},{8,12},{13,1},{1,5},{5,9},{9,13},{14,2},{2,6},{... | collective-permute-start | bytes 983048 | tf_op jit(solution)/shard_map/ppermute | solution.py:361
  36.7 11.5 %collective-permute-start.11 = (bf16[128,1280]{1,0:T(8,128)(2,1)S(1)}, bf16[128,1280]{1,0:T(8,128)(2,1)S(1)}, u32[]{:S(2)}, u32[]{:S(2)}) collective-permute-start(bf16[128,1280]{1,0:T(8,128)(2,1)S(1)} %get-tuple-element.63), channel_id=1, source_target_pairs={{1,0},{2,1},{3,2},{0,3},{5,4},{6,5},{7,6},{4,7},{9,8},{10,9},{11,1... | collective-permute-start | bytes 983048 | tf_op jit(solution)/shard_map/ppermute | solution.py:361
  38.4 9.9 %collective-permute-start.12 = (bf16[128,1280]{1,0:T(8,128)(2,1)S(1)}, bf16[128,1280]{1,0:T(8,128)(2,1)S(1)}, u32[]{:S(2)}, u32[]{:S(2)}) collective-permute-start(bf16[128,1280]{1,0:T(8,128)(2,1)S(1)} %get-tuple-element.65), channel_id=1, source_target_pairs={{3,0},{0,1},{1,2},{2,3},{7,4},{4,5},{5,6},{6,7},{11,8},{8,9},{9,10... | collective-permute-start | bytes 983048 | tf_op jit(solution)/shard_map/ppermute | solution.py:361
  48.2 4.0 %copy-start.3 = (f32[1280]{0:T(1024)S(1)}, f32[1280]{0:T(1024)}, u32[]{:S(2)}) copy-start(f32[1280]{0:T(1024)} %param.19) | copy-start | bytes 15364
  48.3 5.7 %copy-start = (bf16[1280,1280]{1,0:T(8,128)(2,1)S(1)}, bf16[1280,1280]{1,0:T(8,128)(2,1)}, u32[]{:S(2)}) copy-start(bf16[1280,1280]{1,0:T(8,128)(2,1)} %refs_8_.1) | copy-start | bytes 9830404
  48.3 5.7 %copy-start.1 = (bf16[1280,33]{0,1:T(8,128)(2,1)S(1)}, bf16[1280,33]{0,1:T(8,128)(2,1)}, u32[]{:S(2)}) copy-start(bf16[1280,33]{0,1:T(8,128)(2,1)} %param.21) | copy-start | bytes 253444
  48.3 5.7 %copy-start.2 = (f32[33]{0:T(128)S(1)}, f32[33]{0:T(128)}, u32[]{:S(2)}) copy-start(f32[33]{0:T(128)} %param.22) | copy-start | bytes 400
  50.7 3.2 %collective-permute-start.13 = (f32[128,1280]{1,0:T(8,128)S(1)}, f32[128,1280]{1,0:T(8,128)S(1)}, u32[]{:S(2)}, u32[]{:S(2)}) collective-permute-start(f32[128,1280]{1,0:T(8,128)S(1)} %shard_map.155.refs_2_), channel_id=1, source_target_pairs={{0,16},{16,0},{1,17},{17,1},{2,18},{18,2},{3,19},{19,3},{4,20},{20... | collective-permute-start | bytes 1966088 | tf_op jit(solution)/shard_map/ppermute | solution.py:365

commit v9 on v8

--- a/solution.py
+++ b/solution.py
@@ -292,15 +292,11 @@
     return call(join_kernel, line, (low, high))
 
 
-def split_kernel(ahead_ref, behind_ref, low_ref, high_ref):
-    rows = low_ref.shape[0]
-    low_ref[...] = ahead_ref[:rows, :]
-    high_ref[...] = behind_ref[rows:, :]
-
-
-def split(ahead, behind):
-    half = jax.ShapeDtypeStruct((ahead.shape[0] // 2, ahead.shape[1]), ahead.dtype)
-    return call(split_kernel, [half, half], (ahead, behind))
+def part(array, start, end):
+    def kernel(array_ref, part_ref):
+        part_ref[...] = array_ref[start:end, :]
+
+    return call(kernel, jax.ShapeDtypeStruct((end - start, array.shape[1]), array.dtype), (array,))
 
 
 def halves(ref):
@@ -356,6 +352,22 @@
     placed_ref[...] = placed
 
 
+def collect_kernel(arrived_ref, scores_ref):
+    own, rows = scores_ref.shape
+    total = jnp.sum(arrived_ref[...], axis=0, keepdims=True)
+    count = total.shape[1]
+    row = lax.broadcasted_iota(jnp.int32, (count, count), 0)
+    lane = lax.broadcasted_iota(jnp.int32, (count, count), 1)
+    column = jnp.sum(jnp.where(row == lane, total, 0.0), axis=1, keepdims=True)
+    row = lax.broadcasted_iota(jnp.int32, (count, rows), 0)
+    slot = lax.broadcasted_iota(jnp.int32, (count, rows), 1)
+    parts = [
+        jnp.sum(jnp.where(row == slot * own + i, column, 0.0), axis=0, keepdims=True)
+        for i in range(own)
+    ]
+    scores_ref[...] = jnp.concatenate(parts, axis=0)
+
+
 def pull(array, axis, offset):
     size = lax.axis_size(axis)
     return lax.ppermute(array, axis, [((i + offset) % size, i) for i in range(size)])
@@ -369,7 +381,7 @@
     return lax.optimization_barrier((array, *others))[0]
 
 
-def gather_line(block, axis):
+def gather_line(block, axis, reach):
     near, far = [], []
     for core in range(2):
         for y in range(4):
@@ -383,8 +395,8 @@
                 own = (x + y) % 2 == core
                 near.append((source, device(-1 if own else 0)))
                 far.append((source, device(1 if own else 2)))
-    axes = ("core", "y", "x")
-    return lax.ppermute(block, axes, near), lax.ppermute(block, axes, far)
+    pairs = far if reach else near
+    return lax.ppermute(block, ("core", "y", "x"), pairs)
 
 
 def on_device(
@@ -469,8 +481,10 @@
 
     states = hidden_states[0]
     key_block, value_block = pack(jnp.transpose(w_qkv[:, 0, :]), output_weight[:, 0, :])
-    key_low, key_high = gather_line(key_block, "x")
-    value_low, value_high = gather_line(value_block, "y")
+    key_low = gather_line(key_block, "x", False)
+    value_low = gather_line(value_block, "y", False)
+    key_high = gather_line(key_block, "x", True)
+    value_high = gather_line(value_block, "y", True)
     states_other = swap(states)
     key_line = join(key_low, key_high)
     key_ahead = pull(key_line, "y", 1)
@@ -482,10 +496,15 @@
     other = prepare_call(False, after(states_other, mine[0]))
     ready = (mine, other)
     own_probs, own_values = attend_call(ready, (key_line,), (value_line,))
-    key_parts = split(after(key_ahead, own_probs), after(key_behind, own_probs))
-    key_far = (pull(key_parts[0], "y", 1), pull(key_parts[1], "y", 3))
-    value_parts = split(after(value_ahead, own_probs), after(value_behind, own_probs))
-    value_far = (pull(value_parts[0], "x", 1), pull(value_parts[1], "x", 3))
+    rows = key_line.shape[0]
+    key_far = (
+        pull(part(after(key_ahead, own_probs), 0, rows // 2), "y", 1),
+        pull(part(after(key_behind, own_probs), rows // 2, rows), "y", 3),
+    )
+    value_far = (
+        pull(part(after(value_ahead, own_probs), 0, rows // 2), "x", 1),
+        pull(part(after(value_behind, own_probs), rows // 2, rows), "x", 3),
+    )
     near_probs, near_values = attend_call(
         ready, (key_ahead, key_behind), (value_ahead, value_behind)
     )
@@ -532,7 +551,7 @@
         flops=4 * masks * feature * feature,
     )
     arrived = lax.all_to_all(placed, ("z", "y", "x"), 0, 0, tiled=True)
-    return jnp.sum(arrived, axis=0).reshape(16, 4)
+    return call(collect_kernel, shape((4, 16), F32), (arrived,)).T
 
 
 def solution(mesh):

time: 79.1 us -> 79 us (level)
  waiting for transfers between devices: 18.4 us -> 15.6 us
  starting transfers between devices: 17.6 us -> 19.7 us
  Pallas kernels: 19.6 us -> 20.4 us
    ppermute x8, waiting for transfers between devices: 11.6 us -> 8.87 us  [pull(): lax.ppermute(array, axis, [((i + offset) % size, i) for i in range(size)])]
    ppermute x8, starting transfers between devices: 7.82 us -> 10.4 us  [pull(): lax.ppermute(array, axis, [((i + offset) % size, i) for i in range(size)])]
    pallas_call x12 -> x15, Pallas kernels: 19.6 us -> 20.4 us  [call(): pl.pallas_call(kernel, out_shape=outs, in_specs=[IN_PLACE] * n_any + [ON_...]
where the time goes in v9:
time: 79 us; the launch traced here: 78.8 us
  blocking collectives  22.9 us (29%)
  Pallas kernels  20.4 us (26%)
  starting transfers between devices  19.7 us (25%)
  waiting for transfers between devices  15.6 us (20%)
    all_to_all x1, blocking collectives, on_device(): arrived = lax.all_to_all(placed, ('z', 'y', 'x'), 0, 0, tiled=True)  22.9 us
    pallas_call x15, Pallas kernels, call(): pl.pallas_call(kernel, out_shape=outs, in_specs=[IN_PLACE] * n_any + [ON_...  20.4 us
    ppermute x8, starting transfers between devices, pull(): lax.ppermute(array, axis, [((i + offset) % size, i) for i in range(size)])  10.4 us
    ppermute x8, waiting for transfers between devices, pull(): lax.ppermute(array, axis, [((i + offset) % size, i) for i in range(size)])  8.87 us
    ppermute x4, waiting for transfers between devices, gather_line(): return lax.ppermute(block, ('core', 'y', 'x'), pairs)  5.04 us
    ppermute x4, starting transfers between devices, gather_line(): return lax.ppermute(block, ('core', 'y', 'x'), pairs)  4.99 us
    ppermute x2, starting transfers between devices, swap(): return lax.ppermute(array, 'core', [(0, 1), (1, 0)])  4.32 us
    ppermute x2, waiting for transfers between devices, swap(): return lax.ppermute(array, 'core', [(0, 1), (1, 0)])  1.72 us
  transfers between devices with their start and end apart: 14, of which 7 were waited for; matrix products, arithmetic and copies ran while one was open for 0% of the time, Pallas kernels for 20%

profile of v9, /device:TPU:1, one launch (start us, length us, event | category | flops | bytes accessed | tf_op | source)
XLA Modules:
  0.0 78.8 jit_solution(6362203094211019047)
XLA Ops:
  0.0 3.2 %collective-permute-start.4 = (bf16[640,1280]{1,0:T(8,128)(2,1)}, bf16[640,1280]{1,0:T(8,128)(2,1)S(1)}, u32[]{:S(2)}, u32[]{:S(2)}) collective-permute-start(bf16[640,1280]{1,0:T(8,128)(2,1)} %bitcast.17), channel_id=1, source_target_pairs={{0,16},{16,0},{1,17},{17,1},{2,18},{18,2},{3,19},{19,3},{4,20},{20... | collective-permute-start | bytes 4915208 | tf_op jit(solution)/shard_map/ppermute | solution.py:377
  3.2 1.1 %shard_map.145 = (bf16[128,1280]{1,0:T(8,128)(2,1)S(1)}, bf16[128,1280]{1,0:T(8,128)(2,1)S(1)}) custom-call(bf16[192,1280]{1,0:T(8,128)(2,1)} %bitcast.19, bf16[64,1280]{1,0:T(8,128)(2,1)} %bitcast.22), custom_call_target="tpu_custom_call" | custom-call | bytes 1310720 | tf_op jit(solution)/shard_map/pallas_call | solution.py:59
  4.4 0.1 collective-permute-start
  4.5 1.4 %collective-permute-start.1 = (bf16[128,1280]{1,0:T(8,128)(2,1)S(1)}, bf16[128,1280]{1,0:T(8,128)(2,1)S(1)}, u32[]{:S(2)}, u32[]{:S(2)}) collective-permute-start(bf16[128,1280]{1,0:T(8,128)(2,1)S(1)} %get-tuple-element.32), channel_id=1, source_target_pairs={{0,1},{1,19},{2,3},{3,17},{4,22},{5,6},{6,20},{7,4},{8,9},{9,27},{... | collective-permute-start | bytes 983048 | tf_op jit(solution)/shard_map/ppermute | solution.py:399
  5.9 0.0 collective-permute-start.2
  5.9 3.5 %collective-permute-start.3 = (bf16[128,1280]{1,0:T(8,128)(2,1)S(1)}, bf16[128,1280]{1,0:T(8,128)(2,1)S(1)}, u32[]{:S(2)}, u32[]{:S(2)}) collective-permute-start(bf16[128,1280]{1,0:T(8,128)(2,1)S(1)} %get-tuple-element.33), channel_id=1, source_target_pairs={{0,4},{1,25},{2,6},{3,27},{4,28},{5,9},{6,30},{7,11},{8,12},{9,17}... | collective-permute-start | bytes 983048 | tf_op jit(solution)/shard_map/ppermute | solution.py:399
  9.4 3.8 %collective-permute-done.low_ref = bf16[128,1280]{1,0:T(8,128)(2,1)S(1)} collective-permute-done((bf16[128,1280]{1,0:T(8,128)(2,1)S(1)}, bf16[128,1280]{1,0:T(8,128)(2,1)S(1)}, u32[]{:S(2)}, u32[]{:S(2)}) %collective-permute-start) | collective-permute-done | bytes 327712 | tf_op jit(solution)/shard_map/ppermute | solution.py:399
  13.2 1.2 %collective-permute-done.1.high_ref = bf16[128,1280]{1,0:T(8,128)(2,1)S(1)} collective-permute-done((bf16[128,1280]{1,0:T(8,128)(2,1)S(1)}, bf16[128,1280]{1,0:T(8,128)(2,1)S(1)}, u32[]{:S(2)}, u32[]{:S(2)}) %collective-permute-start.1) | collective-permute-done | bytes 327712 | tf_op jit(solution)/shard_map/ppermute | solution.py:399
  14.4 2.9 %collective-permute-start.5 = (bf16[256,1280]{1,0:T(8,128)(2,1)S(1)}, bf16[256,1280]{1,0:T(8,128)(2,1)S(1)}, u32[]{:S(2)}, u32[]{:S(2)}) collective-permute-start(bf16[256,1280]{1,0:T(8,128)(2,1)S(1)} %shard_map.146.refs_9_), channel_id=1, source_target_pairs={{4,0},{8,4},{12,8},{0,12},{5,1},{9,5},{13,9},{1,13},{6,2},{10,6},{... | collective-permute-start | bytes 1966088 | tf_op jit(solution)/shard_map/ppermute | solution.py:373
  17.3 0.0 collective-permute-start.6
  17.3 0.0 collective-permute-done.2.low_ref
  17.3 0.0 collective-permute-done.3.high_ref
  17.4 1.8 %collective-permute-start.7 = (bf16[256,1280]{1,0:T(8,128)(2,1)S(1)}, bf16[256,1280]{1,0:T(8,128)(2,1)S(1)}, u32[]{:S(2)}, u32[]{:S(2)}) collective-permute-start(bf16[256,1280]{1,0:T(8,128)(2,1)S(1)} %shard_map.147.refs_10_.refs_9_), channel_id=1, source_target_pairs={{1,0},{2,1},{3,2},{0,3},{5,4},{6,5},{7,6},{4,7},{9,8},{10,9},{11,1... | collective-permute-start | bytes 1966088 | tf_op jit(solution)/shard_map/ppermute | solution.py:373
  19.1 0.0 collective-permute-start.8
  19.1 3.5 %shard_map.148 = (bf16[640,1280]{1,0:T(8,128)(2,1)S(1)}, bf16[64,1280]{1,0:T(8,128)(2,1)S(1)}, f32[64,1280]{1,0:T(8,128)S(1)}, f32[64,256]{1,0:T(8,128)S(1)}, s3...) custom-call(s32[256]{0:T(256)} %refs_0_.3, s32[24]{0:T(128)} %refs_1_.3, s32[256]{0:T(256)} %refs_2_.3, s32[64,256]{1,0:T(8,128)} %bitcast.20, ...), custom_call_target="tpu_custom_call" | custom-call | flops 217907200 | bytes 5639264 | tf_op jit(solution)/shard_map/pallas_call | solution.py:59
  22.6 0.0 collective-permute-done.4.refs_7_
  22.6 2.8 %shard_map.149 = (bf16[640,1280]{1,0:T(8,128)(2,1)S(1)}, bf16[64,1280]{1,0:T(8,128)(2,1)S(1)}, f32[64,1280]{1,0:T(8,128)S(1)}, f32[64,256]{1,0:T(8,128)S(1)}, s32[64,128]{1,0:T(8,128)S(1)}) custom-call(s32[256]{0:T(256)} %refs_0_.3, s32[24]{0:T(128)} %refs_1_.3, s32[256]{0:T(256)} %refs_2_.3, s32[64,256]{1,0:T(8,128)} %bitcast.21, s32[24,640]{1,0:T(8,128)} %refs_4_.3, ...), custom_call_target="tpu_custom_call" | custom-call | flops 217907200 | bytes 4328544 | tf_op jit(solution)/shard_map/pallas_call | solution.py:59
  25.4 2.5 %shard_map.150 = (bf16[2,128,640]{2,1,0:T(8,128)(2,1)S(1)}, bf16[2,640,128]{2,1,0:T(8,128)(2,1)S(1)}) custom-call(f32[640,256]{1,0:T(8,128)S(1)} %get-tuple-element.39.refs_0_, bf16[640,1280]{1,0:T(8,128)(2,1)S(1)} %get-tuple-element.36.refs_1_.refs_5_, bf16[640,1280]{1,0:T(8,128)(2,1)S(1)} %get-tuple-element.40.refs_2_.refs_6_, ...), custom_call_target="tpu_custom_call" | custom-call | flops 838860800 | bytes 6422528 | tf_op jit(solution)/shard_map/pallas_call | solution.py:59
  27.9 3.1 %collective-permute-done.5.refs_9_.array_ref = bf16[256,1280]{1,0:T(8,128)(2,1)S(1)} collective-permute-done((bf16[256,1280]{1,0:T(8,128)(2,1)S(1)}, bf16[256,1280]{1,0:T(8,128)(2,1)S(1)}, u32[]{:S(2)}, u32[]{:S(2)}) %collective-permute-start.5) | collective-permute-done | bytes 655392 | tf_op jit(solution)/shard_map/ppermute | solution.py:373
  31.0 3.5 %collective-permute-start.9 = (bf16[128,1280]{1,0:T(8,128)(2,1)S(1)}, bf16[128,1280]{1,0:T(8,128)(2,1)S(1)}, u32[]{:S(2)}, u32[]{:S(2)}) collective-permute-start(bf16[128,1280]{1,0:T(8,128)(2,1)S(1)} %shard_map.152), channel_id=1, source_target_pairs={{4,0},{8,4},{12,8},{0,12},{5,1},{9,5},{13,9},{1,13},{6,2},{10,6},{... | collective-permute-start | bytes 983048 | tf_op jit(solution)/shard_map/ppermute | solution.py:373
  34.5 0.6 collective-permute-done.6.refs_10_.array_ref
  35.1 0.3 collective-permute-start.10
  35.4 0.0 collective-permute-done.7.refs_11_.array_ref.refs_10_
  35.4 1.9 %collective-permute-start.11 = (bf16[128,1280]{1,0:T(8,128)(2,1)S(1)}, bf16[128,1280]{1,0:T(8,128)(2,1)S(1)}, u32[]{:S(2)}, u32[]{:S(2)}) collective-permute-start(bf16[128,1280]{1,0:T(8,128)(2,1)S(1)} %shard_map.155), channel_id=1, source_target_pairs={{1,0},{2,1},{3,2},{0,3},{5,4},{6,5},{7,6},{4,7},{9,8},{10,9},{11,1... | collective-permute-start | bytes 983048 | tf_op jit(solution)/shard_map/ppermute | solution.py:373
  37.4 0.0 collective-permute-done.8.refs_12_.array_ref.refs_11_
  37.4 0.1 collective-permute-start.12
  37.5 3.0 %shard_map.151 = (bf16[2,256,640]{2,1,0:T(8,128)(2,1)S(1)}, bf16[2,640,256]{2,1,0:T(8,128)(2,1)S(1)}) custom-call(f32[640,256]{1,0:T(8,128)S(1)} %get-tuple-element.39.refs_0_, bf16[640,1280]{1,0:T(8,128)(2,1)S(1)} %get-tuple-element.36.refs_1_.refs_5_, bf16[640,1280]{1,0:T(8,128)(2,1)S(1)} %get-tuple-element.40.refs_2_.refs_6_, ...), custom_call_target="tpu_custom_call" | custom-call | flops 1677721600 | bytes 8388608 | tf_op jit(solution)/shard_map/pallas_call | solution.py:59
  40.5 1.6 %collective-permute-done.9.refs_9_ = bf16[128,1280]{1,0:T(8,128)(2,1)S(1)} collective-permute-done((bf16[128,1280]{1,0:T(8,128)(2,1)S(1)}, bf16[128,1280]{1,0:T(8,128)(2,1)S(1)}, u32[]{:S(2)}, u32[]{:S(2)}) %collective-permute-start.9) | collective-permute-done | bytes 327712 | tf_op jit(solution)/shard_map/ppermute | solution.py:373
  42.0 3.7 %collective-permute-done.10.refs_10_ = bf16[128,1280]{1,0:T(8,128)(2,1)S(1)} collective-permute-done((bf16[128,1280]{1,0:T(8,128)(2,1)S(1)}, bf16[128,1280]{1,0:T(8,128)(2,1)S(1)}, u32[]{:S(2)}, u32[]{:S(2)}) %collective-permute-start.10) | collective-permute-done | bytes 327712 | tf_op jit(solution)/shard_map/ppermute | solution.py:373
  45.7 2.4 %shard_map.154.refs_2_ = bf16[2,128,640]{2,1,0:T(8,128)(2,1)S(1)} custom-call(f32[640,256]{1,0:T(8,128)S(1)} %get-tuple-element.39.refs_0_, bf16[640,1280]{1,0:T(8,128)(2,1)S(1)} %get-tuple-element.36.refs_1_.refs_5_, bf16[640,1280]{1,0:T(8,128)(2,1)S(1)} %get-tuple-element.40.refs_2_.refs_6_, bf16[64,1280]{1,0:T(8,128)(2,1)S(1)} %get-tuple-element.41.refs_3_, ...), custom_call_target="tpu_custom_call" | custom-call | flops 838860800 | bytes 5439488 | tf_op jit(solution)/shard_map/pallas_call | solution.py:59
  48.1 0.0 collective-permute-done.11.refs_7_
  48.1 0.0 collective-permute-done.12.refs_8_
  48.1 0.0 copy-start.3
  48.1 0.0 copy-start
  48.2 0.0 copy-start.1
  48.2 0.0 copy-start.2
  48.2 2.4 %shard_map.157.refs_2_ = f32[128,1280]{1,0:T(8,128)S(1)} custom-call(bf16[2,128,640]{2,1,0:T(8,128)(2,1)S(1)} %get-tuple-element.47.refs_0_, bf16[2,256,640]{2,1,0:T(8,128)(2,1)S(1)} %get-tuple-element.48.refs_1_, bf16[2,128,640]{2,1,0:T(8,128)(2,1)S(1)} %shard_map.154.refs_2_, bf16[2,640,128]{2,1,0:T(8,128)(2,1)S(1)} %get-tuple-element.53.refs_3_, ...), custom_call_target="tpu_custom_call" | custom-call | flops 1006632960 | bytes 8847360 | tf_op jit(solution)/shard_map/pallas_call | solution.py:59
  50.6 1.1 %collective-permute-start.13 = (f32[128,1280]{1,0:T(8,128)S(1)}, f32[128,1280]{1,0:T(8,128)S(1)}, u32[]{:S(2)}, u32[]{:S(2)}) collective-permute-start(f32[128,1280]{1,0:T(8,128)S(1)} %shard_map.157.refs_2_), channel_id=1, source_target_pairs={{0,16},{16,0},{1,17},{17,1},{2,18},{18,2},{3,19},{19,3},{4,20},{20... | collective-permute-start | bytes 1966088 | tf_op jit(solution)/shard_map/ppermute | solution.py:377
  51.7 0.0 copy-done.3
  51.7 1.7 %collective-permute-done.13.refs_3_ = f32[128,1280]{1,0:T(8,128)S(1)} collective-permute-done((f32[128,1280]{1,0:T(8,128)S(1)}, f32[128,1280]{1,0:T(8,128)S(1)}, u32[]{:S(2)}, u32[]{:S(2)}) %collective-permute-start.13) | collective-permute-done | bytes 655392 | tf_op jit(solution)/shard_map/ppermute | solution.py:377
  53.4 0.0 copy-done
  53.4 0.0 copy-done.1
  53.4 0.0 copy-done.2
  53.4 1.8 %shard_map.158 = f32[128,64]{1,0:T(8,128)S(1)} custom-call(f32[64,1280]{1,0:T(8,128)S(1)} %get-tuple-element.35.refs_0_, f32[64,1280]{1,0:T(8,128)S(1)} %get-tuple-element.38.refs_1_, f32[128,1280]{1,0:T(8,128)S(1)} %shard_map.157.refs_2_, f32[128,1280]{1,0:T(8,128)S(1)} %collective-permute-done.13.refs_3_, s32[64,128]{1,0:T(8,128)S(1)} %get-tuple-element.45.refs_7_.refs_4_, ...), custom_call_target="tpu_custom_call" | custom-call | flops 419430400 | bytes 5430916 | tf_op jit(solution)/shard_map/pallas_call | solution.py:59
  55.2 22.9 %all_to_all.11 = f32[128,1,64]{2,1,0:T(1,128)S(1)} all-to-all(f32[128,1,64]{2,1,0:T(1,128)S(1)} %bitcast.13), channel_id=1, replica_groups=mesh['z'=8,'core'=2,'y'=4,'x'=4] {'z','y','x'}, dimensions={0} | all-to-all | bytes 65536 | tf_op jit(solution)/shard_map/all_to_all | solution.py:553
  78.1 0.7 shard_map.159
  (7 shorter events, 0.2 us)
Async XLA Ops:
  0.0 22.6 %collective-permute-start.4 = (bf16[640,1280]{1,0:T(8,128)(2,1)}, bf16[640,1280]{1,0:T(8,128)(2,1)S(1)}, u32[]{:S(2)}, u32[]{:S(2)}) collective-permute-start(bf16[640,1280]{1,0:T(8,128)(2,1)} %bitcast.17), channel_id=1, source_target_pairs={{0,16},{16,0},{1,17},{17,1},{2,18},{18,2},{3,19},{19,3},{4,20},{20... | collective-permute-start | bytes 4915208 | tf_op jit(solution)/shard_map/ppermute | solution.py:377
  4.4 8.8 %collective-permute-start = (bf16[128,1280]{1,0:T(8,128)(2,1)S(1)}, bf16[128,1280]{1,0:T(8,128)(2,1)S(1)}, u32[]{:S(2)}, u32[]{:S(2)}) collective-permute-start(bf16[128,1280]{1,0:T(8,128)(2,1)S(1)} %get-tuple-element.32), channel_id=1, source_target_pairs={{0,3},{1,17},{2,1},{3,19},{4,20},{5,4},{6,22},{7,6},{8,11},{9,25},... | collective-permute-start | bytes 983048 | tf_op jit(solution)/shard_map/ppermute | solution.py:399
  4.5 9.9 %collective-permute-start.1 = (bf16[128,1280]{1,0:T(8,128)(2,1)S(1)}, bf16[128,1280]{1,0:T(8,128)(2,1)S(1)}, u32[]{:S(2)}, u32[]{:S(2)}) collective-permute-start(bf16[128,1280]{1,0:T(8,128)(2,1)S(1)} %get-tuple-element.32), channel_id=1, source_target_pairs={{0,1},{1,19},{2,3},{3,17},{4,22},{5,6},{6,20},{7,4},{8,9},{9,27},{... | collective-permute-start | bytes 983048 | tf_op jit(solution)/shard_map/ppermute | solution.py:399
  5.9 11.4 %collective-permute-start.2 = (bf16[128,1280]{1,0:T(8,128)(2,1)S(1)}, bf16[128,1280]{1,0:T(8,128)(2,1)S(1)}, u32[]{:S(2)}, u32[]{:S(2)}) collective-permute-start(bf16[128,1280]{1,0:T(8,128)(2,1)S(1)} %get-tuple-element.33), channel_id=1, source_target_pairs={{0,12},{1,17},{2,14},{3,19},{4,20},{5,1},{6,22},{7,3},{8,4},{9,25}... | collective-permute-start | bytes 983048 | tf_op jit(solution)/shard_map/ppermute | solution.py:399
  5.9 11.4 %collective-permute-start.3 = (bf16[128,1280]{1,0:T(8,128)(2,1)S(1)}, bf16[128,1280]{1,0:T(8,128)(2,1)S(1)}, u32[]{:S(2)}, u32[]{:S(2)}) collective-permute-start(bf16[128,1280]{1,0:T(8,128)(2,1)S(1)} %get-tuple-element.33), channel_id=1, source_target_pairs={{0,4},{1,25},{2,6},{3,27},{4,28},{5,9},{6,30},{7,11},{8,12},{9,17}... | collective-permute-start | bytes 983048 | tf_op jit(solution)/shard_map/ppermute | solution.py:399
  14.4 16.6 %collective-permute-start.5 = (bf16[256,1280]{1,0:T(8,128)(2,1)S(1)}, bf16[256,1280]{1,0:T(8,128)(2,1)S(1)}, u32[]{:S(2)}, u32[]{:S(2)}) collective-permute-start(bf16[256,1280]{1,0:T(8,128)(2,1)S(1)} %shard_map.146.refs_9_), channel_id=1, source_target_pairs={{4,0},{8,4},{12,8},{0,12},{5,1},{9,5},{13,9},{1,13},{6,2},{10,6},{... | collective-permute-start | bytes 1966088 | tf_op jit(solution)/shard_map/ppermute | solution.py:373
  17.3 17.8 %collective-permute-start.6 = (bf16[256,1280]{1,0:T(8,128)(2,1)S(1)}, bf16[256,1280]{1,0:T(8,128)(2,1)S(1)}, u32[]{:S(2)}, u32[]{:S(2)}) collective-permute-start(bf16[256,1280]{1,0:T(8,128)(2,1)S(1)} %shard_map.146.refs_9_), channel_id=1, source_target_pairs={{12,0},{0,4},{4,8},{8,12},{13,1},{1,5},{5,9},{9,13},{14,2},{2,6},{... | collective-permute-start | bytes 1966088 | tf_op jit(solution)/shard_map/ppermute | solution.py:373
  17.4 18.0 %collective-permute-start.7 = (bf16[256,1280]{1,0:T(8,128)(2,1)S(1)}, bf16[256,1280]{1,0:T(8,128)(2,1)S(1)}, u32[]{:S(2)}, u32[]{:S(2)}) collective-permute-start(bf16[256,1280]{1,0:T(8,128)(2,1)S(1)} %shard_map.147.refs_10_.refs_9_), channel_id=1, source_target_pairs={{1,0},{2,1},{3,2},{0,3},{5,4},{6,5},{7,6},{4,7},{9,8},{10,9},{11,1... | collective-permute-start | bytes 1966088 | tf_op jit(solution)/shard_map/ppermute | solution.py:373
  19.1 18.2 %collective-permute-start.8 = (bf16[256,1280]{1,0:T(8,128)(2,1)S(1)}, bf16[256,1280]{1,0:T(8,128)(2,1)S(1)}, u32[]{:S(2)}, u32[]{:S(2)}) collective-permute-start(bf16[256,1280]{1,0:T(8,128)(2,1)S(1)} %shard_map.147.refs_10_.refs_9_), channel_id=1, source_target_pairs={{3,0},{0,1},{1,2},{2,3},{7,4},{4,5},{5,6},{6,7},{11,8},{8,9},{9,10... | collective-permute-start | bytes 1966088 | tf_op jit(solution)/shard_map/ppermute | solution.py:373
  31.0 11.0 %collective-permute-start.9 = (bf16[128,1280]{1,0:T(8,128)(2,1)S(1)}, bf16[128,1280]{1,0:T(8,128)(2,1)S(1)}, u32[]{:S(2)}, u32[]{:S(2)}) collective-permute-start(bf16[128,1280]{1,0:T(8,128)(2,1)S(1)} %shard_map.152), channel_id=1, source_target_pairs={{4,0},{8,4},{12,8},{0,12},{5,1},{9,5},{13,9},{1,13},{6,2},{10,6},{... | collective-permute-start | bytes 983048 | tf_op jit(solution)/shard_map/ppermute | solution.py:373
  35.1 10.6 %collective-permute-start.10 = (bf16[128,1280]{1,0:T(8,128)(2,1)S(1)}, bf16[128,1280]{1,0:T(8,128)(2,1)S(1)}, u32[]{:S(2)}, u32[]{:S(2)}) collective-permute-start(bf16[128,1280]{1,0:T(8,128)(2,1)S(1)} %shard_map.153), channel_id=1, source_target_pairs={{12,0},{0,4},{4,8},{8,12},{13,1},{1,5},{5,9},{9,13},{14,2},{2,6},{... | collective-permute-start | bytes 983048 | tf_op jit(solution)/shard_map/ppermute | solution.py:373
  35.4 12.7 %collective-permute-start.11 = (bf16[128,1280]{1,0:T(8,128)(2,1)S(1)}, bf16[128,1280]{1,0:T(8,128)(2,1)S(1)}, u32[]{:S(2)}, u32[]{:S(2)}) collective-permute-start(bf16[128,1280]{1,0:T(8,128)(2,1)S(1)} %shard_map.155), channel_id=1, source_target_pairs={{1,0},{2,1},{3,2},{0,3},{5,4},{6,5},{7,6},{4,7},{9,8},{10,9},{11,1... | collective-permute-start | bytes 983048 | tf_op jit(solution)/shard_map/ppermute | solution.py:373
  37.4 10.7 %collective-permute-start.12 = (bf16[128,1280]{1,0:T(8,128)(2,1)S(1)}, bf16[128,1280]{1,0:T(8,128)(2,1)S(1)}, u32[]{:S(2)}, u32[]{:S(2)}) collective-permute-start(bf16[128,1280]{1,0:T(8,128)(2,1)S(1)} %shard_map.156), channel_id=1, source_target_pairs={{3,0},{0,1},{1,2},{2,3},{7,4},{4,5},{5,6},{6,7},{11,8},{8,9},{9,10... | collective-permute-start | bytes 983048 | tf_op jit(solution)/shard_map/ppermute | solution.py:373
  48.1 3.6 %copy-start.3 = (f32[1280]{0:T(1024)S(1)}, f32[1280]{0:T(1024)}, u32[]{:S(2)}) copy-start(f32[1280]{0:T(1024)} %param.19) | copy-start | bytes 15364
  48.1 5.3 %copy-start = (bf16[1280,1280]{1,0:T(8,128)(2,1)S(1)}, bf16[1280,1280]{1,0:T(8,128)(2,1)}, u32[]{:S(2)}) copy-start(bf16[1280,1280]{1,0:T(8,128)(2,1)} %refs_8_.1) | copy-start | bytes 9830404
  48.2 5.3 %copy-start.1 = (bf16[1280,33]{0,1:T(8,128)(2,1)S(1)}, bf16[1280,33]{0,1:T(8,128)(2,1)}, u32[]{:S(2)}) copy-start(bf16[1280,33]{0,1:T(8,128)(2,1)} %param.21) | copy-start | bytes 253444
  48.2 5.2 %copy-start.2 = (f32[33]{0:T(128)S(1)}, f32[33]{0:T(128)}, u32[]{:S(2)}) copy-start(f32[33]{0:T(128)} %param.22) | copy-start | bytes 400
  50.6 2.8 %collective-permute-start.13 = (f32[128,1280]{1,0:T(8,128)S(1)}, f32[128,1280]{1,0:T(8,128)S(1)}, u32[]{:S(2)}, u32[]{:S(2)}) collective-permute-start(f32[128,1280]{1,0:T(8,128)S(1)} %shard_map.157.refs_2_), channel_id=1, source_target_pairs={{0,16},{16,0},{1,17},{17,1},{2,18},{18,2},{3,19},{19,3},{4,20},{20... | collective-permute-start | bytes 1966088 | tf_op jit(solution)/shard_map/ppermute | solution.py:377

commit v10 on v9

--- a/solution.py
+++ b/solution.py
@@ -497,9 +497,10 @@
     ready = (mine, other)
     own_probs, own_values = attend_call(ready, (key_line,), (value_line,))
     rows = key_line.shape[0]
+    cut = rows * 5 // 8
     key_far = (
-        pull(part(after(key_ahead, own_probs), 0, rows // 2), "y", 1),
-        pull(part(after(key_behind, own_probs), rows // 2, rows), "y", 3),
+        pull(part(after(key_ahead, own_probs), 0, cut), "y", 1),
+        pull(part(after(key_behind, own_probs), cut, rows), "y", 3),
     )
     value_far = (
         pull(part(after(value_ahead, own_probs), 0, rows // 2), "x", 1),
@@ -512,12 +513,16 @@
     far_args = attend_args(ready, key_far, ())
 
     def far_kernel(*refs):
-        probs_kernel(*attend_refs(refs, refs[9:11], ()), refs[-1])
+        low_ref, high_ref, line_ref = refs[9], refs[10], refs[12]
+        line_ref[:cut, :] = low_ref[...]
+        line_ref[cut:, :] = high_ref[...]
+        probs_kernel(*attend_refs(refs, halves(line_ref), ()), refs[11])
 
     far_probs = call(
         far_kernel,
         shape((2, 2 * masks, span), BF16),
         far_args,
+        scratch=[pltpu.VMEM((rows, feature), BF16)],
         flops=4 * span * feature * 256,
         exps=4 * masks * span,
     )

time: 79 us -> 79.8 us (1.010)
  starting transfers between devices: 19.7 us -> 21.4 us
  waiting for transfers between devices: 15.6 us -> 14.3 us
    ppermute x8, waiting for transfers between devices: 8.87 us -> 7.57 us  [pull(): lax.ppermute(array, axis, [((i + offset) % size, i) for i in range(size)])]
    ppermute x2, starting transfers between devices: 4.32 us -> 5.35 us  [swap(): return lax.ppermute(array, 'core', [(0, 1), (1, 0)])]
  transfers between devices with their start and end apart: 14 -> 14, of which waited for: 7 -> 5; matrix products, arithmetic and copies ran while one was open for 0% -> 0% of each run, Pallas kernels for 20% -> 19%
where the time goes in v10:
time: 79.8 us; the launch traced here: 79.6 us
  blocking collectives  23.4 us (29%)
  starting transfers between devices  21.4 us (27%)
  Pallas kernels  20.3 us (25%)
  waiting for transfers between devices  14.3 us (18%)
    all_to_all x1, blocking collectives, on_device(): arrived = lax.all_to_all(placed, ('z', 'y', 'x'), 0, 0, tiled=True)  23.4 us
    pallas_call x15, Pallas kernels, call(): pl.pallas_call(kernel, out_shape=outs, in_specs=[IN_PLACE] * n_any + [ON_...  20.3 us
    ppermute x8, starting transfers between devices, pull(): lax.ppermute(array, axis, [((i + offset) % size, i) for i in range(size)])  11.1 us
    ppermute x8, waiting for transfers between devices, pull(): lax.ppermute(array, axis, [((i + offset) % size, i) for i in range(size)])  7.57 us
    ppermute x2, starting transfers between devices, swap(): return lax.ppermute(array, 'core', [(0, 1), (1, 0)])  5.35 us
    ppermute x4, waiting for transfers between devices, gather_line(): return lax.ppermute(block, ('core', 'y', 'x'), pairs)  5.04 us
    ppermute x4, starting transfers between devices, gather_line(): return lax.ppermute(block, ('core', 'y', 'x'), pairs)  4.99 us
    ppermute x2, waiting for transfers between devices, swap(): return lax.ppermute(array, 'core', [(0, 1), (1, 0)])  1.72 us
  transfers between devices with their start and end apart: 14, of which 5 were waited for; matrix products, arithmetic and copies ran while one was open for 0% of the time, Pallas kernels for 19%

profile of v10, /device:TPU:1, one launch (start us, length us, event | category | flops | bytes accessed | tf_op | source)
XLA Modules:
  0.0 79.6 jit_solution(14816555437986144996)
XLA Ops:
  0.0 3.2 %collective-permute-start.4 = (bf16[640,1280]{1,0:T(8,128)(2,1)}, bf16[640,1280]{1,0:T(8,128)(2,1)S(1)}, u32[]{:S(2)}, u32[]{:S(2)}) collective-permute-start(bf16[640,1280]{1,0:T(8,128)(2,1)} %bitcast.17), channel_id=1, source_target_pairs={{0,16},{16,0},{1,17},{17,1},{2,18},{18,2},{3,19},{19,3},{4,20},{20... | collective-permute-start | bytes 4915208 | tf_op jit(solution)/shard_map/ppermute | solution.py:377
  3.2 1.1 %shard_map.145 = (bf16[128,1280]{1,0:T(8,128)(2,1)S(1)}, bf16[128,1280]{1,0:T(8,128)(2,1)S(1)}) custom-call(bf16[192,1280]{1,0:T(8,128)(2,1)} %bitcast.19, bf16[64,1280]{1,0:T(8,128)(2,1)} %bitcast.22), custom_call_target="tpu_custom_call" | custom-call | bytes 1310720 | tf_op jit(solution)/shard_map/pallas_call | solution.py:59
  4.4 0.1 collective-permute-start
  4.5 1.4 %collective-permute-start.1 = (bf16[128,1280]{1,0:T(8,128)(2,1)S(1)}, bf16[128,1280]{1,0:T(8,128)(2,1)S(1)}, u32[]{:S(2)}, u32[]{:S(2)}) collective-permute-start(bf16[128,1280]{1,0:T(8,128)(2,1)S(1)} %get-tuple-element.32), channel_id=1, source_target_pairs={{0,1},{1,19},{2,3},{3,17},{4,22},{5,6},{6,20},{7,4},{8,9},{9,27},{... | collective-permute-start | bytes 983048 | tf_op jit(solution)/shard_map/ppermute | solution.py:399
  5.9 0.0 collective-permute-start.2
  5.9 3.5 %collective-permute-start.3 = (bf16[128,1280]{1,0:T(8,128)(2,1)S(1)}, bf16[128,1280]{1,0:T(8,128)(2,1)S(1)}, u32[]{:S(2)}, u32[]{:S(2)}) collective-permute-start(bf16[128,1280]{1,0:T(8,128)(2,1)S(1)} %get-tuple-element.33), channel_id=1, source_target_pairs={{0,4},{1,25},{2,6},{3,27},{4,28},{5,9},{6,30},{7,11},{8,12},{9,17}... | collective-permute-start | bytes 983048 | tf_op jit(solution)/shard_map/ppermute | solution.py:399
  9.4 3.8 %collective-permute-done.low_ref = bf16[128,1280]{1,0:T(8,128)(2,1)S(1)} collective-permute-done((bf16[128,1280]{1,0:T(8,128)(2,1)S(1)}, bf16[128,1280]{1,0:T(8,128)(2,1)S(1)}, u32[]{:S(2)}, u32[]{:S(2)}) %collective-permute-start) | collective-permute-done | bytes 327712 | tf_op jit(solution)/shard_map/ppermute | solution.py:399
  13.2 1.2 %collective-permute-done.1.high_ref = bf16[128,1280]{1,0:T(8,128)(2,1)S(1)} collective-permute-done((bf16[128,1280]{1,0:T(8,128)(2,1)S(1)}, bf16[128,1280]{1,0:T(8,128)(2,1)S(1)}, u32[]{:S(2)}, u32[]{:S(2)}) %collective-permute-start.1) | collective-permute-done | bytes 327712 | tf_op jit(solution)/shard_map/ppermute | solution.py:399
  14.4 2.9 %collective-permute-start.5 = (bf16[256,1280]{1,0:T(8,128)(2,1)S(1)}, bf16[256,1280]{1,0:T(8,128)(2,1)S(1)}, u32[]{:S(2)}, u32[]{:S(2)}) collective-permute-start(bf16[256,1280]{1,0:T(8,128)(2,1)S(1)} %shard_map.146.refs_9_), channel_id=1, source_target_pairs={{4,0},{8,4},{12,8},{0,12},{5,1},{9,5},{13,9},{1,13},{6,2},{10,6},{... | collective-permute-start | bytes 1966088 | tf_op jit(solution)/shard_map/ppermute | solution.py:373
  17.3 0.0 collective-permute-done.2.low_ref
  17.3 0.0 collective-permute-done.3.high_ref
  17.4 1.8 %collective-permute-start.7 = (bf16[256,1280]{1,0:T(8,128)(2,1)S(1)}, bf16[256,1280]{1,0:T(8,128)(2,1)S(1)}, u32[]{:S(2)}, u32[]{:S(2)}) collective-permute-start(bf16[256,1280]{1,0:T(8,128)(2,1)S(1)} %shard_map.147.refs_10_.refs_9_), channel_id=1, source_target_pairs={{1,0},{2,1},{3,2},{0,3},{5,4},{6,5},{7,6},{4,7},{9,8},{10,9},{11,1... | collective-permute-start | bytes 1966088 | tf_op jit(solution)/shard_map/ppermute | solution.py:373
  19.1 0.0 collective-permute-start.8
  19.1 0.1 collective-permute-start.6
  19.2 3.5 %shard_map.148 = (bf16[640,1280]{1,0:T(8,128)(2,1)S(1)}, bf16[64,1280]{1,0:T(8,128)(2,1)S(1)}, f32[64,1280]{1,0:T(8,128)S(1)}, f32[64,256]{1,0:T(8,128)S(1)}, s3...) custom-call(s32[256]{0:T(256)} %refs_0_.3, s32[24]{0:T(128)} %refs_1_.3, s32[256]{0:T(256)} %refs_2_.3, s32[64,256]{1,0:T(8,128)} %bitcast.20, ...), custom_call_target="tpu_custom_call" | custom-call | flops 217907200 | bytes 5639264 | tf_op jit(solution)/shard_map/pallas_call | solution.py:59
  22.7 0.0 collective-permute-done.4.refs_7_
  22.7 2.8 %shard_map.149 = (bf16[640,1280]{1,0:T(8,128)(2,1)S(1)}, bf16[64,1280]{1,0:T(8,128)(2,1)S(1)}, f32[64,1280]{1,0:T(8,128)S(1)}, f32[64,256]{1,0:T(8,128)S(1)}, s32[64,128]{1,0:T(8,128)S(1)}) custom-call(s32[256]{0:T(256)} %refs_0_.3, s32[24]{0:T(128)} %refs_1_.3, s32[256]{0:T(256)} %refs_2_.3, s32[64,256]{1,0:T(8,128)} %bitcast.21, s32[24,640]{1,0:T(8,128)} %refs_4_.3, ...), custom_call_target="tpu_custom_call" | custom-call | flops 217907200 | bytes 4328544 | tf_op jit(solution)/shard_map/pallas_call | solution.py:59
  25.5 2.5 %shard_map.150 = (bf16[2,128,640]{2,1,0:T(8,128)(2,1)S(1)}, bf16[2,640,128]{2,1,0:T(8,128)(2,1)S(1)}) custom-call(f32[640,256]{1,0:T(8,128)S(1)} %get-tuple-element.39.refs_0_, bf16[640,1280]{1,0:T(8,128)(2,1)S(1)} %get-tuple-element.36.refs_1_.refs_5_, bf16[640,1280]{1,0:T(8,128)(2,1)S(1)} %get-tuple-element.40.refs_2_.refs_6_, ...), custom_call_target="tpu_custom_call" | custom-call | flops 838860800 | bytes 6422528 | tf_op jit(solution)/shard_map/pallas_call | solution.py:59
  28.0 3.0 %collective-permute-done.5.refs_9_.array_ref = bf16[256,1280]{1,0:T(8,128)(2,1)S(1)} collective-permute-done((bf16[256,1280]{1,0:T(8,128)(2,1)S(1)}, bf16[256,1280]{1,0:T(8,128)(2,1)S(1)}, u32[]{:S(2)}, u32[]{:S(2)}) %collective-permute-start.5) | collective-permute-done | bytes 655392 | tf_op jit(solution)/shard_map/ppermute | solution.py:373
  31.0 3.5 %collective-permute-start.9 = (bf16[160,1280]{1,0:T(8,128)(2,1)S(1)}, bf16[160,1280]{1,0:T(8,128)(2,1)S(1)}, u32[]{:S(2)}, u32[]{:S(2)}) collective-permute-start(bf16[160,1280]{1,0:T(8,128)(2,1)S(1)} %shard_map.152), channel_id=1, source_target_pairs={{4,0},{8,4},{12,8},{0,12},{5,1},{9,5},{13,9},{1,13},{6,2},{10,6},{... | collective-permute-start | bytes 1228808 | tf_op jit(solution)/shard_map/ppermute | solution.py:373
  34.5 0.0 collective-permute-done.7.refs_11_.array_ref.refs_10_
  34.5 2.7 %collective-permute-start.11 = (bf16[128,1280]{1,0:T(8,128)(2,1)S(1)}, bf16[128,1280]{1,0:T(8,128)(2,1)S(1)}, u32[]{:S(2)}, u32[]{:S(2)}) collective-permute-start(bf16[128,1280]{1,0:T(8,128)(2,1)S(1)} %shard_map.155), channel_id=1, source_target_pairs={{1,0},{2,1},{3,2},{0,3},{5,4},{6,5},{7,6},{4,7},{9,8},{10,9},{11,1... | collective-permute-start | bytes 983048 | tf_op jit(solution)/shard_map/ppermute | solution.py:373
  37.2 0.0 collective-permute-done.8.refs_12_.array_ref.refs_11_
  37.3 0.1 collective-permute-start.12
  37.4 0.0 collective-permute-done.6.refs_10_.array_ref
  37.4 0.1 collective-permute-start.10
  37.5 3.0 %shard_map.151 = (bf16[2,256,640]{2,1,0:T(8,128)(2,1)S(1)}, bf16[2,640,256]{2,1,0:T(8,128)(2,1)S(1)}) custom-call(f32[640,256]{1,0:T(8,128)S(1)} %get-tuple-element.39.refs_0_, bf16[640,1280]{1,0:T(8,128)(2,1)S(1)} %get-tuple-element.36.refs_1_.refs_5_, bf16[640,1280]{1,0:T(8,128)(2,1)S(1)} %get-tuple-element.40.refs_2_.refs_6_, ...), custom_call_target="tpu_custom_call" | custom-call | flops 1677721600 | bytes 8388608 | tf_op jit(solution)/shard_map/pallas_call | solution.py:59
  40.5 4.6 %collective-permute-done.10.refs_10_ = bf16[96,1280]{1,0:T(8,128)(2,1)S(1)} collective-permute-done((bf16[96,1280]{1,0:T(8,128)(2,1)S(1)}, bf16[96,1280]{1,0:T(8,128)(2,1)S(1)}, u32[]{:S(2)}, u32[]{:S(2)}) %collective-permute-start.10) | collective-permute-done | bytes 245792 | tf_op jit(solution)/shard_map/ppermute | solution.py:373
  45.0 0.0 collective-permute-done.9.refs_9_
  45.0 2.4 %shard_map.154.refs_2_ = bf16[2,128,640]{2,1,0:T(8,128)(2,1)S(1)} custom-call(f32[640,256]{1,0:T(8,128)S(1)} %get-tuple-element.39.refs_0_, bf16[640,1280]{1,0:T(8,128)(2,1)S(1)} %get-tuple-element.36.refs_1_.refs_5_, bf16[640,1280]{1,0:T(8,128)(2,1)S(1)} %get-tuple-element.40.refs_2_.refs_6_, bf16[64,1280]{1,0:T(8,128)(2,1)S(1)} %get-tuple-element.41.refs_3_, ...), custom_call_target="tpu_custom_call" | custom-call | flops 838860800 | bytes 5439488 | tf_op jit(solution)/shard_map/pallas_call | solution.py:59
  47.5 0.0 collective-permute-done.11.refs_7_
  47.5 0.0 collective-permute-done.12.refs_8_
  47.5 0.0 copy-start.3
  47.5 0.0 copy-start
  47.5 0.0 copy-start.1
  47.5 0.0 copy-start.2
  47.5 2.4 %shard_map.157.refs_2_ = f32[128,1280]{1,0:T(8,128)S(1)} custom-call(bf16[2,128,640]{2,1,0:T(8,128)(2,1)S(1)} %get-tuple-element.47.refs_0_, bf16[2,256,640]{2,1,0:T(8,128)(2,1)S(1)} %get-tuple-element.48.refs_1_, bf16[2,128,640]{2,1,0:T(8,128)(2,1)S(1)} %shard_map.154.refs_2_, bf16[2,640,128]{2,1,0:T(8,128)(2,1)S(1)} %get-tuple-element.53.refs_3_, ...), custom_call_target="tpu_custom_call" | custom-call | flops 1006632960 | bytes 8847360 | tf_op jit(solution)/shard_map/pallas_call | solution.py:59
  49.9 2.1 %collective-permute-start.13 = (f32[128,1280]{1,0:T(8,128)S(1)}, f32[128,1280]{1,0:T(8,128)S(1)}, u32[]{:S(2)}, u32[]{:S(2)}) collective-permute-start(f32[128,1280]{1,0:T(8,128)S(1)} %shard_map.157.refs_2_), channel_id=1, source_target_pairs={{0,16},{16,0},{1,17},{17,1},{2,18},{18,2},{3,19},{19,3},{4,20},{20... | collective-permute-start | bytes 1966088 | tf_op jit(solution)/shard_map/ppermute | solution.py:377
  52.0 0.0 copy-done.3
  52.1 1.7 %collective-permute-done.13.refs_3_ = f32[128,1280]{1,0:T(8,128)S(1)} collective-permute-done((f32[128,1280]{1,0:T(8,128)S(1)}, f32[128,1280]{1,0:T(8,128)S(1)}, u32[]{:S(2)}, u32[]{:S(2)}) %collective-permute-start.13) | collective-permute-done | bytes 655392 | tf_op jit(solution)/shard_map/ppermute | solution.py:377
  53.8 0.0 copy-done
  53.8 0.0 copy-done.1
  53.8 0.0 copy-done.2
  53.8 1.8 %shard_map.158 = f32[128,64]{1,0:T(8,128)S(1)} custom-call(f32[64,1280]{1,0:T(8,128)S(1)} %get-tuple-element.35.refs_0_, f32[64,1280]{1,0:T(8,128)S(1)} %get-tuple-element.38.refs_1_, f32[128,1280]{1,0:T(8,128)S(1)} %shard_map.157.refs_2_, f32[128,1280]{1,0:T(8,128)S(1)} %collective-permute-done.13.refs_3_, s32[64,128]{1,0:T(8,128)S(1)} %get-tuple-element.45.refs_7_.refs_4_, ...), custom_call_target="tpu_custom_call" | custom-call | flops 419430400 | bytes 5430916 | tf_op jit(solution)/shard_map/pallas_call | solution.py:59
  55.6 23.4 %all_to_all.11 = f32[128,1,64]{2,1,0:T(1,128)S(1)} all-to-all(f32[128,1,64]{2,1,0:T(1,128)S(1)} %bitcast.13), channel_id=1, replica_groups=mesh['z'=8,'core'=2,'y'=4,'x'=4] {'z','y','x'}, dimensions={0} | all-to-all | bytes 65536 | tf_op jit(solution)/shard_map/all_to_all | solution.py:558
  78.9 0.7 shard_map.159
  (7 shorter events, 0.2 us)
Async XLA Ops:
  0.0 22.7 %collective-permute-start.4 = (bf16[640,1280]{1,0:T(8,128)(2,1)}, bf16[640,1280]{1,0:T(8,128)(2,1)S(1)}, u32[]{:S(2)}, u32[]{:S(2)}) collective-permute-start(bf16[640,1280]{1,0:T(8,128)(2,1)} %bitcast.17), channel_id=1, source_target_pairs={{0,16},{16,0},{1,17},{17,1},{2,18},{18,2},{3,19},{19,3},{4,20},{20... | collective-permute-start | bytes 4915208 | tf_op jit(solution)/shard_map/ppermute | solution.py:377
  4.4 8.8 %collective-permute-start = (bf16[128,1280]{1,0:T(8,128)(2,1)S(1)}, bf16[128,1280]{1,0:T(8,128)(2,1)S(1)}, u32[]{:S(2)}, u32[]{:S(2)}) collective-permute-start(bf16[128,1280]{1,0:T(8,128)(2,1)S(1)} %get-tuple-element.32), channel_id=1, source_target_pairs={{0,3},{1,17},{2,1},{3,19},{4,20},{5,4},{6,22},{7,6},{8,11},{9,25},... | collective-permute-start | bytes 983048 | tf_op jit(solution)/shard_map/ppermute | solution.py:399
  4.5 9.9 %collective-permute-start.1 = (bf16[128,1280]{1,0:T(8,128)(2,1)S(1)}, bf16[128,1280]{1,0:T(8,128)(2,1)S(1)}, u32[]{:S(2)}, u32[]{:S(2)}) collective-permute-start(bf16[128,1280]{1,0:T(8,128)(2,1)S(1)} %get-tuple-element.32), channel_id=1, source_target_pairs={{0,1},{1,19},{2,3},{3,17},{4,22},{5,6},{6,20},{7,4},{8,9},{9,27},{... | collective-permute-start | bytes 983048 | tf_op jit(solution)/shard_map/ppermute | solution.py:399
  5.9 11.4 %collective-permute-start.2 = (bf16[128,1280]{1,0:T(8,128)(2,1)S(1)}, bf16[128,1280]{1,0:T(8,128)(2,1)S(1)}, u32[]{:S(2)}, u32[]{:S(2)}) collective-permute-start(bf16[128,1280]{1,0:T(8,128)(2,1)S(1)} %get-tuple-element.33), channel_id=1, source_target_pairs={{0,12},{1,17},{2,14},{3,19},{4,20},{5,1},{6,22},{7,3},{8,4},{9,25}... | collective-permute-start | bytes 983048 | tf_op jit(solution)/shard_map/ppermute | solution.py:399
  5.9 11.4 %collective-permute-start.3 = (bf16[128,1280]{1,0:T(8,128)(2,1)S(1)}, bf16[128,1280]{1,0:T(8,128)(2,1)S(1)}, u32[]{:S(2)}, u32[]{:S(2)}) collective-permute-start(bf16[128,1280]{1,0:T(8,128)(2,1)S(1)} %get-tuple-element.33), channel_id=1, source_target_pairs={{0,4},{1,25},{2,6},{3,27},{4,28},{5,9},{6,30},{7,11},{8,12},{9,17}... | collective-permute-start | bytes 983048 | tf_op jit(solution)/shard_map/ppermute | solution.py:399
  14.4 16.6 %collective-permute-start.5 = (bf16[256,1280]{1,0:T(8,128)(2,1)S(1)}, bf16[256,1280]{1,0:T(8,128)(2,1)S(1)}, u32[]{:S(2)}, u32[]{:S(2)}) collective-permute-start(bf16[256,1280]{1,0:T(8,128)(2,1)S(1)} %shard_map.146.refs_9_), channel_id=1, source_target_pairs={{4,0},{8,4},{12,8},{0,12},{5,1},{9,5},{13,9},{1,13},{6,2},{10,6},{... | collective-permute-start | bytes 1966088 | tf_op jit(solution)/shard_map/ppermute | solution.py:373
  17.4 17.2 %collective-permute-start.7 = (bf16[256,1280]{1,0:T(8,128)(2,1)S(1)}, bf16[256,1280]{1,0:T(8,128)(2,1)S(1)}, u32[]{:S(2)}, u32[]{:S(2)}) collective-permute-start(bf16[256,1280]{1,0:T(8,128)(2,1)S(1)} %shard_map.147.refs_10_.refs_9_), channel_id=1, source_target_pairs={{1,0},{2,1},{3,2},{0,3},{5,4},{6,5},{7,6},{4,7},{9,8},{10,9},{11,1... | collective-permute-start | bytes 1966088 | tf_op jit(solution)/shard_map/ppermute | solution.py:373
  19.1 18.1 %collective-permute-start.8 = (bf16[256,1280]{1,0:T(8,128)(2,1)S(1)}, bf16[256,1280]{1,0:T(8,128)(2,1)S(1)}, u32[]{:S(2)}, u32[]{:S(2)}) collective-permute-start(bf16[256,1280]{1,0:T(8,128)(2,1)S(1)} %shard_map.147.refs_10_.refs_9_), channel_id=1, source_target_pairs={{3,0},{0,1},{1,2},{2,3},{7,4},{4,5},{5,6},{6,7},{11,8},{8,9},{9,10... | collective-permute-start | bytes 1966088 | tf_op jit(solution)/shard_map/ppermute | solution.py:373
  19.1 18.2 %collective-permute-start.6 = (bf16[256,1280]{1,0:T(8,128)(2,1)S(1)}, bf16[256,1280]{1,0:T(8,128)(2,1)S(1)}, u32[]{:S(2)}, u32[]{:S(2)}) collective-permute-start(bf16[256,1280]{1,0:T(8,128)(2,1)S(1)} %shard_map.146.refs_9_), channel_id=1, source_target_pairs={{12,0},{0,4},{4,8},{8,12},{13,1},{1,5},{5,9},{9,13},{14,2},{2,6},{... | collective-permute-start | bytes 1966088 | tf_op jit(solution)/shard_map/ppermute | solution.py:373
  31.0 14.0 %collective-permute-start.9 = (bf16[160,1280]{1,0:T(8,128)(2,1)S(1)}, bf16[160,1280]{1,0:T(8,128)(2,1)S(1)}, u32[]{:S(2)}, u32[]{:S(2)}) collective-permute-start(bf16[160,1280]{1,0:T(8,128)(2,1)S(1)} %shard_map.152), channel_id=1, source_target_pairs={{4,0},{8,4},{12,8},{0,12},{5,1},{9,5},{13,9},{1,13},{6,2},{10,6},{... | collective-permute-start | bytes 1228808 | tf_op jit(solution)/shard_map/ppermute | solution.py:373
  34.5 12.9 %collective-permute-start.11 = (bf16[128,1280]{1,0:T(8,128)(2,1)S(1)}, bf16[128,1280]{1,0:T(8,128)(2,1)S(1)}, u32[]{:S(2)}, u32[]{:S(2)}) collective-permute-start(bf16[128,1280]{1,0:T(8,128)(2,1)S(1)} %shard_map.155), channel_id=1, source_target_pairs={{1,0},{2,1},{3,2},{0,3},{5,4},{6,5},{7,6},{4,7},{9,8},{10,9},{11,1... | collective-permute-start | bytes 983048 | tf_op jit(solution)/shard_map/ppermute | solution.py:373
  37.3 10.2 %collective-permute-start.12 = (bf16[128,1280]{1,0:T(8,128)(2,1)S(1)}, bf16[128,1280]{1,0:T(8,128)(2,1)S(1)}, u32[]{:S(2)}, u32[]{:S(2)}) collective-permute-start(bf16[128,1280]{1,0:T(8,128)(2,1)S(1)} %shard_map.156), channel_id=1, source_target_pairs={{3,0},{0,1},{1,2},{2,3},{7,4},{4,5},{5,6},{6,7},{11,8},{8,9},{9,10... | collective-permute-start | bytes 983048 | tf_op jit(solution)/shard_map/ppermute | solution.py:373
  37.4 7.7 %collective-permute-start.10 = (bf16[96,1280]{1,0:T(8,128)(2,1)S(1)}, bf16[96,1280]{1,0:T(8,128)(2,1)S(1)}, u32[]{:S(2)}, u32[]{:S(2)}) collective-permute-start(bf16[96,1280]{1,0:T(8,128)(2,1)S(1)} %shard_map.153), channel_id=1, source_target_pairs={{12,0},{0,4},{4,8},{8,12},{13,1},{1,5},{5,9},{9,13},{14,2},{2,6},{... | collective-permute-start | bytes 737288 | tf_op jit(solution)/shard_map/ppermute | solution.py:373
  47.5 4.6 %copy-start.3 = (f32[1280]{0:T(1024)S(1)}, f32[1280]{0:T(1024)}, u32[]{:S(2)}) copy-start(f32[1280]{0:T(1024)} %param.19) | copy-start | bytes 15364
  47.5 6.3 %copy-start = (bf16[1280,1280]{1,0:T(8,128)(2,1)S(1)}, bf16[1280,1280]{1,0:T(8,128)(2,1)}, u32[]{:S(2)}) copy-start(bf16[1280,1280]{1,0:T(8,128)(2,1)} %refs_8_.1) | copy-start | bytes 9830404
  47.5 6.3 %copy-start.1 = (bf16[1280,33]{0,1:T(8,128)(2,1)S(1)}, bf16[1280,33]{0,1:T(8,128)(2,1)}, u32[]{:S(2)}) copy-start(bf16[1280,33]{0,1:T(8,128)(2,1)} %param.21) | copy-start | bytes 253444
  47.5 6.3 %copy-start.2 = (f32[33]{0:T(128)S(1)}, f32[33]{0:T(128)}, u32[]{:S(2)}) copy-start(f32[33]{0:T(128)} %param.22) | copy-start | bytes 400
  49.9 3.8 %collective-permute-start.13 = (f32[128,1280]{1,0:T(8,128)S(1)}, f32[128,1280]{1,0:T(8,128)S(1)}, u32[]{:S(2)}, u32[]{:S(2)}) collective-permute-start(f32[128,1280]{1,0:T(8,128)S(1)} %shard_map.157.refs_2_), channel_id=1, source_target_pairs={{0,16},{16,0},{1,17},{17,1},{2,18},{18,2},{3,19},{19,3},{4,20},{20... | collective-permute-start | bytes 1966088 | tf_op jit(solution)/shard_map/ppermute | solution.py:377

commit v11 on v9

--- a/solution.py
+++ b/solution.py
@@ -67,27 +67,27 @@
     )(*args)
 
 
-def pack_kernel(turned_ref, out_ref, key_ref, value_ref, sems):
-    size = out_ref.shape[0]
-    copies = (
-        pltpu.make_async_copy(turned_ref.at[: 2 * size], key_ref, sems.at[0]),
-        pltpu.make_async_copy(turned_ref.at[2 * size :], value_ref.at[:size], sems.at[1]),
-        pltpu.make_async_copy(out_ref, value_ref.at[size:], sems.at[2]),
-    )
-    for copy in copies:
-        copy.start()
-    for copy in copies:
-        copy.wait()
-
-
-def pack(turned, out_weight):
-    size, feature = out_weight.shape
+def pack(*sources):
+    def kernel(*refs):
+        packed_ref, sems = refs[-2:]
+        copies, at = [], 0
+        for i, (ref, (_, start, end)) in enumerate(zip(refs, sources)):
+            target = packed_ref.at[at : at + end - start]
+            copies.append(pltpu.make_async_copy(ref.at[start:end], target, sems.at[i]))
+            at += end - start
+        for copy in copies:
+            copy.start()
+        for copy in copies:
+            copy.wait()
+
+    rows = sum(end - start for _, start, end in sources)
+    arrays = [array for array, _, _ in sources]
     return call(
-        pack_kernel,
-        [jax.ShapeDtypeStruct((2 * size, feature), BF16)] * 2,
-        (turned, out_weight),
-        n_any=2,
-        scratch=[pltpu.SemaphoreType.DMA((3,))],
+        kernel,
+        jax.ShapeDtypeStruct((rows, arrays[0].shape[1]), BF16),
+        arrays,
+        n_any=len(arrays),
+        scratch=[pltpu.SemaphoreType.DMA((len(arrays),))],
     )
 
 
@@ -259,7 +259,9 @@
         probs_ref[which] = probs
 
 
-def mix_kernel(probs_refs, values_refs, normed_refs, far_refs, block_refs, partial_ref):
+def mix_kernel(
+    probs_refs, values_refs, normed_refs, far_refs, block_refs, partial_ref, sent_ref
+):
     size = block_refs[0].shape[0] // 2
     masks = probs_refs[0].shape[1] // 2
     value_weight = jnp.concatenate([r[:size, :] for r in far_refs], axis=0)
@@ -278,7 +280,9 @@
             )
         )
     weight = jnp.concatenate([r[size:, :] for r in (*block_refs, *far_refs)], axis=0)
-    partial_ref[...] = nn_dot(jnp.concatenate(contexts, axis=0), weight)
+    partial = nn_dot(jnp.concatenate(contexts, axis=0), weight)
+    partial_ref[...] = partial
+    sent_ref[...] = partial.astype(BF16)
 
 
 def join_kernel(low_ref, high_ref, line_ref):
@@ -309,10 +313,11 @@
     placed_ref,
 ):
     masks = rows_refs[0].shape[0]
+    arrived = arrived_ref[...].astype(F32)
     residual = jnp.concatenate(
         [
-            rows_refs[0][...] + (partial_ref[:masks, :] + arrived_ref[masks:, :]),
-            rows_refs[1][...] + (partial_ref[masks:, :] + arrived_ref[:masks, :]),
+            rows_refs[0][...] + (partial_ref[:masks, :] + arrived[masks:, :]),
+            rows_refs[1][...] + (partial_ref[masks:, :] + arrived[:masks, :]),
         ],
         axis=0,
     )
@@ -480,7 +485,9 @@
         )
 
     states = hidden_states[0]
-    key_block, value_block = pack(jnp.transpose(w_qkv[:, 0, :]), output_weight[:, 0, :])
+    turned = jnp.transpose(w_qkv[:, 0, :])
+    key_block = pack((turned, 0, 2 * size))
+    value_block = pack((turned, 2 * size, 3 * size), (output_weight[:, 0, :], 0, size))
     key_low = gather_line(key_block, "x", False)
     value_low = gather_line(value_block, "y", False)
     key_high = gather_line(key_block, "x", True)
@@ -525,11 +532,11 @@
 
     def mix(*refs):
         blocks = [h for r in refs[9:12] for h in halves(r)]
-        mix_kernel(refs[:3], refs[3:5], refs[5:7], refs[7:9], blocks, refs[12])
-
-    partial = call(
+        mix_kernel(refs[:3], refs[3:5], refs[5:7], refs[7:9], blocks, *refs[12:])
+
+    partial, sent = call(
         mix,
-        shape((2 * masks, feature), F32),
+        [shape((2 * masks, feature), F32), shape((2 * masks, feature), BF16)],
         (
             own_probs, near_probs, far_probs, own_values, near_values, mine[0], other[0],
             *value_far, value_line, value_ahead, value_behind,
@@ -544,7 +551,7 @@
         score,
         shape((128, 64), F32),
         (
-            mine[2], other[2], partial, swap(partial), mine[4], other[4],
+            mine[2], other[2], partial, swap(sent), mine[4], other[4],
             ln_final_gain.reshape(1, -1), decoder_bias.reshape(1, -1), dense_weight,
             decoder_weight.T,
         ),

time: 79 us -> 78.5 us (level)
  waiting for transfers between devices: 15.6 us -> 13.9 us
  Pallas kernels: 20.4 us -> 21.2 us
    pallas_call x15 -> x16, Pallas kernels: 20.4 us -> 21.2 us  [call(): pl.pallas_call(kernel, out_shape=outs, in_specs=[IN_PLACE] * n_any + [ON_...]
    ppermute x8, waiting for transfers between devices: 8.87 us -> 8.06 us  [pull(): lax.ppermute(array, axis, [((i + offset) % size, i) for i in range(size)])]
  transfers between devices with their start and end apart: 14 -> 14, of which waited for: 7 -> 7; matrix products, arithmetic and copies ran while one was open for 0% -> 0% of each run, Pallas kernels for 20% -> 21%
where the time goes in v11:
time: 78.5 us; the launch traced here: 78.3 us
  blocking collectives  22.7 us (29%)
  Pallas kernels  21.2 us (27%)
  starting transfers between devices  20.3 us (26%)
  waiting for transfers between devices  13.9 us (18%)
    all_to_all x1, blocking collectives, on_device(): arrived = lax.all_to_all(placed, ('z', 'y', 'x'), 0, 0, tiled=True)  22.7 us
    pallas_call x16, Pallas kernels, call(): pl.pallas_call(kernel, out_shape=outs, in_specs=[IN_PLACE] * n_any + [ON_...  21.2 us
    ppermute x8, starting transfers between devices, pull(): lax.ppermute(array, axis, [((i + offset) % size, i) for i in range(size)])  10.3 us
    ppermute x8, waiting for transfers between devices, pull(): lax.ppermute(array, axis, [((i + offset) % size, i) for i in range(size)])  8.06 us
    ppermute x4, starting transfers between devices, gather_line(): return lax.ppermute(block, ('core', 'y', 'x'), pairs)  5.07 us
    ppermute x2, starting transfers between devices, swap(): return lax.ppermute(array, 'core', [(0, 1), (1, 0)])  4.94 us
    ppermute x4, waiting for transfers between devices, gather_line(): return lax.ppermute(block, ('core', 'y', 'x'), pairs)  4.61 us
  transfers between devices with their start and end apart: 14, of which 7 were waited for; matrix products, arithmetic and copies ran while one was open for 0% of the time, Pallas kernels for 21%

profile of v11, /device:TPU:1, one launch (start us, length us, event | category | flops | bytes accessed | tf_op | source)
XLA Modules:
  0.0 78.3 jit_solution(7858830283560763018)
XLA Ops:
  0.0 3.2 %collective-permute-start.4 = (bf16[640,1280]{1,0:T(8,128)(2,1)}, bf16[640,1280]{1,0:T(8,128)(2,1)S(1)}, u32[]{:S(2)}, u32[]{:S(2)}) collective-permute-start(bf16[640,1280]{1,0:T(8,128)(2,1)} %bitcast.19), channel_id=1, source_target_pairs={{0,16},{16,0},{1,17},{17,1},{2,18},{18,2},{3,19},{19,3},{4,20},{20... | collective-permute-start | bytes 4915208 | tf_op jit(solution)/shard_map/ppermute | solution.py:382
  3.2 1.0 %shard_map.145 = bf16[128,1280]{1,0:T(8,128)(2,1)S(1)} custom-call(bf16[192,1280]{1,0:T(8,128)(2,1)} %bitcast.17), custom_call_target="tpu_custom_call" | custom-call | bytes 819200 | tf_op jit(solution)/shard_map/pallas_call | solution.py:59
  4.2 0.1 collective-permute-start
  4.3 1.4 %collective-permute-start.1 = (bf16[128,1280]{1,0:T(8,128)(2,1)S(1)}, bf16[128,1280]{1,0:T(8,128)(2,1)S(1)}, u32[]{:S(2)}, u32[]{:S(2)}) collective-permute-start(bf16[128,1280]{1,0:T(8,128)(2,1)S(1)} %shard_map.145), channel_id=1, source_target_pairs={{0,1},{1,19},{2,3},{3,17},{4,22},{5,6},{6,20},{7,4},{8,9},{9,27},{... | collective-permute-start | bytes 983048 | tf_op jit(solution)/shard_map/ppermute | solution.py:404
  5.7 1.0 %shard_map.147 = bf16[128,1280]{1,0:T(8,128)(2,1)S(1)} custom-call(bf16[192,1280]{1,0:T(8,128)(2,1)} %bitcast.18, bf16[64,1280]{1,0:T(8,128)(2,1)} %bitcast.23), custom_call_target="tpu_custom_call" | custom-call | bytes 983040 | tf_op jit(solution)/shard_map/pallas_call | solution.py:59
  6.8 0.1 collective-permute-start.2
  6.9 3.5 %collective-permute-start.3 = (bf16[128,1280]{1,0:T(8,128)(2,1)S(1)}, bf16[128,1280]{1,0:T(8,128)(2,1)S(1)}, u32[]{:S(2)}, u32[]{:S(2)}) collective-permute-start(bf16[128,1280]{1,0:T(8,128)(2,1)S(1)} %shard_map.147), channel_id=1, source_target_pairs={{0,4},{1,25},{2,6},{3,27},{4,28},{5,9},{6,30},{7,11},{8,12},{9,17}... | collective-permute-start | bytes 983048 | tf_op jit(solution)/shard_map/ppermute | solution.py:404
  10.3 2.7 %collective-permute-done.low_ref = bf16[128,1280]{1,0:T(8,128)(2,1)S(1)} collective-permute-done((bf16[128,1280]{1,0:T(8,128)(2,1)S(1)}, bf16[128,1280]{1,0:T(8,128)(2,1)S(1)}, u32[]{:S(2)}, u32[]{:S(2)}) %collective-permute-start) | collective-permute-done | bytes 327712 | tf_op jit(solution)/shard_map/ppermute | solution.py:404
  13.1 1.2 %collective-permute-done.1.high_ref = bf16[128,1280]{1,0:T(8,128)(2,1)S(1)} collective-permute-done((bf16[128,1280]{1,0:T(8,128)(2,1)S(1)}, bf16[128,1280]{1,0:T(8,128)(2,1)S(1)}, u32[]{:S(2)}, u32[]{:S(2)}) %collective-permute-start.1) | collective-permute-done | bytes 327712 | tf_op jit(solution)/shard_map/ppermute | solution.py:404
  14.3 2.9 %collective-permute-start.5 = (bf16[256,1280]{1,0:T(8,128)(2,1)S(1)}, bf16[256,1280]{1,0:T(8,128)(2,1)S(1)}, u32[]{:S(2)}, u32[]{:S(2)}) collective-permute-start(bf16[256,1280]{1,0:T(8,128)(2,1)S(1)} %shard_map.146.refs_9_), channel_id=1, source_target_pairs={{4,0},{8,4},{12,8},{0,12},{5,1},{9,5},{13,9},{1,13},{6,2},{10,6},{... | collective-permute-start | bytes 1966088 | tf_op jit(solution)/shard_map/ppermute | solution.py:378
  17.2 0.0 collective-permute-start.6
  17.2 0.0 collective-permute-done.2.low_ref
  17.2 0.7 collective-permute-done.3.high_ref
  17.9 2.0 %collective-permute-start.7 = (bf16[256,1280]{1,0:T(8,128)(2,1)S(1)}, bf16[256,1280]{1,0:T(8,128)(2,1)S(1)}, u32[]{:S(2)}, u32[]{:S(2)}) collective-permute-start(bf16[256,1280]{1,0:T(8,128)(2,1)S(1)} %shard_map.148.refs_10_.refs_9_), channel_id=1, source_target_pairs={{1,0},{2,1},{3,2},{0,3},{5,4},{6,5},{7,6},{4,7},{9,8},{10,9},{11,1... | collective-permute-start | bytes 1966088 | tf_op jit(solution)/shard_map/ppermute | solution.py:378
  19.9 0.0 collective-permute-start.8
  19.9 3.5 %shard_map.149 = (bf16[640,1280]{1,0:T(8,128)(2,1)S(1)}, bf16[64,1280]{1,0:T(8,128)(2,1)S(1)}, f32[64,1280]{1,0:T(8,128)S(1)}, f32[64,256]{1,0:T(8,128)S(1)}, s3...) custom-call(s32[256]{0:T(256)} %refs_0_.3, s32[24]{0:T(128)} %refs_1_.3, s32[256]{0:T(256)} %refs_2_.3, s32[64,256]{1,0:T(8,128)} %bitcast.21, ...), custom_call_target="tpu_custom_call" | custom-call | flops 217907200 | bytes 5639264 | tf_op jit(solution)/shard_map/pallas_call | solution.py:59
  23.4 0.0 collective-permute-done.4.refs_7_
  23.4 2.8 %shard_map.150 = (bf16[640,1280]{1,0:T(8,128)(2,1)S(1)}, bf16[64,1280]{1,0:T(8,128)(2,1)S(1)}, f32[64,1280]{1,0:T(8,128)S(1)}, f32[64,256]{1,0:T(8,128)S(1)}, s32[64,128]{1,0:T(8,128)S(1)}) custom-call(s32[256]{0:T(256)} %refs_0_.3, s32[24]{0:T(128)} %refs_1_.3, s32[256]{0:T(256)} %refs_2_.3, s32[64,256]{1,0:T(8,128)} %bitcast.22, s32[24,640]{1,0:T(8,128)} %refs_4_.3, ...), custom_call_target="tpu_custom_call" | custom-call | flops 217907200 | bytes 4328544 | tf_op jit(solution)/shard_map/pallas_call | solution.py:59
  26.2 2.5 %shard_map.151 = (bf16[2,128,640]{2,1,0:T(8,128)(2,1)S(1)}, bf16[2,640,128]{2,1,0:T(8,128)(2,1)S(1)}) custom-call(f32[640,256]{1,0:T(8,128)S(1)} %get-tuple-element.37.refs_0_, bf16[640,1280]{1,0:T(8,128)(2,1)S(1)} %get-tuple-element.34.refs_1_.refs_5_, bf16[640,1280]{1,0:T(8,128)(2,1)S(1)} %get-tuple-element.38.refs_2_.refs_6_, ...), custom_call_target="tpu_custom_call" | custom-call | flops 838860800 | bytes 6422528 | tf_op jit(solution)/shard_map/pallas_call | solution.py:59
  28.7 3.1 %collective-permute-done.5.refs_9_.array_ref = bf16[256,1280]{1,0:T(8,128)(2,1)S(1)} collective-permute-done((bf16[256,1280]{1,0:T(8,128)(2,1)S(1)}, bf16[256,1280]{1,0:T(8,128)(2,1)S(1)}, u32[]{:S(2)}, u32[]{:S(2)}) %collective-permute-start.5) | collective-permute-done | bytes 655392 | tf_op jit(solution)/shard_map/ppermute | solution.py:378
  31.8 3.5 %collective-permute-start.9 = (bf16[128,1280]{1,0:T(8,128)(2,1)S(1)}, bf16[128,1280]{1,0:T(8,128)(2,1)S(1)}, u32[]{:S(2)}, u32[]{:S(2)}) collective-permute-start(bf16[128,1280]{1,0:T(8,128)(2,1)S(1)} %shard_map.153), channel_id=1, source_target_pairs={{4,0},{8,4},{12,8},{0,12},{5,1},{9,5},{13,9},{1,13},{6,2},{10,6},{... | collective-permute-start | bytes 983048 | tf_op jit(solution)/shard_map/ppermute | solution.py:378
  35.3 0.0 collective-permute-done.6.refs_10_.array_ref
  35.3 0.3 collective-permute-start.10
  35.6 0.0 collective-permute-done.7.refs_11_.array_ref.refs_10_
  35.6 1.6 %collective-permute-start.11 = (bf16[128,1280]{1,0:T(8,128)(2,1)S(1)}, bf16[128,1280]{1,0:T(8,128)(2,1)S(1)}, u32[]{:S(2)}, u32[]{:S(2)}) collective-permute-start(bf16[128,1280]{1,0:T(8,128)(2,1)S(1)} %shard_map.156), channel_id=1, source_target_pairs={{1,0},{2,1},{3,2},{0,3},{5,4},{6,5},{7,6},{4,7},{9,8},{10,9},{11,1... | collective-permute-start | bytes 983048 | tf_op jit(solution)/shard_map/ppermute | solution.py:378
  37.2 0.0 collective-permute-done.8.refs_12_.array_ref.refs_11_
  37.2 0.1 collective-permute-start.12
  37.3 3.0 %shard_map.152 = (bf16[2,256,640]{2,1,0:T(8,128)(2,1)S(1)}, bf16[2,640,256]{2,1,0:T(8,128)(2,1)S(1)}) custom-call(f32[640,256]{1,0:T(8,128)S(1)} %get-tuple-element.37.refs_0_, bf16[640,1280]{1,0:T(8,128)(2,1)S(1)} %get-tuple-element.34.refs_1_.refs_5_, bf16[640,1280]{1,0:T(8,128)(2,1)S(1)} %get-tuple-element.38.refs_2_.refs_6_, ...), custom_call_target="tpu_custom_call" | custom-call | flops 1677721600 | bytes 8388608 | tf_op jit(solution)/shard_map/pallas_call | solution.py:59
  40.3 1.6 %collective-permute-done.9.refs_9_ = bf16[128,1280]{1,0:T(8,128)(2,1)S(1)} collective-permute-done((bf16[128,1280]{1,0:T(8,128)(2,1)S(1)}, bf16[128,1280]{1,0:T(8,128)(2,1)S(1)}, u32[]{:S(2)}, u32[]{:S(2)}) %collective-permute-start.9) | collective-permute-done | bytes 327712 | tf_op jit(solution)/shard_map/ppermute | solution.py:378
  41.9 3.4 %collective-permute-done.10.refs_10_ = bf16[128,1280]{1,0:T(8,128)(2,1)S(1)} collective-permute-done((bf16[128,1280]{1,0:T(8,128)(2,1)S(1)}, bf16[128,1280]{1,0:T(8,128)(2,1)S(1)}, u32[]{:S(2)}, u32[]{:S(2)}) %collective-permute-start.10) | collective-permute-done | bytes 327712 | tf_op jit(solution)/shard_map/ppermute | solution.py:378
  45.3 2.4 %shard_map.155.refs_2_ = bf16[2,128,640]{2,1,0:T(8,128)(2,1)S(1)} custom-call(f32[640,256]{1,0:T(8,128)S(1)} %get-tuple-element.37.refs_0_, bf16[640,1280]{1,0:T(8,128)(2,1)S(1)} %get-tuple-element.34.refs_1_.refs_5_, bf16[640,1280]{1,0:T(8,128)(2,1)S(1)} %get-tuple-element.38.refs_2_.refs_6_, bf16[64,1280]{1,0:T(8,128)(2,1)S(1)} %get-tuple-element.39.refs_3_, ...), custom_call_target="tpu_custom_call" | custom-call | flops 838860800 | bytes 5439488 | tf_op jit(solution)/shard_map/pallas_call | solution.py:59
  47.7 0.0 collective-permute-done.11.refs_7_
  47.7 0.0 collective-permute-done.12.refs_8_
  47.7 0.0 copy-start.3
  47.8 0.0 copy-start
  47.8 0.0 copy-start.1
  47.8 0.0 copy-start.2
  47.8 2.4 %shard_map.158 = (f32[128,1280]{1,0:T(8,128)S(1)}, bf16[128,1280]{1,0:T(8,128)(2,1)S(1)}) custom-call(bf16[2,128,640]{2,1,0:T(8,128)(2,1)S(1)} %get-tuple-element.45.refs_0_, bf16[2,256,640]{2,1,0:T(8,128)(2,1)S(1)} %get-tuple-element.46.refs_1_, bf16[2,128,640]{2,1,0:T(8,128)(2,1)S(1)} %shard_map.155.refs_2_, ...), custom_call_target="tpu_custom_call" | custom-call | flops 1006632960 | bytes 9175040 | tf_op jit(solution)/shard_map/pallas_call | solution.py:59
  50.2 1.7 %collective-permute-start.13 = (bf16[128,1280]{1,0:T(8,128)(2,1)S(1)}, bf16[128,1280]{1,0:T(8,128)(2,1)S(1)}, u32[]{:S(2)}, u32[]{:S(2)}) collective-permute-start(bf16[128,1280]{1,0:T(8,128)(2,1)S(1)} %get-tuple-element.58), channel_id=1, source_target_pairs={{0,16},{16,0},{1,17},{17,1},{2,18},{18,2},{3,19},{19,3},{4,20},{20... | collective-permute-start | bytes 983048 | tf_op jit(solution)/shard_map/ppermute | solution.py:382
  51.9 0.0 copy-done.3
  51.9 1.2 %collective-permute-done.13.refs_3_ = bf16[128,1280]{1,0:T(8,128)(2,1)S(1)} collective-permute-done((bf16[128,1280]{1,0:T(8,128)(2,1)S(1)}, bf16[128,1280]{1,0:T(8,128)(2,1)S(1)}, u32[]{:S(2)}, u32[]{:S(2)}) %collective-permute-start.13) | collective-permute-done | bytes 327712 | tf_op jit(solution)/shard_map/ppermute | solution.py:382
  53.2 0.0 copy-done
  53.2 0.0 copy-done.1
  53.2 0.0 copy-done.2
  53.2 1.8 %shard_map.159 = f32[128,64]{1,0:T(8,128)S(1)} custom-call(f32[64,1280]{1,0:T(8,128)S(1)} %get-tuple-element.33.refs_0_, f32[64,1280]{1,0:T(8,128)S(1)} %get-tuple-element.36.refs_1_, f32[128,1280]{1,0:T(8,128)S(1)} %get-tuple-element.57.refs_2_, bf16[128,1280]{1,0:T(8,128)(2,1)S(1)} %collective-permute-done.13.refs_3_, ...), custom_call_target="tpu_custom_call" | custom-call | flops 419430400 | bytes 5103236 | tf_op jit(solution)/shard_map/pallas_call | solution.py:59
  55.0 22.7 %all_to_all.11 = f32[128,1,64]{2,1,0:T(1,128)S(1)} all-to-all(f32[128,1,64]{2,1,0:T(1,128)S(1)} %bitcast.13), channel_id=1, replica_groups=mesh['z'=8,'core'=2,'y'=4,'x'=4] {'z','y','x'}, dimensions={0} | all-to-all | bytes 65536 | tf_op jit(solution)/shard_map/all_to_all | solution.py:560
  77.6 0.7 shard_map.160
  (7 shorter events, 0.2 us)
Async XLA Ops:
  0.0 23.4 %collective-permute-start.4 = (bf16[640,1280]{1,0:T(8,128)(2,1)}, bf16[640,1280]{1,0:T(8,128)(2,1)S(1)}, u32[]{:S(2)}, u32[]{:S(2)}) collective-permute-start(bf16[640,1280]{1,0:T(8,128)(2,1)} %bitcast.19), channel_id=1, source_target_pairs={{0,16},{16,0},{1,17},{17,1},{2,18},{18,2},{3,19},{19,3},{4,20},{20... | collective-permute-start | bytes 4915208 | tf_op jit(solution)/shard_map/ppermute | solution.py:382
  4.2 8.8 %collective-permute-start = (bf16[128,1280]{1,0:T(8,128)(2,1)S(1)}, bf16[128,1280]{1,0:T(8,128)(2,1)S(1)}, u32[]{:S(2)}, u32[]{:S(2)}) collective-permute-start(bf16[128,1280]{1,0:T(8,128)(2,1)S(1)} %shard_map.145), channel_id=1, source_target_pairs={{0,3},{1,17},{2,1},{3,19},{4,20},{5,4},{6,22},{7,6},{8,11},{9,25},... | collective-permute-start | bytes 983048 | tf_op jit(solution)/shard_map/ppermute | solution.py:404
  4.3 9.9 %collective-permute-start.1 = (bf16[128,1280]{1,0:T(8,128)(2,1)S(1)}, bf16[128,1280]{1,0:T(8,128)(2,1)S(1)}, u32[]{:S(2)}, u32[]{:S(2)}) collective-permute-start(bf16[128,1280]{1,0:T(8,128)(2,1)S(1)} %shard_map.145), channel_id=1, source_target_pairs={{0,1},{1,19},{2,3},{3,17},{4,22},{5,6},{6,20},{7,4},{8,9},{9,27},{... | collective-permute-start | bytes 983048 | tf_op jit(solution)/shard_map/ppermute | solution.py:404
  6.8 10.4 %collective-permute-start.2 = (bf16[128,1280]{1,0:T(8,128)(2,1)S(1)}, bf16[128,1280]{1,0:T(8,128)(2,1)S(1)}, u32[]{:S(2)}, u32[]{:S(2)}) collective-permute-start(bf16[128,1280]{1,0:T(8,128)(2,1)S(1)} %shard_map.147), channel_id=1, source_target_pairs={{0,12},{1,17},{2,14},{3,19},{4,20},{5,1},{6,22},{7,3},{8,4},{9,25}... | collective-permute-start | bytes 983048 | tf_op jit(solution)/shard_map/ppermute | solution.py:404
  6.9 11.0 %collective-permute-start.3 = (bf16[128,1280]{1,0:T(8,128)(2,1)S(1)}, bf16[128,1280]{1,0:T(8,128)(2,1)S(1)}, u32[]{:S(2)}, u32[]{:S(2)}) collective-permute-start(bf16[128,1280]{1,0:T(8,128)(2,1)S(1)} %shard_map.147), channel_id=1, source_target_pairs={{0,4},{1,25},{2,6},{3,27},{4,28},{5,9},{6,30},{7,11},{8,12},{9,17}... | collective-permute-start | bytes 983048 | tf_op jit(solution)/shard_map/ppermute | solution.py:404
  14.3 17.5 %collective-permute-start.5 = (bf16[256,1280]{1,0:T(8,128)(2,1)S(1)}, bf16[256,1280]{1,0:T(8,128)(2,1)S(1)}, u32[]{:S(2)}, u32[]{:S(2)}) collective-permute-start(bf16[256,1280]{1,0:T(8,128)(2,1)S(1)} %shard_map.146.refs_9_), channel_id=1, source_target_pairs={{4,0},{8,4},{12,8},{0,12},{5,1},{9,5},{13,9},{1,13},{6,2},{10,6},{... | collective-permute-start | bytes 1966088 | tf_op jit(solution)/shard_map/ppermute | solution.py:378
  17.2 18.1 %collective-permute-start.6 = (bf16[256,1280]{1,0:T(8,128)(2,1)S(1)}, bf16[256,1280]{1,0:T(8,128)(2,1)S(1)}, u32[]{:S(2)}, u32[]{:S(2)}) collective-permute-start(bf16[256,1280]{1,0:T(8,128)(2,1)S(1)} %shard_map.146.refs_9_), channel_id=1, source_target_pairs={{12,0},{0,4},{4,8},{8,12},{13,1},{1,5},{5,9},{9,13},{14,2},{2,6},{... | collective-permute-start | bytes 1966088 | tf_op jit(solution)/shard_map/ppermute | solution.py:378
  17.9 17.7 %collective-permute-start.7 = (bf16[256,1280]{1,0:T(8,128)(2,1)S(1)}, bf16[256,1280]{1,0:T(8,128)(2,1)S(1)}, u32[]{:S(2)}, u32[]{:S(2)}) collective-permute-start(bf16[256,1280]{1,0:T(8,128)(2,1)S(1)} %shard_map.148.refs_10_.refs_9_), channel_id=1, source_target_pairs={{1,0},{2,1},{3,2},{0,3},{5,4},{6,5},{7,6},{4,7},{9,8},{10,9},{11,1... | collective-permute-start | bytes 1966088 | tf_op jit(solution)/shard_map/ppermute | solution.py:378
  19.9 17.3 %collective-permute-start.8 = (bf16[256,1280]{1,0:T(8,128)(2,1)S(1)}, bf16[256,1280]{1,0:T(8,128)(2,1)S(1)}, u32[]{:S(2)}, u32[]{:S(2)}) collective-permute-start(bf16[256,1280]{1,0:T(8,128)(2,1)S(1)} %shard_map.148.refs_10_.refs_9_), channel_id=1, source_target_pairs={{3,0},{0,1},{1,2},{2,3},{7,4},{4,5},{5,6},{6,7},{11,8},{8,9},{9,10... | collective-permute-start | bytes 1966088 | tf_op jit(solution)/shard_map/ppermute | solution.py:378
  31.8 10.1 %collective-permute-start.9 = (bf16[128,1280]{1,0:T(8,128)(2,1)S(1)}, bf16[128,1280]{1,0:T(8,128)(2,1)S(1)}, u32[]{:S(2)}, u32[]{:S(2)}) collective-permute-start(bf16[128,1280]{1,0:T(8,128)(2,1)S(1)} %shard_map.153), channel_id=1, source_target_pairs={{4,0},{8,4},{12,8},{0,12},{5,1},{9,5},{13,9},{1,13},{6,2},{10,6},{... | collective-permute-start | bytes 983048 | tf_op jit(solution)/shard_map/ppermute | solution.py:378
  35.3 10.0 %collective-permute-start.10 = (bf16[128,1280]{1,0:T(8,128)(2,1)S(1)}, bf16[128,1280]{1,0:T(8,128)(2,1)S(1)}, u32[]{:S(2)}, u32[]{:S(2)}) collective-permute-start(bf16[128,1280]{1,0:T(8,128)(2,1)S(1)} %shard_map.154), channel_id=1, source_target_pairs={{12,0},{0,4},{4,8},{8,12},{13,1},{1,5},{5,9},{9,13},{14,2},{2,6},{... | collective-permute-start | bytes 983048 | tf_op jit(solution)/shard_map/ppermute | solution.py:378
  35.6 12.1 %collective-permute-start.11 = (bf16[128,1280]{1,0:T(8,128)(2,1)S(1)}, bf16[128,1280]{1,0:T(8,128)(2,1)S(1)}, u32[]{:S(2)}, u32[]{:S(2)}) collective-permute-start(bf16[128,1280]{1,0:T(8,128)(2,1)S(1)} %shard_map.156), channel_id=1, source_target_pairs={{1,0},{2,1},{3,2},{0,3},{5,4},{6,5},{7,6},{4,7},{9,8},{10,9},{11,1... | collective-permute-start | bytes 983048 | tf_op jit(solution)/shard_map/ppermute | solution.py:378
  37.2 10.5 %collective-permute-start.12 = (bf16[128,1280]{1,0:T(8,128)(2,1)S(1)}, bf16[128,1280]{1,0:T(8,128)(2,1)S(1)}, u32[]{:S(2)}, u32[]{:S(2)}) collective-permute-start(bf16[128,1280]{1,0:T(8,128)(2,1)S(1)} %shard_map.157), channel_id=1, source_target_pairs={{3,0},{0,1},{1,2},{2,3},{7,4},{4,5},{5,6},{6,7},{11,8},{8,9},{9,10... | collective-permute-start | bytes 983048 | tf_op jit(solution)/shard_map/ppermute | solution.py:378
  47.7 4.2 %copy-start.3 = (f32[1280]{0:T(1024)S(1)}, f32[1280]{0:T(1024)}, u32[]{:S(2)}) copy-start(f32[1280]{0:T(1024)} %param.19) | copy-start | bytes 15364
  47.8 5.4 %copy-start = (bf16[1280,1280]{1,0:T(8,128)(2,1)S(1)}, bf16[1280,1280]{1,0:T(8,128)(2,1)}, u32[]{:S(2)}) copy-start(bf16[1280,1280]{1,0:T(8,128)(2,1)} %refs_8_.1) | copy-start | bytes 9830404
  47.8 5.4 %copy-start.1 = (bf16[1280,33]{0,1:T(8,128)(2,1)S(1)}, bf16[1280,33]{0,1:T(8,128)(2,1)}, u32[]{:S(2)}) copy-start(bf16[1280,33]{0,1:T(8,128)(2,1)} %param.21) | copy-start | bytes 253444
  47.8 5.4 %copy-start.2 = (f32[33]{0:T(128)S(1)}, f32[33]{0:T(128)}, u32[]{:S(2)}) copy-start(f32[33]{0:T(128)} %param.22) | copy-start | bytes 400
  50.2 3.0 %collective-permute-start.13 = (bf16[128,1280]{1,0:T(8,128)(2,1)S(1)}, bf16[128,1280]{1,0:T(8,128)(2,1)S(1)}, u32[]{:S(2)}, u32[]{:S(2)}) collective-permute-start(bf16[128,1280]{1,0:T(8,128)(2,1)S(1)} %get-tuple-element.58), channel_id=1, source_target_pairs={{0,16},{16,0},{1,17},{17,1},{2,18},{18,2},{3,19},{19,3},{4,20},{20... | collective-permute-start | bytes 983048 | tf_op jit(solution)/shard_map/ppermute | solution.py:382

commit v12 on v9

--- a/solution.py
+++ b/solution.py
@@ -259,7 +259,9 @@
         probs_ref[which] = probs
 
 
-def mix_kernel(probs_refs, values_refs, normed_refs, far_refs, block_refs, partial_ref):
+def mix_kernel(
+    probs_refs, values_refs, normed_refs, far_refs, block_refs, partial_ref, sent_ref
+):
     size = block_refs[0].shape[0] // 2
     masks = probs_refs[0].shape[1] // 2
     value_weight = jnp.concatenate([r[:size, :] for r in far_refs], axis=0)
@@ -278,7 +280,9 @@
             )
         )
     weight = jnp.concatenate([r[size:, :] for r in (*block_refs, *far_refs)], axis=0)
-    partial_ref[...] = nn_dot(jnp.concatenate(contexts, axis=0), weight)
+    partial = nn_dot(jnp.concatenate(contexts, axis=0), weight)
+    partial_ref[...] = partial
+    sent_ref[...] = partial.astype(BF16)
 
 
 def join_kernel(low_ref, high_ref, line_ref):
@@ -309,10 +313,11 @@
     placed_ref,
 ):
     masks = rows_refs[0].shape[0]
+    arrived = arrived_ref[...].astype(F32)
     residual = jnp.concatenate(
         [
-            rows_refs[0][...] + (partial_ref[:masks, :] + arrived_ref[masks:, :]),
-            rows_refs[1][...] + (partial_ref[masks:, :] + arrived_ref[:masks, :]),
+            rows_refs[0][...] + (partial_ref[:masks, :] + arrived[masks:, :]),
+            rows_refs[1][...] + (partial_ref[masks:, :] + arrived[:masks, :]),
         ],
         axis=0,
     )
@@ -485,13 +490,13 @@
     value_low = gather_line(value_block, "y", False)
     key_high = gather_line(key_block, "x", True)
     value_high = gather_line(value_block, "y", True)
-    states_other = swap(states)
     key_line = join(key_low, key_high)
     key_ahead = pull(key_line, "y", 1)
     key_behind = pull(key_line, "y", 3)
     value_line = join(value_low, value_high)
     value_ahead = pull(value_line, "x", 1)
     value_behind = pull(value_line, "x", 3)
+    states_other = swap(after(states, key_line, value_line))
     mine = prepare_call(True, after(states, key_line, value_line))
     other = prepare_call(False, after(states_other, mine[0]))
     ready = (mine, other)
@@ -525,11 +530,11 @@
 
     def mix(*refs):
         blocks = [h for r in refs[9:12] for h in halves(r)]
-        mix_kernel(refs[:3], refs[3:5], refs[5:7], refs[7:9], blocks, refs[12])
-
-    partial = call(
+        mix_kernel(refs[:3], refs[3:5], refs[5:7], refs[7:9], blocks, *refs[12:])
+
+    partial, sent = call(
         mix,
-        shape((2 * masks, feature), F32),
+        [shape((2 * masks, feature), F32), shape((2 * masks, feature), BF16)],
         (
             own_probs, near_probs, far_probs, own_values, near_values, mine[0], other[0],
             *value_far, value_line, value_ahead, value_behind,
@@ -544,7 +549,7 @@
         score,
         shape((128, 64), F32),
         (
-            mine[2], other[2], partial, swap(partial), mine[4], other[4],
+            mine[2], other[2], partial, swap(sent), mine[4], other[4],
             ln_final_gain.reshape(1, -1), decoder_bias.reshape(1, -1), dense_weight,
             decoder_weight.T,
         ),

time: 79 us -> 81.5 us (1.032)
  waiting for transfers between devices: 15.6 us -> 17.8 us
    ppermute x8, starting transfers between devices: 10.4 us -> 7.62 us  [pull(): lax.ppermute(array, axis, [((i + offset) % size, i) for i in range(size)])]
    ppermute x4, starting transfers between devices: 4.99 us -> 7.56 us  [gather_line(): return lax.ppermute(block, ('core', 'y', 'x'), pairs)]
    ppermute x4, waiting for transfers between devices: 5.04 us -> 7.47 us  [gather_line(): return lax.ppermute(block, ('core', 'y', 'x'), pairs)]
  transfers between devices with their start and end apart: 14 -> 14, of which waited for: 7 -> 6; matrix products, arithmetic and copies ran while one was open for 0% -> 0% of each run, Pallas kernels for 20% -> 18%
where the time goes in v12:
time: 81.5 us; the launch traced here: 81.3 us
  blocking collectives  23.1 us (28%)
  Pallas kernels  20.5 us (25%)
  starting transfers between devices  19.7 us (24%)
  waiting for transfers between devices  17.8 us (22%)
    all_to_all x1, blocking collectives, on_device(): arrived = lax.all_to_all(placed, ('z', 'y', 'x'), 0, 0, tiled=True)  23.1 us
    pallas_call x15, Pallas kernels, call(): pl.pallas_call(kernel, out_shape=outs, in_specs=[IN_PLACE] * n_any + [ON_...  20.5 us
    ppermute x8, waiting for transfers between devices, pull(): lax.ppermute(array, axis, [((i + offset) % size, i) for i in range(size)])  9.12 us
    ppermute x8, starting transfers between devices, pull(): lax.ppermute(array, axis, [((i + offset) % size, i) for i in range(size)])  7.62 us
    ppermute x4, starting transfers between devices, gather_line(): return lax.ppermute(block, ('core', 'y', 'x'), pairs)  7.56 us
    ppermute x4, waiting for transfers between devices, gather_line(): return lax.ppermute(block, ('core', 'y', 'x'), pairs)  7.47 us
    ppermute x2, starting transfers between devices, swap(): return lax.ppermute(array, 'core', [(0, 1), (1, 0)])  4.51 us
  transfers between devices with their start and end apart: 14, of which 6 were waited for; matrix products, arithmetic and copies ran while one was open for 0% of the time, Pallas kernels for 18%

profile of v12, /device:TPU:1, one launch (start us, length us, event | category | flops | bytes accessed | tf_op | source)
XLA Modules:
  0.0 81.3 jit_solution(6400676167540075158)
XLA Ops:
  0.0 0.0 copy-start.3
  0.0 1.2 %shard_map.145 = (bf16[128,1280]{1,0:T(8,128)(2,1)S(1)}, bf16[128,1280]{1,0:T(8,128)(2,1)S(1)}) custom-call(bf16[192,1280]{1,0:T(8,128)(2,1)} %bitcast.19, bf16[64,1280]{1,0:T(8,128)(2,1)} %bitcast.22), custom_call_target="tpu_custom_call" | custom-call | bytes 1310720 | tf_op jit(solution)/shard_map/pallas_call | solution.py:59
  1.3 3.3 %collective-permute-start = (bf16[128,1280]{1,0:T(8,128)(2,1)S(1)}, bf16[128,1280]{1,0:T(8,128)(2,1)S(1)}, u32[]{:S(2)}, u32[]{:S(2)}) collective-permute-start(bf16[128,1280]{1,0:T(8,128)(2,1)S(1)} %get-tuple-element.34), channel_id=1, source_target_pairs={{0,3},{1,17},{2,1},{3,19},{4,20},{5,4},{6,22},{7,6},{8,11},{9,25},... | collective-permute-start | bytes 983048 | tf_op jit(solution)/shard_map/ppermute | solution.py:404
  4.6 1.4 %collective-permute-start.1 = (bf16[128,1280]{1,0:T(8,128)(2,1)S(1)}, bf16[128,1280]{1,0:T(8,128)(2,1)S(1)}, u32[]{:S(2)}, u32[]{:S(2)}) collective-permute-start(bf16[128,1280]{1,0:T(8,128)(2,1)S(1)} %get-tuple-element.34), channel_id=1, source_target_pairs={{0,1},{1,19},{2,3},{3,17},{4,22},{5,6},{6,20},{7,4},{8,9},{9,27},{... | collective-permute-start | bytes 983048 | tf_op jit(solution)/shard_map/ppermute | solution.py:404
  6.0 0.0 collective-permute-start.2
  6.0 2.8 %collective-permute-start.3 = (bf16[128,1280]{1,0:T(8,128)(2,1)S(1)}, bf16[128,1280]{1,0:T(8,128)(2,1)S(1)}, u32[]{:S(2)}, u32[]{:S(2)}) collective-permute-start(bf16[128,1280]{1,0:T(8,128)(2,1)S(1)} %get-tuple-element.35), channel_id=1, source_target_pairs={{0,4},{1,25},{2,6},{3,27},{4,28},{5,9},{6,30},{7,11},{8,12},{9,17}... | collective-permute-start | bytes 983048 | tf_op jit(solution)/shard_map/ppermute | solution.py:404
  8.8 0.0 collective-permute-done.low_ref
  8.8 6.7 %collective-permute-done.1.high_ref = bf16[128,1280]{1,0:T(8,128)(2,1)S(1)} collective-permute-done((bf16[128,1280]{1,0:T(8,128)(2,1)S(1)}, bf16[128,1280]{1,0:T(8,128)(2,1)S(1)}, u32[]{:S(2)}, u32[]{:S(2)}) %collective-permute-start.1) | collective-permute-done | bytes 327712 | tf_op jit(solution)/shard_map/ppermute | solution.py:404
  15.6 0.0 collective-permute-done.2.low_ref
  15.6 0.8 collective-permute-done.3.high_ref
  16.4 0.0 copy-done.3
  16.4 2.4 %collective-permute-start.4 = (bf16[640,1280]{1,0:T(8,128)(2,1)S(1)}, bf16[640,1280]{1,0:T(8,128)(2,1)S(1)}, u32[]{:S(2)}, u32[]{:S(2)}) collective-permute-start(bf16[640,1280]{1,0:T(8,128)(2,1)S(1)} %bitcast.18), channel_id=1, source_target_pairs={{0,16},{16,0},{1,17},{17,1},{2,18},{18,2},{3,19},{19,3},{4,20},{20... | collective-permute-start | bytes 4915208 | tf_op jit(solution)/shard_map/ppermute | solution.py:382
  18.7 1.5 %collective-permute-start.5 = (bf16[256,1280]{1,0:T(8,128)(2,1)S(1)}, bf16[256,1280]{1,0:T(8,128)(2,1)S(1)}, u32[]{:S(2)}, u32[]{:S(2)}) collective-permute-start(bf16[256,1280]{1,0:T(8,128)(2,1)S(1)} %shard_map.146.refs_9_), channel_id=1, source_target_pairs={{4,0},{8,4},{12,8},{0,12},{5,1},{9,5},{13,9},{1,13},{6,2},{10,6},{... | collective-permute-start | bytes 1966088 | tf_op jit(solution)/shard_map/ppermute | solution.py:378
  20.3 0.0 collective-permute-start.6
  20.3 0.9 %collective-permute-start.7 = (bf16[256,1280]{1,0:T(8,128)(2,1)S(1)}, bf16[256,1280]{1,0:T(8,128)(2,1)S(1)}, u32[]{:S(2)}, u32[]{:S(2)}) collective-permute-start(bf16[256,1280]{1,0:T(8,128)(2,1)S(1)} %shard_map.147.refs_10_.refs_9_), channel_id=1, source_target_pairs={{1,0},{2,1},{3,2},{0,3},{5,4},{6,5},{7,6},{4,7},{9,8},{10,9},{11,1... | collective-permute-start | bytes 1966088 | tf_op jit(solution)/shard_map/ppermute | solution.py:378
  21.2 0.5 collective-permute-start.8
  21.7 3.5 %shard_map.148 = (bf16[640,1280]{1,0:T(8,128)(2,1)S(1)}, bf16[64,1280]{1,0:T(8,128)(2,1)S(1)}, f32[64,1280]{1,0:T(8,128)S(1)}, f32[64,256]{1,0:T(8,128)S(1)}, s3...) custom-call(s32[256]{0:T(256)} %refs_0_.3, s32[24]{0:T(128)} %refs_1_.3, s32[256]{0:T(256)} %refs_2_.3, s32[64,256]{1,0:T(8,128)} %bitcast.20, ...), custom_call_target="tpu_custom_call" | custom-call | flops 217907200 | bytes 5639264 | tf_op jit(solution)/shard_map/pallas_call | solution.py:59
  25.2 0.0 collective-permute-done.4.refs_7_
  25.2 2.8 %shard_map.149 = (bf16[640,1280]{1,0:T(8,128)(2,1)S(1)}, bf16[64,1280]{1,0:T(8,128)(2,1)S(1)}, f32[64,1280]{1,0:T(8,128)S(1)}, f32[64,256]{1,0:T(8,128)S(1)}, s32[64,128]{1,0:T(8,128)S(1)}) custom-call(s32[256]{0:T(256)} %refs_0_.3, s32[24]{0:T(128)} %refs_1_.3, s32[256]{0:T(256)} %refs_2_.3, s32[64,256]{1,0:T(8,128)} %bitcast.21, s32[24,640]{1,0:T(8,128)} %refs_4_.3, ...), custom_call_target="tpu_custom_call" | custom-call | flops 217907200 | bytes 4328544 | tf_op jit(solution)/shard_map/pallas_call | solution.py:59
  28.0 2.5 %shard_map.150 = (bf16[2,128,640]{2,1,0:T(8,128)(2,1)S(1)}, bf16[2,640,128]{2,1,0:T(8,128)(2,1)S(1)}) custom-call(f32[640,256]{1,0:T(8,128)S(1)} %get-tuple-element.41.refs_0_, bf16[640,1280]{1,0:T(8,128)(2,1)S(1)} %get-tuple-element.38.refs_1_.refs_5_, bf16[640,1280]{1,0:T(8,128)(2,1)S(1)} %get-tuple-element.42.refs_2_.refs_6_, ...), custom_call_target="tpu_custom_call" | custom-call | flops 838860800 | bytes 6422528 | tf_op jit(solution)/shard_map/pallas_call | solution.py:59
  30.5 4.5 %collective-permute-done.5.refs_9_.array_ref = bf16[256,1280]{1,0:T(8,128)(2,1)S(1)} collective-permute-done((bf16[256,1280]{1,0:T(8,128)(2,1)S(1)}, bf16[256,1280]{1,0:T(8,128)(2,1)S(1)}, u32[]{:S(2)}, u32[]{:S(2)}) %collective-permute-start.5) | collective-permute-done | bytes 655392 | tf_op jit(solution)/shard_map/ppermute | solution.py:378
  35.1 2.8 %collective-permute-start.9 = (bf16[128,1280]{1,0:T(8,128)(2,1)S(1)}, bf16[128,1280]{1,0:T(8,128)(2,1)S(1)}, u32[]{:S(2)}, u32[]{:S(2)}) collective-permute-start(bf16[128,1280]{1,0:T(8,128)(2,1)S(1)} %shard_map.152), channel_id=1, source_target_pairs={{4,0},{8,4},{12,8},{0,12},{5,1},{9,5},{13,9},{1,13},{6,2},{10,6},{... | collective-permute-start | bytes 983048 | tf_op jit(solution)/shard_map/ppermute | solution.py:378
  37.9 0.0 collective-permute-done.6.refs_10_.array_ref
  37.9 0.3 collective-permute-start.10
  38.2 0.0 collective-permute-done.7.refs_11_.array_ref.refs_10_
  38.2 0.1 collective-permute-start.11
  38.3 0.0 collective-permute-done.8.refs_12_.array_ref.refs_11_
  38.3 1.5 %collective-permute-start.12 = (bf16[128,1280]{1,0:T(8,128)(2,1)S(1)}, bf16[128,1280]{1,0:T(8,128)(2,1)S(1)}, u32[]{:S(2)}, u32[]{:S(2)}) collective-permute-start(bf16[128,1280]{1,0:T(8,128)(2,1)S(1)} %shard_map.156), channel_id=1, source_target_pairs={{3,0},{0,1},{1,2},{2,3},{7,4},{4,5},{5,6},{6,7},{11,8},{8,9},{9,10... | collective-permute-start | bytes 983048 | tf_op jit(solution)/shard_map/ppermute | solution.py:378
  39.8 3.0 %shard_map.151 = (bf16[2,256,640]{2,1,0:T(8,128)(2,1)S(1)}, bf16[2,640,256]{2,1,0:T(8,128)(2,1)S(1)}) custom-call(f32[640,256]{1,0:T(8,128)S(1)} %get-tuple-element.41.refs_0_, bf16[640,1280]{1,0:T(8,128)(2,1)S(1)} %get-tuple-element.38.refs_1_.refs_5_, bf16[640,1280]{1,0:T(8,128)(2,1)S(1)} %get-tuple-element.42.refs_2_.refs_6_, ...), custom_call_target="tpu_custom_call" | custom-call | flops 1677721600 | bytes 8388608 | tf_op jit(solution)/shard_map/pallas_call | solution.py:59
  42.8 1.2 %collective-permute-done.9.refs_9_ = bf16[128,1280]{1,0:T(8,128)(2,1)S(1)} collective-permute-done((bf16[128,1280]{1,0:T(8,128)(2,1)S(1)}, bf16[128,1280]{1,0:T(8,128)(2,1)S(1)}, u32[]{:S(2)}, u32[]{:S(2)}) %collective-permute-start.9) | collective-permute-done | bytes 327712 | tf_op jit(solution)/shard_map/ppermute | solution.py:378
  44.0 3.4 %collective-permute-done.10.refs_10_ = bf16[128,1280]{1,0:T(8,128)(2,1)S(1)} collective-permute-done((bf16[128,1280]{1,0:T(8,128)(2,1)S(1)}, bf16[128,1280]{1,0:T(8,128)(2,1)S(1)}, u32[]{:S(2)}, u32[]{:S(2)}) %collective-permute-start.10) | collective-permute-done | bytes 327712 | tf_op jit(solution)/shard_map/ppermute | solution.py:378
  47.4 2.4 %shard_map.154.refs_2_ = bf16[2,128,640]{2,1,0:T(8,128)(2,1)S(1)} custom-call(f32[640,256]{1,0:T(8,128)S(1)} %get-tuple-element.41.refs_0_, bf16[640,1280]{1,0:T(8,128)(2,1)S(1)} %get-tuple-element.38.refs_1_.refs_5_, bf16[640,1280]{1,0:T(8,128)(2,1)S(1)} %get-tuple-element.42.refs_2_.refs_6_, bf16[64,1280]{1,0:T(8,128)(2,1)S(1)} %get-tuple-element.43.refs_3_, ...), custom_call_target="tpu_custom_call" | custom-call | flops 838860800 | bytes 5439488 | tf_op jit(solution)/shard_map/pallas_call | solution.py:59
  49.8 0.0 collective-permute-done.11.refs_7_
  49.8 0.0 collective-permute-done.12.refs_8_
  49.8 0.0 copy-start.4
  49.9 0.0 copy-start
  49.9 0.0 copy-start.1
  49.9 0.0 copy-start.2
  49.9 2.4 %shard_map.157 = (f32[128,1280]{1,0:T(8,128)S(1)}, bf16[128,1280]{1,0:T(8,128)(2,1)S(1)}) custom-call(bf16[2,128,640]{2,1,0:T(8,128)(2,1)S(1)} %get-tuple-element.49.refs_0_, bf16[2,256,640]{2,1,0:T(8,128)(2,1)S(1)} %get-tuple-element.50.refs_1_, bf16[2,128,640]{2,1,0:T(8,128)(2,1)S(1)} %shard_map.154.refs_2_, ...), custom_call_target="tpu_custom_call" | custom-call | flops 1006632960 | bytes 9175040 | tf_op jit(solution)/shard_map/pallas_call | solution.py:59
  52.3 2.2 %collective-permute-start.13 = (bf16[128,1280]{1,0:T(8,128)(2,1)S(1)}, bf16[128,1280]{1,0:T(8,128)(2,1)S(1)}, u32[]{:S(2)}, u32[]{:S(2)}) collective-permute-start(bf16[128,1280]{1,0:T(8,128)(2,1)S(1)} %get-tuple-element.62), channel_id=1, source_target_pairs={{0,16},{16,0},{1,17},{17,1},{2,18},{18,2},{3,19},{19,3},{4,20},{20... | collective-permute-start | bytes 983048 | tf_op jit(solution)/shard_map/ppermute | solution.py:382
  54.5 0.0 copy-done.4
  54.5 1.2 %collective-permute-done.13.refs_3_ = bf16[128,1280]{1,0:T(8,128)(2,1)S(1)} collective-permute-done((bf16[128,1280]{1,0:T(8,128)(2,1)S(1)}, bf16[128,1280]{1,0:T(8,128)(2,1)S(1)}, u32[]{:S(2)}, u32[]{:S(2)}) %collective-permute-start.13) | collective-permute-done | bytes 327712 | tf_op jit(solution)/shard_map/ppermute | solution.py:382
  55.7 0.0 copy-done
  55.7 0.0 copy-done.1
  55.7 0.0 copy-done.2
  55.7 1.8 %shard_map.158 = f32[128,64]{1,0:T(8,128)S(1)} custom-call(f32[64,1280]{1,0:T(8,128)S(1)} %get-tuple-element.37.refs_0_, f32[64,1280]{1,0:T(8,128)S(1)} %get-tuple-element.40.refs_1_, f32[128,1280]{1,0:T(8,128)S(1)} %get-tuple-element.61.refs_2_, bf16[128,1280]{1,0:T(8,128)(2,1)S(1)} %collective-permute-done.13.refs_3_, ...), custom_call_target="tpu_custom_call" | custom-call | flops 419430400 | bytes 5103236 | tf_op jit(solution)/shard_map/pallas_call | solution.py:59
  57.5 23.1 %all_to_all.11 = f32[128,1,64]{2,1,0:T(1,128)S(1)} all-to-all(f32[128,1,64]{2,1,0:T(1,128)S(1)} %bitcast.13), channel_id=1, replica_groups=mesh['z'=8,'core'=2,'y'=4,'x'=4] {'z','y','x'}, dimensions={0} | all-to-all | bytes 65536 | tf_op jit(solution)/shard_map/all_to_all | solution.py:558
  80.6 0.7 shard_map.159
  (7 shorter events, 0.2 us)
Async XLA Ops:
  0.0 16.4 %copy-start.3 = (bf16[1,640,1280]{2,1,0:T(8,128)(2,1)S(1)}, bf16[1,640,1280]{2,1,0:T(8,128)(2,1)}, u32[]{:S(2)}) copy-start(bf16[1,640,1280]{2,1,0:T(8,128)(2,1)} %param.15) | copy-start | bytes 4915204
  1.3 7.6 %collective-permute-start = (bf16[128,1280]{1,0:T(8,128)(2,1)S(1)}, bf16[128,1280]{1,0:T(8,128)(2,1)S(1)}, u32[]{:S(2)}, u32[]{:S(2)}) collective-permute-start(bf16[128,1280]{1,0:T(8,128)(2,1)S(1)} %get-tuple-element.34), channel_id=1, source_target_pairs={{0,3},{1,17},{2,1},{3,19},{4,20},{5,4},{6,22},{7,6},{8,11},{9,25},... | collective-permute-start | bytes 983048 | tf_op jit(solution)/shard_map/ppermute | solution.py:404
  4.6 10.9 %collective-permute-start.1 = (bf16[128,1280]{1,0:T(8,128)(2,1)S(1)}, bf16[128,1280]{1,0:T(8,128)(2,1)S(1)}, u32[]{:S(2)}, u32[]{:S(2)}) collective-permute-start(bf16[128,1280]{1,0:T(8,128)(2,1)S(1)} %get-tuple-element.34), channel_id=1, source_target_pairs={{0,1},{1,19},{2,3},{3,17},{4,22},{5,6},{6,20},{7,4},{8,9},{9,27},{... | collective-permute-start | bytes 983048 | tf_op jit(solution)/shard_map/ppermute | solution.py:404
  6.0 9.6 %collective-permute-start.2 = (bf16[128,1280]{1,0:T(8,128)(2,1)S(1)}, bf16[128,1280]{1,0:T(8,128)(2,1)S(1)}, u32[]{:S(2)}, u32[]{:S(2)}) collective-permute-start(bf16[128,1280]{1,0:T(8,128)(2,1)S(1)} %get-tuple-element.35), channel_id=1, source_target_pairs={{0,12},{1,17},{2,14},{3,19},{4,20},{5,1},{6,22},{7,3},{8,4},{9,25}... | collective-permute-start | bytes 983048 | tf_op jit(solution)/shard_map/ppermute | solution.py:404
  6.0 10.3 %collective-permute-start.3 = (bf16[128,1280]{1,0:T(8,128)(2,1)S(1)}, bf16[128,1280]{1,0:T(8,128)(2,1)S(1)}, u32[]{:S(2)}, u32[]{:S(2)}) collective-permute-start(bf16[128,1280]{1,0:T(8,128)(2,1)S(1)} %get-tuple-element.35), channel_id=1, source_target_pairs={{0,4},{1,25},{2,6},{3,27},{4,28},{5,9},{6,30},{7,11},{8,12},{9,17}... | collective-permute-start | bytes 983048 | tf_op jit(solution)/shard_map/ppermute | solution.py:404
  16.4 8.8 %collective-permute-start.4 = (bf16[640,1280]{1,0:T(8,128)(2,1)S(1)}, bf16[640,1280]{1,0:T(8,128)(2,1)S(1)}, u32[]{:S(2)}, u32[]{:S(2)}) collective-permute-start(bf16[640,1280]{1,0:T(8,128)(2,1)S(1)} %bitcast.18), channel_id=1, source_target_pairs={{0,16},{16,0},{1,17},{17,1},{2,18},{18,2},{3,19},{19,3},{4,20},{20... | collective-permute-start | bytes 4915208 | tf_op jit(solution)/shard_map/ppermute | solution.py:382
  18.7 16.3 %collective-permute-start.5 = (bf16[256,1280]{1,0:T(8,128)(2,1)S(1)}, bf16[256,1280]{1,0:T(8,128)(2,1)S(1)}, u32[]{:S(2)}, u32[]{:S(2)}) collective-permute-start(bf16[256,1280]{1,0:T(8,128)(2,1)S(1)} %shard_map.146.refs_9_), channel_id=1, source_target_pairs={{4,0},{8,4},{12,8},{0,12},{5,1},{9,5},{13,9},{1,13},{6,2},{10,6},{... | collective-permute-start | bytes 1966088 | tf_op jit(solution)/shard_map/ppermute | solution.py:378
  20.3 17.6 %collective-permute-start.6 = (bf16[256,1280]{1,0:T(8,128)(2,1)S(1)}, bf16[256,1280]{1,0:T(8,128)(2,1)S(1)}, u32[]{:S(2)}, u32[]{:S(2)}) collective-permute-start(bf16[256,1280]{1,0:T(8,128)(2,1)S(1)} %shard_map.146.refs_9_), channel_id=1, source_target_pairs={{12,0},{0,4},{4,8},{8,12},{13,1},{1,5},{5,9},{9,13},{14,2},{2,6},{... | collective-permute-start | bytes 1966088 | tf_op jit(solution)/shard_map/ppermute | solution.py:378
  20.3 17.9 %collective-permute-start.7 = (bf16[256,1280]{1,0:T(8,128)(2,1)S(1)}, bf16[256,1280]{1,0:T(8,128)(2,1)S(1)}, u32[]{:S(2)}, u32[]{:S(2)}) collective-permute-start(bf16[256,1280]{1,0:T(8,128)(2,1)S(1)} %shard_map.147.refs_10_.refs_9_), channel_id=1, source_target_pairs={{1,0},{2,1},{3,2},{0,3},{5,4},{6,5},{7,6},{4,7},{9,8},{10,9},{11,1... | collective-permute-start | bytes 1966088 | tf_op jit(solution)/shard_map/ppermute | solution.py:378
  21.2 17.1 %collective-permute-start.8 = (bf16[256,1280]{1,0:T(8,128)(2,1)S(1)}, bf16[256,1280]{1,0:T(8,128)(2,1)S(1)}, u32[]{:S(2)}, u32[]{:S(2)}) collective-permute-start(bf16[256,1280]{1,0:T(8,128)(2,1)S(1)} %shard_map.147.refs_10_.refs_9_), channel_id=1, source_target_pairs={{3,0},{0,1},{1,2},{2,3},{7,4},{4,5},{5,6},{6,7},{11,8},{8,9},{9,10... | collective-permute-start | bytes 1966088 | tf_op jit(solution)/shard_map/ppermute | solution.py:378
  35.1 8.9 %collective-permute-start.9 = (bf16[128,1280]{1,0:T(8,128)(2,1)S(1)}, bf16[128,1280]{1,0:T(8,128)(2,1)S(1)}, u32[]{:S(2)}, u32[]{:S(2)}) collective-permute-start(bf16[128,1280]{1,0:T(8,128)(2,1)S(1)} %shard_map.152), channel_id=1, source_target_pairs={{4,0},{8,4},{12,8},{0,12},{5,1},{9,5},{13,9},{1,13},{6,2},{10,6},{... | collective-permute-start | bytes 983048 | tf_op jit(solution)/shard_map/ppermute | solution.py:378
  37.9 9.5 %collective-permute-start.10 = (bf16[128,1280]{1,0:T(8,128)(2,1)S(1)}, bf16[128,1280]{1,0:T(8,128)(2,1)S(1)}, u32[]{:S(2)}, u32[]{:S(2)}) collective-permute-start(bf16[128,1280]{1,0:T(8,128)(2,1)S(1)} %shard_map.153), channel_id=1, source_target_pairs={{12,0},{0,4},{4,8},{8,12},{13,1},{1,5},{5,9},{9,13},{14,2},{2,6},{... | collective-permute-start | bytes 983048 | tf_op jit(solution)/shard_map/ppermute | solution.py:378
  38.2 11.6 %collective-permute-start.11 = (bf16[128,1280]{1,0:T(8,128)(2,1)S(1)}, bf16[128,1280]{1,0:T(8,128)(2,1)S(1)}, u32[]{:S(2)}, u32[]{:S(2)}) collective-permute-start(bf16[128,1280]{1,0:T(8,128)(2,1)S(1)} %shard_map.155), channel_id=1, source_target_pairs={{1,0},{2,1},{3,2},{0,3},{5,4},{6,5},{7,6},{4,7},{9,8},{10,9},{11,1... | collective-permute-start | bytes 983048 | tf_op jit(solution)/shard_map/ppermute | solution.py:378
  38.3 11.5 %collective-permute-start.12 = (bf16[128,1280]{1,0:T(8,128)(2,1)S(1)}, bf16[128,1280]{1,0:T(8,128)(2,1)S(1)}, u32[]{:S(2)}, u32[]{:S(2)}) collective-permute-start(bf16[128,1280]{1,0:T(8,128)(2,1)S(1)} %shard_map.156), channel_id=1, source_target_pairs={{3,0},{0,1},{1,2},{2,3},{7,4},{4,5},{5,6},{6,7},{11,8},{8,9},{9,10... | collective-permute-start | bytes 983048 | tf_op jit(solution)/shard_map/ppermute | solution.py:378
  49.8 4.6 %copy-start.4 = (f32[1280]{0:T(1024)S(1)}, f32[1280]{0:T(1024)}, u32[]{:S(2)}) copy-start(f32[1280]{0:T(1024)} %param.19) | copy-start | bytes 15364
  49.9 5.9 %copy-start = (bf16[1280,1280]{1,0:T(8,128)(2,1)S(1)}, bf16[1280,1280]{1,0:T(8,128)(2,1)}, u32[]{:S(2)}) copy-start(bf16[1280,1280]{1,0:T(8,128)(2,1)} %refs_8_.1) | copy-start | bytes 9830404
  49.9 5.9 %copy-start.1 = (bf16[1280,33]{0,1:T(8,128)(2,1)S(1)}, bf16[1280,33]{0,1:T(8,128)(2,1)}, u32[]{:S(2)}) copy-start(bf16[1280,33]{0,1:T(8,128)(2,1)} %param.21) | copy-start | bytes 253444
  49.9 5.9 %copy-start.2 = (f32[33]{0:T(128)S(1)}, f32[33]{0:T(128)}, u32[]{:S(2)}) copy-start(f32[33]{0:T(128)} %param.22) | copy-start | bytes 400
  52.3 3.4 %collective-permute-start.13 = (bf16[128,1280]{1,0:T(8,128)(2,1)S(1)}, bf16[128,1280]{1,0:T(8,128)(2,1)S(1)}, u32[]{:S(2)}, u32[]{:S(2)}) collective-permute-start(bf16[128,1280]{1,0:T(8,128)(2,1)S(1)} %get-tuple-element.62), channel_id=1, source_target_pairs={{0,16},{16,0},{1,17},{17,1},{2,18},{18,2},{3,19},{19,3},{4,20},{20... | collective-permute-start | bytes 983048 | tf_op jit(solution)/shard_map/ppermute | solution.py:382

commit v13 on v12

--- a/solution.py
+++ b/solution.py
@@ -180,7 +180,9 @@
     picked_ref[...] = norm_rows(rows, gain_ref[...].reshape(1, -1))
 
 
-def attend(table_ref, normed_refs, picked_refs, qtable_refs, meta_refs, key_refs, value_refs):
+def attend(
+    table_ref, normed_refs, picked_refs, qtable_refs, meta_refs, key_refs, value_refs, kept=None
+):
     size = key_refs[0].shape[0] // 2
     masks = picked_refs[0].shape[0]
     heads = len(key_refs)
@@ -203,7 +205,7 @@
             turned_queries.append(rotate(own[:, lanes], qtable_refs[which][...], size // 2))
         key_rows = jnp.concatenate(turned_keys, axis=1).astype(BF16)
         query_rows = jnp.concatenate(turned_queries, axis=1).astype(BF16)
-        spread = jnp.concatenate([query_rows] * heads, axis=0)
+        spread = jnp.concatenate([query_rows] * (kept or heads), axis=0)
         row = lax.broadcasted_iota(jnp.int32, spread.shape, 0) // masks
         lane = lax.broadcasted_iota(jnp.int32, spread.shape, 1) // size
         spread = jnp.where(row == lane, spread, jnp.zeros_like(spread))
@@ -254,8 +256,8 @@
 
 
 def probs_kernel(*refs):
-    inputs, probs_ref = refs[:-1], refs[-1]
-    for which, (probs, _) in enumerate(attend(*inputs)):
+    inputs, block_ref, probs_ref = refs[:-2], refs[-2], refs[-1]
+    for which, (probs, _) in enumerate(attend(*inputs, (block_ref, block_ref), (), kept=1)):
         probs_ref[which] = probs
 
 
@@ -267,7 +269,9 @@
     value_weight = jnp.concatenate([r[:size, :] for r in far_refs], axis=0)
     contexts = []
     for copy in range(2):
-        readers = [rows_reader(r, copy) for r in probs_refs]
+        readers = [rows_reader(r, copy) for r in probs_refs[:2]]
+        ends = [r[copy] for r in probs_refs[2:]]
+        readers.append(lambda start, end, ends=ends: ends[start // masks])
         far = nt_dot(normed_refs[copy][...], value_weight).astype(BF16)
         values = (values_refs[0][copy], values_refs[1][copy], far)
         contexts.append(
@@ -490,13 +494,13 @@
     value_low = gather_line(value_block, "y", False)
     key_high = gather_line(key_block, "x", True)
     value_high = gather_line(value_block, "y", True)
+    states_other = swap(states)
     key_line = join(key_low, key_high)
     key_ahead = pull(key_line, "y", 1)
     key_behind = pull(key_line, "y", 3)
     value_line = join(value_low, value_high)
     value_ahead = pull(value_line, "x", 1)
     value_behind = pull(value_line, "x", 3)
-    states_other = swap(after(states, key_line, value_line))
     mine = prepare_call(True, after(states, key_line, value_line))
     other = prepare_call(False, after(states_other, mine[0]))
     ready = (mine, other)
@@ -514,29 +518,32 @@
         ready, (key_ahead, key_behind), (value_ahead, value_behind)
     )
     key_far = tuple(after(b, near_probs) for b in key_far)
-    far_args = attend_args(ready, key_far, ())
-
-    def far_kernel(*refs):
-        probs_kernel(*attend_refs(refs, refs[9:11], ()), refs[-1])
-
-    far_probs = call(
-        far_kernel,
-        shape((2, 2 * masks, span), BF16),
-        far_args,
-        flops=4 * span * feature * 256,
-        exps=4 * masks * span,
-    )
+
+    def far_call(block):
+        def kernel(*refs):
+            probs_kernel(*attend_refs(refs, (), ())[:5], *refs[9:])
+
+        return call(
+            kernel,
+            shape((2, masks, span), BF16),
+            attend_args(ready, (block,), ()),
+            flops=4 * span * feature * 256,
+            exps=2 * masks * span,
+        )
+
+    low_probs = far_call(key_far[0])
+    far_probs = far_call(after(key_far[1], low_probs))
     value_far = tuple(after(b, far_probs) for b in value_far)
 
     def mix(*refs):
-        blocks = [h for r in refs[9:12] for h in halves(r)]
-        mix_kernel(refs[:3], refs[3:5], refs[5:7], refs[7:9], blocks, *refs[12:])
+        blocks = [h for r in refs[10:13] for h in halves(r)]
+        mix_kernel(refs[:4], refs[4:6], refs[6:8], refs[8:10], blocks, *refs[13:])
 
     partial, sent = call(
         mix,
         [shape((2 * masks, feature), F32), shape((2 * masks, feature), BF16)],
         (
-            own_probs, near_probs, far_probs, own_values, near_values, mine[0], other[0],
+            own_probs, near_probs, low_probs, far_probs, own_values, near_values, mine[0], other[0],
             *value_far, value_line, value_ahead, value_behind,
         ),
         flops=4 * span * feature * 256 + 4 * masks * feature * 8 * size,

time: 81.5 us -> 80.6 us (0.989)
  waiting for transfers between devices: 17.8 us -> 15.2 us
  Pallas kernels: 20.5 us -> 22.7 us
    ppermute x8, starting transfers between devices: 7.62 us -> 10.4 us  [pull(): lax.ppermute(array, axis, [((i + offset) % size, i) for i in range(size)])]
    ppermute x4, starting transfers between devices: 7.56 us -> 4.99 us  [gather_line(): return lax.ppermute(block, ('core', 'y', 'x'), pairs)]
    ppermute x4, waiting for transfers between devices: 7.47 us -> 5.04 us  [gather_line(): return lax.ppermute(block, ('core', 'y', 'x'), pairs)]
    pallas_call x15 -> x16, Pallas kernels: 20.5 us -> 22.7 us  [call(): pl.pallas_call(kernel, out_shape=outs, in_specs=[IN_PLACE] * n_any + [ON_...]
  transfers between devices with their start and end apart: 14 -> 14, of which waited for: 6 -> 7; matrix products, arithmetic and copies ran while one was open for 0% -> 0% of each run, Pallas kernels for 18% -> 22%
where the time goes in v13:
time: 80.6 us; the launch traced here: 80.4 us
  Pallas kernels  22.7 us (28%)
  blocking collectives  22.6 us (28%)
  starting transfers between devices  19.7 us (24%)
  waiting for transfers between devices  15.2 us (19%)
    pallas_call x16, Pallas kernels, call(): pl.pallas_call(kernel, out_shape=outs, in_specs=[IN_PLACE] * n_any + [ON_...  22.7 us
    all_to_all x1, blocking collectives, on_device(): arrived = lax.all_to_all(placed, ('z', 'y', 'x'), 0, 0, tiled=True)  22.6 us
    ppermute x8, starting transfers between devices, pull(): lax.ppermute(array, axis, [((i + offset) % size, i) for i in range(size)])  10.4 us
    ppermute x8, waiting for transfers between devices, pull(): lax.ppermute(array, axis, [((i + offset) % size, i) for i in range(size)])  8.87 us
    ppermute x4, waiting for transfers between devices, gather_line(): return lax.ppermute(block, ('core', 'y', 'x'), pairs)  5.04 us
    ppermute x4, starting transfers between devices, gather_line(): return lax.ppermute(block, ('core', 'y', 'x'), pairs)  4.99 us
    ppermute x2, starting transfers between devices, swap(): return lax.ppermute(array, 'core', [(0, 1), (1, 0)])  4.34 us
  transfers between devices with their start and end apart: 14, of which 7 were waited for; matrix products, arithmetic and copies ran while one was open for 0% of the time, Pallas kernels for 22%

profile of v13, /device:TPU:1, one launch (start us, length us, event | category | flops | bytes accessed | tf_op | source)
XLA Modules:
  0.0 80.4 jit_solution(14308076952407105862)
XLA Ops:
  0.0 3.2 %collective-permute-start.4 = (bf16[640,1280]{1,0:T(8,128)(2,1)}, bf16[640,1280]{1,0:T(8,128)(2,1)S(1)}, u32[]{:S(2)}, u32[]{:S(2)}) collective-permute-start(bf16[640,1280]{1,0:T(8,128)(2,1)} %bitcast.17), channel_id=1, source_target_pairs={{0,16},{16,0},{1,17},{17,1},{2,18},{18,2},{3,19},{19,3},{4,20},{20... | collective-permute-start | bytes 4915208 | tf_op jit(solution)/shard_map/ppermute | solution.py:386
  3.2 1.1 %shard_map.145 = (bf16[128,1280]{1,0:T(8,128)(2,1)S(1)}, bf16[128,1280]{1,0:T(8,128)(2,1)S(1)}) custom-call(bf16[192,1280]{1,0:T(8,128)(2,1)} %bitcast.19, bf16[64,1280]{1,0:T(8,128)(2,1)} %bitcast.22), custom_call_target="tpu_custom_call" | custom-call | bytes 1310720 | tf_op jit(solution)/shard_map/pallas_call | solution.py:59
  4.4 0.1 collective-permute-start
  4.5 1.4 %collective-permute-start.1 = (bf16[128,1280]{1,0:T(8,128)(2,1)S(1)}, bf16[128,1280]{1,0:T(8,128)(2,1)S(1)}, u32[]{:S(2)}, u32[]{:S(2)}) collective-permute-start(bf16[128,1280]{1,0:T(8,128)(2,1)S(1)} %get-tuple-element.35), channel_id=1, source_target_pairs={{0,1},{1,19},{2,3},{3,17},{4,22},{5,6},{6,20},{7,4},{8,9},{9,27},{... | collective-permute-start | bytes 983048 | tf_op jit(solution)/shard_map/ppermute | solution.py:408
  5.9 0.0 collective-permute-start.2
  5.9 3.5 %collective-permute-start.3 = (bf16[128,1280]{1,0:T(8,128)(2,1)S(1)}, bf16[128,1280]{1,0:T(8,128)(2,1)S(1)}, u32[]{:S(2)}, u32[]{:S(2)}) collective-permute-start(bf16[128,1280]{1,0:T(8,128)(2,1)S(1)} %get-tuple-element.36), channel_id=1, source_target_pairs={{0,4},{1,25},{2,6},{3,27},{4,28},{5,9},{6,30},{7,11},{8,12},{9,17}... | collective-permute-start | bytes 983048 | tf_op jit(solution)/shard_map/ppermute | solution.py:408
  9.4 3.8 %collective-permute-done.low_ref = bf16[128,1280]{1,0:T(8,128)(2,1)S(1)} collective-permute-done((bf16[128,1280]{1,0:T(8,128)(2,1)S(1)}, bf16[128,1280]{1,0:T(8,128)(2,1)S(1)}, u32[]{:S(2)}, u32[]{:S(2)}) %collective-permute-start) | collective-permute-done | bytes 327712 | tf_op jit(solution)/shard_map/ppermute | solution.py:408
  13.2 1.2 %collective-permute-done.1.high_ref = bf16[128,1280]{1,0:T(8,128)(2,1)S(1)} collective-permute-done((bf16[128,1280]{1,0:T(8,128)(2,1)S(1)}, bf16[128,1280]{1,0:T(8,128)(2,1)S(1)}, u32[]{:S(2)}, u32[]{:S(2)}) %collective-permute-start.1) | collective-permute-done | bytes 327712 | tf_op jit(solution)/shard_map/ppermute | solution.py:408
  14.4 2.9 %collective-permute-start.5 = (bf16[256,1280]{1,0:T(8,128)(2,1)S(1)}, bf16[256,1280]{1,0:T(8,128)(2,1)S(1)}, u32[]{:S(2)}, u32[]{:S(2)}) collective-permute-start(bf16[256,1280]{1,0:T(8,128)(2,1)S(1)} %shard_map.146.refs_9_), channel_id=1, source_target_pairs={{4,0},{8,4},{12,8},{0,12},{5,1},{9,5},{13,9},{1,13},{6,2},{10,6},{... | collective-permute-start | bytes 1966088 | tf_op jit(solution)/shard_map/ppermute | solution.py:382
  17.3 0.0 collective-permute-start.6
  17.3 0.0 collective-permute-done.2.low_ref
  17.3 0.0 collective-permute-done.3.high_ref
  17.4 1.8 %collective-permute-start.7 = (bf16[256,1280]{1,0:T(8,128)(2,1)S(1)}, bf16[256,1280]{1,0:T(8,128)(2,1)S(1)}, u32[]{:S(2)}, u32[]{:S(2)}) collective-permute-start(bf16[256,1280]{1,0:T(8,128)(2,1)S(1)} %shard_map.147.refs_10_), channel_id=1, source_target_pairs={{1,0},{2,1},{3,2},{0,3},{5,4},{6,5},{7,6},{4,7},{9,8},{10,9},{11,1... | collective-permute-start | bytes 1966088 | tf_op jit(solution)/shard_map/ppermute | solution.py:382
  19.1 0.0 collective-permute-start.8
  19.1 3.5 %shard_map.148 = (bf16[640,1280]{1,0:T(8,128)(2,1)S(1)}, bf16[64,1280]{1,0:T(8,128)(2,1)S(1)}, f32[64,1280]{1,0:T(8,128)S(1)}, f32[64,256]{1,0:T(8,128)S(1)}, s3...) custom-call(s32[256]{0:T(256)} %refs_0_.3, s32[24]{0:T(128)} %refs_1_.3, s32[256]{0:T(256)} %refs_2_.3, s32[64,256]{1,0:T(8,128)} %bitcast.20, ...), custom_call_target="tpu_custom_call" | custom-call | flops 217907200 | bytes 5639264 | tf_op jit(solution)/shard_map/pallas_call | solution.py:59
  22.6 0.0 collective-permute-done.4.refs_7_
  22.6 2.8 %shard_map.149 = (bf16[640,1280]{1,0:T(8,128)(2,1)S(1)}, bf16[64,1280]{1,0:T(8,128)(2,1)S(1)}, f32[64,1280]{1,0:T(8,128)S(1)}, f32[64,256]{1,0:T(8,128)S(1)}, s32[64,128]{1,0:T(8,128)S(1)}) custom-call(s32[256]{0:T(256)} %refs_0_.3, s32[24]{0:T(128)} %refs_1_.3, s32[256]{0:T(256)} %refs_2_.3, s32[64,256]{1,0:T(8,128)} %bitcast.21, s32[24,640]{1,0:T(8,128)} %refs_4_.3, ...), custom_call_target="tpu_custom_call" | custom-call | flops 217907200 | bytes 4328544 | tf_op jit(solution)/shard_map/pallas_call | solution.py:59
  25.4 2.5 %shard_map.150 = (bf16[2,128,640]{2,1,0:T(8,128)(2,1)S(1)}, bf16[2,640,128]{2,1,0:T(8,128)(2,1)S(1)}) custom-call(f32[640,256]{1,0:T(8,128)S(1)} %get-tuple-element.42.refs_0_, bf16[640,1280]{1,0:T(8,128)(2,1)S(1)} %get-tuple-element.39.refs_1_.refs_6_, bf16[640,1280]{1,0:T(8,128)(2,1)S(1)} %get-tuple-element.43.refs_2_.refs_7_, ...), custom_call_target="tpu_custom_call" | custom-call | flops 838860800 | bytes 6422528 | tf_op jit(solution)/shard_map/pallas_call | solution.py:59
  27.9 3.1 %collective-permute-done.5.refs_9_.array_ref = bf16[256,1280]{1,0:T(8,128)(2,1)S(1)} collective-permute-done((bf16[256,1280]{1,0:T(8,128)(2,1)S(1)}, bf16[256,1280]{1,0:T(8,128)(2,1)S(1)}, u32[]{:S(2)}, u32[]{:S(2)}) %collective-permute-start.5) | collective-permute-done | bytes 655392 | tf_op jit(solution)/shard_map/ppermute | solution.py:382
  31.0 3.5 %collective-permute-start.9 = (bf16[128,1280]{1,0:T(8,128)(2,1)S(1)}, bf16[128,1280]{1,0:T(8,128)(2,1)S(1)}, u32[]{:S(2)}, u32[]{:S(2)}) collective-permute-start(bf16[128,1280]{1,0:T(8,128)(2,1)S(1)} %shard_map.152), channel_id=1, source_target_pairs={{4,0},{8,4},{12,8},{0,12},{5,1},{9,5},{13,9},{1,13},{6,2},{10,6},{... | collective-permute-start | bytes 983048 | tf_op jit(solution)/shard_map/ppermute | solution.py:382
  34.5 0.6 collective-permute-done.6.refs_10_.array_ref
  35.1 0.3 collective-permute-start.10
  35.4 0.0 collective-permute-done.7.refs_11_.array_ref
  35.4 1.9 %collective-permute-start.11 = (bf16[128,1280]{1,0:T(8,128)(2,1)S(1)}, bf16[128,1280]{1,0:T(8,128)(2,1)S(1)}, u32[]{:S(2)}, u32[]{:S(2)}) collective-permute-start(bf16[128,1280]{1,0:T(8,128)(2,1)S(1)} %shard_map.156), channel_id=1, source_target_pairs={{1,0},{2,1},{3,2},{0,3},{5,4},{6,5},{7,6},{4,7},{9,8},{10,9},{11,1... | collective-permute-start | bytes 983048 | tf_op jit(solution)/shard_map/ppermute | solution.py:382
  37.4 0.0 collective-permute-done.8.refs_12_.array_ref
  37.4 0.1 collective-permute-start.12
  37.5 3.0 %shard_map.151 = (bf16[2,256,640]{2,1,0:T(8,128)(2,1)S(1)}, bf16[2,640,256]{2,1,0:T(8,128)(2,1)S(1)}) custom-call(f32[640,256]{1,0:T(8,128)S(1)} %get-tuple-element.42.refs_0_, bf16[640,1280]{1,0:T(8,128)(2,1)S(1)} %get-tuple-element.39.refs_1_.refs_6_, bf16[640,1280]{1,0:T(8,128)(2,1)S(1)} %get-tuple-element.43.refs_2_.refs_7_, ...), custom_call_target="tpu_custom_call" | custom-call | flops 1677721600 | bytes 8388608 | tf_op jit(solution)/shard_map/pallas_call | solution.py:59
  40.5 1.6 %collective-permute-done.9.refs_9_ = bf16[128,1280]{1,0:T(8,128)(2,1)S(1)} collective-permute-done((bf16[128,1280]{1,0:T(8,128)(2,1)S(1)}, bf16[128,1280]{1,0:T(8,128)(2,1)S(1)}, u32[]{:S(2)}, u32[]{:S(2)}) %collective-permute-start.9) | collective-permute-done | bytes 327712 | tf_op jit(solution)/shard_map/ppermute | solution.py:382
  42.0 3.7 %collective-permute-done.10.refs_9_ = bf16[128,1280]{1,0:T(8,128)(2,1)S(1)} collective-permute-done((bf16[128,1280]{1,0:T(8,128)(2,1)S(1)}, bf16[128,1280]{1,0:T(8,128)(2,1)S(1)}, u32[]{:S(2)}, u32[]{:S(2)}) %collective-permute-start.10) | collective-permute-done | bytes 327712 | tf_op jit(solution)/shard_map/ppermute | solution.py:382
  45.7 2.4 %shard_map.153.refs_2_ = bf16[2,64,640]{2,1,0:T(8,128)(2,1)S(1)} custom-call(f32[640,256]{1,0:T(8,128)S(1)} %get-tuple-element.42.refs_0_, bf16[640,1280]{1,0:T(8,128)(2,1)S(1)} %get-tuple-element.39.refs_1_.refs_6_, bf16[640,1280]{1,0:T(8,128)(2,1)S(1)} %get-tuple-element.43.refs_2_.refs_7_, bf16[64,1280]{1,0:T(8,128)(2,1)S(1)} %get-tuple-element.44.refs_3_, ...), custom_call_target="tpu_custom_call" | custom-call | flops 838860800 | bytes 4947968 | tf_op jit(solution)/shard_map/pallas_call | solution.py:59
  48.1 2.4 %shard_map.155.refs_3_ = bf16[2,64,640]{2,1,0:T(8,128)(2,1)S(1)} custom-call(f32[640,256]{1,0:T(8,128)S(1)} %get-tuple-element.42.refs_0_, bf16[640,1280]{1,0:T(8,128)(2,1)S(1)} %get-tuple-element.39.refs_1_.refs_6_, bf16[640,1280]{1,0:T(8,128)(2,1)S(1)} %get-tuple-element.43.refs_2_.refs_7_, bf16[64,1280]{1,0:T(8,128)(2,1)S(1)} %get-tuple-element.44.refs_3_, ...), custom_call_target="tpu_custom_call" | custom-call | flops 838860800 | bytes 4947968 | tf_op jit(solution)/shard_map/pallas_call | solution.py:59
  50.5 0.0 collective-permute-done.11.refs_8_
  50.5 0.0 collective-permute-done.12.refs_9_
  50.5 0.0 copy-start.3
  50.5 0.0 copy-start
  50.5 0.0 copy-start.1
  50.5 0.0 copy-start.2
  50.5 2.4 %shard_map.158 = (f32[128,1280]{1,0:T(8,128)S(1)}, bf16[128,1280]{1,0:T(8,128)(2,1)S(1)}) custom-call(bf16[2,128,640]{2,1,0:T(8,128)(2,1)S(1)} %get-tuple-element.50.refs_0_, bf16[2,256,640]{2,1,0:T(8,128)(2,1)S(1)} %get-tuple-element.51.refs_1_, bf16[2,64,640]{2,1,0:T(8,128)(2,1)S(1)} %shard_map.153.refs_2_, bf16[2,64,640]{2,1,0:T(8,128)(2,1)S(1)} %shard_map.155.refs_3_, ...), custom_call_target="tpu_custom_call" | custom-call | flops 1006632960 | bytes 9175040 | tf_op jit(solution)/shard_map/pallas_call | solution.py:59
  52.9 1.1 %collective-permute-start.13 = (bf16[128,1280]{1,0:T(8,128)(2,1)S(1)}, bf16[128,1280]{1,0:T(8,128)(2,1)S(1)}, u32[]{:S(2)}, u32[]{:S(2)}) collective-permute-start(bf16[128,1280]{1,0:T(8,128)(2,1)S(1)} %get-tuple-element.64), channel_id=1, source_target_pairs={{0,16},{16,0},{1,17},{17,1},{2,18},{18,2},{3,19},{19,3},{4,20},{20... | collective-permute-start | bytes 983048 | tf_op jit(solution)/shard_map/ppermute | solution.py:386
  54.0 0.0 copy-done.3
  54.1 1.2 %collective-permute-done.13.refs_3_ = bf16[128,1280]{1,0:T(8,128)(2,1)S(1)} collective-permute-done((bf16[128,1280]{1,0:T(8,128)(2,1)S(1)}, bf16[128,1280]{1,0:T(8,128)(2,1)S(1)}, u32[]{:S(2)}, u32[]{:S(2)}) %collective-permute-start.13) | collective-permute-done | bytes 327712 | tf_op jit(solution)/shard_map/ppermute | solution.py:386
  55.3 0.0 copy-done
  55.3 0.0 copy-done.1
  55.3 0.0 copy-done.2
  55.3 1.8 %shard_map.159 = f32[128,64]{1,0:T(8,128)S(1)} custom-call(f32[64,1280]{1,0:T(8,128)S(1)} %get-tuple-element.38.refs_0_, f32[64,1280]{1,0:T(8,128)S(1)} %get-tuple-element.41.refs_1_, f32[128,1280]{1,0:T(8,128)S(1)} %get-tuple-element.63.refs_2_, bf16[128,1280]{1,0:T(8,128)(2,1)S(1)} %collective-permute-done.13.refs_3_, ...), custom_call_target="tpu_custom_call" | custom-call | flops 419430400 | bytes 5103236 | tf_op jit(solution)/shard_map/pallas_call | solution.py:59
  57.1 22.6 %all_to_all.11 = f32[128,1,64]{2,1,0:T(1,128)S(1)} all-to-all(f32[128,1,64]{2,1,0:T(1,128)S(1)} %bitcast.13), channel_id=1, replica_groups=mesh['z'=8,'core'=2,'y'=4,'x'=4] {'z','y','x'}, dimensions={0} | all-to-all | bytes 65536 | tf_op jit(solution)/shard_map/all_to_all | solution.py:565
  79.7 0.7 shard_map.160
  (7 shorter events, 0.2 us)
Async XLA Ops:
  0.0 22.6 %collective-permute-start.4 = (bf16[640,1280]{1,0:T(8,128)(2,1)}, bf16[640,1280]{1,0:T(8,128)(2,1)S(1)}, u32[]{:S(2)}, u32[]{:S(2)}) collective-permute-start(bf16[640,1280]{1,0:T(8,128)(2,1)} %bitcast.17), channel_id=1, source_target_pairs={{0,16},{16,0},{1,17},{17,1},{2,18},{18,2},{3,19},{19,3},{4,20},{20... | collective-permute-start | bytes 4915208 | tf_op jit(solution)/shard_map/ppermute | solution.py:386
  4.4 8.8 %collective-permute-start = (bf16[128,1280]{1,0:T(8,128)(2,1)S(1)}, bf16[128,1280]{1,0:T(8,128)(2,1)S(1)}, u32[]{:S(2)}, u32[]{:S(2)}) collective-permute-start(bf16[128,1280]{1,0:T(8,128)(2,1)S(1)} %get-tuple-element.35), channel_id=1, source_target_pairs={{0,3},{1,17},{2,1},{3,19},{4,20},{5,4},{6,22},{7,6},{8,11},{9,25},... | collective-permute-start | bytes 983048 | tf_op jit(solution)/shard_map/ppermute | solution.py:408
  4.5 9.9 %collective-permute-start.1 = (bf16[128,1280]{1,0:T(8,128)(2,1)S(1)}, bf16[128,1280]{1,0:T(8,128)(2,1)S(1)}, u32[]{:S(2)}, u32[]{:S(2)}) collective-permute-start(bf16[128,1280]{1,0:T(8,128)(2,1)S(1)} %get-tuple-element.35), channel_id=1, source_target_pairs={{0,1},{1,19},{2,3},{3,17},{4,22},{5,6},{6,20},{7,4},{8,9},{9,27},{... | collective-permute-start | bytes 983048 | tf_op jit(solution)/shard_map/ppermute | solution.py:408
  5.9 11.4 %collective-permute-start.2 = (bf16[128,1280]{1,0:T(8,128)(2,1)S(1)}, bf16[128,1280]{1,0:T(8,128)(2,1)S(1)}, u32[]{:S(2)}, u32[]{:S(2)}) collective-permute-start(bf16[128,1280]{1,0:T(8,128)(2,1)S(1)} %get-tuple-element.36), channel_id=1, source_target_pairs={{0,12},{1,17},{2,14},{3,19},{4,20},{5,1},{6,22},{7,3},{8,4},{9,25}... | collective-permute-start | bytes 983048 | tf_op jit(solution)/shard_map/ppermute | solution.py:408
  5.9 11.4 %collective-permute-start.3 = (bf16[128,1280]{1,0:T(8,128)(2,1)S(1)}, bf16[128,1280]{1,0:T(8,128)(2,1)S(1)}, u32[]{:S(2)}, u32[]{:S(2)}) collective-permute-start(bf16[128,1280]{1,0:T(8,128)(2,1)S(1)} %get-tuple-element.36), channel_id=1, source_target_pairs={{0,4},{1,25},{2,6},{3,27},{4,28},{5,9},{6,30},{7,11},{8,12},{9,17}... | collective-permute-start | bytes 983048 | tf_op jit(solution)/shard_map/ppermute | solution.py:408
  14.4 16.6 %collective-permute-start.5 = (bf16[256,1280]{1,0:T(8,128)(2,1)S(1)}, bf16[256,1280]{1,0:T(8,128)(2,1)S(1)}, u32[]{:S(2)}, u32[]{:S(2)}) collective-permute-start(bf16[256,1280]{1,0:T(8,128)(2,1)S(1)} %shard_map.146.refs_9_), channel_id=1, source_target_pairs={{4,0},{8,4},{12,8},{0,12},{5,1},{9,5},{13,9},{1,13},{6,2},{10,6},{... | collective-permute-start | bytes 1966088 | tf_op jit(solution)/shard_map/ppermute | solution.py:382
  17.3 17.8 %collective-permute-start.6 = (bf16[256,1280]{1,0:T(8,128)(2,1)S(1)}, bf16[256,1280]{1,0:T(8,128)(2,1)S(1)}, u32[]{:S(2)}, u32[]{:S(2)}) collective-permute-start(bf16[256,1280]{1,0:T(8,128)(2,1)S(1)} %shard_map.146.refs_9_), channel_id=1, source_target_pairs={{12,0},{0,4},{4,8},{8,12},{13,1},{1,5},{5,9},{9,13},{14,2},{2,6},{... | collective-permute-start | bytes 1966088 | tf_op jit(solution)/shard_map/ppermute | solution.py:382
  17.4 18.0 %collective-permute-start.7 = (bf16[256,1280]{1,0:T(8,128)(2,1)S(1)}, bf16[256,1280]{1,0:T(8,128)(2,1)S(1)}, u32[]{:S(2)}, u32[]{:S(2)}) collective-permute-start(bf16[256,1280]{1,0:T(8,128)(2,1)S(1)} %shard_map.147.refs_10_), channel_id=1, source_target_pairs={{1,0},{2,1},{3,2},{0,3},{5,4},{6,5},{7,6},{4,7},{9,8},{10,9},{11,1... | collective-permute-start | bytes 1966088 | tf_op jit(solution)/shard_map/ppermute | solution.py:382
  19.1 18.2 %collective-permute-start.8 = (bf16[256,1280]{1,0:T(8,128)(2,1)S(1)}, bf16[256,1280]{1,0:T(8,128)(2,1)S(1)}, u32[]{:S(2)}, u32[]{:S(2)}) collective-permute-start(bf16[256,1280]{1,0:T(8,128)(2,1)S(1)} %shard_map.147.refs_10_), channel_id=1, source_target_pairs={{3,0},{0,1},{1,2},{2,3},{7,4},{4,5},{5,6},{6,7},{11,8},{8,9},{9,10... | collective-permute-start | bytes 1966088 | tf_op jit(solution)/shard_map/ppermute | solution.py:382
  31.0 11.0 %collective-permute-start.9 = (bf16[128,1280]{1,0:T(8,128)(2,1)S(1)}, bf16[128,1280]{1,0:T(8,128)(2,1)S(1)}, u32[]{:S(2)}, u32[]{:S(2)}) collective-permute-start(bf16[128,1280]{1,0:T(8,128)(2,1)S(1)} %shard_map.152), channel_id=1, source_target_pairs={{4,0},{8,4},{12,8},{0,12},{5,1},{9,5},{13,9},{1,13},{6,2},{10,6},{... | collective-permute-start | bytes 983048 | tf_op jit(solution)/shard_map/ppermute | solution.py:382
  35.1 10.6 %collective-permute-start.10 = (bf16[128,1280]{1,0:T(8,128)(2,1)S(1)}, bf16[128,1280]{1,0:T(8,128)(2,1)S(1)}, u32[]{:S(2)}, u32[]{:S(2)}) collective-permute-start(bf16[128,1280]{1,0:T(8,128)(2,1)S(1)} %shard_map.154), channel_id=1, source_target_pairs={{12,0},{0,4},{4,8},{8,12},{13,1},{1,5},{5,9},{9,13},{14,2},{2,6},{... | collective-permute-start | bytes 983048 | tf_op jit(solution)/shard_map/ppermute | solution.py:382
  35.4 15.0 %collective-permute-start.11 = (bf16[128,1280]{1,0:T(8,128)(2,1)S(1)}, bf16[128,1280]{1,0:T(8,128)(2,1)S(1)}, u32[]{:S(2)}, u32[]{:S(2)}) collective-permute-start(bf16[128,1280]{1,0:T(8,128)(2,1)S(1)} %shard_map.156), channel_id=1, source_target_pairs={{1,0},{2,1},{3,2},{0,3},{5,4},{6,5},{7,6},{4,7},{9,8},{10,9},{11,1... | collective-permute-start | bytes 983048 | tf_op jit(solution)/shard_map/ppermute | solution.py:382
  37.4 13.1 %collective-permute-start.12 = (bf16[128,1280]{1,0:T(8,128)(2,1)S(1)}, bf16[128,1280]{1,0:T(8,128)(2,1)S(1)}, u32[]{:S(2)}, u32[]{:S(2)}) collective-permute-start(bf16[128,1280]{1,0:T(8,128)(2,1)S(1)} %shard_map.157), channel_id=1, source_target_pairs={{3,0},{0,1},{1,2},{2,3},{7,4},{4,5},{5,6},{6,7},{11,8},{8,9},{9,10... | collective-permute-start | bytes 983048 | tf_op jit(solution)/shard_map/ppermute | solution.py:382
  50.5 3.6 %copy-start.3 = (f32[1280]{0:T(1024)S(1)}, f32[1280]{0:T(1024)}, u32[]{:S(2)}) copy-start(f32[1280]{0:T(1024)} %param.19) | copy-start | bytes 15364
  50.5 4.8 %copy-start = (bf16[1280,1280]{1,0:T(8,128)(2,1)S(1)}, bf16[1280,1280]{1,0:T(8,128)(2,1)}, u32[]{:S(2)}) copy-start(bf16[1280,1280]{1,0:T(8,128)(2,1)} %refs_8_.1) | copy-start | bytes 9830404
  50.5 4.8 %copy-start.1 = (bf16[1280,33]{0,1:T(8,128)(2,1)S(1)}, bf16[1280,33]{0,1:T(8,128)(2,1)}, u32[]{:S(2)}) copy-start(bf16[1280,33]{0,1:T(8,128)(2,1)} %param.21) | copy-start | bytes 253444
  50.5 4.8 %copy-start.2 = (f32[33]{0:T(128)S(1)}, f32[33]{0:T(128)}, u32[]{:S(2)}) copy-start(f32[33]{0:T(128)} %param.22) | copy-start | bytes 400
  52.9 2.4 %collective-permute-start.13 = (bf16[128,1280]{1,0:T(8,128)(2,1)S(1)}, bf16[128,1280]{1,0:T(8,128)(2,1)S(1)}, u32[]{:S(2)}, u32[]{:S(2)}) collective-permute-start(bf16[128,1280]{1,0:T(8,128)(2,1)S(1)} %get-tuple-element.64), channel_id=1, source_target_pairs={{0,16},{16,0},{1,17},{17,1},{2,18},{18,2},{3,19},{19,3},{4,20},{20... | collective-permute-start | bytes 983048 | tf_op jit(solution)/shard_map/ppermute | solution.py:386

commit v14 on v12

--- a/solution.py
+++ b/solution.py
@@ -185,9 +185,12 @@
     masks = picked_refs[0].shape[0]
     heads = len(key_refs)
     width = heads * size
-    weight = jnp.concatenate(
-        [r[size:, :] for r in key_refs] + [r[:size, :] for r in value_refs], axis=0
-    )
+    half = size // 2
+    if value_refs:
+        beside = [r[:size, :] for r in value_refs]
+    else:
+        beside = [r[start : start + half, :] for r in key_refs for start in (size + half, size)]
+    weight = jnp.concatenate([r[size:, :] for r in key_refs] + beside, axis=0)
     query_weight = jnp.concatenate([r[:size, :] for r in key_refs], axis=0)
     picked = jnp.concatenate([r[...] for r in picked_refs], axis=0)
     queries = nt_dot(picked, query_weight) * 0.125
@@ -199,7 +202,14 @@
         turned_keys, turned_queries = [], []
         for i in range(heads // 2):
             lanes = slice(128 * i, 128 * (i + 1))
-            turned_keys.append(rotate(projected[:, lanes], table_ref[...], size // 2))
+            if value_refs:
+                turned_keys.append(rotate(projected[:, lanes], table_ref[...], half))
+            else:
+                exchanged = projected[:, width + 128 * i : width + 128 * (i + 1)]
+                table = table_ref[...]
+                turned_keys.append(
+                    projected[:, lanes] * table[:, :128] + exchanged * table[:, 128:]
+                )
             turned_queries.append(rotate(own[:, lanes], qtable_refs[which][...], size // 2))
         key_rows = jnp.concatenate(turned_keys, axis=1).astype(BF16)
         query_rows = jnp.concatenate(turned_queries, axis=1).astype(BF16)
@@ -490,13 +500,13 @@
     value_low = gather_line(value_block, "y", False)
     key_high = gather_line(key_block, "x", True)
     value_high = gather_line(value_block, "y", True)
+    states_other = swap(states)
     key_line = join(key_low, key_high)
     key_ahead = pull(key_line, "y", 1)
     key_behind = pull(key_line, "y", 3)
     value_line = join(value_low, value_high)
     value_ahead = pull(value_line, "x", 1)
     value_behind = pull(value_line, "x", 3)
-    states_other = swap(after(states, key_line, value_line))
     mine = prepare_call(True, after(states, key_line, value_line))
     other = prepare_call(False, after(states_other, mine[0]))
     ready = (mine, other)

time: 81.5 us -> 78.6 us (0.964)
  waiting for transfers between devices: 17.8 us -> 15.2 us
    ppermute x8, starting transfers between devices: 7.62 us -> 10.4 us  [pull(): lax.ppermute(array, axis, [((i + offset) % size, i) for i in range(size)])]
    ppermute x4, starting transfers between devices: 7.56 us -> 4.99 us  [gather_line(): return lax.ppermute(block, ('core', 'y', 'x'), pairs)]
    ppermute x4, waiting for transfers between devices: 7.47 us -> 5.04 us  [gather_line(): return lax.ppermute(block, ('core', 'y', 'x'), pairs)]
  transfers between devices with their start and end apart: 14 -> 14, of which waited for: 6 -> 7; matrix products, arithmetic and copies ran while one was open for 0% -> 0% of each run, Pallas kernels for 18% -> 20%
where the time goes in v14:
time: 78.6 us; the launch traced here: 78.4 us
  blocking collectives  23 us (29%)
  Pallas kernels  20.3 us (26%)
  starting transfers between devices  19.7 us (25%)
  waiting for transfers between devices  15.2 us (19%)
    all_to_all x1, blocking collectives, on_device(): arrived = lax.all_to_all(placed, ('z', 'y', 'x'), 0, 0, tiled=True)  23 us
    pallas_call x15, Pallas kernels, call(): pl.pallas_call(kernel, out_shape=outs, in_specs=[IN_PLACE] * n_any + [ON_...  20.3 us
    ppermute x8, starting transfers between devices, pull(): lax.ppermute(array, axis, [((i + offset) % size, i) for i in range(size)])  10.4 us
    ppermute x8, waiting for transfers between devices, pull(): lax.ppermute(array, axis, [((i + offset) % size, i) for i in range(size)])  8.87 us
    ppermute x4, waiting for transfers between devices, gather_line(): return lax.ppermute(block, ('core', 'y', 'x'), pairs)  5.04 us
    ppermute x4, starting transfers between devices, gather_line(): return lax.ppermute(block, ('core', 'y', 'x'), pairs)  4.99 us
    ppermute x2, starting transfers between devices, swap(): return lax.ppermute(array, 'core', [(0, 1), (1, 0)])  4.33 us
  transfers between devices with their start and end apart: 14, of which 7 were waited for; matrix products, arithmetic and copies ran while one was open for 0% of the time, Pallas kernels for 20%

profile of v14, /device:TPU:1, one launch (start us, length us, event | category | flops | bytes accessed | tf_op | source)
XLA Modules:
  0.0 78.4 jit_solution(12511442046340958043)
XLA Ops:
  0.0 3.2 %collective-permute-start.4 = (bf16[640,1280]{1,0:T(8,128)(2,1)}, bf16[640,1280]{1,0:T(8,128)(2,1)S(1)}, u32[]{:S(2)}, u32[]{:S(2)}) collective-permute-start(bf16[640,1280]{1,0:T(8,128)(2,1)} %bitcast.17), channel_id=1, source_target_pairs={{0,16},{16,0},{1,17},{17,1},{2,18},{18,2},{3,19},{19,3},{4,20},{20... | collective-permute-start | bytes 4915208 | tf_op jit(solution)/shard_map/ppermute | solution.py:392
  3.2 1.1 %shard_map.145 = (bf16[128,1280]{1,0:T(8,128)(2,1)S(1)}, bf16[128,1280]{1,0:T(8,128)(2,1)S(1)}) custom-call(bf16[192,1280]{1,0:T(8,128)(2,1)} %bitcast.19, bf16[64,1280]{1,0:T(8,128)(2,1)} %bitcast.22), custom_call_target="tpu_custom_call" | custom-call | bytes 1310720 | tf_op jit(solution)/shard_map/pallas_call | solution.py:59
  4.4 0.1 collective-permute-start
  4.5 1.4 %collective-permute-start.1 = (bf16[128,1280]{1,0:T(8,128)(2,1)S(1)}, bf16[128,1280]{1,0:T(8,128)(2,1)S(1)}, u32[]{:S(2)}, u32[]{:S(2)}) collective-permute-start(bf16[128,1280]{1,0:T(8,128)(2,1)S(1)} %get-tuple-element.34), channel_id=1, source_target_pairs={{0,1},{1,19},{2,3},{3,17},{4,22},{5,6},{6,20},{7,4},{8,9},{9,27},{... | collective-permute-start | bytes 983048 | tf_op jit(solution)/shard_map/ppermute | solution.py:414
  5.9 0.0 collective-permute-start.2
  5.9 3.5 %collective-permute-start.3 = (bf16[128,1280]{1,0:T(8,128)(2,1)S(1)}, bf16[128,1280]{1,0:T(8,128)(2,1)S(1)}, u32[]{:S(2)}, u32[]{:S(2)}) collective-permute-start(bf16[128,1280]{1,0:T(8,128)(2,1)S(1)} %get-tuple-element.35), channel_id=1, source_target_pairs={{0,4},{1,25},{2,6},{3,27},{4,28},{5,9},{6,30},{7,11},{8,12},{9,17}... | collective-permute-start | bytes 983048 | tf_op jit(solution)/shard_map/ppermute | solution.py:414
  9.4 3.8 %collective-permute-done.low_ref = bf16[128,1280]{1,0:T(8,128)(2,1)S(1)} collective-permute-done((bf16[128,1280]{1,0:T(8,128)(2,1)S(1)}, bf16[128,1280]{1,0:T(8,128)(2,1)S(1)}, u32[]{:S(2)}, u32[]{:S(2)}) %collective-permute-start) | collective-permute-done | bytes 327712 | tf_op jit(solution)/shard_map/ppermute | solution.py:414
  13.2 1.2 %collective-permute-done.1.high_ref = bf16[128,1280]{1,0:T(8,128)(2,1)S(1)} collective-permute-done((bf16[128,1280]{1,0:T(8,128)(2,1)S(1)}, bf16[128,1280]{1,0:T(8,128)(2,1)S(1)}, u32[]{:S(2)}, u32[]{:S(2)}) %collective-permute-start.1) | collective-permute-done | bytes 327712 | tf_op jit(solution)/shard_map/ppermute | solution.py:414
  14.4 2.9 %collective-permute-start.5 = (bf16[256,1280]{1,0:T(8,128)(2,1)S(1)}, bf16[256,1280]{1,0:T(8,128)(2,1)S(1)}, u32[]{:S(2)}, u32[]{:S(2)}) collective-permute-start(bf16[256,1280]{1,0:T(8,128)(2,1)S(1)} %shard_map.146.refs_9_), channel_id=1, source_target_pairs={{4,0},{8,4},{12,8},{0,12},{5,1},{9,5},{13,9},{1,13},{6,2},{10,6},{... | collective-permute-start | bytes 1966088 | tf_op jit(solution)/shard_map/ppermute | solution.py:388
  17.3 0.0 collective-permute-start.6
  17.3 0.0 collective-permute-done.2.low_ref
  17.3 0.0 collective-permute-done.3.high_ref
  17.4 1.8 %collective-permute-start.7 = (bf16[256,1280]{1,0:T(8,128)(2,1)S(1)}, bf16[256,1280]{1,0:T(8,128)(2,1)S(1)}, u32[]{:S(2)}, u32[]{:S(2)}) collective-permute-start(bf16[256,1280]{1,0:T(8,128)(2,1)S(1)} %shard_map.147.refs_10_.refs_9_), channel_id=1, source_target_pairs={{1,0},{2,1},{3,2},{0,3},{5,4},{6,5},{7,6},{4,7},{9,8},{10,9},{11,1... | collective-permute-start | bytes 1966088 | tf_op jit(solution)/shard_map/ppermute | solution.py:388
  19.1 0.0 collective-permute-start.8
  19.1 3.5 %shard_map.148 = (bf16[640,1280]{1,0:T(8,128)(2,1)S(1)}, bf16[64,1280]{1,0:T(8,128)(2,1)S(1)}, f32[64,1280]{1,0:T(8,128)S(1)}, f32[64,256]{1,0:T(8,128)S(1)}, s3...) custom-call(s32[256]{0:T(256)} %refs_0_.3, s32[24]{0:T(128)} %refs_1_.3, s32[256]{0:T(256)} %refs_2_.3, s32[64,256]{1,0:T(8,128)} %bitcast.20, ...), custom_call_target="tpu_custom_call" | custom-call | flops 217907200 | bytes 5639264 | tf_op jit(solution)/shard_map/pallas_call | solution.py:59
  22.6 0.0 collective-permute-done.4.refs_7_
  22.6 2.8 %shard_map.149 = (bf16[640,1280]{1,0:T(8,128)(2,1)S(1)}, bf16[64,1280]{1,0:T(8,128)(2,1)S(1)}, f32[64,1280]{1,0:T(8,128)S(1)}, f32[64,256]{1,0:T(8,128)S(1)}, s32[64,128]{1,0:T(8,128)S(1)}) custom-call(s32[256]{0:T(256)} %refs_0_.3, s32[24]{0:T(128)} %refs_1_.3, s32[256]{0:T(256)} %refs_2_.3, s32[64,256]{1,0:T(8,128)} %bitcast.21, s32[24,640]{1,0:T(8,128)} %refs_4_.3, ...), custom_call_target="tpu_custom_call" | custom-call | flops 217907200 | bytes 4328544 | tf_op jit(solution)/shard_map/pallas_call | solution.py:59
  25.4 2.5 %shard_map.150 = (bf16[2,128,640]{2,1,0:T(8,128)(2,1)S(1)}, bf16[2,640,128]{2,1,0:T(8,128)(2,1)S(1)}) custom-call(f32[640,256]{1,0:T(8,128)S(1)} %get-tuple-element.41.refs_0_, bf16[640,1280]{1,0:T(8,128)(2,1)S(1)} %get-tuple-element.38.refs_1_.refs_5_, bf16[640,1280]{1,0:T(8,128)(2,1)S(1)} %get-tuple-element.42.refs_2_.refs_6_, ...), custom_call_target="tpu_custom_call" | custom-call | flops 838860800 | bytes 6422528 | tf_op jit(solution)/shard_map/pallas_call | solution.py:59
  27.9 3.1 %collective-permute-done.5.refs_9_.array_ref = bf16[256,1280]{1,0:T(8,128)(2,1)S(1)} collective-permute-done((bf16[256,1280]{1,0:T(8,128)(2,1)S(1)}, bf16[256,1280]{1,0:T(8,128)(2,1)S(1)}, u32[]{:S(2)}, u32[]{:S(2)}) %collective-permute-start.5) | collective-permute-done | bytes 655392 | tf_op jit(solution)/shard_map/ppermute | solution.py:388
  31.0 3.5 %collective-permute-start.9 = (bf16[128,1280]{1,0:T(8,128)(2,1)S(1)}, bf16[128,1280]{1,0:T(8,128)(2,1)S(1)}, u32[]{:S(2)}, u32[]{:S(2)}) collective-permute-start(bf16[128,1280]{1,0:T(8,128)(2,1)S(1)} %shard_map.152), channel_id=1, source_target_pairs={{4,0},{8,4},{12,8},{0,12},{5,1},{9,5},{13,9},{1,13},{6,2},{10,6},{... | collective-permute-start | bytes 983048 | tf_op jit(solution)/shard_map/ppermute | solution.py:388
  34.5 0.6 collective-permute-done.6.refs_10_.array_ref
  35.1 0.3 collective-permute-start.10
  35.4 0.0 collective-permute-done.7.refs_11_.array_ref.refs_10_
  35.4 1.9 %collective-permute-start.11 = (bf16[128,1280]{1,0:T(8,128)(2,1)S(1)}, bf16[128,1280]{1,0:T(8,128)(2,1)S(1)}, u32[]{:S(2)}, u32[]{:S(2)}) collective-permute-start(bf16[128,1280]{1,0:T(8,128)(2,1)S(1)} %shard_map.155), channel_id=1, source_target_pairs={{1,0},{2,1},{3,2},{0,3},{5,4},{6,5},{7,6},{4,7},{9,8},{10,9},{11,1... | collective-permute-start | bytes 983048 | tf_op jit(solution)/shard_map/ppermute | solution.py:388
  37.4 0.0 collective-permute-done.8.refs_12_.array_ref.refs_11_
  37.4 0.1 collective-permute-start.12
  37.5 3.0 %shard_map.151 = (bf16[2,256,640]{2,1,0:T(8,128)(2,1)S(1)}, bf16[2,640,256]{2,1,0:T(8,128)(2,1)S(1)}) custom-call(f32[640,256]{1,0:T(8,128)S(1)} %get-tuple-element.41.refs_0_, bf16[640,1280]{1,0:T(8,128)(2,1)S(1)} %get-tuple-element.38.refs_1_.refs_5_, bf16[640,1280]{1,0:T(8,128)(2,1)S(1)} %get-tuple-element.42.refs_2_.refs_6_, ...), custom_call_target="tpu_custom_call" | custom-call | flops 1677721600 | bytes 8388608 | tf_op jit(solution)/shard_map/pallas_call | solution.py:59
  40.5 1.6 %collective-permute-done.9.refs_9_ = bf16[128,1280]{1,0:T(8,128)(2,1)S(1)} collective-permute-done((bf16[128,1280]{1,0:T(8,128)(2,1)S(1)}, bf16[128,1280]{1,0:T(8,128)(2,1)S(1)}, u32[]{:S(2)}, u32[]{:S(2)}) %collective-permute-start.9) | collective-permute-done | bytes 327712 | tf_op jit(solution)/shard_map/ppermute | solution.py:388
  42.0 3.7 %collective-permute-done.10.refs_10_ = bf16[128,1280]{1,0:T(8,128)(2,1)S(1)} collective-permute-done((bf16[128,1280]{1,0:T(8,128)(2,1)S(1)}, bf16[128,1280]{1,0:T(8,128)(2,1)S(1)}, u32[]{:S(2)}, u32[]{:S(2)}) %collective-permute-start.10) | collective-permute-done | bytes 327712 | tf_op jit(solution)/shard_map/ppermute | solution.py:388
  45.7 2.3 %shard_map.154.refs_2_ = bf16[2,128,640]{2,1,0:T(8,128)(2,1)S(1)} custom-call(f32[640,256]{1,0:T(8,128)S(1)} %get-tuple-element.41.refs_0_, bf16[640,1280]{1,0:T(8,128)(2,1)S(1)} %get-tuple-element.38.refs_1_.refs_5_, bf16[640,1280]{1,0:T(8,128)(2,1)S(1)} %get-tuple-element.42.refs_2_.refs_6_, bf16[64,1280]{1,0:T(8,128)(2,1)S(1)} %get-tuple-element.43.refs_3_, ...), custom_call_target="tpu_custom_call" | custom-call | flops 838860800 | bytes 5439488 | tf_op jit(solution)/shard_map/pallas_call | solution.py:59
  48.0 0.0 collective-permute-done.11.refs_7_
  48.0 0.0 collective-permute-done.12.refs_8_
  48.0 0.0 copy-start.3
  48.1 0.0 copy-start
  48.1 0.0 copy-start.1
  48.1 0.0 copy-start.2
  48.1 2.4 %shard_map.157 = (f32[128,1280]{1,0:T(8,128)S(1)}, bf16[128,1280]{1,0:T(8,128)(2,1)S(1)}) custom-call(bf16[2,128,640]{2,1,0:T(8,128)(2,1)S(1)} %get-tuple-element.49.refs_0_, bf16[2,256,640]{2,1,0:T(8,128)(2,1)S(1)} %get-tuple-element.50.refs_1_, bf16[2,128,640]{2,1,0:T(8,128)(2,1)S(1)} %shard_map.154.refs_2_, ...), custom_call_target="tpu_custom_call" | custom-call | flops 1006632960 | bytes 9175040 | tf_op jit(solution)/shard_map/pallas_call | solution.py:59
  50.5 1.1 %collective-permute-start.13 = (bf16[128,1280]{1,0:T(8,128)(2,1)S(1)}, bf16[128,1280]{1,0:T(8,128)(2,1)S(1)}, u32[]{:S(2)}, u32[]{:S(2)}) collective-permute-start(bf16[128,1280]{1,0:T(8,128)(2,1)S(1)} %get-tuple-element.62), channel_id=1, source_target_pairs={{0,16},{16,0},{1,17},{17,1},{2,18},{18,2},{3,19},{19,3},{4,20},{20... | collective-permute-start | bytes 983048 | tf_op jit(solution)/shard_map/ppermute | solution.py:392
  51.6 0.0 copy-done.3
  51.6 1.2 %collective-permute-done.13.refs_3_ = bf16[128,1280]{1,0:T(8,128)(2,1)S(1)} collective-permute-done((bf16[128,1280]{1,0:T(8,128)(2,1)S(1)}, bf16[128,1280]{1,0:T(8,128)(2,1)S(1)}, u32[]{:S(2)}, u32[]{:S(2)}) %collective-permute-start.13) | collective-permute-done | bytes 327712 | tf_op jit(solution)/shard_map/ppermute | solution.py:392
  52.9 0.0 copy-done
  52.9 0.0 copy-done.1
  52.9 0.0 copy-done.2
  52.9 1.8 %shard_map.158 = f32[128,64]{1,0:T(8,128)S(1)} custom-call(f32[64,1280]{1,0:T(8,128)S(1)} %get-tuple-element.37.refs_0_, f32[64,1280]{1,0:T(8,128)S(1)} %get-tuple-element.40.refs_1_, f32[128,1280]{1,0:T(8,128)S(1)} %get-tuple-element.61.refs_2_, bf16[128,1280]{1,0:T(8,128)(2,1)S(1)} %collective-permute-done.13.refs_3_, ...), custom_call_target="tpu_custom_call" | custom-call | flops 419430400 | bytes 5103236 | tf_op jit(solution)/shard_map/pallas_call | solution.py:59
  54.6 23.0 %all_to_all.11 = f32[128,1,64]{2,1,0:T(1,128)S(1)} all-to-all(f32[128,1,64]{2,1,0:T(1,128)S(1)} %bitcast.13), channel_id=1, replica_groups=mesh['z'=8,'core'=2,'y'=4,'x'=4] {'z','y','x'}, dimensions={0} | all-to-all | bytes 65536 | tf_op jit(solution)/shard_map/all_to_all | solution.py:568
  77.7 0.7 shard_map.159
  (7 shorter events, 0.2 us)
Async XLA Ops:
  0.0 22.6 %collective-permute-start.4 = (bf16[640,1280]{1,0:T(8,128)(2,1)}, bf16[640,1280]{1,0:T(8,128)(2,1)S(1)}, u32[]{:S(2)}, u32[]{:S(2)}) collective-permute-start(bf16[640,1280]{1,0:T(8,128)(2,1)} %bitcast.17), channel_id=1, source_target_pairs={{0,16},{16,0},{1,17},{17,1},{2,18},{18,2},{3,19},{19,3},{4,20},{20... | collective-permute-start | bytes 4915208 | tf_op jit(solution)/shard_map/ppermute | solution.py:392
  4.4 8.8 %collective-permute-start = (bf16[128,1280]{1,0:T(8,128)(2,1)S(1)}, bf16[128,1280]{1,0:T(8,128)(2,1)S(1)}, u32[]{:S(2)}, u32[]{:S(2)}) collective-permute-start(bf16[128,1280]{1,0:T(8,128)(2,1)S(1)} %get-tuple-element.34), channel_id=1, source_target_pairs={{0,3},{1,17},{2,1},{3,19},{4,20},{5,4},{6,22},{7,6},{8,11},{9,25},... | collective-permute-start | bytes 983048 | tf_op jit(solution)/shard_map/ppermute | solution.py:414
  4.5 9.9 %collective-permute-start.1 = (bf16[128,1280]{1,0:T(8,128)(2,1)S(1)}, bf16[128,1280]{1,0:T(8,128)(2,1)S(1)}, u32[]{:S(2)}, u32[]{:S(2)}) collective-permute-start(bf16[128,1280]{1,0:T(8,128)(2,1)S(1)} %get-tuple-element.34), channel_id=1, source_target_pairs={{0,1},{1,19},{2,3},{3,17},{4,22},{5,6},{6,20},{7,4},{8,9},{9,27},{... | collective-permute-start | bytes 983048 | tf_op jit(solution)/shard_map/ppermute | solution.py:414
  5.9 11.4 %collective-permute-start.2 = (bf16[128,1280]{1,0:T(8,128)(2,1)S(1)}, bf16[128,1280]{1,0:T(8,128)(2,1)S(1)}, u32[]{:S(2)}, u32[]{:S(2)}) collective-permute-start(bf16[128,1280]{1,0:T(8,128)(2,1)S(1)} %get-tuple-element.35), channel_id=1, source_target_pairs={{0,12},{1,17},{2,14},{3,19},{4,20},{5,1},{6,22},{7,3},{8,4},{9,25}... | collective-permute-start | bytes 983048 | tf_op jit(solution)/shard_map/ppermute | solution.py:414
  5.9 11.4 %collective-permute-start.3 = (bf16[128,1280]{1,0:T(8,128)(2,1)S(1)}, bf16[128,1280]{1,0:T(8,128)(2,1)S(1)}, u32[]{:S(2)}, u32[]{:S(2)}) collective-permute-start(bf16[128,1280]{1,0:T(8,128)(2,1)S(1)} %get-tuple-element.35), channel_id=1, source_target_pairs={{0,4},{1,25},{2,6},{3,27},{4,28},{5,9},{6,30},{7,11},{8,12},{9,17}... | collective-permute-start | bytes 983048 | tf_op jit(solution)/shard_map/ppermute | solution.py:414
  14.4 16.6 %collective-permute-start.5 = (bf16[256,1280]{1,0:T(8,128)(2,1)S(1)}, bf16[256,1280]{1,0:T(8,128)(2,1)S(1)}, u32[]{:S(2)}, u32[]{:S(2)}) collective-permute-start(bf16[256,1280]{1,0:T(8,128)(2,1)S(1)} %shard_map.146.refs_9_), channel_id=1, source_target_pairs={{4,0},{8,4},{12,8},{0,12},{5,1},{9,5},{13,9},{1,13},{6,2},{10,6},{... | collective-permute-start | bytes 1966088 | tf_op jit(solution)/shard_map/ppermute | solution.py:388
  17.3 17.8 %collective-permute-start.6 = (bf16[256,1280]{1,0:T(8,128)(2,1)S(1)}, bf16[256,1280]{1,0:T(8,128)(2,1)S(1)}, u32[]{:S(2)}, u32[]{:S(2)}) collective-permute-start(bf16[256,1280]{1,0:T(8,128)(2,1)S(1)} %shard_map.146.refs_9_), channel_id=1, source_target_pairs={{12,0},{0,4},{4,8},{8,12},{13,1},{1,5},{5,9},{9,13},{14,2},{2,6},{... | collective-permute-start | bytes 1966088 | tf_op jit(solution)/shard_map/ppermute | solution.py:388
  17.4 18.0 %collective-permute-start.7 = (bf16[256,1280]{1,0:T(8,128)(2,1)S(1)}, bf16[256,1280]{1,0:T(8,128)(2,1)S(1)}, u32[]{:S(2)}, u32[]{:S(2)}) collective-permute-start(bf16[256,1280]{1,0:T(8,128)(2,1)S(1)} %shard_map.147.refs_10_.refs_9_), channel_id=1, source_target_pairs={{1,0},{2,1},{3,2},{0,3},{5,4},{6,5},{7,6},{4,7},{9,8},{10,9},{11,1... | collective-permute-start | bytes 1966088 | tf_op jit(solution)/shard_map/ppermute | solution.py:388
  19.1 18.2 %collective-permute-start.8 = (bf16[256,1280]{1,0:T(8,128)(2,1)S(1)}, bf16[256,1280]{1,0:T(8,128)(2,1)S(1)}, u32[]{:S(2)}, u32[]{:S(2)}) collective-permute-start(bf16[256,1280]{1,0:T(8,128)(2,1)S(1)} %shard_map.147.refs_10_.refs_9_), channel_id=1, source_target_pairs={{3,0},{0,1},{1,2},{2,3},{7,4},{4,5},{5,6},{6,7},{11,8},{8,9},{9,10... | collective-permute-start | bytes 1966088 | tf_op jit(solution)/shard_map/ppermute | solution.py:388
  31.0 11.0 %collective-permute-start.9 = (bf16[128,1280]{1,0:T(8,128)(2,1)S(1)}, bf16[128,1280]{1,0:T(8,128)(2,1)S(1)}, u32[]{:S(2)}, u32[]{:S(2)}) collective-permute-start(bf16[128,1280]{1,0:T(8,128)(2,1)S(1)} %shard_map.152), channel_id=1, source_target_pairs={{4,0},{8,4},{12,8},{0,12},{5,1},{9,5},{13,9},{1,13},{6,2},{10,6},{... | collective-permute-start | bytes 983048 | tf_op jit(solution)/shard_map/ppermute | solution.py:388
  35.1 10.6 %collective-permute-start.10 = (bf16[128,1280]{1,0:T(8,128)(2,1)S(1)}, bf16[128,1280]{1,0:T(8,128)(2,1)S(1)}, u32[]{:S(2)}, u32[]{:S(2)}) collective-permute-start(bf16[128,1280]{1,0:T(8,128)(2,1)S(1)} %shard_map.153), channel_id=1, source_target_pairs={{12,0},{0,4},{4,8},{8,12},{13,1},{1,5},{5,9},{9,13},{14,2},{2,6},{... | collective-permute-start | bytes 983048 | tf_op jit(solution)/shard_map/ppermute | solution.py:388
  35.4 12.6 %collective-permute-start.11 = (bf16[128,1280]{1,0:T(8,128)(2,1)S(1)}, bf16[128,1280]{1,0:T(8,128)(2,1)S(1)}, u32[]{:S(2)}, u32[]{:S(2)}) collective-permute-start(bf16[128,1280]{1,0:T(8,128)(2,1)S(1)} %shard_map.155), channel_id=1, source_target_pairs={{1,0},{2,1},{3,2},{0,3},{5,4},{6,5},{7,6},{4,7},{9,8},{10,9},{11,1... | collective-permute-start | bytes 983048 | tf_op jit(solution)/shard_map/ppermute | solution.py:388
  37.4 10.6 %collective-permute-start.12 = (bf16[128,1280]{1,0:T(8,128)(2,1)S(1)}, bf16[128,1280]{1,0:T(8,128)(2,1)S(1)}, u32[]{:S(2)}, u32[]{:S(2)}) collective-permute-start(bf16[128,1280]{1,0:T(8,128)(2,1)S(1)} %shard_map.156), channel_id=1, source_target_pairs={{3,0},{0,1},{1,2},{2,3},{7,4},{4,5},{5,6},{6,7},{11,8},{8,9},{9,10... | collective-permute-start | bytes 983048 | tf_op jit(solution)/shard_map/ppermute | solution.py:388
  48.0 3.6 %copy-start.3 = (f32[1280]{0:T(1024)S(1)}, f32[1280]{0:T(1024)}, u32[]{:S(2)}) copy-start(f32[1280]{0:T(1024)} %param.19) | copy-start | bytes 15364
  48.1 4.8 %copy-start = (bf16[1280,1280]{1,0:T(8,128)(2,1)S(1)}, bf16[1280,1280]{1,0:T(8,128)(2,1)}, u32[]{:S(2)}) copy-start(bf16[1280,1280]{1,0:T(8,128)(2,1)} %refs_8_.1) | copy-start | bytes 9830404
  48.1 4.8 %copy-start.1 = (bf16[1280,33]{0,1:T(8,128)(2,1)S(1)}, bf16[1280,33]{0,1:T(8,128)(2,1)}, u32[]{:S(2)}) copy-start(bf16[1280,33]{0,1:T(8,128)(2,1)} %param.21) | copy-start | bytes 253444
  48.1 4.8 %copy-start.2 = (f32[33]{0:T(128)S(1)}, f32[33]{0:T(128)}, u32[]{:S(2)}) copy-start(f32[33]{0:T(128)} %param.22) | copy-start | bytes 400
  50.5 2.3 %collective-permute-start.13 = (bf16[128,1280]{1,0:T(8,128)(2,1)S(1)}, bf16[128,1280]{1,0:T(8,128)(2,1)S(1)}, u32[]{:S(2)}, u32[]{:S(2)}) collective-permute-start(bf16[128,1280]{1,0:T(8,128)(2,1)S(1)} %get-tuple-element.62), channel_id=1, source_target_pairs={{0,16},{16,0},{1,17},{17,1},{2,18},{18,2},{3,19},{19,3},{4,20},{20... | collective-permute-start | bytes 983048 | tf_op jit(solution)/shard_map/ppermute | solution.py:392

commit v15 on v14

--- a/solution.py
+++ b/solution.py
@@ -496,29 +496,29 @@
 
     states = hidden_states[0]
     key_block, value_block = pack(jnp.transpose(w_qkv[:, 0, :]), output_weight[:, 0, :])
-    key_low = gather_line(key_block, "x", False)
-    value_low = gather_line(value_block, "y", False)
-    key_high = gather_line(key_block, "x", True)
-    value_high = gather_line(value_block, "y", True)
+    key_low = gather_line(key_block, "y", False)
+    value_low = gather_line(value_block, "x", False)
+    key_high = gather_line(key_block, "y", True)
+    value_high = gather_line(value_block, "x", True)
     states_other = swap(states)
     key_line = join(key_low, key_high)
-    key_ahead = pull(key_line, "y", 1)
-    key_behind = pull(key_line, "y", 3)
+    key_ahead = pull(key_line, "x", 1)
+    key_behind = pull(key_line, "x", 3)
     value_line = join(value_low, value_high)
-    value_ahead = pull(value_line, "x", 1)
-    value_behind = pull(value_line, "x", 3)
+    value_ahead = pull(value_line, "y", 1)
+    value_behind = pull(value_line, "y", 3)
     mine = prepare_call(True, after(states, key_line, value_line))
     other = prepare_call(False, after(states_other, mine[0]))
     ready = (mine, other)
     own_probs, own_values = attend_call(ready, (key_line,), (value_line,))
     rows = key_line.shape[0]
     key_far = (
-        pull(part(after(key_ahead, own_probs), 0, rows // 2), "y", 1),
-        pull(part(after(key_behind, own_probs), rows // 2, rows), "y", 3),
+        pull(part(after(key_ahead, own_probs), 0, rows // 2), "x", 1),
+        pull(part(after(key_behind, own_probs), rows // 2, rows), "x", 3),
     )
     value_far = (
-        pull(part(after(value_ahead, own_probs), 0, rows // 2), "x", 1),
-        pull(part(after(value_behind, own_probs), rows // 2, rows), "x", 3),
+        pull(part(after(value_ahead, own_probs), 0, rows // 2), "y", 1),
+        pull(part(after(value_behind, own_probs), rows // 2, rows), "y", 3),
     )
     near_probs, near_values = attend_call(
         ready, (key_ahead, key_behind), (value_ahead, value_behind)

time: 78.6 us -> 78.6 us (level)
  no operation moved by 1% of the time
where the time goes in v15:
time: 78.6 us; the launch traced here: 78.4 us
  blocking collectives  22.9 us (29%)
  Pallas kernels  20.3 us (26%)
  starting transfers between devices  20 us (25%)
  waiting for transfers between devices  15 us (19%)
    all_to_all x1, blocking collectives, on_device(): arrived = lax.all_to_all(placed, ('z', 'y', 'x'), 0, 0, tiled=True)  22.9 us
    pallas_call x15, Pallas kernels, call(): pl.pallas_call(kernel, out_shape=outs, in_specs=[IN_PLACE] * n_any + [ON_...  20.3 us
    ppermute x8, starting transfers between devices, pull(): lax.ppermute(array, axis, [((i + offset) % size, i) for i in range(size)])  10.6 us
    ppermute x8, waiting for transfers between devices, pull(): lax.ppermute(array, axis, [((i + offset) % size, i) for i in range(size)])  8.94 us
    ppermute x4, starting transfers between devices, gather_line(): return lax.ppermute(block, ('core', 'y', 'x'), pairs)  4.99 us
    ppermute x4, waiting for transfers between devices, gather_line(): return lax.ppermute(block, ('core', 'y', 'x'), pairs)  4.78 us
    ppermute x2, starting transfers between devices, swap(): return lax.ppermute(array, 'core', [(0, 1), (1, 0)])  4.43 us
  transfers between devices with their start and end apart: 14, of which 7 were waited for; matrix products, arithmetic and copies ran while one was open for 0% of the time, Pallas kernels for 20%

profile of v15, /device:TPU:1, one launch (start us, length us, event | category | flops | bytes accessed | tf_op | source)
XLA Modules:
  0.0 78.4 jit_solution(6331011735396054816)
XLA Ops:
  0.0 3.2 %collective-permute-start.4 = (bf16[640,1280]{1,0:T(8,128)(2,1)}, bf16[640,1280]{1,0:T(8,128)(2,1)S(1)}, u32[]{:S(2)}, u32[]{:S(2)}) collective-permute-start(bf16[640,1280]{1,0:T(8,128)(2,1)} %bitcast.17), channel_id=1, source_target_pairs={{0,16},{16,0},{1,17},{17,1},{2,18},{18,2},{3,19},{19,3},{4,20},{20... | collective-permute-start | bytes 4915208 | tf_op jit(solution)/shard_map/ppermute | solution.py:392
  3.2 1.1 %shard_map.145 = (bf16[128,1280]{1,0:T(8,128)(2,1)S(1)}, bf16[128,1280]{1,0:T(8,128)(2,1)S(1)}) custom-call(bf16[192,1280]{1,0:T(8,128)(2,1)} %bitcast.19, bf16[64,1280]{1,0:T(8,128)(2,1)} %bitcast.22), custom_call_target="tpu_custom_call" | custom-call | bytes 1310720 | tf_op jit(solution)/shard_map/pallas_call | solution.py:59
  4.4 0.1 collective-permute-start
  4.5 1.5 %collective-permute-start.1 = (bf16[128,1280]{1,0:T(8,128)(2,1)S(1)}, bf16[128,1280]{1,0:T(8,128)(2,1)S(1)}, u32[]{:S(2)}, u32[]{:S(2)}) collective-permute-start(bf16[128,1280]{1,0:T(8,128)(2,1)S(1)} %get-tuple-element.34), channel_id=1, source_target_pairs={{0,4},{1,25},{2,6},{3,27},{4,28},{5,9},{6,30},{7,11},{8,12},{9,17}... | collective-permute-start | bytes 983048 | tf_op jit(solution)/shard_map/ppermute | solution.py:414
  6.0 0.0 collective-permute-start.2
  6.0 3.4 %collective-permute-start.3 = (bf16[128,1280]{1,0:T(8,128)(2,1)S(1)}, bf16[128,1280]{1,0:T(8,128)(2,1)S(1)}, u32[]{:S(2)}, u32[]{:S(2)}) collective-permute-start(bf16[128,1280]{1,0:T(8,128)(2,1)S(1)} %get-tuple-element.35), channel_id=1, source_target_pairs={{0,1},{1,19},{2,3},{3,17},{4,22},{5,6},{6,20},{7,4},{8,9},{9,27},{... | collective-permute-start | bytes 983048 | tf_op jit(solution)/shard_map/ppermute | solution.py:414
  9.4 3.7 %collective-permute-done.low_ref = bf16[128,1280]{1,0:T(8,128)(2,1)S(1)} collective-permute-done((bf16[128,1280]{1,0:T(8,128)(2,1)S(1)}, bf16[128,1280]{1,0:T(8,128)(2,1)S(1)}, u32[]{:S(2)}, u32[]{:S(2)}) %collective-permute-start) | collective-permute-done | bytes 327712 | tf_op jit(solution)/shard_map/ppermute | solution.py:414
  13.0 1.1 %collective-permute-done.1.high_ref = bf16[128,1280]{1,0:T(8,128)(2,1)S(1)} collective-permute-done((bf16[128,1280]{1,0:T(8,128)(2,1)S(1)}, bf16[128,1280]{1,0:T(8,128)(2,1)S(1)}, u32[]{:S(2)}, u32[]{:S(2)}) %collective-permute-start.1) | collective-permute-done | bytes 327712 | tf_op jit(solution)/shard_map/ppermute | solution.py:414
  14.2 3.1 %collective-permute-start.5 = (bf16[256,1280]{1,0:T(8,128)(2,1)S(1)}, bf16[256,1280]{1,0:T(8,128)(2,1)S(1)}, u32[]{:S(2)}, u32[]{:S(2)}) collective-permute-start(bf16[256,1280]{1,0:T(8,128)(2,1)S(1)} %shard_map.146.refs_9_), channel_id=1, source_target_pairs={{1,0},{2,1},{3,2},{0,3},{5,4},{6,5},{7,6},{4,7},{9,8},{10,9},{11,1... | collective-permute-start | bytes 1966088 | tf_op jit(solution)/shard_map/ppermute | solution.py:388
  17.3 0.0 collective-permute-start.6
  17.3 0.0 collective-permute-done.2.low_ref
  17.3 0.0 collective-permute-done.3.high_ref
  17.4 1.8 %collective-permute-start.7 = (bf16[256,1280]{1,0:T(8,128)(2,1)S(1)}, bf16[256,1280]{1,0:T(8,128)(2,1)S(1)}, u32[]{:S(2)}, u32[]{:S(2)}) collective-permute-start(bf16[256,1280]{1,0:T(8,128)(2,1)S(1)} %shard_map.147.refs_10_.refs_9_), channel_id=1, source_target_pairs={{4,0},{8,4},{12,8},{0,12},{5,1},{9,5},{13,9},{1,13},{6,2},{10,6},{... | collective-permute-start | bytes 1966088 | tf_op jit(solution)/shard_map/ppermute | solution.py:388
  19.1 0.0 collective-permute-start.8
  19.1 3.5 %shard_map.148 = (bf16[640,1280]{1,0:T(8,128)(2,1)S(1)}, bf16[64,1280]{1,0:T(8,128)(2,1)S(1)}, f32[64,1280]{1,0:T(8,128)S(1)}, f32[64,256]{1,0:T(8,128)S(1)}, s3...) custom-call(s32[256]{0:T(256)} %refs_0_.3, s32[24]{0:T(128)} %refs_1_.3, s32[256]{0:T(256)} %refs_2_.3, s32[64,256]{1,0:T(8,128)} %bitcast.20, ...), custom_call_target="tpu_custom_call" | custom-call | flops 217907200 | bytes 5639264 | tf_op jit(solution)/shard_map/pallas_call | solution.py:59
  22.6 0.0 collective-permute-done.4.refs_7_
  22.6 2.8 %shard_map.149 = (bf16[640,1280]{1,0:T(8,128)(2,1)S(1)}, bf16[64,1280]{1,0:T(8,128)(2,1)S(1)}, f32[64,1280]{1,0:T(8,128)S(1)}, f32[64,256]{1,0:T(8,128)S(1)}, s32[64,128]{1,0:T(8,128)S(1)}) custom-call(s32[256]{0:T(256)} %refs_0_.3, s32[24]{0:T(128)} %refs_1_.3, s32[256]{0:T(256)} %refs_2_.3, s32[64,256]{1,0:T(8,128)} %bitcast.21, s32[24,640]{1,0:T(8,128)} %refs_4_.3, ...), custom_call_target="tpu_custom_call" | custom-call | flops 217907200 | bytes 4328544 | tf_op jit(solution)/shard_map/pallas_call | solution.py:59
  25.4 2.5 %shard_map.150 = (bf16[2,128,640]{2,1,0:T(8,128)(2,1)S(1)}, bf16[2,640,128]{2,1,0:T(8,128)(2,1)S(1)}) custom-call(f32[640,256]{1,0:T(8,128)S(1)} %get-tuple-element.41.refs_0_, bf16[640,1280]{1,0:T(8,128)(2,1)S(1)} %get-tuple-element.38.refs_1_.refs_5_, bf16[640,1280]{1,0:T(8,128)(2,1)S(1)} %get-tuple-element.42.refs_2_.refs_6_, ...), custom_call_target="tpu_custom_call" | custom-call | flops 838860800 | bytes 6422528 | tf_op jit(solution)/shard_map/pallas_call | solution.py:59
  27.9 3.2 %collective-permute-done.5.refs_9_.array_ref = bf16[256,1280]{1,0:T(8,128)(2,1)S(1)} collective-permute-done((bf16[256,1280]{1,0:T(8,128)(2,1)S(1)}, bf16[256,1280]{1,0:T(8,128)(2,1)S(1)}, u32[]{:S(2)}, u32[]{:S(2)}) %collective-permute-start.5) | collective-permute-done | bytes 655392 | tf_op jit(solution)/shard_map/ppermute | solution.py:388
  31.2 3.5 %collective-permute-start.9 = (bf16[128,1280]{1,0:T(8,128)(2,1)S(1)}, bf16[128,1280]{1,0:T(8,128)(2,1)S(1)}, u32[]{:S(2)}, u32[]{:S(2)}) collective-permute-start(bf16[128,1280]{1,0:T(8,128)(2,1)S(1)} %shard_map.152), channel_id=1, source_target_pairs={{1,0},{2,1},{3,2},{0,3},{5,4},{6,5},{7,6},{4,7},{9,8},{10,9},{11,1... | collective-permute-start | bytes 983048 | tf_op jit(solution)/shard_map/ppermute | solution.py:388
  34.6 0.5 collective-permute-done.6.refs_10_.array_ref
  35.2 0.3 collective-permute-start.10
  35.5 0.0 collective-permute-done.7.refs_11_.array_ref.refs_10_
  35.5 1.9 %collective-permute-start.11 = (bf16[128,1280]{1,0:T(8,128)(2,1)S(1)}, bf16[128,1280]{1,0:T(8,128)(2,1)S(1)}, u32[]{:S(2)}, u32[]{:S(2)}) collective-permute-start(bf16[128,1280]{1,0:T(8,128)(2,1)S(1)} %shard_map.155), channel_id=1, source_target_pairs={{4,0},{8,4},{12,8},{0,12},{5,1},{9,5},{13,9},{1,13},{6,2},{10,6},{... | collective-permute-start | bytes 983048 | tf_op jit(solution)/shard_map/ppermute | solution.py:388
  37.4 0.0 collective-permute-done.8.refs_12_.array_ref.refs_11_
  37.4 0.1 collective-permute-start.12
  37.5 3.0 %shard_map.151 = (bf16[2,256,640]{2,1,0:T(8,128)(2,1)S(1)}, bf16[2,640,256]{2,1,0:T(8,128)(2,1)S(1)}) custom-call(f32[640,256]{1,0:T(8,128)S(1)} %get-tuple-element.41.refs_0_, bf16[640,1280]{1,0:T(8,128)(2,1)S(1)} %get-tuple-element.38.refs_1_.refs_5_, bf16[640,1280]{1,0:T(8,128)(2,1)S(1)} %get-tuple-element.42.refs_2_.refs_6_, ...), custom_call_target="tpu_custom_call" | custom-call | flops 1677721600 | bytes 8388608 | tf_op jit(solution)/shard_map/pallas_call | solution.py:59
  40.5 1.5 %collective-permute-done.9.refs_9_ = bf16[128,1280]{1,0:T(8,128)(2,1)S(1)} collective-permute-done((bf16[128,1280]{1,0:T(8,128)(2,1)S(1)}, bf16[128,1280]{1,0:T(8,128)(2,1)S(1)}, u32[]{:S(2)}, u32[]{:S(2)}) %collective-permute-start.9) | collective-permute-done | bytes 327712 | tf_op jit(solution)/shard_map/ppermute | solution.py:388
  42.0 3.7 %collective-permute-done.10.refs_10_ = bf16[128,1280]{1,0:T(8,128)(2,1)S(1)} collective-permute-done((bf16[128,1280]{1,0:T(8,128)(2,1)S(1)}, bf16[128,1280]{1,0:T(8,128)(2,1)S(1)}, u32[]{:S(2)}, u32[]{:S(2)}) %collective-permute-start.10) | collective-permute-done | bytes 327712 | tf_op jit(solution)/shard_map/ppermute | solution.py:388
  45.7 2.3 %shard_map.154.refs_2_ = bf16[2,128,640]{2,1,0:T(8,128)(2,1)S(1)} custom-call(f32[640,256]{1,0:T(8,128)S(1)} %get-tuple-element.41.refs_0_, bf16[640,1280]{1,0:T(8,128)(2,1)S(1)} %get-tuple-element.38.refs_1_.refs_5_, bf16[640,1280]{1,0:T(8,128)(2,1)S(1)} %get-tuple-element.42.refs_2_.refs_6_, bf16[64,1280]{1,0:T(8,128)(2,1)S(1)} %get-tuple-element.43.refs_3_, ...), custom_call_target="tpu_custom_call" | custom-call | flops 838860800 | bytes 5439488 | tf_op jit(solution)/shard_map/pallas_call | solution.py:59
  48.0 0.0 collective-permute-done.11.refs_7_
  48.0 0.0 collective-permute-done.12.refs_8_
  48.0 0.0 copy-start.3
  48.0 0.0 copy-start
  48.1 0.0 copy-start.1
  48.1 0.0 copy-start.2
  48.1 2.4 %shard_map.157 = (f32[128,1280]{1,0:T(8,128)S(1)}, bf16[128,1280]{1,0:T(8,128)(2,1)S(1)}) custom-call(bf16[2,128,640]{2,1,0:T(8,128)(2,1)S(1)} %get-tuple-element.49.refs_0_, bf16[2,256,640]{2,1,0:T(8,128)(2,1)S(1)} %get-tuple-element.50.refs_1_, bf16[2,128,640]{2,1,0:T(8,128)(2,1)S(1)} %shard_map.154.refs_2_, ...), custom_call_target="tpu_custom_call" | custom-call | flops 1006632960 | bytes 9175040 | tf_op jit(solution)/shard_map/pallas_call | solution.py:59
  50.5 1.2 %collective-permute-start.13 = (bf16[128,1280]{1,0:T(8,128)(2,1)S(1)}, bf16[128,1280]{1,0:T(8,128)(2,1)S(1)}, u32[]{:S(2)}, u32[]{:S(2)}) collective-permute-start(bf16[128,1280]{1,0:T(8,128)(2,1)S(1)} %get-tuple-element.62), channel_id=1, source_target_pairs={{0,16},{16,0},{1,17},{17,1},{2,18},{18,2},{3,19},{19,3},{4,20},{20... | collective-permute-start | bytes 983048 | tf_op jit(solution)/shard_map/ppermute | solution.py:392
  51.7 0.0 copy-done.3
  51.7 1.2 %collective-permute-done.13.refs_3_ = bf16[128,1280]{1,0:T(8,128)(2,1)S(1)} collective-permute-done((bf16[128,1280]{1,0:T(8,128)(2,1)S(1)}, bf16[128,1280]{1,0:T(8,128)(2,1)S(1)}, u32[]{:S(2)}, u32[]{:S(2)}) %collective-permute-start.13) | collective-permute-done | bytes 327712 | tf_op jit(solution)/shard_map/ppermute | solution.py:392
  52.9 0.0 copy-done
  53.0 0.0 copy-done.1
  53.0 0.0 copy-done.2
  53.0 1.8 %shard_map.158 = f32[128,64]{1,0:T(8,128)S(1)} custom-call(f32[64,1280]{1,0:T(8,128)S(1)} %get-tuple-element.37.refs_0_, f32[64,1280]{1,0:T(8,128)S(1)} %get-tuple-element.40.refs_1_, f32[128,1280]{1,0:T(8,128)S(1)} %get-tuple-element.61.refs_2_, bf16[128,1280]{1,0:T(8,128)(2,1)S(1)} %collective-permute-done.13.refs_3_, ...), custom_call_target="tpu_custom_call" | custom-call | flops 419430400 | bytes 5103236 | tf_op jit(solution)/shard_map/pallas_call | solution.py:59
  54.7 22.9 %all_to_all.11 = f32[128,1,64]{2,1,0:T(1,128)S(1)} all-to-all(f32[128,1,64]{2,1,0:T(1,128)S(1)} %bitcast.13), channel_id=1, replica_groups=mesh['z'=8,'core'=2,'y'=4,'x'=4] {'z','y','x'}, dimensions={0} | all-to-all | bytes 65536 | tf_op jit(solution)/shard_map/all_to_all | solution.py:568
  77.7 0.7 shard_map.159
  (7 shorter events, 0.2 us)
Async XLA Ops:
  0.0 22.6 %collective-permute-start.4 = (bf16[640,1280]{1,0:T(8,128)(2,1)}, bf16[640,1280]{1,0:T(8,128)(2,1)S(1)}, u32[]{:S(2)}, u32[]{:S(2)}) collective-permute-start(bf16[640,1280]{1,0:T(8,128)(2,1)} %bitcast.17), channel_id=1, source_target_pairs={{0,16},{16,0},{1,17},{17,1},{2,18},{18,2},{3,19},{19,3},{4,20},{20... | collective-permute-start | bytes 4915208 | tf_op jit(solution)/shard_map/ppermute | solution.py:392
  4.4 8.6 %collective-permute-start = (bf16[128,1280]{1,0:T(8,128)(2,1)S(1)}, bf16[128,1280]{1,0:T(8,128)(2,1)S(1)}, u32[]{:S(2)}, u32[]{:S(2)}) collective-permute-start(bf16[128,1280]{1,0:T(8,128)(2,1)S(1)} %get-tuple-element.34), channel_id=1, source_target_pairs={{0,12},{1,17},{2,14},{3,19},{4,20},{5,1},{6,22},{7,3},{8,4},{9,25}... | collective-permute-start | bytes 983048 | tf_op jit(solution)/shard_map/ppermute | solution.py:414
  4.5 9.7 %collective-permute-start.1 = (bf16[128,1280]{1,0:T(8,128)(2,1)S(1)}, bf16[128,1280]{1,0:T(8,128)(2,1)S(1)}, u32[]{:S(2)}, u32[]{:S(2)}) collective-permute-start(bf16[128,1280]{1,0:T(8,128)(2,1)S(1)} %get-tuple-element.34), channel_id=1, source_target_pairs={{0,4},{1,25},{2,6},{3,27},{4,28},{5,9},{6,30},{7,11},{8,12},{9,17}... | collective-permute-start | bytes 983048 | tf_op jit(solution)/shard_map/ppermute | solution.py:414
  6.0 11.3 %collective-permute-start.2 = (bf16[128,1280]{1,0:T(8,128)(2,1)S(1)}, bf16[128,1280]{1,0:T(8,128)(2,1)S(1)}, u32[]{:S(2)}, u32[]{:S(2)}) collective-permute-start(bf16[128,1280]{1,0:T(8,128)(2,1)S(1)} %get-tuple-element.35), channel_id=1, source_target_pairs={{0,3},{1,17},{2,1},{3,19},{4,20},{5,4},{6,22},{7,6},{8,11},{9,25},... | collective-permute-start | bytes 983048 | tf_op jit(solution)/shard_map/ppermute | solution.py:414
  6.0 11.3 %collective-permute-start.3 = (bf16[128,1280]{1,0:T(8,128)(2,1)S(1)}, bf16[128,1280]{1,0:T(8,128)(2,1)S(1)}, u32[]{:S(2)}, u32[]{:S(2)}) collective-permute-start(bf16[128,1280]{1,0:T(8,128)(2,1)S(1)} %get-tuple-element.35), channel_id=1, source_target_pairs={{0,1},{1,19},{2,3},{3,17},{4,22},{5,6},{6,20},{7,4},{8,9},{9,27},{... | collective-permute-start | bytes 983048 | tf_op jit(solution)/shard_map/ppermute | solution.py:414
  14.2 16.9 %collective-permute-start.5 = (bf16[256,1280]{1,0:T(8,128)(2,1)S(1)}, bf16[256,1280]{1,0:T(8,128)(2,1)S(1)}, u32[]{:S(2)}, u32[]{:S(2)}) collective-permute-start(bf16[256,1280]{1,0:T(8,128)(2,1)S(1)} %shard_map.146.refs_9_), channel_id=1, source_target_pairs={{1,0},{2,1},{3,2},{0,3},{5,4},{6,5},{7,6},{4,7},{9,8},{10,9},{11,1... | collective-permute-start | bytes 1966088 | tf_op jit(solution)/shard_map/ppermute | solution.py:388
  17.3 17.9 %collective-permute-start.6 = (bf16[256,1280]{1,0:T(8,128)(2,1)S(1)}, bf16[256,1280]{1,0:T(8,128)(2,1)S(1)}, u32[]{:S(2)}, u32[]{:S(2)}) collective-permute-start(bf16[256,1280]{1,0:T(8,128)(2,1)S(1)} %shard_map.146.refs_9_), channel_id=1, source_target_pairs={{3,0},{0,1},{1,2},{2,3},{7,4},{4,5},{5,6},{6,7},{11,8},{8,9},{9,10... | collective-permute-start | bytes 1966088 | tf_op jit(solution)/shard_map/ppermute | solution.py:388
  17.4 18.1 %collective-permute-start.7 = (bf16[256,1280]{1,0:T(8,128)(2,1)S(1)}, bf16[256,1280]{1,0:T(8,128)(2,1)S(1)}, u32[]{:S(2)}, u32[]{:S(2)}) collective-permute-start(bf16[256,1280]{1,0:T(8,128)(2,1)S(1)} %shard_map.147.refs_10_.refs_9_), channel_id=1, source_target_pairs={{4,0},{8,4},{12,8},{0,12},{5,1},{9,5},{13,9},{1,13},{6,2},{10,6},{... | collective-permute-start | bytes 1966088 | tf_op jit(solution)/shard_map/ppermute | solution.py:388
  19.1 18.2 %collective-permute-start.8 = (bf16[256,1280]{1,0:T(8,128)(2,1)S(1)}, bf16[256,1280]{1,0:T(8,128)(2,1)S(1)}, u32[]{:S(2)}, u32[]{:S(2)}) collective-permute-start(bf16[256,1280]{1,0:T(8,128)(2,1)S(1)} %shard_map.147.refs_10_.refs_9_), channel_id=1, source_target_pairs={{12,0},{0,4},{4,8},{8,12},{13,1},{1,5},{5,9},{9,13},{14,2},{2,6},{... | collective-permute-start | bytes 1966088 | tf_op jit(solution)/shard_map/ppermute | solution.py:388
  31.2 10.9 %collective-permute-start.9 = (bf16[128,1280]{1,0:T(8,128)(2,1)S(1)}, bf16[128,1280]{1,0:T(8,128)(2,1)S(1)}, u32[]{:S(2)}, u32[]{:S(2)}) collective-permute-start(bf16[128,1280]{1,0:T(8,128)(2,1)S(1)} %shard_map.152), channel_id=1, source_target_pairs={{1,0},{2,1},{3,2},{0,3},{5,4},{6,5},{7,6},{4,7},{9,8},{10,9},{11,1... | collective-permute-start | bytes 983048 | tf_op jit(solution)/shard_map/ppermute | solution.py:388
  35.2 10.5 %collective-permute-start.10 = (bf16[128,1280]{1,0:T(8,128)(2,1)S(1)}, bf16[128,1280]{1,0:T(8,128)(2,1)S(1)}, u32[]{:S(2)}, u32[]{:S(2)}) collective-permute-start(bf16[128,1280]{1,0:T(8,128)(2,1)S(1)} %shard_map.153), channel_id=1, source_target_pairs={{3,0},{0,1},{1,2},{2,3},{7,4},{4,5},{5,6},{6,7},{11,8},{8,9},{9,10... | collective-permute-start | bytes 983048 | tf_op jit(solution)/shard_map/ppermute | solution.py:388
  35.5 12.5 %collective-permute-start.11 = (bf16[128,1280]{1,0:T(8,128)(2,1)S(1)}, bf16[128,1280]{1,0:T(8,128)(2,1)S(1)}, u32[]{:S(2)}, u32[]{:S(2)}) collective-permute-start(bf16[128,1280]{1,0:T(8,128)(2,1)S(1)} %shard_map.155), channel_id=1, source_target_pairs={{4,0},{8,4},{12,8},{0,12},{5,1},{9,5},{13,9},{1,13},{6,2},{10,6},{... | collective-permute-start | bytes 983048 | tf_op jit(solution)/shard_map/ppermute | solution.py:388
  37.4 10.6 %collective-permute-start.12 = (bf16[128,1280]{1,0:T(8,128)(2,1)S(1)}, bf16[128,1280]{1,0:T(8,128)(2,1)S(1)}, u32[]{:S(2)}, u32[]{:S(2)}) collective-permute-start(bf16[128,1280]{1,0:T(8,128)(2,1)S(1)} %shard_map.156), channel_id=1, source_target_pairs={{12,0},{0,4},{4,8},{8,12},{13,1},{1,5},{5,9},{9,13},{14,2},{2,6},{... | collective-permute-start | bytes 983048 | tf_op jit(solution)/shard_map/ppermute | solution.py:388
  48.0 3.7 %copy-start.3 = (f32[1280]{0:T(1024)S(1)}, f32[1280]{0:T(1024)}, u32[]{:S(2)}) copy-start(f32[1280]{0:T(1024)} %param.19) | copy-start | bytes 15364
  48.0 4.9 %copy-start = (bf16[1280,1280]{1,0:T(8,128)(2,1)S(1)}, bf16[1280,1280]{1,0:T(8,128)(2,1)}, u32[]{:S(2)}) copy-start(bf16[1280,1280]{1,0:T(8,128)(2,1)} %refs_8_.1) | copy-start | bytes 9830404
  48.1 4.9 %copy-start.1 = (bf16[1280,33]{0,1:T(8,128)(2,1)S(1)}, bf16[1280,33]{0,1:T(8,128)(2,1)}, u32[]{:S(2)}) copy-start(bf16[1280,33]{0,1:T(8,128)(2,1)} %param.21) | copy-start | bytes 253444
  48.1 4.9 %copy-start.2 = (f32[33]{0:T(128)S(1)}, f32[33]{0:T(128)}, u32[]{:S(2)}) copy-start(f32[33]{0:T(128)} %param.22) | copy-start | bytes 400
  50.5 2.4 %collective-permute-start.13 = (bf16[128,1280]{1,0:T(8,128)(2,1)S(1)}, bf16[128,1280]{1,0:T(8,128)(2,1)S(1)}, u32[]{:S(2)}, u32[]{:S(2)}) collective-permute-start(bf16[128,1280]{1,0:T(8,128)(2,1)S(1)} %get-tuple-element.62), channel_id=1, source_target_pairs={{0,16},{16,0},{1,17},{17,1},{2,18},{18,2},{3,19},{19,3},{4,20},{20... | collective-permute-start | bytes 983048 | tf_op jit(solution)/shard_map/ppermute | solution.py:392
